TPU v7x, 32 devices: a whole 2x2x4 slice. The times are simulated.
32 devices in a mesh: section: 4 (over z), st: 4 (over y, core), dp: 2 (over x).
Axes of the slice: x: 2, y: 2, z: 4, core: 2. Of those that a mesh axis runs over, the one named last changes fastest.
Arguments:
- saved_qkv: bfloat16 [4, 2, 3, 128, 48, 128], P('section', 'dp', None, None, 'st'), may hold values from -9 to 9
- positions: int32 [4, 2, 128], P('section', 'dp'), may hold values from 0 to 127, as said below
- w_out: bfloat16 [4, 6144, 6144], P('section', None, 'st'), may hold values from -0.078125 to 0.078125
- grad_out: bfloat16 [4, 2, 128, 6144], P('section', 'dp', None, 'st'), may hold values from -6 to 6
Outputs:
- grad_weight: bfloat16 [4, 6144, 6144], P('section', 'dp', 'st')
- upstream: bfloat16 [4, 2, 3, 128, 48, 128], P('section', 'dp', None, None, 'st')
Inputs may be any that keep to these rules, and one draw needn't show every extreme that they name: `positions`: each row holds every number 0 to 127 once.
All inputs are finite; a program needn't handle non-finite values.
Results may differ from a plain program's by a relative error of at most 0.0095.
Values may be sent and summed in bfloat16 or wider, within the bound.
No kernel may reach another device: no remote copies, remote signals or barrier semaphores. Data moves between devices by JAX's collectives and lax.ppermute only.
A program may use at most 128 MiB of HBM per device.

v0:
```python
import math

import jax
import jax.numpy as jnp
from jax import lax
from jax.sharding import PartitionSpec as P


def from_behind(value, axis, steps):
    count = lax.axis_size(axis)
    initial, last = (max(0, -steps), min(count, count - steps))
    return lax.ppermute(value, axis, [(source, source + steps) for source in range(initial, last)])


def local(saved_qkv, positions, w_out, grad_out):
    head_major = saved_qkv[0, 0]
    queries = head_major[0]
    key_rows = head_major[1]
    values = head_major[2]
    token_pos = positions[0, 0]
    inv_root = 1.0 / math.sqrt(queries.shape[-1])
    scores = (
        jnp.einsum("qhd,khd->hqk", queries, key_rows, preferred_element_type=jnp.float32) * inv_root
    )
    visible = token_pos[None, :] <= token_pos[:, None]
    scores = jnp.where(visible[None], scores, -1e30)
    highest = jnp.max(scores, axis=2, keepdims=True)
    exponent = jnp.exp(scores - highest)
    softmax_out = exponent / jnp.sum(exponent, axis=2, keepdims=True)
    weights_bf = softmax_out.astype(jnp.bfloat16)
    attended = jnp.einsum(
        "hqk,khd->qhd", weights_bf, values, preferred_element_type=jnp.float32
    ).astype(jnp.bfloat16)
    seq_len = attended.shape[0]
    flat_att = attended.reshape(seq_len, -1)
    full_grad = lax.all_gather(grad_out[0, 0], "st", axis=1, tiled=True)
    d_flat = jnp.dot(full_grad, w_out[0], preferred_element_type=jnp.float32).astype(jnp.bfloat16)
    replicas = lax.axis_size("dp")
    grad_columns = lax.all_to_all(full_grad, "dp", split_axis=1, concat_axis=0, tiled=True)
    acts_rows = lax.all_gather(flat_att, "dp", axis=0, tiled=True)
    partials = jnp.einsum(
        "rsd,rsh->rdh",
        grad_columns.reshape(replicas, seq_len, -1),
        acts_rows.reshape(replicas, seq_len, -1),
        preferred_element_type=jnp.float32,
    )
    rounded = lax.optimization_barrier(partials.astype(jnp.bfloat16))
    grad_weight = jnp.sum(rounded.astype(jnp.float32), axis=0).astype(jnp.bfloat16)
    d_heads = d_flat.reshape(attended.shape)
    d_values = jnp.einsum(
        "hqk,qhd->khd", weights_bf, d_heads, preferred_element_type=jnp.float32
    ).astype(jnp.bfloat16)
    d_weights = jnp.einsum("qhd,khd->hqk", d_heads, values, preferred_element_type=jnp.float32)
    row_dot = jnp.sum(softmax_out * d_weights, axis=2, keepdims=True)
    d_scores = (softmax_out * (d_weights - row_dot)).astype(jnp.bfloat16)
    d_queries = (
        jnp.einsum("hqk,khd->qhd", d_scores, key_rows, preferred_element_type=jnp.float32)
        * inv_root
    ).astype(jnp.bfloat16)
    d_keys = (
        jnp.einsum("hqk,qhd->khd", d_scores, queries, preferred_element_type=jnp.float32) * inv_root
    ).astype(jnp.bfloat16)
    stacked = jnp.stack([d_queries, d_keys, d_values])[None, None]
    received = from_behind(stacked, "section", -1)
    return (grad_weight[None], received)


def solution(mesh):
    in_specs = (
        P("section", "dp", None, None, "st", None),
        P("section", "dp", None),
        P("section", None, "st"),
        P("section", "dp", None, "st"),
    )
    out_specs = (P("section", "dp", "st"), P("section", "dp", None, None, "st", None))
    return jax.shard_map(local, mesh=mesh, in_specs=in_specs, out_specs=out_specs, check_vma=False)
```

profile of v0, /device:TPU:0, one launch (start us, length us, event | category | flops | bytes accessed | tf_op | source)
XLA Modules:
  0.0 124.5 jit_solution(11489933163909309656)
XLA Ops:
  7.2 0.0 copy-start.4
  7.2 0.0 copy-start.2
  7.2 0.0 all-gather.3.cloned.1.call-start
  7.2 2.0 %copy.33 = bf16[1,1,128,1536]{2,3,1,0:T(8,128)(2,1)} copy(bf16[1,1,128,1536]{3,2,1,0:T(8,128)(2,1)} %param.7) | data formatting | bytes 786432 | tf_op args[3]
  9.2 0.0 all-gather.3.cloned.1.call-update
  9.3 0.0 copy-done.4
  9.3 0.1 broadcast_compare_fusion
  9.4 0.0 copy-done.2
  9.4 0.4 fusion.10
  9.8 0.0 copy-start.1
  9.8 0.7 fusion.31
  10.5 0.4 convolution_convert_fusion
  10.9 0.0 copy-done.1
  10.9 0.2 copy.32
  11.1 21.4 %all-gather.3.cloned.1.call-done = bf16[1,1,128,6144]{2,3,1,0:T(8,128)(2,1)} async-done(((bf16[1,1,128,1536]{2,3,1,0:T(8,128)(2,1)}), bf16[1,1,128,6144]{2,3,1,0:T(8,128)(2,1)}) %all-gather.3.cloned.1.call-update) | async-done | bytes 1572880 | tf_op jit(solution)/shard_map/all_gather | solution.py:36
  32.5 0.0 copy-start
  32.5 9.6 %fusion.3 = bf16[128,1536]{1,0:T(8,128)(2,1)S(1)} fusion(bf16[1,6144,1536]{2,1,0:T(8,128)(2,1)} %param.6, bf16[1,1,128,6144]{2,3,1,0:T(8,128)(2,1)} %all-gather.3.cloned.1.call-done), kind=kOutput, calls=%fused_computation.4 | convolution fusion | flops 2416115712 | bytes 20840448 | tf_op jit(solution)/shard_map/dot_general | solution.py:37
  42.1 0.9 copy.36
  43.0 0.0 copy-done
  43.0 1.6 %copy.34 = bf16[128,2,3072]{2,0,1:T(8,128)(2,1)} copy(bf16[128,2,3072]{0,2,1:T(8,128)(2,1)S(1)} %bitcast.63) | data formatting | bytes 3145728 | tf_op jit(solution)/shard_map/all_to_all | solution.py:39
  44.6 0.0 copy-start.3
  44.6 3.8 %all-to-all-start = ((bf16[128,2,3072]{2,0,1:T(8,128)(2,1)}), bf16[128,2,3072]{2,0,1:T(8,128)(2,1)S(1)}, u32[]{:S(2)}, u32[]{:S(2)}) async-start(bf16[128,2,3072]{2,0,1:T(8,128)(2,1)} %copy.34), calls=%async_computation | async-start | bytes 3145728 | tf_op jit(solution)/shard_map/all_to_all | solution.py:39
  48.4 0.0 copy-done.3
  48.4 1.3 %multiply_reduce_fusion = (f32[12,128]{1,0:T(8,128)S(1)}, f32[12,128,128]{1,2,0:T(8,128)S(1)}) fusion(f32[12,128,128]{1,2,0:T(8,128)S(1)} %get-tuple-element.9, f32[12,128]{1,0:T(8,128)S(1)} %get-tuple-element.8, bf16[128,12,128]{0,2,1:T(8,128)(2,1)S(1)} %bitcast.65, bf16[1,1,3,128,12,128]{5,3,4,2,1,0:T(8,128)(2,1)} %param.4), kind=kOutput, calls=%fused_computation.22 | convolution fusion | flops 50919936 | bytes 2371584 | tf_op jit(solution)/shard_map/qhd,khd->hqk/dot_general | solution.py:53
  49.7 0.1 multiply_convert_fusion
  49.8 1.8 %fusion.13 = bf16[1,128,12,128]{1,3,2,0:T(8,128)(2,1)S(1)} fusion(bf16[128,12,128]{0,2,1:T(8,128)(2,1)S(1)} %bitcast.66, f32[12,128]{1,0:T(8,128)S(1)} %get-tuple-element.8, f32[12,128,128]{1,2,0:T(8,128)} %copy-done.1), kind=kOutput, calls=%fused_computation.17 | convolution fusion | flops 51119744 | bytes 1579008 | tf_op jit(solution)/shard_map/hqk,qhd->khd/dot_general | solution.py:50
  51.6 1.4 %fusion.14 = bf16[1,128,12,128]{1,3,2,0:T(8,128)(2,1)S(1)} fusion(bf16[12,128,128]{1,2,0:T(8,128)(2,1)S(1)} %multiply_convert_fusion, bf16[1,1,3,128,12,128]{5,3,4,2,1,0:T(8,128)(2,1)} %param.4), kind=kOutput, calls=%fused_computation.18 | convolution fusion | flops 50724864 | bytes 1179648 | tf_op jit(solution)/shard_map/hqk,qhd->khd/dot_general | solution.py:61
  53.1 1.3 %fusion.15 = bf16[1,128,12,128]{1,3,2,0:T(8,128)(2,1)S(1)} fusion(bf16[12,128,128]{1,2,0:T(8,128)(2,1)S(1)} %multiply_convert_fusion, bf16[1,1,3,128,12,128]{5,3,4,2,1,0:T(8,128)(2,1)} %param.4), kind=kOutput, calls=%fused_computation.19 | convolution fusion | flops 50724864 | bytes 1179648 | tf_op jit(solution)/shard_map/hqk,khd->qhd/dot_general | solution.py:57
  54.4 1.1 maximum_bitcast_fusion
  55.5 1.3 %collective-permute-start = (bf16[1,1,3,128,12,128]{3,5,4,2,1,0:T(8,128)(2,1)}, bf16[1,1,3,128,12,128]{3,5,4,2,1,0:T(8,128)(2,1)}, u32[]{:S(2)}, u32[]{:S(2)}) collective-permute-start(bf16[1,1,3,128,12,128]{3,5,4,2,1,0:T(8,128)(2,1)} %maximum_bitcast_fusion), channel_id=1, source_target_pairs={{8,0},{16,8},{24,16},{9,1},{17,9},{25,17},{10,2},{18,10},{26,18},{... | collective-permute-start | bytes 3538952 | tf_op jit(solution)/shard_map/ppermute | solution.py:12
  56.8 19.9 %all_gather.6 = bf16[256,1536]{1,0:T(8,128)(2,1)S(1)} all-gather(bf16[128,1536]{1,0:T(8,128)(2,1)S(1)} %copy.32), channel_id=1, replica_groups=mesh['section'=4,'st'=4,'dp'=2] {'dp'}, dimensions={0}, use_global_device_ids=true | all-gather | bytes 1179648 | tf_op jit(solution)/shard_map/all_gather | solution.py:40
  76.7 0.0 all-to-all-done
  76.7 9.1 %convert_bitcast_fusion = bf16[2,3072,1536]{1,2,0:T(8,128)(2,1)} fusion(bf16[2,128,1536]{2,1,0:T(8,128)(2,1)S(1)} %bitcast.64, bf16[128,2,3072]{2,0,1:T(8,128)(2,1)S(1)} %all-to-all-done), kind=kOutput, calls=%fused_computation.3 | convolution fusion | flops 2425356288 | bytes 21233664 | tf_op jit(solution)/shard_map/rsd,rsh->rdh/dot_general | solution.py:41
  85.8 16.8 %reduce_sum.31 = bf16[3072,1536]{0,1:T(8,128)(2,1)} reduce(bf16[2,3072,1536]{1,2,0:T(8,128)(2,1)} %convert_bitcast_fusion, bf16[]{:T(256)} %constant.10.clone.1), dimensions={0}, to_apply=%region_2.3 | reduce | flops 4718592 | bytes 28311554 | tf_op jit(solution)/shard_map/reduce_sum | solution.py:48
  102.7 12.6 %copy.43 = bf16[1,3072,1536]{2,1,0:T(8,128)(2,1)} copy(bf16[1,3072,1536]{1,2,0:T(8,128)(2,1)} %bitcast.62) | data formatting | bytes 18874368
  115.3 0.0 collective-permute-done
  115.3 2.4 %copy.44 = bf16[1,1,3,128,12,128]{5,3,4,2,1,0:T(8,128)(2,1)} copy(bf16[1,1,3,128,12,128]{3,5,4,2,1,0:T(8,128)(2,1)} %collective-permute-done) | data formatting | bytes 2359296
Async XLA Ops:
  7.2 2.1 %copy-start.4 = (s32[1,1,128]{2,1,0:T(1,128)S(1)}, s32[1,1,128]{2,1,0:T(1,128)}, u32[]{:S(2)}) copy-start(s32[1,1,128]{2,1,0:T(1,128)} %param.5) | copy-start | bytes 1540
  7.2 2.2 %copy-start.2 = (bf16[1,1,3,128,12,128]{5,3,4,2,1,0:T(8,128)(2,1)S(1)}, bf16[1,1,3,128,12,128]{5,3,4,2,1,0:T(8,128)(2,1)}, u32[]{:S(2)}) copy-start(bf16[1,1,3,128,12,128]{5,3,4,2,1,0:T(8,128)(2,1)} %param.4) | copy-start | bytes 3538948
  7.2 25.3 %all-gather.3.cloned.1.call-start = ((), (), s32[]{:S(2)}) async-start(), calls=%async_computation.1 | async-start | bytes 1966080 | tf_op jit(solution)/shard_map/all_gather | solution.py:36
  9.8 1.1 copy-start.1
  32.5 10.5 %copy-start = (bf16[1,1,128,6144]{2,3,1,0:T(8,128)(2,1)S(1)}, bf16[1,1,128,6144]{2,3,1,0:T(8,128)(2,1)}, u32[]{:S(2)}) copy-start(bf16[1,1,128,6144]{2,3,1,0:T(8,128)(2,1)} %all-gather.3.cloned.1.call-done) | copy-start | bytes 4718596
  44.6 3.8 %copy-start.3 = (bf16[128,1536]{0,1:T(8,128)(2,1)S(1)}, bf16[128,1536]{0,1:T(8,128)(2,1)}, u32[]{:S(2)}) copy-start(bf16[128,1536]{0,1:T(8,128)(2,1)} %copy.36) | copy-start | bytes 1179652
  44.6 32.1 %all-to-all-start = ((bf16[128,2,3072]{2,0,1:T(8,128)(2,1)}), bf16[128,2,3072]{2,0,1:T(8,128)(2,1)S(1)}, u32[]{:S(2)}, u32[]{:S(2)}) async-start(bf16[128,2,3072]{2,0,1:T(8,128)(2,1)} %copy.34), calls=%async_computation | async-start | bytes 3145728 | tf_op jit(solution)/shard_map/all_to_all | solution.py:39
  55.5 59.7 %collective-permute-start = (bf16[1,1,3,128,12,128]{3,5,4,2,1,0:T(8,128)(2,1)}, bf16[1,1,3,128,12,128]{3,5,4,2,1,0:T(8,128)(2,1)}, u32[]{:S(2)}, u32[]{:S(2)}) collective-permute-start(bf16[1,1,3,128,12,128]{3,5,4,2,1,0:T(8,128)(2,1)} %maximum_bitcast_fusion), channel_id=1, source_target_pairs={{8,0},{16,8},{24,16},{9,1},{17,9},{25,17},{10,2},{18,10},{26,18},{... | collective-permute-start | bytes 3538952 | tf_op jit(solution)/shard_map/ppermute | solution.py:12
Sparse Core Ops, SparseCore 0:
  10.1 22.3 all-gather.2
where the time goes:
time: 125 us; the launch traced here: 124 us
  matrix products  25.3 us (20%)
  waiting for transfers between devices  21.5 us (17%)
  blocking collectives  19.9 us (16%)
  local copies, waits for them, and re-layouts  19.7 us (16%)
  other arithmetic  18.8 us (15%)
  between operations  14.2 us (11%)
  starting transfers between devices  5.12 us (4%)
    all_gather x1, waiting for transfers between devices, local(): full_grad = lax.all_gather(grad_out[0, 0], 'st', axis=1, tiled=True)  21.4 us
    all_gather x1, blocking collectives, local(): acts_rows = lax.all_gather(flat_att, 'dp', axis=0, tiled=True)  19.9 us
    unnamed x13, local copies, waits for them, and re-layouts  17 us
    reduce_sum x1, other arithmetic, local(): jnp.sum(rounded.astype(jnp.float32), axis=0).astype(jnp.bfloat16)  16.8 us
    dot_general x1, matrix products, local(): jnp.dot(full_grad, w_out[0], preferred_element_type=jnp.float32)  9.6 us
    dot_general x1, matrix products, local(): jnp.einsum('rsd,rsh->rdh', grad_columns.reshape(replicas, seq_len, -1), a...  9.12 us
    all_to_all x1, starting transfers between devices, local(): lax.all_to_all(full_grad, 'dp', split_axis=1, concat_axis=0, tiled=True)  3.8 us
  transfers between devices with their start and end apart: 3, of which 1 were waited for; matrix products, arithmetic and copies ran while one was open for 38% of the time, Pallas kernels for 0%

commit v1 on v0

v1 whole, which is shorter than its diff:
```python
import functools
import math

import jax
import jax.numpy as jnp
from jax import lax
from jax.experimental import pallas as pl
from jax.experimental.pallas import tpu as pltpu
from jax.sharding import PartitionSpec as P

F32 = jnp.float32
BF16 = jnp.bfloat16


def dot(a, b, dims):
    return lax.dot_general(a, b, ((dims[0], dims[1]), ((), ())), preferred_element_type=F32)


def rotate(value, axis, steps):
    count = lax.axis_size(axis)
    return lax.ppermute(value, axis, [(i, (i + steps) % count) for i in range(count)])


def swap(value, axis):
    count = lax.axis_size(axis)
    return lax.ppermute(value, axis, [(i, i ^ 1) for i in range(count)])


def down(value, axis):
    count = lax.axis_size(axis)
    return lax.ppermute(value, axis, [(i, i - 1) for i in range(1, count)])


def pick(index, options):
    result = options[0]
    for number, option in enumerate(options[1:], 1):
        result = jnp.where(index == number, option, result)
    return result


def rows_as_lanes(pos_ref):
    seq = pos_ref.shape[-1]
    lanes = jnp.broadcast_to(pos_ref[...].astype(F32), (seq, seq))
    return lanes, lanes.T


def forward_kernel(pos_ref, qkv_ref, out_ref):
    _, heads, _, width = qkv_ref.shape
    scale = 1.0 / math.sqrt(width)
    across, along = rows_as_lanes(pos_ref)
    visible = across <= along
    for head in range(heads):
        scores = dot(qkv_ref[0, head], qkv_ref[1, head], ((1,), (1,))) * scale
        scores = jnp.where(visible, scores, -1e30)
        exponent = jnp.exp(scores - jnp.max(scores, axis=1, keepdims=True))
        probs = exponent / jnp.sum(exponent, axis=1, keepdims=True)
        attended = dot(probs.astype(BF16), qkv_ref[2, head], ((1,), (0,)))
        out_ref[:, head * width : (head + 1) * width] = attended.astype(BF16)


def head_block(heads, most=4):
    return max(size for size in range(1, most + 1) if heads % size == 0)


def forward(pos, qkv):
    _, heads, seq, width = qkv.shape
    block = head_block(heads)
    return pl.pallas_call(
        forward_kernel,
        name="forward",
        grid=(heads // block,),
        in_specs=[
            pl.BlockSpec((1, seq), lambda h: (0, 0)),
            pl.BlockSpec((3, block, seq, width), lambda h: (0, h, 0, 0)),
        ],
        out_specs=pl.BlockSpec((seq, block * width), lambda h: (0, h)),
        out_shape=jax.ShapeDtypeStruct((seq, heads * width), BF16),
    )(pos, qkv)


def backward_kernel(pos_ref, qkv_ref, grad_ref, out_ref):
    _, heads, _, width = qkv_ref.shape
    scale = 1.0 / math.sqrt(width)
    across, along = rows_as_lanes(pos_ref)
    visible = along <= across
    for head in range(heads):
        query, key, value = qkv_ref[0, head], qkv_ref[1, head], qkv_ref[2, head]
        grad = grad_ref[:, head * width : (head + 1) * width]
        scores = dot(key, query, ((1,), (1,))) * scale
        scores = jnp.where(visible, scores, -1e30)
        exponent = jnp.exp(scores - jnp.max(scores, axis=0, keepdims=True))
        probs = exponent / jnp.sum(exponent, axis=0, keepdims=True)
        d_value = dot(probs.astype(BF16), grad, ((1,), (0,)))
        d_probs = dot(value, grad, ((1,), (1,)))
        row_dot = jnp.sum(probs * d_probs, axis=0, keepdims=True)
        d_scores = (probs * (d_probs - row_dot)).astype(BF16)
        d_key = dot(d_scores, query, ((1,), (0,))) * scale
        d_query = dot(d_scores, key, ((0,), (0,))) * scale
        out_ref[0, head] = d_query.astype(BF16)
        out_ref[1, head] = d_key.astype(BF16)
        out_ref[2, head] = d_value.astype(BF16)


def backward(pos, qkv, grad, first, count, total):
    _, _, seq, width = qkv.shape
    block = head_block(math.gcd(count, first) if first else count)
    start = first // block
    return pl.pallas_call(
        backward_kernel,
        name="backward",
        grid=(count // block,),
        in_specs=[
            pl.BlockSpec((1, seq), lambda h: (0, 0)),
            pl.BlockSpec((3, block, seq, width), lambda h: (0, h + start, 0, 0)),
            pl.BlockSpec((seq, block * width), lambda h: (0, h)),
        ],
        out_specs=pl.BlockSpec((3, block, seq, width), lambda h: (0, h, 0, 0)),
        out_shape=jax.ShapeDtypeStruct((3, total, seq, width), BF16),
    )(pos, qkv, grad)


def fill_kernel(late_ref, whole_ref, out_ref, sem):
    first = out_ref.shape[1] - late_ref.shape[1]
    copies = [
        pltpu.make_async_copy(late_ref.at[i], out_ref.at[i, pl.ds(first, late_ref.shape[1])], sem.at[i])
        for i in range(3)
    ]
    for copy in copies:
        copy.start()
    for copy in copies:
        copy.wait()


def fill(late, whole):
    return pl.pallas_call(
        fill_kernel,
        name="fill",
        in_specs=[pl.BlockSpec(memory_space=pl.ANY)] * 2,
        out_specs=pl.BlockSpec(memory_space=pl.ANY),
        out_shape=jax.ShapeDtypeStruct(whole.shape, whole.dtype),
        scratch_shapes=[pltpu.SemaphoreType.DMA((3,))],
        input_output_aliases={1: 0},
    )(late, whole)


def project_kernel(has_total, splits, shard_ref, *refs):
    refs = list(refs)
    grad_ref, weight_ref = refs[:2]
    total_ref = refs[2] if has_total else None
    outs = refs[3:] if has_total else refs[2:]
    scratch = None
    if splits:
        scratch = outs.pop()
    acc_ref = scratch if splits else outs[0]
    step = pl.program_id(0)
    product = jnp.dot(grad_ref[...], weight_ref[...], preferred_element_type=F32)

    @pl.when(step == 0)
    def _():
        acc_ref[...] = product + total_ref[...] if has_total else product

    @pl.when(step > 0)
    def _():
        acc_ref[...] += product

    if splits:

        @pl.when(step == pl.num_programs(0) - 1)
        def _():
            at = 0
            for out, size in zip(outs, splits):
                out[...] = acc_ref[:, at : at + size].astype(BF16)
                at += size


def project(shard, grad, weight, total, splits):
    seq, features = grad.shape
    columns = weight.shape[1]
    steps = max(1, features // 512)
    while features % steps or (features // steps) % 128:
        steps -= 1
    depth = features // steps
    whole = lambda k, s: (0, 0)
    in_specs = [
        pl.BlockSpec((seq, depth), lambda k, s: (0, k)),
        pl.BlockSpec((depth, columns), lambda k, s: (s[0] * steps + k, 0)),
    ]
    args = [grad, weight]
    if total is not None:
        in_specs.append(pl.BlockSpec((seq, columns), whole))
        args.append(total)
    if splits:
        out_specs = [pl.BlockSpec((seq, size), whole) for size in splits]
        out_shape = [jax.ShapeDtypeStruct((seq, size), BF16) for size in splits]
        scratch = [pltpu.VMEM((seq, columns), F32)]
    else:
        out_specs = pl.BlockSpec((seq, columns), whole)
        out_shape = jax.ShapeDtypeStruct((seq, columns), F32)
        scratch = []
    return pl.pallas_call(
        functools.partial(project_kernel, total is not None, splits),
        name="project",
        grid_spec=pltpu.PrefetchScalarGridSpec(
            num_scalar_prefetch=1,
            grid=(steps,),
            in_specs=in_specs,
            out_specs=out_specs,
            scratch_shapes=scratch,
        ),
        out_shape=out_shape,
    )(shard.reshape(1).astype(jnp.int32), *args)


def weight_kernel(slots, replicas, blocks, rows_ref, *refs):
    acts = refs[:replicas]
    grads = refs[replicas : replicas * (1 + slots)]
    out_ref, stacked = refs[-2:]
    step = pl.program_id(0)
    seq = acts[0].shape[0]

    @pl.when(step == 0)
    def _():
        for number, act in enumerate(acts):
            stacked[number * seq : (number + 1) * seq] = act[...]

    for slot in range(slots):

        @pl.when(step // blocks == slot)
        def _():
            own = grads[slot * replicas : (slot + 1) * replicas]
            left = jnp.concatenate([ref[...] for ref in own], axis=0)
            out_ref[...] = dot(left, stacked[...], ((0,), (0,))).astype(BF16)


def weight_gradient(rows, acts, grads):
    replicas = len(acts)
    slots = len(grads)
    seq, columns = acts[0].shape
    features = grads[0][0].shape[1]
    blocks = max(1, features // 512)
    while features % blocks or (features // blocks) % 128:
        blocks -= 1
    size = features // blocks
    in_specs = [pl.BlockSpec((seq, columns), lambda s, p: (0, 0))] * replicas
    for slot in range(slots):
        spec = pl.BlockSpec(
            (seq, size),
            lambda s, p, slot=slot: (0, jnp.clip(s - slot * blocks, 0, blocks - 1)),
        )
        in_specs += [spec] * replicas
    return pl.pallas_call(
        functools.partial(weight_kernel, slots, replicas, blocks),
        name="weight_gradient",
        grid_spec=pltpu.PrefetchScalarGridSpec(
            num_scalar_prefetch=1,
            grid=(slots * blocks,),
            in_specs=in_specs,
            out_specs=pl.BlockSpec(
                (size, columns), lambda s, p: (p[s // blocks] * blocks + s % blocks, 0)
            ),
            scratch_shapes=[pltpu.VMEM((replicas * seq, columns), BF16)],
        ),
        out_shape=jax.ShapeDtypeStruct((slots * features, columns), BF16),
    )(rows, *acts, *[ref for slot in grads for ref in slot])


def local(saved_qkv, positions, w_out, grad_out):
    qkv = saved_qkv[0, 0].transpose(0, 2, 1, 3)
    pos = positions[0]
    weight = w_out[0]
    heads, seq, width = qkv.shape[1:]
    early = max(1, (heads * 7) // 12)
    late = heads - early
    shards = lax.axis_size("st")
    replicas = lax.axis_size("dp")
    chips = shards // 2
    me = lax.axis_index("st")
    chip, core = me // 2, me % 2
    replica = lax.axis_index("dp")
    per_replica = chips // replicas

    qkv_above = down(qkv[:, :early], "section")
    pos_above = down(pos, "section")

    same = [grad_out[0, 0]]
    for step in range(1, chips):
        same.append(rotate(same[0], "st", 2 * step))
    other = [swap(value, "st") for value in same]

    attended = forward(pos, qkv)
    acts = [attended] + [rotate(attended, "dp", step) for step in range(1, replicas)]

    total = None
    for step in range(chips):
        source = 2 * ((chip - step) % chips)
        for shard, value in ((source + core, same[step]), (source + 1 - core, other[step])):
            last = step == chips - 1 and value is other[step]
            splits = (early * width, late * width) if last else None
            total = project(shard, value, weight, total, splits)
    d_early, d_late = total
    d_above = down(d_early, "section")
    grads_late = backward(pos, qkv[:, early:], d_late, 0, late, late)
    late_above = down(grads_late, "section")

    slots = []
    rows = []
    for number in range(per_replica):
        mine = (chip - (replica * per_replica + number)) % chips
        own_core, other_core = [pick(mine, same)], [pick(mine, other)]
        for step in range(1, replicas):
            target = (replica + step) % replicas
            theirs = (chip - (target * per_replica + number)) % chips
            got = rotate(pick(theirs, same), "dp", step)
            own_core.append(got)
            other_core.append(swap(got, "st"))
        slots += [own_core, other_core]
        rows += [2 * number + core, 2 * number + 1 - core]
    grad_weight = weight_gradient(jnp.stack(rows).astype(jnp.int32), acts, slots)

    whole = backward(pos_above, qkv_above, d_above, 0, early, heads)
    upstream = fill(late_above, whole)
    return (grad_weight[None], upstream.transpose(0, 2, 1, 3)[None, None])


def solution(mesh):
    in_specs = (
        P("section", "dp", None, None, "st", None),
        P("section", "dp", None),
        P("section", None, "st"),
        P("section", "dp", None, "st"),
    )
    out_specs = (P("section", "dp", "st"), P("section", "dp", None, None, "st", None))
    return jax.shard_map(local, mesh=mesh, in_specs=in_specs, out_specs=out_specs, check_vma=False)
```

time: 125 us -> 110 us (0.88)
  Pallas kernels: 0 us -> 62.2 us
  matrix products: 25.3 us -> 0 us
  blocking collectives: 19.9 us -> 0 us
  other arithmetic: 18.8 us -> 3.37 us
  local copies, waits for them, and re-layouts: 19.7 us -> 5.59 us
  between operations: 14.2 us -> 0.8 us
  starting transfers between devices: 5.12 us -> 10.4 us
  waiting for transfers between devices: 21.5 us -> 26.7 us
    pallas_call x0 -> x9, Pallas kernels: none -> 62.2 us  [the longest x4 19.5 us: project(): pl.pallas_call(functools.partial(project_kernel, total is not None, split...]
    ppermute x1 -> x10, waiting for transfers between devices: 0.01 us -> 26.7 us  [the longest x4 17.4 us: down(): return lax.ppermute(value, axis, [(i, i - 1) for i in range(1, count)])]
    dot_general x8 -> x0, matrix products: 25.3 us -> none  [the longest x1 9.6 us: local(): jnp.dot(full_grad, w_out[0], preferred_element_type=jnp.float32)]
    all_gather x1 -> x0, waiting for transfers between devices: 21.4 us -> none  [local(): full_grad = lax.all_gather(grad_out[0, 0], 'st', axis=1, tiled=True)]
    all_gather x1 -> x0, blocking collectives: 19.9 us -> none  [local(): acts_rows = lax.all_gather(flat_att, 'dp', axis=0, tiled=True)]
    reduce_sum x1 -> x0, other arithmetic: 16.8 us -> none  [local(): jnp.sum(rounded.astype(jnp.float32), axis=0).astype(jnp.bfloat16)]
    unnamed x13 -> x28, local copies, waits for them, and re-layouts: 17 us -> 2.81 us
    ppermute x1 -> x10, starting transfers between devices: 1.28 us -> 10.4 us  [the longest x3 5.14 us: rotate(): lax.ppermute(value, axis, [(i, (i + steps) % count) for i in range(count)])]
  transfers between devices with their start and end apart: 3 -> 10, of which waited for: 1 -> 2; matrix products, arithmetic and copies ran while one was open for 38% -> 6% of each run, Pallas kernels for 0% -> 42%
where the time goes in v1:
time: 110 us; the launch traced here: 109 us
  Pallas kernels  62.2 us (57%)
  waiting for transfers between devices  26.7 us (24%)
  starting transfers between devices  10.4 us (9%)
  local copies, waits for them, and re-layouts  5.59 us (5%)
  other arithmetic  3.37 us (3%)
    pallas_call x4, Pallas kernels, project(): pl.pallas_call(functools.partial(project_kernel, total is not None, split...  19.5 us
    ppermute x4, waiting for transfers between devices, down(): return lax.ppermute(value, axis, [(i, i - 1) for i in range(1, count)])  17.4 us
    pallas_call x1, Pallas kernels, fill(): pl.pallas_call(fill_kernel, name='fill', in_specs=[pl.BlockSpec(memory_sp...  16 us
    pallas_call x2, Pallas kernels, backward(): pl.pallas_call(backward_kernel, name='backward', grid=(count // block,),...  12 us
    ppermute x3, waiting for transfers between devices, rotate(): lax.ppermute(value, axis, [(i, (i + steps) % count) for i in range(count)])  9.33 us
    pallas_call x1, Pallas kernels, weight_gradient(): pl.pallas_call(functools.partial(weight_kernel, slots, replicas, blocks),...  8.67 us
    pallas_call x1, Pallas kernels, forward(): pl.pallas_call(forward_kernel, name='forward', grid=(heads // block,), in...  5.97 us
    ppermute x3, starting transfers between devices, rotate(): lax.ppermute(value, axis, [(i, (i + steps) % count) for i in range(count)])  5.14 us
  transfers between devices with their start and end apart: 10, of which 2 were waited for; matrix products, arithmetic and copies ran while one was open for 6% of the time, Pallas kernels for 42%

profile of v1, /device:TPU:0, one launch (start us, length us, event | category | flops | bytes accessed | tf_op | source)
XLA Modules:
  0.0 109.1 jit_solution(14571816977895941341)
XLA Ops:
  0.6 0.0 copy-start
  0.6 3.1 %collective-permute-start.1 = (bf16[128,1536]{1,0:T(8,128)(2,1)}, bf16[128,1536]{1,0:T(8,128)(2,1)S(1)}, u32[]{:S(2)}, u32[]{:S(2)}) collective-permute-start(bf16[128,1536]{1,0:T(8,128)(2,1)} %bitcast.27), channel_id=1, source_target_pairs={{0,4},{2,6},{4,0},{6,2},{1,5},{3,7},{5,1},{7,3},{8,12},{10,14},{12... | collective-permute-start | bytes 1179656 | tf_op jit(solution)/shard_map/ppermute | solution.py:21
  3.7 0.0 collective-permute-start.4
  3.7 0.0 copy-start.12
  3.7 9.3 %collective-permute-done.1.refs_0_ = bf16[128,1536]{1,0:T(8,128)(2,1)S(1)} collective-permute-done((bf16[128,1536]{1,0:T(8,128)(2,1)}, bf16[128,1536]{1,0:T(8,128)(2,1)S(1)}, u32[]{:S(2)}, u32[]{:S(2)}) %collective-permute-start.1) | collective-permute-done | bytes 393248 | tf_op jit(solution)/shard_map/ppermute | solution.py:21
  13.0 0.0 copy-start.4
  13.0 0.0 collective-permute-start.3
  13.0 2.0 %broadcast_select_fusion = (bf16[128,1536]{1,0:T(8,128)(2,1)S(1)}, bf16[128,1536]{1,0:T(8,128)(2,1)}) fusion(bf16[128,1536]{1,0:T(8,128)(2,1)S(1)} %collective-permute-done.1.refs_0_, pred[]{:T(512)S(6)} %eq.15, bf16[1,1,128,1536]{3,2,1,0:T(8,128)(2,1)} %param.7, pred[]{:T(512)S(6)} %eq.14), kind=kLoop, calls=%fused_computation | loop fusion | flops 393216 | bytes 1572866 | tf_op jit(solution)/shard_map/jit(_where)/select_n | solution.py:37
  15.0 1.7 %collective-permute-start.2 = (bf16[128,1536]{1,0:T(8,128)(2,1)S(1)}, bf16[128,1536]{1,0:T(8,128)(2,1)S(1)}, u32[]{:S(2)}, u32[]{:S(2)}) collective-permute-start(bf16[128,1536]{1,0:T(8,128)(2,1)S(1)} %get-tuple-element.6), channel_id=1, source_target_pairs={{0,1},{1,0},{2,3},{3,2},{4,5},{5,4},{6,7},{7,6},{8,9},{9,8},{10,11... | collective-permute-start | bytes 1179656 | tf_op jit(solution)/shard_map/ppermute | solution.py:21
  16.7 0.0 copy-done
  16.7 0.9 slice.9
  17.6 0.0 copy-done.4
  17.6 1.3 %collective-permute-start.8 = (bf16[3,7,128,128]{3,2,1,0:T(8,128)(2,1)}, bf16[3,7,128,128]{3,2,1,0:T(8,128)(2,1)S(1)}, u32[]{:S(2)}, u32[]{:S(2)}) collective-permute-start(bf16[3,7,128,128]{3,2,1,0:T(8,128)(2,1)} %slice.9), channel_id=1, source_target_pairs={{8,0},{16,8},{24,16},{9,1},{17,9},{25,17},{10,2},{18,10},{26,18},{... | collective-permute-start | bytes 2064392 | tf_op jit(solution)/shard_map/ppermute | solution.py:31
  18.9 0.0 copy-done.12
  18.9 1.3 %collective-permute-start.7 = (s32[1,128]{1,0:T(1,128)S(1)}, s32[1,128]{1,0:T(1,128)S(1)}, u32[]{:S(2)}, u32[]{:S(2)}) collective-permute-start(s32[1,128]{1,0:T(1,128)S(1)} %bitcast.32), channel_id=1, source_target_pairs={{8,0},{16,8},{24,16},{9,1},{17,9},{25,17},{10,2},{18,10},{26,18},{... | collective-permute-start | bytes 1544 | tf_op jit(solution)/shard_map/ppermute | solution.py:31
  20.3 6.0 %forward.1.refs_0_ = bf16[128,1536]{1,0:T(8,128)(2,1)} custom-call(s32[1,128]{1,0:T(1,128)} %bitcast.30, bf16[3,12,128,128]{3,2,1,0:T(8,128)(2,1)} %bitcast.23), custom_call_target="tpu_custom_call" | custom-call | tf_op jit(solution)/shard_map/forward/pallas_call | solution.py:68
  26.2 1.9 %slice.8.qkv_ref = bf16[3,5,128,128]{3,2,1,0:T(8,128)(2,1)} slice(bf16[3,12,128,128]{3,2,1,0:T(8,128)(2,1)} %bitcast.24), slice={[0:3], [7:12], [0:128], [0:128]} | slice | bytes 983040 | tf_op jit(solution)/shard_map/slice | solution.py:302
  28.1 0.0 copy-start.1
  28.1 4.8 %project.4.refs_2_ = f32[128,1536]{1,0:T(8,128)} custom-call(s32[1]{0:T(128)} %bitcast.12.shard_ref, bf16[128,1536]{1,0:T(8,128)(2,1)} %bitcast.29, bf16[6144,1536]{1,0:T(8,128)(2,1)} %bitcast.18), custom_call_target="tpu_custom_call" | custom-call | tf_op jit(solution)/shard_map/project/pallas_call | solution.py:200
  32.9 0.0 collective-permute-done.4.refs_0_
  32.9 0.0 copy-done.1
  32.9 0.0 copy-start.2
  32.9 0.4 collective-permute-start
  33.3 0.4 copy-done.2
  33.6 5.0 %project.5.refs_2_ = f32[128,1536]{1,0:T(8,128)} custom-call(s32[1]{0:T(128)} %bitcast.11.shard_ref, bf16[128,1536]{1,0:T(8,128)(2,1)} %copy-done.2, bf16[6144,1536]{1,0:T(8,128)(2,1)} %bitcast.19, f32[128,1536]{1,0:T(8,128)} %project.4.refs_2_), custom_call_target="tpu_custom_call" | custom-call | tf_op jit(solution)/shard_map/project/pallas_call | solution.py:200
  38.6 5.0 %project.6.refs_2_ = f32[128,1536]{1,0:T(8,128)} custom-call(s32[1]{0:T(128)} %bitcast.10.shard_ref, bf16[128,1536]{1,0:T(8,128)(2,1)} %copy-done.4, bf16[6144,1536]{1,0:T(8,128)(2,1)} %bitcast.20, f32[128,1536]{1,0:T(8,128)} %project.5.refs_2_), custom_call_target="tpu_custom_call" | custom-call | tf_op jit(solution)/shard_map/project/pallas_call | solution.py:200
  43.5 0.0 collective-permute-done.3.refs_0_
  43.5 0.0 copy-start.5
  43.5 0.7 copy-done.5
  44.3 4.9 %project.7 = (bf16[128,896]{1,0:T(8,128)(2,1)}, bf16[128,640]{1,0:T(8,128)(2,1)}) custom-call(s32[1]{0:T(128)} %bitcast.8.shard_ref, bf16[128,1536]{1,0:T(8,128)(2,1)} %copy-done.5, bf16[6144,1536]{1,0:T(8,128)(2,1)} %bitcast.21, f32[128,1536]{1,0:T(8,128)} %project.6.refs_2_), custom_call_target="tpu_custom_call" | custom-call | tf_op jit(solution)/shard_map/project/pallas_call | solution.py:200
  49.2 0.0 copy-start.3
  49.2 0.0 copy-start.6
  49.2 5.2 %backward.2 = bf16[3,5,128,128]{3,2,1,0:T(8,128)(2,1)} custom-call(s32[1,128]{1,0:T(1,128)} %bitcast.31, bf16[3,5,128,128]{3,2,1,0:T(8,128)(2,1)} %slice.8.qkv_ref, bf16[128,640]{1,0:T(8,128)(2,1)} %get-tuple-element.4.grad_ref), custom_call_target="tpu_custom_call" | custom-call | tf_op jit(solution)/shard_map/backward/pallas_call | solution.py:108
  54.4 1.3 %collective-permute-start.6 = (bf16[3,5,128,128]{3,2,1,0:T(8,128)(2,1)}, bf16[3,5,128,128]{3,2,1,0:T(8,128)(2,1)S(1)}, u32[]{:S(2)}, u32[]{:S(2)}) collective-permute-start(bf16[3,5,128,128]{3,2,1,0:T(8,128)(2,1)} %backward.2), channel_id=1, source_target_pairs={{8,0},{16,8},{24,16},{9,1},{17,9},{25,17},{10,2},{18,10},{26,18},{... | collective-permute-start | bytes 1474568 | tf_op jit(solution)/shard_map/ppermute | solution.py:31
  55.7 0.6 pad_add_fusion.rows_ref
  56.3 0.0 collective-permute-done.7.pos_ref
  56.3 0.0 copy-start.13
  56.3 1.3 %collective-permute-start.9 = (bf16[128,896]{1,0:T(8,128)(2,1)}, bf16[128,896]{1,0:T(8,128)(2,1)}, u32[]{:S(2)}, u32[]{:S(2)}) collective-permute-start(bf16[128,896]{1,0:T(8,128)(2,1)} %get-tuple-element.5), channel_id=1, source_target_pairs={{8,0},{16,8},{24,16},{9,1},{17,9},{25,17},{10,2},{18,10},{26,18},{... | collective-permute-start | bytes 688136 | tf_op jit(solution)/shard_map/ppermute | solution.py:31
  57.6 0.0 collective-permute-done.2.refs_3_
  57.6 0.0 copy-start.9
  57.6 0.2 collective-permute-start.5
  57.8 0.0 copy-done.3
  57.8 0.0 copy-done.6
  57.8 0.8 broadcast_select_fusion.1.refs_4_
  58.6 0.0 collective-permute-done.8.qkv_ref
  58.6 0.0 copy-start.7
  58.6 17.4 %collective-permute-done.9.grad_ref = bf16[128,896]{1,0:T(8,128)(2,1)} collective-permute-done((bf16[128,896]{1,0:T(8,128)(2,1)}, bf16[128,896]{1,0:T(8,128)(2,1)}, u32[]{:S(2)}, u32[]{:S(2)}) %collective-permute-start.9) | collective-permute-done | bytes 229408 | tf_op jit(solution)/shard_map/ppermute | solution.py:31
  76.0 0.0 copy-done.13
  76.0 0.0 copy-done.7
  76.0 6.7 %backward.3.whole_ref = bf16[3,12,128,128]{3,2,1,0:T(8,128)(2,1)} custom-call(s32[1,128]{1,0:T(1,128)} %copy-done.13, bf16[3,7,128,128]{3,2,1,0:T(8,128)(2,1)} %copy-done.7, bf16[128,896]{1,0:T(8,128)(2,1)} %collective-permute-done.9.grad_ref), custom_call_target="tpu_custom_call" | custom-call | tf_op jit(solution)/shard_map/backward/pallas_call | solution.py:108
  82.7 0.0 copy-done.9
  82.7 0.0 collective-permute-done.refs_1_
  82.7 0.0 copy-start.10
  82.7 0.0 collective-permute-done.5.refs_5_
  82.7 0.0 copy-start.11
  82.8 0.7 copy-done.10
  83.5 0.1 copy-done.11
  83.6 8.7 %weight_gradient.1 = bf16[3072,1536]{1,0:T(8,128)(2,1)} custom-call(s32[2]{0:T(128)} %pad_add_fusion.rows_ref, bf16[128,1536]{1,0:T(8,128)(2,1)} %forward.1.refs_0_, bf16[128,1536]{1,0:T(8,128)(2,1)} %copy-done.10, bf16[128,1536]{1,0:T(8,128)(2,1)} %get-tuple-element.7.refs_2_, bf16[128,1536]{1,0:T(8,128)(2,1)} %copy-done.9, ...), custom_call_target="tpu_custom_call" | custom-call | tf_op jit(solution)/shard_map/weight_gradient/pallas_call | solution.py:251
  92.3 0.0 collective-permute-done.6.late_ref
  92.3 0.0 copy-start.8
  92.3 0.8 copy-done.8
  93.1 16.0 %fill.1 = bf16[3,12,128,128]{3,2,1,0:T(8,128)(2,1)} custom-call(bf16[3,5,128,128]{3,2,1,0:T(8,128)(2,1)} %copy-done.8, bf16[3,12,128,128]{3,2,1,0:T(8,128)(2,1)} %backward.3.whole_ref), custom_call_target="tpu_custom_call", output_to_operand_aliasing={{}: (1, {})} | custom-call | tf_op jit(solution)/shard_map/fill/pallas_call | solution.py:135
Async XLA Ops:
  0.6 16.1 %copy-start = (bf16[1,1,3,128,12,128]{5,3,4,2,1,0:T(8,128)(2,1)S(1)}, bf16[1,1,3,128,12,128]{5,3,4,2,1,0:T(8,128)(2,1)}, u32[]{:S(2)}) copy-start(bf16[1,1,3,128,12,128]{5,3,4,2,1,0:T(8,128)(2,1)} %param.4) | copy-start | bytes 3538948
  0.6 12.4 %collective-permute-start.1 = (bf16[128,1536]{1,0:T(8,128)(2,1)}, bf16[128,1536]{1,0:T(8,128)(2,1)S(1)}, u32[]{:S(2)}, u32[]{:S(2)}) collective-permute-start(bf16[128,1536]{1,0:T(8,128)(2,1)} %bitcast.27), channel_id=1, source_target_pairs={{0,4},{2,6},{4,0},{6,2},{1,5},{3,7},{5,1},{7,3},{8,12},{10,14},{12... | collective-permute-start | bytes 1179656 | tf_op jit(solution)/shard_map/ppermute | solution.py:21
  3.7 29.2 %collective-permute-start.4 = (bf16[128,1536]{1,0:T(8,128)(2,1)}, bf16[128,1536]{1,0:T(8,128)(2,1)S(1)}, u32[]{:S(2)}, u32[]{:S(2)}) collective-permute-start(bf16[128,1536]{1,0:T(8,128)(2,1)} %bitcast.28), channel_id=1, source_target_pairs={{0,2},{2,0},{4,6},{6,4},{1,3},{3,1},{5,7},{7,5},{8,10},{10,8},{12,... | collective-permute-start | bytes 1179656 | tf_op jit(solution)/shard_map/ppermute | solution.py:26
  3.7 15.2 %copy-start.12 = (s32[1,1,128]{2,1,0:T(1,128)S(1)}, s32[1,1,128]{2,1,0:T(1,128)}, u32[]{:S(2)}) copy-start(s32[1,1,128]{2,1,0:T(1,128)} %param.5) | copy-start | bytes 1540
  13.0 4.6 %copy-start.4 = (bf16[128,1536]{1,0:T(8,128)(2,1)}, bf16[128,1536]{1,0:T(8,128)(2,1)S(1)}, u32[]{:S(2)}) copy-start(bf16[128,1536]{1,0:T(8,128)(2,1)S(1)} %collective-permute-done.1.refs_0_) | copy-start | bytes 1179652
  13.0 30.5 %collective-permute-start.3 = (bf16[128,1536]{1,0:T(8,128)(2,1)S(1)}, bf16[128,1536]{1,0:T(8,128)(2,1)S(1)}, u32[]{:S(2)}, u32[]{:S(2)}) collective-permute-start(bf16[128,1536]{1,0:T(8,128)(2,1)S(1)} %collective-permute-done.1.refs_0_), channel_id=1, source_target_pairs={{0,2},{2,0},{4,6},{6,4},{1,3},{3,1},{5,7},{7,5},{8,10},{10,8},{12,... | collective-permute-start | bytes 1179656 | tf_op jit(solution)/shard_map/ppermute | solution.py:26
  15.0 42.6 %collective-permute-start.2 = (bf16[128,1536]{1,0:T(8,128)(2,1)S(1)}, bf16[128,1536]{1,0:T(8,128)(2,1)S(1)}, u32[]{:S(2)}, u32[]{:S(2)}) collective-permute-start(bf16[128,1536]{1,0:T(8,128)(2,1)S(1)} %get-tuple-element.6), channel_id=1, source_target_pairs={{0,1},{1,0},{2,3},{3,2},{4,5},{5,4},{6,7},{7,6},{8,9},{9,8},{10,11... | collective-permute-start | bytes 1179656 | tf_op jit(solution)/shard_map/ppermute | solution.py:21
  17.6 41.0 %collective-permute-start.8 = (bf16[3,7,128,128]{3,2,1,0:T(8,128)(2,1)}, bf16[3,7,128,128]{3,2,1,0:T(8,128)(2,1)S(1)}, u32[]{:S(2)}, u32[]{:S(2)}) collective-permute-start(bf16[3,7,128,128]{3,2,1,0:T(8,128)(2,1)} %slice.9), channel_id=1, source_target_pairs={{8,0},{16,8},{24,16},{9,1},{17,9},{25,17},{10,2},{18,10},{26,18},{... | collective-permute-start | bytes 2064392 | tf_op jit(solution)/shard_map/ppermute | solution.py:31
  18.9 37.4 %collective-permute-start.7 = (s32[1,128]{1,0:T(1,128)S(1)}, s32[1,128]{1,0:T(1,128)S(1)}, u32[]{:S(2)}, u32[]{:S(2)}) collective-permute-start(s32[1,128]{1,0:T(1,128)S(1)} %bitcast.32), channel_id=1, source_target_pairs={{8,0},{16,8},{24,16},{9,1},{17,9},{25,17},{10,2},{18,10},{26,18},{... | collective-permute-start | bytes 1544 | tf_op jit(solution)/shard_map/ppermute | solution.py:31
  28.1 4.8 %copy-start.1 = (bf16[128,1536]{1,0:T(8,128)(2,1)S(1)}, bf16[128,1536]{1,0:T(8,128)(2,1)}, u32[]{:S(2)}) copy-start(bf16[128,1536]{1,0:T(8,128)(2,1)} %forward.1.refs_0_) | copy-start | bytes 1179652
  32.9 0.8 copy-start.2
  32.9 49.8 %collective-permute-start = (bf16[128,1536]{1,0:T(8,128)(2,1)S(1)}, bf16[128,1536]{1,0:T(8,128)(2,1)S(1)}, u32[]{:S(2)}, u32[]{:S(2)}) collective-permute-start(bf16[128,1536]{1,0:T(8,128)(2,1)S(1)} %copy-done.1), channel_id=1, source_target_pairs={{0,1},{1,0},{2,3},{3,2},{4,5},{5,4},{6,7},{7,6},{8,9},{9,8},{10,11... | collective-permute-start | bytes 1179656 | tf_op jit(solution)/shard_map/ppermute | solution.py:21
  43.5 0.7 copy-start.5
  49.2 8.6 %copy-start.3 = (bf16[128,1536]{1,0:T(8,128)(2,1)S(1)}, bf16[128,1536]{1,0:T(8,128)(2,1)}, u32[]{:S(2)}) copy-start(bf16[128,1536]{1,0:T(8,128)(2,1)} %copy-done.2) | copy-start | bytes 1179652
  49.2 8.6 %copy-start.6 = (bf16[128,1536]{1,0:T(8,128)(2,1)S(1)}, bf16[128,1536]{1,0:T(8,128)(2,1)}, u32[]{:S(2)}) copy-start(bf16[128,1536]{1,0:T(8,128)(2,1)} %copy-done.5) | copy-start | bytes 1179652
  54.4 37.9 %collective-permute-start.6 = (bf16[3,5,128,128]{3,2,1,0:T(8,128)(2,1)}, bf16[3,5,128,128]{3,2,1,0:T(8,128)(2,1)S(1)}, u32[]{:S(2)}, u32[]{:S(2)}) collective-permute-start(bf16[3,5,128,128]{3,2,1,0:T(8,128)(2,1)} %backward.2), channel_id=1, source_target_pairs={{8,0},{16,8},{24,16},{9,1},{17,9},{25,17},{10,2},{18,10},{26,18},{... | collective-permute-start | bytes 1474568 | tf_op jit(solution)/shard_map/ppermute | solution.py:31
  56.3 19.7 %copy-start.13 = (s32[1,128]{1,0:T(1,128)}, s32[1,128]{1,0:T(1,128)S(1)}, u32[]{:S(2)}) copy-start(s32[1,128]{1,0:T(1,128)S(1)} %collective-permute-done.7.pos_ref) | copy-start | bytes 1540
  56.3 19.7 %collective-permute-start.9 = (bf16[128,896]{1,0:T(8,128)(2,1)}, bf16[128,896]{1,0:T(8,128)(2,1)}, u32[]{:S(2)}, u32[]{:S(2)}) collective-permute-start(bf16[128,896]{1,0:T(8,128)(2,1)} %get-tuple-element.5), channel_id=1, source_target_pairs={{8,0},{16,8},{24,16},{9,1},{17,9},{25,17},{10,2},{18,10},{26,18},{... | collective-permute-start | bytes 688136 | tf_op jit(solution)/shard_map/ppermute | solution.py:31
  57.6 25.1 %copy-start.9 = (bf16[128,1536]{1,0:T(8,128)(2,1)}, bf16[128,1536]{1,0:T(8,128)(2,1)S(1)}, u32[]{:S(2)}) copy-start(bf16[128,1536]{1,0:T(8,128)(2,1)S(1)} %collective-permute-done.2.refs_3_) | copy-start | bytes 1179652
  57.6 25.1 %collective-permute-start.5 = (bf16[128,1536]{1,0:T(8,128)(2,1)S(1)}, bf16[128,1536]{1,0:T(8,128)(2,1)S(1)}, u32[]{:S(2)}, u32[]{:S(2)}) collective-permute-start(bf16[128,1536]{1,0:T(8,128)(2,1)S(1)} %collective-permute-done.2.refs_3_), channel_id=1, source_target_pairs={{0,2},{2,0},{4,6},{6,4},{1,3},{3,1},{5,7},{7,5},{8,10},{10,8},{12,... | collective-permute-start | bytes 1179656 | tf_op jit(solution)/shard_map/ppermute | solution.py:26
  58.6 17.4 %copy-start.7 = (bf16[3,7,128,128]{3,2,1,0:T(8,128)(2,1)}, bf16[3,7,128,128]{3,2,1,0:T(8,128)(2,1)S(1)}, u32[]{:S(2)}) copy-start(bf16[3,7,128,128]{3,2,1,0:T(8,128)(2,1)S(1)} %collective-permute-done.8.qkv_ref) | copy-start | bytes 2064388
  82.7 0.7 copy-start.10
  82.7 0.9 copy-start.11
  92.3 0.8 copy-start.8

commit v2 on v0

v2 whole, which is shorter than its diff:
```python
import functools
import math

import jax
import jax.numpy as jnp
from jax import lax
from jax.experimental import pallas as pl
from jax.experimental.pallas import tpu as pltpu
from jax.sharding import PartitionSpec as P


F32 = jnp.float32
BF16 = jnp.bfloat16
VMEM = pl.BlockSpec(memory_space=pltpu.VMEM)
SMEM = pl.BlockSpec(memory_space=pltpu.SMEM)
ANY = pl.BlockSpec(memory_space=pl.ANY)
HBM = pl.BlockSpec(memory_space=pltpu.HBM)
PARAMS = pltpu.CompilerParams(vmem_limit_bytes=24 * 2**20)


def dot(a, b, dims):
    return lax.dot_general(a, b, ((dims[0], dims[1]), ((), ())), preferred_element_type=F32)


def rotate(value, axis, steps):
    count = lax.axis_size(axis)
    return lax.ppermute(value, axis, [(i, (i + steps) % count) for i in range(count)])


def swap(value, axis):
    count = lax.axis_size(axis)
    return lax.ppermute(value, axis, [(i, i ^ 1) for i in range(count)])


def down(value, axis):
    count = lax.axis_size(axis)
    return lax.ppermute(value, axis, [(i, i - 1) for i in range(1, count)])


def masked_softmax(pos_ref, qkv_ref, heads):
    width = qkv_ref.shape[-1]
    seq = pos_ref.shape[-1]
    scale = 1.0 / math.sqrt(width)
    queries = jnp.broadcast_to(pos_ref[...].astype(F32), (seq, seq))
    visible = queries.T <= queries
    probs = []
    for head in heads:
        scores = dot(qkv_ref[1, head], qkv_ref[0, head], ((1,), (1,))) * scale
        scores = jnp.where(visible, scores, -1e30)
        exponent = jnp.exp(scores - jnp.max(scores, axis=0, keepdims=True))
        probs.append(exponent * (1.0 / jnp.sum(exponent, axis=0, keepdims=True)))
    return probs


def place():
    me = lax.axis_index("st")
    return lax.div(me, 2), lax.rem(me, 2)


def rows_of(weight_ref, depth, chips, step, crossed):
    chip, core = place()
    owner = 2 * lax.rem(chip - step + chips, chips) + (1 - core if crossed else core)
    return weight_ref.at[pl.ds(pl.multiple_of(owner * depth, depth), depth)]


def forward_kernel(chips, pos_ref, qkv_ref, weight_ref, out_ref, *refs):
    heads, _, width = qkv_ref.shape[1:]
    kept, sems = refs[:-1], refs[-1]
    gets = [
        pltpu.make_async_copy(
            rows_of(weight_ref, ref.shape[0], chips, step, False), ref, sems.at[step]
        )
        for step, ref in enumerate(kept, 1)
    ]
    for get in gets:
        get.start()
    for head, probs in enumerate(masked_softmax(pos_ref, qkv_ref, range(heads))):
        attended = dot(probs.astype(BF16), qkv_ref[2, head], ((0,), (0,)))
        out_ref[:, head * width : (head + 1) * width] = attended.astype(BF16)
    for get in gets:
        get.wait()


def forward(chips, depth, pos, qkv, weight):
    _, heads, seq, width = qkv.shape
    kept = [pltpu.VMEM((depth, weight.shape[1]), BF16)] * (chips - 1)
    return pl.pallas_call(
        functools.partial(forward_kernel, chips),
        name="forward",
        in_specs=[VMEM, VMEM, HBM],
        out_specs=[VMEM] * chips,
        out_shape=[jax.ShapeDtypeStruct((seq, heads * width), BF16)] + kept,
        scratch_shapes=[pltpu.SemaphoreType.DMA((chips,))],
        compiler_params=PARAMS,
    )(pos, qkv, weight)


def backward_kernel(first, pos_ref, qkv_ref, grad_ref, out_ref, buffer, sems):
    heads, _, width = buffer.shape[1:]
    scale = 1.0 / math.sqrt(width)
    copies = []
    all_probs = masked_softmax(pos_ref, qkv_ref, range(first, first + heads))
    for number, probs in enumerate(all_probs):
        head = first + number
        query, key, value = qkv_ref[0, head], qkv_ref[1, head], qkv_ref[2, head]
        grad = grad_ref[:, number * width : (number + 1) * width]
        d_value = dot(probs.astype(BF16), grad, ((1,), (0,)))
        d_probs = dot(value, grad, ((1,), (1,)))
        row_dot = jnp.sum(probs * d_probs, axis=0, keepdims=True)
        d_scores = (probs * (d_probs - row_dot)).astype(BF16)
        d_key = dot(d_scores, query, ((1,), (0,))) * scale
        d_query = dot(d_scores, key, ((0,), (0,))) * scale
        buffer[0, number] = d_query.astype(BF16)
        buffer[1, number] = d_key.astype(BF16)
        buffer[2, number] = d_value.astype(BF16)
        copy = pltpu.make_async_copy(
            buffer.at[:, number], out_ref.at[:, number], sems.at[number]
        )
        copy.start()
        copies.append(copy)
    for copy in copies:
        copy.wait()


def backward(pos, qkv, grad, first, total):
    _, _, seq, width = qkv.shape
    heads = grad.shape[1] // width
    return pl.pallas_call(
        functools.partial(backward_kernel, first),
        name="backward",
        in_specs=[VMEM, VMEM, VMEM],
        out_specs=ANY,
        out_shape=jax.ShapeDtypeStruct((3, total, seq, width), BF16),
        scratch_shapes=[
            pltpu.VMEM((3, heads, seq, width), BF16),
            pltpu.SemaphoreType.DMA((heads,)),
        ],
        compiler_params=PARAMS,
    )(pos, qkv, grad)


def fill_kernel(late_ref, whole_ref, out_ref, buffer, in_sems, out_sems):
    late = late_ref.shape[1]
    first = out_ref.shape[1] - late
    gets = [
        pltpu.make_async_copy(late_ref.at[i], buffer.at[i], in_sems.at[i]) for i in range(3)
    ]
    puts = [
        pltpu.make_async_copy(buffer.at[i], out_ref.at[i, pl.ds(first, late)], out_sems.at[i])
        for i in range(3)
    ]
    for get in gets:
        get.start()
    for get, put in zip(gets, puts):
        get.wait()
        put.start()
    for put in puts:
        put.wait()


def fill(late, whole):
    return pl.pallas_call(
        fill_kernel,
        name="fill",
        in_specs=[ANY, ANY],
        out_specs=ANY,
        out_shape=jax.ShapeDtypeStruct(whole.shape, whole.dtype),
        scratch_shapes=[
            pltpu.VMEM(late.shape, late.dtype),
            pltpu.SemaphoreType.DMA((3,)),
            pltpu.SemaphoreType.DMA((3,)),
        ],
        input_output_aliases={1: 0},
        compiler_params=PARAMS,
    )(late, whole)


def open_kernel(chips, weight_ref, own_ref, mate_ref, total_ref, *refs):
    kept, (buffer, sems) = refs[:-2], refs[-2:]
    depth = own_ref.shape[1]
    gets = [
        pltpu.make_async_copy(
            rows_of(weight_ref, depth, chips, 0, crossed), buffer.at[crossed], sems.at[chips + crossed]
        )
        for crossed in range(2)
    ]
    gets += [
        pltpu.make_async_copy(
            rows_of(weight_ref, depth, chips, step, True), ref, sems.at[step]
        )
        for step, ref in enumerate(kept, 1)
    ]
    for get in gets:
        get.start()
    gets[0].wait()
    total_ref[...] = jnp.dot(own_ref[...], buffer[0], preferred_element_type=F32)
    gets[1].wait()
    total_ref[...] += jnp.dot(mate_ref[...], buffer[1], preferred_element_type=F32)
    for get in gets[2:]:
        get.wait()


def open_project(chips, weight, own, mate):
    seq, depth = own.shape
    columns = weight.shape[1]
    kept = [pltpu.VMEM((depth, columns), BF16)] * (chips - 1)
    return pl.pallas_call(
        functools.partial(open_kernel, chips),
        name="open_project",
        in_specs=[HBM, VMEM, VMEM],
        out_specs=[VMEM] * chips,
        out_shape=[jax.ShapeDtypeStruct((seq, columns), F32)] + kept,
        scratch_shapes=[
            pltpu.VMEM((2, depth, columns), BF16),
            pltpu.SemaphoreType.DMA((chips + 2,)),
        ],
        compiler_params=PARAMS,
    )(weight, own, mate)


def project_kernel(splits, weight_ref, grad_ref, carried_ref, *outs):
    total = carried_ref[...] + jnp.dot(
        grad_ref[...], weight_ref[...], preferred_element_type=F32
    )
    at = 0
    for out, size in zip(outs, splits):
        out[...] = total[:, at : at + size].astype(out.dtype)
        at += size


def project(weight, grad, total, splits, dtype):
    seq = grad.shape[0]
    return pl.pallas_call(
        functools.partial(project_kernel, splits),
        name="project",
        in_specs=[VMEM] * 3,
        out_specs=[VMEM] * len(splits),
        out_shape=[jax.ShapeDtypeStruct((seq, size), dtype) for size in splits],
        compiler_params=PARAMS,
    )(weight, grad, total)


def choose_kernel(chips, per_replica, number, step, replicas, *refs):
    chip, _ = place()
    target = lax.rem(lax.axis_index("dp") + step, replicas)
    index = lax.rem(chip - (target * per_replica + number) + chips, chips)
    out_ref = refs[-1]
    for option, ref in enumerate(refs[:-1]):

        @pl.when(index == option)
        def _():
            out_ref[...] = ref[...]


def choose(replicas, number, step, options):
    chips = len(options)
    return pl.pallas_call(
        functools.partial(choose_kernel, chips, chips // replicas, number, step, replicas),
        name="choose",
        in_specs=[VMEM] * chips,
        out_specs=VMEM,
        out_shape=jax.ShapeDtypeStruct(options[0].shape, options[0].dtype),
        compiler_params=PARAMS,
    )(*options)


def weight_kernel(replicas, chips, slots, blocks, *refs):
    acts = refs[:replicas]
    same = refs[replicas : replicas + chips]
    other = refs[replicas + chips : replicas + 2 * chips]
    far = refs[replicas + 2 * chips : -2]
    out_ref, stacked = refs[-2:]
    step = pl.program_id(0)
    seq = acts[0].shape[0]
    size = out_ref.shape[0]
    chip, _ = place()

    @pl.when(step == 0)
    def _():
        for number, act in enumerate(acts):
            stacked[number * seq : (number + 1) * seq] = act[...]

    columns = pl.ds(pl.multiple_of(lax.rem(step, blocks) * size, size), size)
    for slot in range(slots):

        @pl.when(lax.div(step, blocks) == slot)
        def _():
            options = other if slot % 2 else same
            index = lax.rem(
                chip - (lax.axis_index("dp") * (slots // 2) + slot // 2) + chips, chips
            )
            near = options[0][:, columns]
            for number in range(1, chips):
                near = jnp.where(index == number, options[number][:, columns], near)
            ours = far[slot * (replicas - 1) : (slot + 1) * (replicas - 1)]
            left = jnp.concatenate([near] + [ref[:, columns] for ref in ours], axis=0)
            out_ref[...] = dot(left, stacked[...], ((0,), (0,))).astype(BF16)


def weight_gradient(acts, same, other, far):
    replicas, chips, slots = len(acts), len(same), len(far)
    seq, columns = acts[0].shape
    features = same[0].shape[1]
    blocks = max(1, features // 768)
    while features % blocks or (features // blocks) % 128:
        blocks -= 1
    size = features // blocks

    def target(step):
        slot = lax.div(step, blocks)
        core = lax.rem(lax.axis_index("st") + slot, 2)
        return (2 * lax.div(slot, 2) + core) * blocks + lax.rem(step, blocks), 0

    args = [*acts, *same, *other, *[ref for slot in far for ref in slot]]
    return pl.pallas_call(
        functools.partial(weight_kernel, replicas, chips, slots, blocks),
        name="weight_gradient",
        grid=(slots * blocks,),
        in_specs=[VMEM] * len(args),
        out_specs=pl.BlockSpec((size, columns), target),
        scratch_shapes=[pltpu.VMEM((replicas * seq, columns), BF16)],
        out_shape=jax.ShapeDtypeStruct((slots * features, columns), BF16),
        compiler_params=PARAMS,
    )(*args)


def local(saved_qkv, positions, w_out, grad_out):
    qkv = saved_qkv[0, 0].transpose(0, 2, 1, 3)
    pos = positions[0]
    weight = pltpu.with_memory_space_constraint(w_out[0], pltpu.HBM)
    heads, _, width = qkv.shape[1:]
    early = max(1, heads // 2)
    late = heads - early
    shards = lax.axis_size("st")
    replicas = lax.axis_size("dp")
    chips = shards // 2
    per_replica = chips // replicas

    qkv_above = down(qkv[:, :early], "section")
    same = [grad_out[0, 0]]
    for step in range(1, chips):
        same.append(rotate(same[0], "st", 2 * step))
    other = []
    for step in range(chips):
        other.append(swap(same[step], "st"))

    attended, *straight_rows = forward(chips, grad_out.shape[-1], pos, qkv, weight)
    acts = [attended]
    for step in range(1, replicas):
        acts.append(rotate(attended, "dp", step))
    pos_above = down(pos, "section")

    whole = (heads * width,)
    halves = (early * width, late * width)
    total, *crossed_rows = open_project(chips, weight, same[0], other[0])
    for step in range(1, chips):
        last = step == chips - 1
        (total,) = project(straight_rows[step - 1], same[step], total, whole, F32)
        total = project(
            crossed_rows[step - 1],
            other[step],
            total,
            halves if last else whole,
            BF16 if last else F32,
        )
        if not last:
            (total,) = total
    d_early, d_late = total
    d_above = down(d_early, "section")
    grads_late = backward(pos, qkv, d_late, early, late)
    late_above = down(grads_late, "section")

    far = []
    for number in range(per_replica):
        direct, crossed = [], []
        for step in range(1, replicas):
            chosen = choose(replicas, number, step, same)
            direct.append(rotate(chosen, "dp", step))
            crossed.append(swap(direct[-1], "st"))
        far += [direct, crossed]

    begun = backward(pos_above, qkv_above, d_above, 0, heads)
    grad_weight = weight_gradient(acts, same, other, far)
    upstream = fill(late_above, begun)
    return (grad_weight[None], upstream.transpose(0, 2, 1, 3)[None, None])


def solution(mesh):
    in_specs = (
        P("section", "dp", None, None, "st", None),
        P("section", "dp", None),
        P("section", None, "st"),
        P("section", "dp", None, "st"),
    )
    out_specs = (P("section", "dp", "st"), P("section", "dp", None, None, "st", None))

    return jax.shard_map(local, mesh=mesh, in_specs=in_specs, out_specs=out_specs, check_vma=False)
```

time: 125 us -> 68.4 us (0.55)
  matrix products: 25.3 us -> 0 us
  Pallas kernels: 0 us -> 21.8 us
  blocking collectives: 19.9 us -> 0 us
  other arithmetic: 18.8 us -> 0 us
  local copies, waits for them, and re-layouts: 19.7 us -> 4.03 us
  between operations: 14.2 us -> 0.8 us
  waiting for transfers between devices: 21.5 us -> 31.1 us
  starting transfers between devices: 5.12 us -> 10.4 us
    ppermute x1 -> x10, waiting for transfers between devices: 0.01 us -> 31.1 us  [the longest x4 21.8 us: down(): return lax.ppermute(value, axis, [(i, i - 1) for i in range(1, count)])]
    dot_general x8 -> x0, matrix products: 25.3 us -> none  [the longest x1 9.6 us: local(): jnp.dot(full_grad, w_out[0], preferred_element_type=jnp.float32)]
    pallas_call x0 -> x9, Pallas kernels: none -> 21.8 us  [the longest x1 5.51 us: weight_gradient(): pl.pallas_call(functools.partial(weight_kernel, replicas, chips, slots, b...]
    all_gather x1 -> x0, waiting for transfers between devices: 21.4 us -> none  [local(): full_grad = lax.all_gather(grad_out[0, 0], 'st', axis=1, tiled=True)]
    all_gather x1 -> x0, blocking collectives: 19.9 us -> none  [local(): acts_rows = lax.all_gather(flat_att, 'dp', axis=0, tiled=True)]
    reduce_sum x1 -> x0, other arithmetic: 16.8 us -> none  [local(): jnp.sum(rounded.astype(jnp.float32), axis=0).astype(jnp.bfloat16)]
    unnamed x13 -> x10, local copies, waits for them, and re-layouts: 17 us -> 2.93 us
    ppermute x1 -> x10, starting transfers between devices: 1.28 us -> 10.4 us  [the longest x3 5.22 us: rotate(): lax.ppermute(value, axis, [(i, (i + steps) % count) for i in range(count)])]
  transfers between devices with their start and end apart: 3 -> 10, of which waited for: 1 -> 3; matrix products, arithmetic and copies ran while one was open for 38% -> 2% of each run, Pallas kernels for 0% -> 30%
where the time goes in v2:
time: 68.4 us; the launch traced here: 68.1 us
  waiting for transfers between devices  31.1 us (45%)
  Pallas kernels  21.8 us (32%)
  starting transfers between devices  10.4 us (15%)
  local copies, waits for them, and re-layouts  4.03 us (6%)
  between operations  0.8 us (1%)
    ppermute x4, waiting for transfers between devices, down(): return lax.ppermute(value, axis, [(i, i - 1) for i in range(1, count)])  21.8 us
    ppermute x3, waiting for transfers between devices, rotate(): lax.ppermute(value, axis, [(i, (i + steps) % count) for i in range(count)])  9.33 us
    pallas_call x1, Pallas kernels, weight_gradient(): pl.pallas_call(functools.partial(weight_kernel, replicas, chips, slots, b...  5.51 us
    ppermute x3, starting transfers between devices, rotate(): lax.ppermute(value, axis, [(i, (i + steps) % count) for i in range(count)])  5.22 us
    pallas_call x1, Pallas kernels, open_project(): pl.pallas_call(functools.partial(open_kernel, chips), name='open_project'...  5.17 us
    ppermute x4, starting transfers between devices, down(): return lax.ppermute(value, axis, [(i, i - 1) for i in range(1, count)])  5.15 us
    pallas_call x2, Pallas kernels, backward(): pl.pallas_call(functools.partial(backward_kernel, first), name='backward'...  4.99 us
    unnamed x10, local copies, waits for them, and re-layouts  2.93 us
  transfers between devices with their start and end apart: 10, of which 3 were waited for; matrix products, arithmetic and copies ran while one was open for 2% of the time, Pallas kernels for 30%

profile of v2, /device:TPU:0, one launch (start us, length us, event | category | flops | bytes accessed | tf_op | source)
XLA Modules:
  0.0 68.1 jit_solution(12228076384686210526)
XLA Ops:
  0.6 3.1 %collective-permute-start.1 = (bf16[128,1536]{1,0:T(8,128)(2,1)}, bf16[128,1536]{1,0:T(8,128)(2,1)S(1)}, u32[]{:S(2)}, u32[]{:S(2)}) collective-permute-start(bf16[128,1536]{1,0:T(8,128)(2,1)} %bitcast.13), channel_id=1, source_target_pairs={{0,4},{2,6},{4,0},{6,2},{1,5},{3,7},{5,1},{7,3},{8,12},{10,14},{12... | collective-permute-start | bytes 1179656 | tf_op jit(solution)/shard_map/ppermute | solution.py:27
  3.7 0.0 collective-permute-start.2
  3.7 9.3 %collective-permute-done.1.refs_1_.refs_3_.grad_ref = bf16[128,1536]{1,0:T(8,128)(2,1)S(1)} collective-permute-done((bf16[128,1536]{1,0:T(8,128)(2,1)}, bf16[128,1536]{1,0:T(8,128)(2,1)S(1)}, u32[]{:S(2)}, u32[]{:S(2)}) %collective-permute-start.1) | collective-permute-done | bytes 393248 | tf_op jit(solution)/shard_map/ppermute | solution.py:27
  13.0 0.0 collective-permute-start.3
  13.0 0.0 copy-start.2
  13.0 1.0 %copy-done.2 = bf16[1,1,128,1536]{3,2,1,0:T(8,128)(2,1)S(1)} copy-done((bf16[1,1,128,1536]{3,2,1,0:T(8,128)(2,1)S(1)}, bf16[1,1,128,1536]{3,2,1,0:T(8,128)(2,1)}, u32[]{:S(2)}) %copy-start.2) | copy-done | bytes 393240
  14.0 1.8 %collective-permute-start.4 = (bf16[128,1536]{1,0:T(8,128)(2,1)S(1)}, bf16[128,1536]{1,0:T(8,128)(2,1)S(1)}, u32[]{:S(2)}, u32[]{:S(2)}) collective-permute-start(bf16[128,1536]{1,0:T(8,128)(2,1)S(1)} %choose.1), channel_id=1, source_target_pairs={{0,1},{1,0},{2,3},{3,2},{4,5},{5,4},{6,7},{7,6},{8,9},{9,8},{10,11... | collective-permute-start | bytes 1179656 | tf_op jit(solution)/shard_map/ppermute | solution.py:27
  15.8 1.1 %slice.4 = bf16[3,6,128,128]{3,2,1,0:T(8,128)(2,1)S(1)} slice(bf16[3,12,128,128]{3,2,1,0:T(8,128)(2,1)} %bitcast.10), slice={[0:3], [0:6], [0:128], [0:128]} | slice | bytes 1179648 | tf_op jit(solution)/shard_map/slice | solution.py:339
  16.9 1.3 %collective-permute-start.8 = (bf16[3,6,128,128]{3,2,1,0:T(8,128)(2,1)S(1)}, bf16[3,6,128,128]{3,2,1,0:T(8,128)(2,1)S(1)}, u32[]{:S(2)}, u32[]{:S(2)}) collective-permute-start(bf16[3,6,128,128]{3,2,1,0:T(8,128)(2,1)S(1)} %slice.4), channel_id=1, source_target_pairs={{8,0},{16,8},{24,16},{9,1},{17,9},{25,17},{10,2},{18,10},{26,18},{... | collective-permute-start | bytes 1769480 | tf_op jit(solution)/shard_map/ppermute | solution.py:37
  18.2 0.0 copy-start
  18.3 1.3 %copy-done = bf16[1,1,3,128,12,128]{5,3,4,2,1,0:T(8,128)(2,1)S(1)} copy-done((bf16[1,1,3,128,12,128]{5,3,4,2,1,0:T(8,128)(2,1)S(1)}, bf16[1,1,3,128,12,128]{5,3,4,2,1,0:T(8,128)(2,1)}, u32[]{:S(2)}) %copy-start) | copy-done | bytes 1179672
  19.5 0.0 copy-start.4
  19.5 0.7 copy-done.4
  20.2 0.0 copy-start.3
  20.2 2.9 %forward.1 = (bf16[128,1536]{1,0:T(8,128)(2,1)S(1)}, bf16[1536,1536]{1,0:T(8,128)(2,1)S(1)}) custom-call(s32[1,128]{1,0:T(1,128)S(1)} %bitcast.18, bf16[3,12,128,128]{3,2,1,0:T(8,128)(2,1)S(1)} %bitcast.11, bf16[6144,1536]{1,0:T(8,128)(2,1)} %bitcast.21), custom_call_target="tpu_custom_call" | custom-call | tf_op jit(solution)/shard_map/forward/pallas_call | solution.py:87
  23.1 0.0 collective-permute-done.2.refs_4_.mate_ref
  23.1 0.0 copy-done.3
  23.1 5.2 %open_project.1 = (f32[128,1536]{1,0:T(8,128)S(1)}, bf16[1536,1536]{1,0:T(8,128)(2,1)S(1)}) custom-call(bf16[6144,1536]{1,0:T(8,128)(2,1)} %bitcast.22, bf16[128,1536]{1,0:T(8,128)(2,1)S(1)} %bitcast.16, bf16[128,1536]{1,0:T(8,128)(2,1)S(1)} %collective-permute-done.2.refs_4_.mate_ref), custom_call_target="tpu_custom_call" | custom-call | tf_op jit(solution)/shard_map/open_project/pallas_call | solution.py:207
  28.3 0.0 copy-start.1
  28.3 0.8 %project.2.carried_ref = f32[128,1536]{1,0:T(8,128)S(1)} custom-call(bf16[1536,1536]{1,0:T(8,128)(2,1)S(1)} %get-tuple-element.10.weight_ref, bf16[128,1536]{1,0:T(8,128)(2,1)S(1)} %collective-permute-done.1.refs_1_.refs_3_.grad_ref, f32[128,1536]{1,0:T(8,128)S(1)} %get-tuple-element.11.carried_ref), custom_call_target="tpu_custom_call" | custom-call | tf_op jit(solution)/shard_map/project/pallas_call | solution.py:233
  29.1 0.0 collective-permute-done.3.refs_5_.grad_ref
  29.1 0.8 %project.3 = (bf16[128,768]{1,0:T(8,128)(2,1)S(1)}, bf16[128,768]{1,0:T(8,128)(2,1)S(1)}) custom-call(bf16[1536,1536]{1,0:T(8,128)(2,1)S(1)} %get-tuple-element.9.weight_ref, bf16[128,1536]{1,0:T(8,128)(2,1)S(1)} %collective-permute-done.3.refs_5_.grad_ref, f32[128,1536]{1,0:T(8,128)S(1)} %project.2.carried_ref), custom_call_target="tpu_custom_call" | custom-call | tf_op jit(solution)/shard_map/project/pallas_call | solution.py:233
  29.9 0.0 copy-done.1
  29.9 2.6 %backward.2 = bf16[3,6,128,128]{3,2,1,0:T(8,128)(2,1)S(1)} custom-call(s32[1,128]{1,0:T(1,128)S(1)} %bitcast.19, bf16[3,12,128,128]{3,2,1,0:T(8,128)(2,1)S(1)} %bitcast.12, bf16[128,768]{1,0:T(8,128)(2,1)S(1)} %get-tuple-element.12.grad_ref), custom_call_target="tpu_custom_call" | custom-call | tf_op jit(solution)/shard_map/backward/pallas_call | solution.py:128
  32.5 1.3 %collective-permute-start.6 = (bf16[3,6,128,128]{3,2,1,0:T(8,128)(2,1)S(1)}, bf16[3,6,128,128]{3,2,1,0:T(8,128)(2,1)S(1)}, u32[]{:S(2)}, u32[]{:S(2)}) collective-permute-start(bf16[3,6,128,128]{3,2,1,0:T(8,128)(2,1)S(1)} %backward.2), channel_id=1, source_target_pairs={{8,0},{16,8},{24,16},{9,1},{17,9},{25,17},{10,2},{18,10},{26,18},{... | collective-permute-start | bytes 1769480 | tf_op jit(solution)/shard_map/ppermute | solution.py:37
  33.8 0.4 collective-permute-start
  34.2 0.0 collective-permute-done.4.refs_6_
  34.2 0.0 collective-permute-start.5
  34.2 1.3 %collective-permute-start.7 = (s32[1,128]{1,0:T(1,128)S(1)}, s32[1,128]{1,0:T(1,128)S(1)}, u32[]{:S(2)}, u32[]{:S(2)}) collective-permute-start(s32[1,128]{1,0:T(1,128)S(1)} %bitcast.20), channel_id=1, source_target_pairs={{8,0},{16,8},{24,16},{9,1},{17,9},{25,17},{10,2},{18,10},{26,18},{... | collective-permute-start | bytes 1544 | tf_op jit(solution)/shard_map/ppermute | solution.py:37
  35.5 15.1 %collective-permute-done.7.pos_ref = s32[1,128]{1,0:T(1,128)S(1)} collective-permute-done((s32[1,128]{1,0:T(1,128)S(1)}, s32[1,128]{1,0:T(1,128)S(1)}, u32[]{:S(2)}, u32[]{:S(2)}) %collective-permute-start.7) | collective-permute-done | bytes 544 | tf_op jit(solution)/shard_map/ppermute | solution.py:37
  50.6 1.3 %collective-permute-start.9 = (bf16[128,768]{1,0:T(8,128)(2,1)S(1)}, bf16[128,768]{1,0:T(8,128)(2,1)S(1)}, u32[]{:S(2)}, u32[]{:S(2)}) collective-permute-start(bf16[128,768]{1,0:T(8,128)(2,1)S(1)} %get-tuple-element.13), channel_id=1, source_target_pairs={{8,0},{16,8},{24,16},{9,1},{17,9},{25,17},{10,2},{18,10},{26,18},{... | collective-permute-start | bytes 589832 | tf_op jit(solution)/shard_map/ppermute | solution.py:37
  51.9 0.0 collective-permute-done.8.qkv_ref
  51.9 6.7 %collective-permute-done.9.grad_ref = bf16[128,768]{1,0:T(8,128)(2,1)S(1)} collective-permute-done((bf16[128,768]{1,0:T(8,128)(2,1)S(1)}, bf16[128,768]{1,0:T(8,128)(2,1)S(1)}, u32[]{:S(2)}, u32[]{:S(2)}) %collective-permute-start.9) | collective-permute-done | bytes 196640 | tf_op jit(solution)/shard_map/ppermute | solution.py:37
  58.6 2.4 %backward.3.whole_ref = bf16[3,12,128,128]{3,2,1,0:T(8,128)(2,1)} custom-call(s32[1,128]{1,0:T(1,128)S(1)} %collective-permute-done.7.pos_ref, bf16[3,6,128,128]{3,2,1,0:T(8,128)(2,1)S(1)} %collective-permute-done.8.qkv_ref, bf16[128,768]{1,0:T(8,128)(2,1)S(1)} %collective-permute-done.9.grad_ref), custom_call_target="tpu_custom_call" | custom-call | tf_op jit(solution)/shard_map/backward/pallas_call | solution.py:128
  61.0 0.0 collective-permute-done.refs_1_
  61.0 0.0 collective-permute-done.5.refs_7_
  61.0 5.5 %weight_gradient.1 = bf16[3072,1536]{1,0:T(8,128)(2,1)} custom-call(bf16[128,1536]{1,0:T(8,128)(2,1)S(1)} %get-tuple-element.8.refs_0_, bf16[128,1536]{1,0:T(8,128)(2,1)S(1)} %collective-permute-done.refs_1_, bf16[128,1536]{1,0:T(8,128)(2,1)S(1)} %bitcast.17, bf16[128,1536]{1,0:T(8,128)(2,1)S(1)} %collective-permute-done.1.refs_1_.refs_3_.grad_ref, ...), custom_call_target="tpu_custom_call" | custom-call | tf_op jit(solution)/shard_map/weight_gradient/pallas_call | solution.py:315
  66.5 0.0 collective-permute-done.6.late_ref
  66.5 1.6 %fill.1 = bf16[3,12,128,128]{3,2,1,0:T(8,128)(2,1)} custom-call(bf16[3,6,128,128]{3,2,1,0:T(8,128)(2,1)S(1)} %collective-permute-done.6.late_ref, bf16[3,12,128,128]{3,2,1,0:T(8,128)(2,1)} %backward.3.whole_ref), custom_call_target="tpu_custom_call", output_to_operand_aliasing={{}: (1, {})} | custom-call | tf_op jit(solution)/shard_map/fill/pallas_call | solution.py:162
  (1 shorter events, 0.0 us)
Async XLA Ops:
  0.6 12.4 %collective-permute-start.1 = (bf16[128,1536]{1,0:T(8,128)(2,1)}, bf16[128,1536]{1,0:T(8,128)(2,1)S(1)}, u32[]{:S(2)}, u32[]{:S(2)}) collective-permute-start(bf16[128,1536]{1,0:T(8,128)(2,1)} %bitcast.13), channel_id=1, source_target_pairs={{0,4},{2,6},{4,0},{6,2},{1,5},{3,7},{5,1},{7,3},{8,12},{10,14},{12... | collective-permute-start | bytes 1179656 | tf_op jit(solution)/shard_map/ppermute | solution.py:27
  3.7 19.4 %collective-permute-start.2 = (bf16[128,1536]{1,0:T(8,128)(2,1)}, bf16[128,1536]{1,0:T(8,128)(2,1)S(1)}, u32[]{:S(2)}, u32[]{:S(2)}) collective-permute-start(bf16[128,1536]{1,0:T(8,128)(2,1)} %bitcast.14), channel_id=1, source_target_pairs={{0,2},{2,0},{4,6},{6,4},{1,3},{3,1},{5,7},{7,5},{8,10},{10,8},{12,... | collective-permute-start | bytes 1179656 | tf_op jit(solution)/shard_map/ppermute | solution.py:32
  13.0 16.1 %collective-permute-start.3 = (bf16[128,1536]{1,0:T(8,128)(2,1)S(1)}, bf16[128,1536]{1,0:T(8,128)(2,1)S(1)}, u32[]{:S(2)}, u32[]{:S(2)}) collective-permute-start(bf16[128,1536]{1,0:T(8,128)(2,1)S(1)} %collective-permute-done.1.refs_1_.refs_3_.grad_ref), channel_id=1, source_target_pairs={{0,2},{2,0},{4,6},{6,4},{1,3},{3,1},{5,7},{7,5},{8,10},{10,8},{12,... | collective-permute-start | bytes 1179656 | tf_op jit(solution)/shard_map/ppermute | solution.py:32
  13.0 1.0 %copy-start.2 = (bf16[1,1,128,1536]{3,2,1,0:T(8,128)(2,1)S(1)}, bf16[1,1,128,1536]{3,2,1,0:T(8,128)(2,1)}, u32[]{:S(2)}) copy-start(bf16[1,1,128,1536]{3,2,1,0:T(8,128)(2,1)} %param.7) | copy-start | bytes 1179652
  14.0 20.1 %collective-permute-start.4 = (bf16[128,1536]{1,0:T(8,128)(2,1)S(1)}, bf16[128,1536]{1,0:T(8,128)(2,1)S(1)}, u32[]{:S(2)}, u32[]{:S(2)}) collective-permute-start(bf16[128,1536]{1,0:T(8,128)(2,1)S(1)} %choose.1), channel_id=1, source_target_pairs={{0,1},{1,0},{2,3},{3,2},{4,5},{5,4},{6,7},{7,6},{8,9},{9,8},{10,11... | collective-permute-start | bytes 1179656 | tf_op jit(solution)/shard_map/ppermute | solution.py:27
  16.9 34.9 %collective-permute-start.8 = (bf16[3,6,128,128]{3,2,1,0:T(8,128)(2,1)S(1)}, bf16[3,6,128,128]{3,2,1,0:T(8,128)(2,1)S(1)}, u32[]{:S(2)}, u32[]{:S(2)}) collective-permute-start(bf16[3,6,128,128]{3,2,1,0:T(8,128)(2,1)S(1)} %slice.4), channel_id=1, source_target_pairs={{8,0},{16,8},{24,16},{9,1},{17,9},{25,17},{10,2},{18,10},{26,18},{... | collective-permute-start | bytes 1769480 | tf_op jit(solution)/shard_map/ppermute | solution.py:37
  18.2 1.3 %copy-start = (bf16[1,1,3,128,12,128]{5,3,4,2,1,0:T(8,128)(2,1)S(1)}, bf16[1,1,3,128,12,128]{5,3,4,2,1,0:T(8,128)(2,1)}, u32[]{:S(2)}) copy-start(bf16[1,1,3,128,12,128]{5,3,4,2,1,0:T(8,128)(2,1)} %param.4) | copy-start | bytes 3538948
  19.5 0.7 copy-start.4
  20.2 2.9 %copy-start.3 = (bf16[1,1,128,1536]{3,2,1,0:T(8,128)(2,1)S(1)}, bf16[1,1,128,1536]{3,2,1,0:T(8,128)(2,1)}, u32[]{:S(2)}) copy-start(bf16[1,1,128,1536]{3,2,1,0:T(8,128)(2,1)} %param.7) | copy-start | bytes 1179652
  28.3 1.6 %copy-start.1 = (bf16[1,1,3,128,12,128]{5,3,4,2,1,0:T(8,128)(2,1)S(1)}, bf16[1,1,3,128,12,128]{5,3,4,2,1,0:T(8,128)(2,1)}, u32[]{:S(2)}) copy-start(bf16[1,1,3,128,12,128]{5,3,4,2,1,0:T(8,128)(2,1)} %param.4) | copy-start | bytes 3538948
  32.5 34.0 %collective-permute-start.6 = (bf16[3,6,128,128]{3,2,1,0:T(8,128)(2,1)S(1)}, bf16[3,6,128,128]{3,2,1,0:T(8,128)(2,1)S(1)}, u32[]{:S(2)}, u32[]{:S(2)}) collective-permute-start(bf16[3,6,128,128]{3,2,1,0:T(8,128)(2,1)S(1)} %backward.2), channel_id=1, source_target_pairs={{8,0},{16,8},{24,16},{9,1},{17,9},{25,17},{10,2},{18,10},{26,18},{... | collective-permute-start | bytes 1769480 | tf_op jit(solution)/shard_map/ppermute | solution.py:37
  33.8 27.1 %collective-permute-start = (bf16[128,1536]{1,0:T(8,128)(2,1)S(1)}, bf16[128,1536]{1,0:T(8,128)(2,1)S(1)}, u32[]{:S(2)}, u32[]{:S(2)}) collective-permute-start(bf16[128,1536]{1,0:T(8,128)(2,1)S(1)} %get-tuple-element.8.refs_0_), channel_id=1, source_target_pairs={{0,1},{1,0},{2,3},{3,2},{4,5},{5,4},{6,7},{7,6},{8,9},{9,8},{10,11... | collective-permute-start | bytes 1179656 | tf_op jit(solution)/shard_map/ppermute | solution.py:27
  34.2 26.8 %collective-permute-start.5 = (bf16[128,1536]{1,0:T(8,128)(2,1)S(1)}, bf16[128,1536]{1,0:T(8,128)(2,1)S(1)}, u32[]{:S(2)}, u32[]{:S(2)}) collective-permute-start(bf16[128,1536]{1,0:T(8,128)(2,1)S(1)} %collective-permute-done.4.refs_6_), channel_id=1, source_target_pairs={{0,2},{2,0},{4,6},{6,4},{1,3},{3,1},{5,7},{7,5},{8,10},{10,8},{12,... | collective-permute-start | bytes 1179656 | tf_op jit(solution)/shard_map/ppermute | solution.py:32
  34.2 16.4 %collective-permute-start.7 = (s32[1,128]{1,0:T(1,128)S(1)}, s32[1,128]{1,0:T(1,128)S(1)}, u32[]{:S(2)}, u32[]{:S(2)}) collective-permute-start(s32[1,128]{1,0:T(1,128)S(1)} %bitcast.20), channel_id=1, source_target_pairs={{8,0},{16,8},{24,16},{9,1},{17,9},{25,17},{10,2},{18,10},{26,18},{... | collective-permute-start | bytes 1544 | tf_op jit(solution)/shard_map/ppermute | solution.py:37
  50.6 8.0 %collective-permute-start.9 = (bf16[128,768]{1,0:T(8,128)(2,1)S(1)}, bf16[128,768]{1,0:T(8,128)(2,1)S(1)}, u32[]{:S(2)}, u32[]{:S(2)}) collective-permute-start(bf16[128,768]{1,0:T(8,128)(2,1)S(1)} %get-tuple-element.13), channel_id=1, source_target_pairs={{8,0},{16,8},{24,16},{9,1},{17,9},{25,17},{10,2},{18,10},{26,18},{... | collective-permute-start | bytes 589832 | tf_op jit(solution)/shard_map/ppermute | solution.py:37

commit v3 on v2

--- a/solution.py
+++ b/solution.py
@@ -14,8 +14,11 @@
 VMEM = pl.BlockSpec(memory_space=pltpu.VMEM)
 SMEM = pl.BlockSpec(memory_space=pltpu.SMEM)
 ANY = pl.BlockSpec(memory_space=pl.ANY)
-HBM = pl.BlockSpec(memory_space=pltpu.HBM)
 PARAMS = pltpu.CompilerParams(vmem_limit_bytes=24 * 2**20)
+
+
+def in_hbm(value):
+    return pltpu.with_memory_space_constraint(value, pltpu.HBM)
 
 
 def dot(a, b, dims):
@@ -37,19 +40,49 @@
     return lax.ppermute(value, axis, [(i, i - 1) for i in range(1, count)])
 
 
-def masked_softmax(pos_ref, qkv_ref, heads):
-    width = qkv_ref.shape[-1]
-    seq = pos_ref.shape[-1]
-    scale = 1.0 / math.sqrt(width)
-    queries = jnp.broadcast_to(pos_ref[...].astype(F32), (seq, seq))
-    visible = queries.T <= queries
-    probs = []
-    for head in heads:
-        scores = dot(qkv_ref[1, head], qkv_ref[0, head], ((1,), (1,))) * scale
-        scores = jnp.where(visible, scores, -1e30)
-        exponent = jnp.exp(scores - jnp.max(scores, axis=0, keepdims=True))
-        probs.append(exponent * (1.0 / jnp.sum(exponent, axis=0, keepdims=True)))
-    return probs
+def visibility(positions):
+    seq = positions.shape[-1]
+    queries = jnp.broadcast_to(positions.astype(F32), (seq, seq))
+    return queries.T <= queries
+
+
+def softmax(visible, query, key):
+    scores = dot(key, query, ((1,), (1,))) * (1.0 / math.sqrt(query.shape[-1]))
+    scores = jnp.where(visible, scores, -1e30)
+    exponent = jnp.exp(scores - jnp.max(scores, axis=0, keepdims=True))
+    return exponent * (1.0 / jnp.sum(exponent, axis=0, keepdims=True))
+
+
+def pack_kernel(rows, pos_ref, qkv_ref, out_ref, held, sems):
+    gets = [
+        pltpu.make_async_copy(
+            qkv_ref.at[i, pl.ds(0, rows)], out_ref.at[pl.ds(i * rows, rows)], sems.at[i]
+        )
+        for i in range(3)
+    ]
+    pos_get = pltpu.make_async_copy(pos_ref, held, sems.at[3])
+    pos_get.start()
+    for get in gets:
+        get.start()
+    pos_get.wait()
+    spare = (out_ref.shape[0] - 3 * rows, out_ref.shape[1])
+    out_ref[3 * rows :] = jnp.broadcast_to(held[...].astype(F32), spare).astype(BF16)
+    for get in gets:
+        get.wait()
+
+
+def pack(pos, qkv, early):
+    _, _, seq, width = qkv.shape
+    rows = early * seq
+    return pl.pallas_call(
+        functools.partial(pack_kernel, rows),
+        name="pack",
+        in_specs=[ANY, ANY],
+        out_specs=VMEM,
+        out_shape=pltpu.VMEM((3 * rows + 16, width), BF16),
+        scratch_shapes=[pltpu.VMEM(pos.shape, pos.dtype), pltpu.SemaphoreType.DMA((4,))],
+        compiler_params=PARAMS,
+    )(in_hbm(pos), in_hbm(qkv.reshape(3, -1, width)))
 
 
 def place():
@@ -63,19 +96,32 @@
     return weight_ref.at[pl.ds(pl.multiple_of(owner * depth, depth), depth)]
 
 
-def forward_kernel(chips, pos_ref, qkv_ref, weight_ref, out_ref, *refs):
-    heads, _, width = qkv_ref.shape[1:]
-    kept, sems = refs[:-1], refs[-1]
+def forward_kernel(chips, groups, pos_ref, qkv_ref, weight_ref, out_ref, *refs):
+    kept, (buffer, head_sems, sems) = refs[:-3], refs[-3:]
+    heads, _, width = buffer.shape[1:]
+    size = heads // groups
+    fetches = []
+    for group in range(groups):
+        part = pl.ds(group * size, size)
+        fetches.append(
+            pltpu.make_async_copy(qkv_ref.at[:, part], buffer.at[:, part], head_sems.at[group])
+        )
     gets = [
         pltpu.make_async_copy(
-            rows_of(weight_ref, ref.shape[0], chips, step, False), ref, sems.at[step]
+            rows_of(weight_ref, ref.shape[0], chips, 1 + number // 2, number % 2),
+            ref,
+            sems.at[number],
         )
-        for step, ref in enumerate(kept, 1)
+        for number, ref in enumerate(kept)
     ]
-    for get in gets:
+    for get in fetches + gets:
         get.start()
-    for head, probs in enumerate(masked_softmax(pos_ref, qkv_ref, range(heads))):
-        attended = dot(probs.astype(BF16), qkv_ref[2, head], ((0,), (0,)))
+    visible = visibility(pos_ref[...])
+    for head in range(heads):
+        if head % size == 0:
+            fetches[head // size].wait()
+        probs = softmax(visible, buffer[0, head], buffer[1, head])
+        attended = dot(probs.astype(BF16), buffer[2, head], ((0,), (0,)))
         out_ref[:, head * width : (head + 1) * width] = attended.astype(BF16)
     for get in gets:
         get.wait()
@@ -83,52 +129,67 @@
 
 def forward(chips, depth, pos, qkv, weight):
     _, heads, seq, width = qkv.shape
-    kept = [pltpu.VMEM((depth, weight.shape[1]), BF16)] * (chips - 1)
-    return pl.pallas_call(
-        functools.partial(forward_kernel, chips),
+    count = 2 * (chips - 1)
+    groups = max(size for size in (1, 2, 3) if heads % size == 0)
+    return pl.pallas_call(
+        functools.partial(forward_kernel, chips, groups),
         name="forward",
-        in_specs=[VMEM, VMEM, HBM],
-        out_specs=[VMEM] * chips,
-        out_shape=[jax.ShapeDtypeStruct((seq, heads * width), BF16)] + kept,
-        scratch_shapes=[pltpu.SemaphoreType.DMA((chips,))],
-        compiler_params=PARAMS,
-    )(pos, qkv, weight)
-
-
-def backward_kernel(first, pos_ref, qkv_ref, grad_ref, out_ref, buffer, sems):
-    heads, _, width = buffer.shape[1:]
+        in_specs=[VMEM, ANY, ANY],
+        out_specs=[VMEM] * (1 + count),
+        out_shape=[jax.ShapeDtypeStruct((seq, heads * width), BF16)]
+        + [pltpu.VMEM((depth, weight.shape[1]), BF16)] * count,
+        scratch_shapes=[
+            pltpu.VMEM(qkv.shape, BF16),
+            pltpu.SemaphoreType.DMA((groups,)),
+            pltpu.SemaphoreType.DMA((count,)),
+        ],
+        compiler_params=PARAMS,
+    )(pos, in_hbm(qkv), weight)
+
+
+def backward_kernel(first, packed, *refs):
+    if packed:
+        packed_ref, grad_ref, out_ref, buffer, sems = refs
+    else:
+        pos_ref, qkv_ref, grad_ref, out_ref, buffer, sems = refs
+    heads, seq, width = buffer.shape[1:]
     scale = 1.0 / math.sqrt(width)
+    positions = packed_ref[3 * heads * seq :][:1] if packed else pos_ref[...]
+    visible = visibility(positions)
     copies = []
-    all_probs = masked_softmax(pos_ref, qkv_ref, range(first, first + heads))
-    for number, probs in enumerate(all_probs):
-        head = first + number
-        query, key, value = qkv_ref[0, head], qkv_ref[1, head], qkv_ref[2, head]
-        grad = grad_ref[:, number * width : (number + 1) * width]
+    for head in range(heads):
+        if packed:
+            query, key, value = (
+                packed_ref[(i * heads + head) * seq : (i * heads + head + 1) * seq]
+                for i in range(3)
+            )
+        else:
+            query, key, value = (qkv_ref[i, first + head] for i in range(3))
+        grad = grad_ref[:, head * width : (head + 1) * width]
+        probs = softmax(visible, query, key)
         d_value = dot(probs.astype(BF16), grad, ((1,), (0,)))
         d_probs = dot(value, grad, ((1,), (1,)))
         row_dot = jnp.sum(probs * d_probs, axis=0, keepdims=True)
         d_scores = (probs * (d_probs - row_dot)).astype(BF16)
         d_key = dot(d_scores, query, ((1,), (0,))) * scale
         d_query = dot(d_scores, key, ((0,), (0,))) * scale
-        buffer[0, number] = d_query.astype(BF16)
-        buffer[1, number] = d_key.astype(BF16)
-        buffer[2, number] = d_value.astype(BF16)
-        copy = pltpu.make_async_copy(
-            buffer.at[:, number], out_ref.at[:, number], sems.at[number]
-        )
+        buffer[0, head] = d_query.astype(BF16)
+        buffer[1, head] = d_key.astype(BF16)
+        buffer[2, head] = d_value.astype(BF16)
+        copy = pltpu.make_async_copy(buffer.at[:, head], out_ref.at[:, head], sems.at[head])
         copy.start()
         copies.append(copy)
     for copy in copies:
         copy.wait()
 
 
-def backward(pos, qkv, grad, first, total):
-    _, _, seq, width = qkv.shape
+def backward(args, grad, first, total, seq):
+    width = args[-1].shape[-1]
     heads = grad.shape[1] // width
     return pl.pallas_call(
-        functools.partial(backward_kernel, first),
+        functools.partial(backward_kernel, first, len(args) == 1),
         name="backward",
-        in_specs=[VMEM, VMEM, VMEM],
+        in_specs=[VMEM] * (len(args) + 1),
         out_specs=ANY,
         out_shape=jax.ShapeDtypeStruct((3, total, seq, width), BF16),
         scratch_shapes=[
@@ -136,23 +197,17 @@
             pltpu.SemaphoreType.DMA((heads,)),
         ],
         compiler_params=PARAMS,
-    )(pos, qkv, grad)
-
-
-def fill_kernel(late_ref, whole_ref, out_ref, buffer, in_sems, out_sems):
+    )(*args, grad)
+
+
+def fill_kernel(late_ref, whole_ref, out_ref, sems):
     late = late_ref.shape[1]
     first = out_ref.shape[1] - late
-    gets = [
-        pltpu.make_async_copy(late_ref.at[i], buffer.at[i], in_sems.at[i]) for i in range(3)
-    ]
     puts = [
-        pltpu.make_async_copy(buffer.at[i], out_ref.at[i, pl.ds(first, late)], out_sems.at[i])
+        pltpu.make_async_copy(late_ref.at[i], out_ref.at[i, pl.ds(first, late)], sems.at[i])
         for i in range(3)
     ]
-    for get in gets:
-        get.start()
-    for get, put in zip(gets, puts):
-        get.wait()
+    for put in puts:
         put.start()
     for put in puts:
         put.wait()
@@ -162,57 +217,43 @@
     return pl.pallas_call(
         fill_kernel,
         name="fill",
-        in_specs=[ANY, ANY],
+        in_specs=[VMEM, ANY],
         out_specs=ANY,
         out_shape=jax.ShapeDtypeStruct(whole.shape, whole.dtype),
-        scratch_shapes=[
-            pltpu.VMEM(late.shape, late.dtype),
-            pltpu.SemaphoreType.DMA((3,)),
-            pltpu.SemaphoreType.DMA((3,)),
-        ],
+        scratch_shapes=[pltpu.SemaphoreType.DMA((3,))],
         input_output_aliases={1: 0},
         compiler_params=PARAMS,
     )(late, whole)
 
 
-def open_kernel(chips, weight_ref, own_ref, mate_ref, total_ref, *refs):
-    kept, (buffer, sems) = refs[:-2], refs[-2:]
+def open_kernel(chips, weight_ref, own_ref, mate_ref, total_ref, buffer, sems):
     depth = own_ref.shape[1]
     gets = [
         pltpu.make_async_copy(
-            rows_of(weight_ref, depth, chips, 0, crossed), buffer.at[crossed], sems.at[chips + crossed]
+            rows_of(weight_ref, depth, chips, 0, crossed), buffer.at[crossed], sems.at[crossed]
         )
         for crossed in range(2)
-    ]
-    gets += [
-        pltpu.make_async_copy(
-            rows_of(weight_ref, depth, chips, step, True), ref, sems.at[step]
-        )
-        for step, ref in enumerate(kept, 1)
     ]
     for get in gets:
         get.start()
     gets[0].wait()
-    total_ref[...] = jnp.dot(own_ref[...], buffer[0], preferred_element_type=F32)
+    product = jnp.dot(own_ref[...], buffer[0], preferred_element_type=F32)
     gets[1].wait()
-    total_ref[...] += jnp.dot(mate_ref[...], buffer[1], preferred_element_type=F32)
-    for get in gets[2:]:
-        get.wait()
+    total_ref[...] = product + jnp.dot(mate_ref[...], buffer[1], preferred_element_type=F32)
 
 
 def open_project(chips, weight, own, mate):
     seq, depth = own.shape
     columns = weight.shape[1]
-    kept = [pltpu.VMEM((depth, columns), BF16)] * (chips - 1)
     return pl.pallas_call(
         functools.partial(open_kernel, chips),
         name="open_project",
-        in_specs=[HBM, VMEM, VMEM],
-        out_specs=[VMEM] * chips,
-        out_shape=[jax.ShapeDtypeStruct((seq, columns), F32)] + kept,
+        in_specs=[ANY, VMEM, VMEM],
+        out_specs=VMEM,
+        out_shape=jax.ShapeDtypeStruct((seq, columns), F32),
         scratch_shapes=[
             pltpu.VMEM((2, depth, columns), BF16),
-            pltpu.SemaphoreType.DMA((chips + 2,)),
+            pltpu.SemaphoreType.DMA((2,)),
         ],
         compiler_params=PARAMS,
     )(weight, own, mate)
@@ -327,8 +368,8 @@
 def local(saved_qkv, positions, w_out, grad_out):
     qkv = saved_qkv[0, 0].transpose(0, 2, 1, 3)
     pos = positions[0]
-    weight = pltpu.with_memory_space_constraint(w_out[0], pltpu.HBM)
-    heads, _, width = qkv.shape[1:]
+    weight = in_hbm(w_out[0])
+    heads, seq, width = qkv.shape[1:]
     early = max(1, heads // 2)
     late = heads - early
     shards = lax.axis_size("st")
@@ -336,7 +377,7 @@
     chips = shards // 2
     per_replica = chips // replicas
 
-    qkv_above = down(qkv[:, :early], "section")
+    packed_above = down(pack(pos, qkv, early), "section")
     same = [grad_out[0, 0]]
     for step in range(1, chips):
         same.append(rotate(same[0], "st", 2 * step))
@@ -344,20 +385,19 @@
     for step in range(chips):
         other.append(swap(same[step], "st"))
 
-    attended, *straight_rows = forward(chips, grad_out.shape[-1], pos, qkv, weight)
+    attended, *far_rows = forward(chips, grad_out.shape[-1], pos, qkv, weight)
     acts = [attended]
     for step in range(1, replicas):
         acts.append(rotate(attended, "dp", step))
-    pos_above = down(pos, "section")
 
     whole = (heads * width,)
     halves = (early * width, late * width)
-    total, *crossed_rows = open_project(chips, weight, same[0], other[0])
+    total = open_project(chips, weight, same[0], other[0])
     for step in range(1, chips):
         last = step == chips - 1
-        (total,) = project(straight_rows[step - 1], same[step], total, whole, F32)
+        (total,) = project(far_rows[2 * step - 2], same[step], total, whole, F32)
         total = project(
-            crossed_rows[step - 1],
+            far_rows[2 * step - 1],
             other[step],
             total,
             halves if last else whole,
@@ -367,7 +407,7 @@
             (total,) = total
     d_early, d_late = total
     d_above = down(d_early, "section")
-    grads_late = backward(pos, qkv, d_late, early, late)
+    grads_late = backward((pos, qkv), d_late, early, late, seq)
     late_above = down(grads_late, "section")
 
     far = []
@@ -379,7 +419,7 @@
             crossed.append(swap(direct[-1], "st"))
         far += [direct, crossed]
 
-    begun = backward(pos_above, qkv_above, d_above, 0, heads)
+    begun = backward((packed_above,), d_above, 0, heads, seq)
     grad_weight = weight_gradient(acts, same, other, far)
     upstream = fill(late_above, begun)
     return (grad_weight[None], upstream.transpose(0, 2, 1, 3)[None, None])

time: 68.4 us -> 65.7 us (0.961)
  Pallas kernels: 21.8 us -> 25.4 us
  waiting for transfers between devices: 31.1 us -> 28.6 us
  local copies, waits for them, and re-layouts: 4.03 us -> 1.66 us
  starting transfers between devices: 10.4 us -> 9.09 us
    pallas_call x4 -> x5, Pallas kernels: 9.5 us -> 13 us  [the longest x2 6.3 us: backward(): pl.pallas_call(functools.partial(backward_kernel, first, len(args) == 1),...]
    ppermute x4 -> x3, waiting for transfers between devices: 21.8 us -> 19.2 us  [down(): return lax.ppermute(value, axis, [(i, i - 1) for i in range(1, count)])]
    ppermute x4 -> x3, starting transfers between devices: 5.15 us -> 3.87 us  [down(): return lax.ppermute(value, axis, [(i, i - 1) for i in range(1, count)])]
    unnamed x10 -> x8, local copies, waits for them, and re-layouts: 2.93 us -> 1.66 us
    slice x1 -> x0, local copies, waits for them, and re-layouts: 1.11 us -> none  [local(): qkv_above = down(qkv[:, :early], 'section')]
  transfers between devices with their start and end apart: 10 -> 9, of which waited for: 3 -> 2; matrix products, arithmetic and copies ran while one was open for 2% -> 0% of each run, Pallas kernels for 30% -> 37%
where the time goes in v3:
time: 65.7 us; the launch traced here: 65.5 us
  waiting for transfers between devices  28.6 us (44%)
  Pallas kernels  25.4 us (39%)
  starting transfers between devices  9.09 us (14%)
  local copies, waits for them, and re-layouts  1.66 us (3%)
  between operations  0.79 us (1%)
    ppermute x3, waiting for transfers between devices, down(): return lax.ppermute(value, axis, [(i, i - 1) for i in range(1, count)])  19.2 us
    ppermute x3, waiting for transfers between devices, rotate(): lax.ppermute(value, axis, [(i, (i + steps) % count) for i in range(count)])  9.33 us
    pallas_call x2, Pallas kernels, backward(): pl.pallas_call(functools.partial(backward_kernel, first, len(args) == 1),...  6.3 us
    pallas_call x1, Pallas kernels, weight_gradient(): pl.pallas_call(functools.partial(weight_kernel, replicas, chips, slots, b...  5.51 us
    ppermute x3, starting transfers between devices, rotate(): lax.ppermute(value, axis, [(i, (i + steps) % count) for i in range(count)])  5.22 us
    pallas_call x1, Pallas kernels, open_project(): pl.pallas_call(functools.partial(open_kernel, chips), name='open_project'...  5.21 us
    pallas_call x1, Pallas kernels, forward(): pl.pallas_call(functools.partial(forward_kernel, chips, groups), name='fo...  4.72 us
    ppermute x3, starting transfers between devices, down(): return lax.ppermute(value, axis, [(i, i - 1) for i in range(1, count)])  3.87 us
  transfers between devices with their start and end apart: 9, of which 2 were waited for; matrix products, arithmetic and copies ran while one was open for 0% of the time, Pallas kernels for 37%

profile of v3, /device:TPU:0, one launch (start us, length us, event | category | flops | bytes accessed | tf_op | source)
XLA Modules:
  0.0 65.5 jit_solution(46094690640341939)
XLA Ops:
  0.6 3.1 %collective-permute-start.1 = (bf16[128,1536]{1,0:T(8,128)(2,1)}, bf16[128,1536]{1,0:T(8,128)(2,1)S(1)}, u32[]{:S(2)}, u32[]{:S(2)}) collective-permute-start(bf16[128,1536]{1,0:T(8,128)(2,1)} %bitcast.15), channel_id=1, source_target_pairs={{0,4},{2,6},{4,0},{6,2},{1,5},{3,7},{5,1},{7,3},{8,12},{10,14},{12... | collective-permute-start | bytes 1179656 | tf_op jit(solution)/shard_map/ppermute | solution.py:30
  3.7 0.0 collective-permute-start.2
  3.7 9.3 %collective-permute-done.1.refs_1_.refs_3_.grad_ref = bf16[128,1536]{1,0:T(8,128)(2,1)S(1)} collective-permute-done((bf16[128,1536]{1,0:T(8,128)(2,1)}, bf16[128,1536]{1,0:T(8,128)(2,1)S(1)}, u32[]{:S(2)}, u32[]{:S(2)}) %collective-permute-start.1) | collective-permute-done | bytes 393248 | tf_op jit(solution)/shard_map/ppermute | solution.py:30
  13.0 0.0 collective-permute-start.3
  13.0 0.0 copy-start.1
  13.0 1.0 %copy-done.1 = bf16[1,1,128,1536]{3,2,1,0:T(8,128)(2,1)S(1)} copy-done((bf16[1,1,128,1536]{3,2,1,0:T(8,128)(2,1)S(1)}, bf16[1,1,128,1536]{3,2,1,0:T(8,128)(2,1)}, u32[]{:S(2)}) %copy-start.1) | copy-done | bytes 393240
  14.0 1.8 %collective-permute-start.4 = (bf16[128,1536]{1,0:T(8,128)(2,1)S(1)}, bf16[128,1536]{1,0:T(8,128)(2,1)S(1)}, u32[]{:S(2)}, u32[]{:S(2)}) collective-permute-start(bf16[128,1536]{1,0:T(8,128)(2,1)S(1)} %choose.1), channel_id=1, source_target_pairs={{0,1},{1,0},{2,3},{3,2},{4,5},{5,4},{6,7},{7,6},{8,9},{9,8},{10,11... | collective-permute-start | bytes 1179656 | tf_op jit(solution)/shard_map/ppermute | solution.py:30
  15.8 1.2 %pack.1 = bf16[2320,128]{1,0:T(8,128)(2,1)S(1)} custom-call(s32[1,128]{1,0:T(1,128)} %bitcast.20, bf16[3,1536,128]{2,1,0:T(8,128)(2,1)} %bitcast.12), custom_call_target="tpu_custom_call" | custom-call | tf_op jit(solution)/shard_map/pack/pallas_call | solution.py:77
  17.0 1.3 %collective-permute-start.7 = (bf16[2320,128]{1,0:T(8,128)(2,1)S(1)}, bf16[2320,128]{1,0:T(8,128)(2,1)S(1)}, u32[]{:S(2)}, u32[]{:S(2)}) collective-permute-start(bf16[2320,128]{1,0:T(8,128)(2,1)S(1)} %pack.1), channel_id=1, source_target_pairs={{8,0},{16,8},{24,16},{9,1},{17,9},{25,17},{10,2},{18,10},{26,18},{... | collective-permute-start | bytes 1781768 | tf_op jit(solution)/shard_map/ppermute | solution.py:40
  18.3 0.0 copy-start.3
  18.3 0.6 copy-done.3
  19.0 0.0 copy-start.2
  19.0 4.7 %forward.1 = (bf16[128,1536]{1,0:T(8,128)(2,1)S(1)}, bf16[1536,1536]{1,0:T(8,128)(2,1)S(1)}, bf16[1536,1536]{1,0:T(8,128)(2,1)S(1)}) custom-call(s32[1,128]{1,0:T(1,128)S(1)} %bitcast.21, bf16[3,12,128,128]{3,2,1,0:T(8,128)(2,1)} %bitcast.13, bf16[6144,1536]{1,0:T(8,128)(2,1)} %bitcast.23), custom_call_target="tpu_custom_call" | custom-call | tf_op jit(solution)/shard_map/forward/pallas_call | solution.py:134
  23.7 0.0 collective-permute-done.2.refs_4_.mate_ref
  23.7 0.0 copy-done.2
  23.7 5.2 %open_project.1.carried_ref = f32[128,1536]{1,0:T(8,128)S(1)} custom-call(bf16[6144,1536]{1,0:T(8,128)(2,1)} %bitcast.24, bf16[128,1536]{1,0:T(8,128)(2,1)S(1)} %bitcast.18, bf16[128,1536]{1,0:T(8,128)(2,1)S(1)} %collective-permute-done.2.refs_4_.mate_ref), custom_call_target="tpu_custom_call" | custom-call | tf_op jit(solution)/shard_map/open_project/pallas_call | solution.py:248
  28.9 0.0 copy-start
  28.9 0.8 %project.2.carried_ref = f32[128,1536]{1,0:T(8,128)S(1)} custom-call(bf16[1536,1536]{1,0:T(8,128)(2,1)S(1)} %get-tuple-element.9.weight_ref, bf16[128,1536]{1,0:T(8,128)(2,1)S(1)} %collective-permute-done.1.refs_1_.refs_3_.grad_ref, f32[128,1536]{1,0:T(8,128)S(1)} %open_project.1.carried_ref), custom_call_target="tpu_custom_call" | custom-call | tf_op jit(solution)/shard_map/project/pallas_call | solution.py:274
  29.8 0.0 collective-permute-done.3.refs_5_.grad_ref
  29.8 0.8 %project.3 = (bf16[128,768]{1,0:T(8,128)(2,1)S(1)}, bf16[128,768]{1,0:T(8,128)(2,1)S(1)}) custom-call(bf16[1536,1536]{1,0:T(8,128)(2,1)S(1)} %get-tuple-element.8.weight_ref, bf16[128,1536]{1,0:T(8,128)(2,1)S(1)} %collective-permute-done.3.refs_5_.grad_ref, f32[128,1536]{1,0:T(8,128)S(1)} %project.2.carried_ref), custom_call_target="tpu_custom_call" | custom-call | tf_op jit(solution)/shard_map/project/pallas_call | solution.py:274
  30.6 0.0 copy-done
  30.6 3.7 %backward.2 = bf16[3,6,128,128]{3,2,1,0:T(8,128)(2,1)S(1)} custom-call(s32[1,128]{1,0:T(1,128)S(1)} %bitcast.22, bf16[3,12,128,128]{3,2,1,0:T(8,128)(2,1)S(1)} %bitcast.14, bf16[128,768]{1,0:T(8,128)(2,1)S(1)} %get-tuple-element.10.refs_2_), custom_call_target="tpu_custom_call" | custom-call | tf_op jit(solution)/shard_map/backward/pallas_call | solution.py:189
  34.4 1.3 %collective-permute-start.6 = (bf16[3,6,128,128]{3,2,1,0:T(8,128)(2,1)S(1)}, bf16[3,6,128,128]{3,2,1,0:T(8,128)(2,1)S(1)}, u32[]{:S(2)}, u32[]{:S(2)}) collective-permute-start(bf16[3,6,128,128]{3,2,1,0:T(8,128)(2,1)S(1)} %backward.2), channel_id=1, source_target_pairs={{8,0},{16,8},{24,16},{9,1},{17,9},{25,17},{10,2},{18,10},{26,18},{... | collective-permute-start | bytes 1769480 | tf_op jit(solution)/shard_map/ppermute | solution.py:40
  35.7 0.4 collective-permute-start
  36.0 0.0 collective-permute-done.4.refs_6_
  36.0 0.0 collective-permute-start.5
  36.0 1.3 %collective-permute-start.8 = (bf16[128,768]{1,0:T(8,128)(2,1)S(1)}, bf16[128,768]{1,0:T(8,128)(2,1)S(1)}, u32[]{:S(2)}, u32[]{:S(2)}) collective-permute-start(bf16[128,768]{1,0:T(8,128)(2,1)S(1)} %get-tuple-element.11), channel_id=1, source_target_pairs={{8,0},{16,8},{24,16},{9,1},{17,9},{25,17},{10,2},{18,10},{26,18},{... | collective-permute-start | bytes 589832 | tf_op jit(solution)/shard_map/ppermute | solution.py:40
  37.3 0.0 collective-permute-done.7.refs_0_
  37.3 19.2 %collective-permute-done.8.refs_1_ = bf16[128,768]{1,0:T(8,128)(2,1)S(1)} collective-permute-done((bf16[128,768]{1,0:T(8,128)(2,1)S(1)}, bf16[128,768]{1,0:T(8,128)(2,1)S(1)}, u32[]{:S(2)}, u32[]{:S(2)}) %collective-permute-start.8) | collective-permute-done | bytes 196640 | tf_op jit(solution)/shard_map/ppermute | solution.py:40
  56.6 2.6 %backward.3.whole_ref = bf16[3,12,128,128]{3,2,1,0:T(8,128)(2,1)} custom-call(bf16[2320,128]{1,0:T(8,128)(2,1)S(1)} %collective-permute-done.7.refs_0_, bf16[128,768]{1,0:T(8,128)(2,1)S(1)} %collective-permute-done.8.refs_1_), custom_call_target="tpu_custom_call" | custom-call | tf_op jit(solution)/shard_map/backward/pallas_call | solution.py:189
  59.1 0.0 collective-permute-done.refs_1_
  59.1 0.0 collective-permute-done.5.refs_7_
  59.1 5.5 %weight_gradient.1 = bf16[3072,1536]{1,0:T(8,128)(2,1)} custom-call(bf16[128,1536]{1,0:T(8,128)(2,1)S(1)} %get-tuple-element.7.refs_0_, bf16[128,1536]{1,0:T(8,128)(2,1)S(1)} %collective-permute-done.refs_1_, bf16[128,1536]{1,0:T(8,128)(2,1)S(1)} %bitcast.19, bf16[128,1536]{1,0:T(8,128)(2,1)S(1)} %collective-permute-done.1.refs_1_.refs_3_.grad_ref, ...), custom_call_target="tpu_custom_call" | custom-call | tf_op jit(solution)/shard_map/weight_gradient/pallas_call | solution.py:356
  64.7 0.0 collective-permute-done.6.late_ref
  64.7 0.8 %fill.1 = bf16[3,12,128,128]{3,2,1,0:T(8,128)(2,1)} custom-call(bf16[3,6,128,128]{3,2,1,0:T(8,128)(2,1)S(1)} %collective-permute-done.6.late_ref, bf16[3,12,128,128]{3,2,1,0:T(8,128)(2,1)} %backward.3.whole_ref), custom_call_target="tpu_custom_call", output_to_operand_aliasing={{}: (1, {})} | custom-call | tf_op jit(solution)/shard_map/fill/pallas_call | solution.py:217
  (1 shorter events, 0.0 us)
Async XLA Ops:
  0.6 12.4 %collective-permute-start.1 = (bf16[128,1536]{1,0:T(8,128)(2,1)}, bf16[128,1536]{1,0:T(8,128)(2,1)S(1)}, u32[]{:S(2)}, u32[]{:S(2)}) collective-permute-start(bf16[128,1536]{1,0:T(8,128)(2,1)} %bitcast.15), channel_id=1, source_target_pairs={{0,4},{2,6},{4,0},{6,2},{1,5},{3,7},{5,1},{7,3},{8,12},{10,14},{12... | collective-permute-start | bytes 1179656 | tf_op jit(solution)/shard_map/ppermute | solution.py:30
  3.7 20.0 %collective-permute-start.2 = (bf16[128,1536]{1,0:T(8,128)(2,1)}, bf16[128,1536]{1,0:T(8,128)(2,1)S(1)}, u32[]{:S(2)}, u32[]{:S(2)}) collective-permute-start(bf16[128,1536]{1,0:T(8,128)(2,1)} %bitcast.16), channel_id=1, source_target_pairs={{0,2},{2,0},{4,6},{6,4},{1,3},{3,1},{5,7},{7,5},{8,10},{10,8},{12,... | collective-permute-start | bytes 1179656 | tf_op jit(solution)/shard_map/ppermute | solution.py:35
  13.0 16.8 %collective-permute-start.3 = (bf16[128,1536]{1,0:T(8,128)(2,1)S(1)}, bf16[128,1536]{1,0:T(8,128)(2,1)S(1)}, u32[]{:S(2)}, u32[]{:S(2)}) collective-permute-start(bf16[128,1536]{1,0:T(8,128)(2,1)S(1)} %collective-permute-done.1.refs_1_.refs_3_.grad_ref), channel_id=1, source_target_pairs={{0,2},{2,0},{4,6},{6,4},{1,3},{3,1},{5,7},{7,5},{8,10},{10,8},{12,... | collective-permute-start | bytes 1179656 | tf_op jit(solution)/shard_map/ppermute | solution.py:35
  13.0 1.0 %copy-start.1 = (bf16[1,1,128,1536]{3,2,1,0:T(8,128)(2,1)S(1)}, bf16[1,1,128,1536]{3,2,1,0:T(8,128)(2,1)}, u32[]{:S(2)}) copy-start(bf16[1,1,128,1536]{3,2,1,0:T(8,128)(2,1)} %param.7) | copy-start | bytes 1179652
  14.0 22.0 %collective-permute-start.4 = (bf16[128,1536]{1,0:T(8,128)(2,1)S(1)}, bf16[128,1536]{1,0:T(8,128)(2,1)S(1)}, u32[]{:S(2)}, u32[]{:S(2)}) collective-permute-start(bf16[128,1536]{1,0:T(8,128)(2,1)S(1)} %choose.1), channel_id=1, source_target_pairs={{0,1},{1,0},{2,3},{3,2},{4,5},{5,4},{6,7},{7,6},{8,9},{9,8},{10,11... | collective-permute-start | bytes 1179656 | tf_op jit(solution)/shard_map/ppermute | solution.py:30
  17.0 20.3 %collective-permute-start.7 = (bf16[2320,128]{1,0:T(8,128)(2,1)S(1)}, bf16[2320,128]{1,0:T(8,128)(2,1)S(1)}, u32[]{:S(2)}, u32[]{:S(2)}) collective-permute-start(bf16[2320,128]{1,0:T(8,128)(2,1)S(1)} %pack.1), channel_id=1, source_target_pairs={{8,0},{16,8},{24,16},{9,1},{17,9},{25,17},{10,2},{18,10},{26,18},{... | collective-permute-start | bytes 1781768 | tf_op jit(solution)/shard_map/ppermute | solution.py:40
  18.3 0.7 %copy-start.3 = (s32[1,1,128]{2,1,0:T(1,128)S(1)}, s32[1,1,128]{2,1,0:T(1,128)}, u32[]{:S(2)}) copy-start(s32[1,1,128]{2,1,0:T(1,128)} %param.5) | copy-start | bytes 1540
  19.0 4.7 %copy-start.2 = (bf16[1,1,128,1536]{3,2,1,0:T(8,128)(2,1)S(1)}, bf16[1,1,128,1536]{3,2,1,0:T(8,128)(2,1)}, u32[]{:S(2)}) copy-start(bf16[1,1,128,1536]{3,2,1,0:T(8,128)(2,1)} %param.7) | copy-start | bytes 1179652
  28.9 1.7 %copy-start = (bf16[1,1,3,128,12,128]{5,3,4,2,1,0:T(8,128)(2,1)S(1)}, bf16[1,1,3,128,12,128]{5,3,4,2,1,0:T(8,128)(2,1)}, u32[]{:S(2)}) copy-start(bf16[1,1,3,128,12,128]{5,3,4,2,1,0:T(8,128)(2,1)} %param.4) | copy-start | bytes 3538948
  34.4 30.3 %collective-permute-start.6 = (bf16[3,6,128,128]{3,2,1,0:T(8,128)(2,1)S(1)}, bf16[3,6,128,128]{3,2,1,0:T(8,128)(2,1)S(1)}, u32[]{:S(2)}, u32[]{:S(2)}) collective-permute-start(bf16[3,6,128,128]{3,2,1,0:T(8,128)(2,1)S(1)} %backward.2), channel_id=1, source_target_pairs={{8,0},{16,8},{24,16},{9,1},{17,9},{25,17},{10,2},{18,10},{26,18},{... | collective-permute-start | bytes 1769480 | tf_op jit(solution)/shard_map/ppermute | solution.py:40
  35.7 23.5 %collective-permute-start = (bf16[128,1536]{1,0:T(8,128)(2,1)S(1)}, bf16[128,1536]{1,0:T(8,128)(2,1)S(1)}, u32[]{:S(2)}, u32[]{:S(2)}) collective-permute-start(bf16[128,1536]{1,0:T(8,128)(2,1)S(1)} %get-tuple-element.7.refs_0_), channel_id=1, source_target_pairs={{0,1},{1,0},{2,3},{3,2},{4,5},{5,4},{6,7},{7,6},{8,9},{9,8},{10,11... | collective-permute-start | bytes 1179656 | tf_op jit(solution)/shard_map/ppermute | solution.py:30
  36.0 23.1 %collective-permute-start.5 = (bf16[128,1536]{1,0:T(8,128)(2,1)S(1)}, bf16[128,1536]{1,0:T(8,128)(2,1)S(1)}, u32[]{:S(2)}, u32[]{:S(2)}) collective-permute-start(bf16[128,1536]{1,0:T(8,128)(2,1)S(1)} %collective-permute-done.4.refs_6_), channel_id=1, source_target_pairs={{0,2},{2,0},{4,6},{6,4},{1,3},{3,1},{5,7},{7,5},{8,10},{10,8},{12,... | collective-permute-start | bytes 1179656 | tf_op jit(solution)/shard_map/ppermute | solution.py:35
  36.0 20.5 %collective-permute-start.8 = (bf16[128,768]{1,0:T(8,128)(2,1)S(1)}, bf16[128,768]{1,0:T(8,128)(2,1)S(1)}, u32[]{:S(2)}, u32[]{:S(2)}) collective-permute-start(bf16[128,768]{1,0:T(8,128)(2,1)S(1)} %get-tuple-element.11), channel_id=1, source_target_pairs={{8,0},{16,8},{24,16},{9,1},{17,9},{25,17},{10,2},{18,10},{26,18},{... | collective-permute-start | bytes 589832 | tf_op jit(solution)/shard_map/ppermute | solution.py:40

commit v4 on v3

--- a/solution.py
+++ b/solution.py
@@ -96,86 +96,116 @@
     return weight_ref.at[pl.ds(pl.multiple_of(owner * depth, depth), depth)]
 
 
-def forward_kernel(chips, groups, pos_ref, qkv_ref, weight_ref, out_ref, *refs):
-    kept, (buffer, head_sems, sems) = refs[:-3], refs[-3:]
+def forward_kernel(chips, groups, pos_ref, qkv_ref, weight_ref, own_ref, out_ref, total_ref, *refs):
+    kept, (held, shard, buffer, rows, head_sems, sems) = refs[:-6], refs[-6:]
     heads, _, width = buffer.shape[1:]
     size = heads // groups
-    fetches = []
+    gets = [pltpu.make_async_copy(pos_ref, held, head_sems.at[groups])]
     for group in range(groups):
         part = pl.ds(group * size, size)
-        fetches.append(
+        gets.append(
             pltpu.make_async_copy(qkv_ref.at[:, part], buffer.at[:, part], head_sems.at[group])
         )
-    gets = [
+    fetches = [
         pltpu.make_async_copy(
-            rows_of(weight_ref, ref.shape[0], chips, 1 + number // 2, number % 2),
-            ref,
+            rows_of(weight_ref, rows.shape[0], chips, number // 2, number % 2),
+            target,
             sems.at[number],
         )
-        for number, ref in enumerate(kept)
+        for number, target in enumerate((rows, *kept))
     ]
-    for get in fetches + gets:
+    gets.append(pltpu.make_async_copy(own_ref, shard, head_sems.at[groups + 1]))
+    for get in gets + fetches:
         get.start()
-    visible = visibility(pos_ref[...])
+    gets[0].wait()
+    visible = visibility(held[...])
     for head in range(heads):
         if head % size == 0:
-            fetches[head // size].wait()
+            gets[1 + head // size].wait()
         probs = softmax(visible, buffer[0, head], buffer[1, head])
         attended = dot(probs.astype(BF16), buffer[2, head], ((0,), (0,)))
         out_ref[:, head * width : (head + 1) * width] = attended.astype(BF16)
-    for get in gets:
-        get.wait()
-
-
-def forward(chips, depth, pos, qkv, weight):
+    gets[-1].wait()
+    fetches[0].wait()
+    total_ref[...] = jnp.dot(shard[...], rows[...], preferred_element_type=F32)
+    for fetch in fetches[1:]:
+        fetch.wait()
+
+
+def forward(chips, pos, qkv, weight, own):
     _, heads, seq, width = qkv.shape
-    count = 2 * (chips - 1)
+    depth, columns = own.shape[1], weight.shape[1]
+    count = 2 * chips - 1
     groups = max(size for size in (1, 2, 3) if heads % size == 0)
     return pl.pallas_call(
         functools.partial(forward_kernel, chips, groups),
         name="forward",
-        in_specs=[VMEM, ANY, ANY],
-        out_specs=[VMEM] * (1 + count),
-        out_shape=[jax.ShapeDtypeStruct((seq, heads * width), BF16)]
-        + [pltpu.VMEM((depth, weight.shape[1]), BF16)] * count,
+        in_specs=[ANY] * 4,
+        out_specs=[VMEM] * (2 + count),
+        out_shape=[
+            jax.ShapeDtypeStruct((seq, heads * width), BF16),
+            jax.ShapeDtypeStruct((seq, columns), F32),
+        ]
+        + [pltpu.VMEM((depth, columns), BF16)] * count,
         scratch_shapes=[
+            pltpu.VMEM(pos.shape, pos.dtype),
+            pltpu.VMEM(own.shape, BF16),
             pltpu.VMEM(qkv.shape, BF16),
-            pltpu.SemaphoreType.DMA((groups,)),
-            pltpu.SemaphoreType.DMA((count,)),
+            pltpu.VMEM((depth, columns), BF16),
+            pltpu.SemaphoreType.DMA((groups + 2,)),
+            pltpu.SemaphoreType.DMA((count + 1,)),
         ],
         compiler_params=PARAMS,
-    )(pos, in_hbm(qkv), weight)
-
-
-def backward_kernel(first, packed, *refs):
-    if packed:
-        packed_ref, grad_ref, out_ref, buffer, sems = refs
-    else:
-        pos_ref, qkv_ref, grad_ref, out_ref, buffer, sems = refs
+    )(in_hbm(pos), in_hbm(qkv), weight, in_hbm(own))
+
+
+def head_gradients(visible, query, key, value, grad):
+    scale = 1.0 / math.sqrt(query.shape[-1])
+    probs = softmax(visible, query, key)
+    d_value = dot(probs.astype(BF16), grad, ((1,), (0,)))
+    d_probs = dot(value, grad, ((1,), (1,)))
+    row_dot = jnp.sum(probs * d_probs, axis=0, keepdims=True)
+    d_scores = (probs * (d_probs - row_dot)).astype(BF16)
+    d_key = dot(d_scores, query, ((1,), (0,))) * scale
+    d_query = dot(d_scores, key, ((0,), (0,))) * scale
+    return d_query.astype(BF16), d_key.astype(BF16), d_value.astype(BF16)
+
+
+def late_kernel(pos_ref, qkv_ref, grad_ref, out_ref):
+    heads, _, width = out_ref.shape[1:]
+    first = qkv_ref.shape[1] - heads
+    visible = visibility(pos_ref[...])
+    for head in range(heads):
+        query, key, value = (qkv_ref[i, first + head] for i in range(3))
+        grad = grad_ref[:, head * width : (head + 1) * width]
+        for i, result in enumerate(head_gradients(visible, query, key, value, grad)):
+            out_ref[i, head] = result
+
+
+def late_backward(pos, qkv, grad):
+    _, _, seq, width = qkv.shape
+    heads = grad.shape[1] // width
+    return pl.pallas_call(
+        late_kernel,
+        name="late_backward",
+        in_specs=[VMEM] * 3,
+        out_specs=VMEM,
+        out_shape=pltpu.VMEM((3, heads, seq, width), BF16),
+        compiler_params=PARAMS,
+    )(pos, qkv, grad)
+
+
+def early_kernel(packed_ref, grad_ref, out_ref, buffer, sems):
     heads, seq, width = buffer.shape[1:]
-    scale = 1.0 / math.sqrt(width)
-    positions = packed_ref[3 * heads * seq :][:1] if packed else pos_ref[...]
-    visible = visibility(positions)
+    visible = visibility(packed_ref[3 * heads * seq :][:1])
     copies = []
     for head in range(heads):
-        if packed:
-            query, key, value = (
-                packed_ref[(i * heads + head) * seq : (i * heads + head + 1) * seq]
-                for i in range(3)
-            )
-        else:
-            query, key, value = (qkv_ref[i, first + head] for i in range(3))
+        query, key, value = (
+            packed_ref[(i * heads + head) * seq : (i * heads + head + 1) * seq] for i in range(3)
+        )
         grad = grad_ref[:, head * width : (head + 1) * width]
-        probs = softmax(visible, query, key)
-        d_value = dot(probs.astype(BF16), grad, ((1,), (0,)))
-        d_probs = dot(value, grad, ((1,), (1,)))
-        row_dot = jnp.sum(probs * d_probs, axis=0, keepdims=True)
-        d_scores = (probs * (d_probs - row_dot)).astype(BF16)
-        d_key = dot(d_scores, query, ((1,), (0,))) * scale
-        d_query = dot(d_scores, key, ((0,), (0,))) * scale
-        buffer[0, head] = d_query.astype(BF16)
-        buffer[1, head] = d_key.astype(BF16)
-        buffer[2, head] = d_value.astype(BF16)
+        for i, result in enumerate(head_gradients(visible, query, key, value, grad)):
+            buffer[i, head] = result
         copy = pltpu.make_async_copy(buffer.at[:, head], out_ref.at[:, head], sems.at[head])
         copy.start()
         copies.append(copy)
@@ -183,13 +213,13 @@
         copy.wait()
 
 
-def backward(args, grad, first, total, seq):
-    width = args[-1].shape[-1]
+def early_backward(packed, grad, total):
+    seq, width = grad.shape[0], packed.shape[1]
     heads = grad.shape[1] // width
     return pl.pallas_call(
-        functools.partial(backward_kernel, first, len(args) == 1),
-        name="backward",
-        in_specs=[VMEM] * (len(args) + 1),
+        early_kernel,
+        name="early_backward",
+        in_specs=[VMEM] * 2,
         out_specs=ANY,
         out_shape=jax.ShapeDtypeStruct((3, total, seq, width), BF16),
         scratch_shapes=[
@@ -197,7 +227,7 @@
             pltpu.SemaphoreType.DMA((heads,)),
         ],
         compiler_params=PARAMS,
-    )(*args, grad)
+    )(packed, grad)
 
 
 def fill_kernel(late_ref, whole_ref, out_ref, sems):
@@ -226,39 +256,6 @@
     )(late, whole)
 
 
-def open_kernel(chips, weight_ref, own_ref, mate_ref, total_ref, buffer, sems):
-    depth = own_ref.shape[1]
-    gets = [
-        pltpu.make_async_copy(
-            rows_of(weight_ref, depth, chips, 0, crossed), buffer.at[crossed], sems.at[crossed]
-        )
-        for crossed in range(2)
-    ]
-    for get in gets:
-        get.start()
-    gets[0].wait()
-    product = jnp.dot(own_ref[...], buffer[0], preferred_element_type=F32)
-    gets[1].wait()
-    total_ref[...] = product + jnp.dot(mate_ref[...], buffer[1], preferred_element_type=F32)
-
-
-def open_project(chips, weight, own, mate):
-    seq, depth = own.shape
-    columns = weight.shape[1]
-    return pl.pallas_call(
-        functools.partial(open_kernel, chips),
-        name="open_project",
-        in_specs=[ANY, VMEM, VMEM],
-        out_specs=VMEM,
-        out_shape=jax.ShapeDtypeStruct((seq, columns), F32),
-        scratch_shapes=[
-            pltpu.VMEM((2, depth, columns), BF16),
-            pltpu.SemaphoreType.DMA((2,)),
-        ],
-        compiler_params=PARAMS,
-    )(weight, own, mate)
-
-
 def project_kernel(splits, weight_ref, grad_ref, carried_ref, *outs):
     total = carried_ref[...] + jnp.dot(
         grad_ref[...], weight_ref[...], preferred_element_type=F32
@@ -305,31 +302,28 @@
     )(*options)
 
 
-def weight_kernel(replicas, chips, slots, blocks, *refs):
+def weight_kernel(replicas, chips, blocks, *refs):
     acts = refs[:replicas]
-    same = refs[replicas : replicas + chips]
-    other = refs[replicas + chips : replicas + 2 * chips]
-    far = refs[replicas + 2 * chips : -2]
+    options = refs[replicas : replicas + chips]
     out_ref, stacked = refs[-2:]
     step = pl.program_id(0)
+    slots = pl.num_programs(0) // blocks
+    far = refs[replicas + chips : replicas + chips + slots * (replicas - 1)]
     seq = acts[0].shape[0]
     size = out_ref.shape[0]
-    chip, _ = place()
 
     @pl.when(step == 0)
     def _():
         for number, act in enumerate(acts):
             stacked[number * seq : (number + 1) * seq] = act[...]
 
+    chip, _ = place()
     columns = pl.ds(pl.multiple_of(lax.rem(step, blocks) * size, size), size)
     for slot in range(slots):
 
         @pl.when(lax.div(step, blocks) == slot)
         def _():
-            options = other if slot % 2 else same
-            index = lax.rem(
-                chip - (lax.axis_index("dp") * (slots // 2) + slot // 2) + chips, chips
-            )
+            index = lax.rem(chip - (lax.axis_index("dp") * slots + slot) + chips, chips)
             near = options[0][:, columns]
             for number in range(1, chips):
                 near = jnp.where(index == number, options[number][:, columns], near)
@@ -338,29 +332,35 @@
             out_ref[...] = dot(left, stacked[...], ((0,), (0,))).astype(BF16)
 
 
-def weight_gradient(acts, same, other, far):
-    replicas, chips, slots = len(acts), len(same), len(far)
+def weight_gradient(parity, acts, options, far, begun):
+    replicas, chips, slots = len(acts), len(options), len(far)
     seq, columns = acts[0].shape
-    features = same[0].shape[1]
+    features = options[0].shape[1]
     blocks = max(1, features // 768)
     while features % blocks or (features // blocks) % 128:
         blocks -= 1
     size = features // blocks
 
     def target(step):
-        slot = lax.div(step, blocks)
-        core = lax.rem(lax.axis_index("st") + slot, 2)
-        return (2 * lax.div(slot, 2) + core) * blocks + lax.rem(step, blocks), 0
-
-    args = [*acts, *same, *other, *[ref for slot in far for ref in slot]]
-    return pl.pallas_call(
-        functools.partial(weight_kernel, replicas, chips, slots, blocks),
+        core = lax.rem(lax.axis_index("st") + parity, 2)
+        return (2 * lax.div(step, blocks) + core) * blocks + lax.rem(step, blocks), 0
+
+    args = [*acts, *options, *[ref for slot in far for ref in slot]]
+    specs = [VMEM] * len(args)
+    aliases = {}
+    if begun is not None:
+        aliases = {len(args): 0}
+        args.append(begun)
+        specs.append(ANY)
+    return pl.pallas_call(
+        functools.partial(weight_kernel, replicas, chips, blocks),
         name="weight_gradient",
         grid=(slots * blocks,),
-        in_specs=[VMEM] * len(args),
+        in_specs=specs,
         out_specs=pl.BlockSpec((size, columns), target),
         scratch_shapes=[pltpu.VMEM((replicas * seq, columns), BF16)],
-        out_shape=jax.ShapeDtypeStruct((slots * features, columns), BF16),
+        out_shape=jax.ShapeDtypeStruct((2 * slots * features, columns), BF16),
+        input_output_aliases=aliases,
         compiler_params=PARAMS,
     )(*args)
 
@@ -369,7 +369,7 @@
     qkv = saved_qkv[0, 0].transpose(0, 2, 1, 3)
     pos = positions[0]
     weight = in_hbm(w_out[0])
-    heads, seq, width = qkv.shape[1:]
+    heads, _, width = qkv.shape[1:]
     early = max(1, heads // 2)
     late = heads - early
     shards = lax.axis_size("st")
@@ -385,19 +385,19 @@
     for step in range(chips):
         other.append(swap(same[step], "st"))
 
-    attended, *far_rows = forward(chips, grad_out.shape[-1], pos, qkv, weight)
+    attended, total, *far_rows = forward(chips, pos, qkv, weight, same[0])
     acts = [attended]
     for step in range(1, replicas):
         acts.append(rotate(attended, "dp", step))
 
     whole = (heads * width,)
     halves = (early * width, late * width)
-    total = open_project(chips, weight, same[0], other[0])
+    (total,) = project(far_rows[0], other[0], total, whole, F32)
     for step in range(1, chips):
         last = step == chips - 1
-        (total,) = project(far_rows[2 * step - 2], same[step], total, whole, F32)
+        (total,) = project(far_rows[2 * step - 1], same[step], total, whole, F32)
         total = project(
-            far_rows[2 * step - 1],
+            far_rows[2 * step],
             other[step],
             total,
             halves if last else whole,
@@ -407,20 +407,22 @@
             (total,) = total
     d_early, d_late = total
     d_above = down(d_early, "section")
-    grads_late = backward((pos, qkv), d_late, early, late, seq)
+    grads_late = late_backward(pos, qkv, d_late)
     late_above = down(grads_late, "section")
 
-    far = []
+    near_far, cross_far = [], []
     for number in range(per_replica):
         direct, crossed = [], []
         for step in range(1, replicas):
             chosen = choose(replicas, number, step, same)
             direct.append(rotate(chosen, "dp", step))
             crossed.append(swap(direct[-1], "st"))
-        far += [direct, crossed]
-
-    begun = backward((packed_above,), d_above, 0, heads, seq)
-    grad_weight = weight_gradient(acts, same, other, far)
+        near_far.append(direct)
+        cross_far.append(crossed)
+
+    begun = early_backward(packed_above, d_above, heads)
+    grad_weight = weight_gradient(0, acts, same, near_far, None)
+    grad_weight = weight_gradient(1, acts, other, cross_far, grad_weight)
     upstream = fill(late_above, begun)
     return (grad_weight[None], upstream.transpose(0, 2, 1, 3)[None, None])
 

time: 65.7 us -> 58.7 us (0.89)
  waiting for transfers between devices: 28.6 us -> 25.4 us
  Pallas kernels: 25.4 us -> 22.2 us
    ppermute x3, waiting for transfers between devices: 19.2 us -> 6.39 us  [down(): return lax.ppermute(value, axis, [(i, i - 1) for i in range(1, count)])]
    ppermute x3, waiting for transfers between devices: 9.33 us -> 19 us  [rotate(): lax.ppermute(value, axis, [(i, (i + steps) % count) for i in range(count)])]
    pallas_call x4, Pallas kernels: 17 us -> 10.8 us  [the longest x2 6.44 us: weight_gradient(): pl.pallas_call(functools.partial(weight_kernel, replicas, chips, blocks),...]
    pallas_call x1, Pallas kernels: 4.72 us -> 6.99 us  [forward(): pl.pallas_call(functools.partial(forward_kernel, chips, groups), name='fo...]
    pallas_call x2 -> x3, Pallas kernels: 1.64 us -> 2.36 us  [project(): pl.pallas_call(functools.partial(project_kernel, splits), name='project',...]
  transfers between devices with their start and end apart: 9 -> 9, of which waited for: 2 -> 3; matrix products, arithmetic and copies ran while one was open for 0% -> 0% of each run, Pallas kernels for 37% -> 37%
where the time goes in v4:
time: 58.7 us; the launch traced here: 58.5 us
  waiting for transfers between devices  25.4 us (43%)
  Pallas kernels  22.2 us (38%)
  starting transfers between devices  9.09 us (15%)
  local copies, waits for them, and re-layouts  1.02 us (2%)
  between operations  0.78 us (1%)
    ppermute x3, waiting for transfers between devices, rotate(): lax.ppermute(value, axis, [(i, (i + steps) % count) for i in range(count)])  19 us
    pallas_call x1, Pallas kernels, forward(): pl.pallas_call(functools.partial(forward_kernel, chips, groups), name='fo...  6.99 us
    pallas_call x2, Pallas kernels, weight_gradient(): pl.pallas_call(functools.partial(weight_kernel, replicas, chips, blocks),...  6.44 us
    ppermute x3, waiting for transfers between devices, down(): return lax.ppermute(value, axis, [(i, i - 1) for i in range(1, count)])  6.39 us
    ppermute x3, starting transfers between devices, rotate(): lax.ppermute(value, axis, [(i, (i + steps) % count) for i in range(count)])  5.21 us
    ppermute x3, starting transfers between devices, down(): return lax.ppermute(value, axis, [(i, i - 1) for i in range(1, count)])  3.86 us
    pallas_call x1, Pallas kernels, early_backward(): pl.pallas_call(early_kernel, name='early_backward', in_specs=[VMEM] * 2,...  2.55 us
    pallas_call x3, Pallas kernels, project(): pl.pallas_call(functools.partial(project_kernel, splits), name='project',...  2.36 us
  transfers between devices with their start and end apart: 9, of which 3 were waited for; matrix products, arithmetic and copies ran while one was open for 0% of the time, Pallas kernels for 37%

profile of v4, /device:TPU:0, one launch (start us, length us, event | category | flops | bytes accessed | tf_op | source)
XLA Modules:
  0.0 58.5 jit_solution(6186299317064037672)
XLA Ops:
  0.6 3.1 %collective-permute-start.2 = (bf16[128,1536]{1,0:T(8,128)(2,1)}, bf16[128,1536]{1,0:T(8,128)(2,1)S(1)}, u32[]{:S(2)}, u32[]{:S(2)}) collective-permute-start(bf16[128,1536]{1,0:T(8,128)(2,1)} %bitcast.15), channel_id=1, source_target_pairs={{0,4},{2,6},{4,0},{6,2},{1,5},{3,7},{5,1},{7,3},{8,12},{10,14},{12... | collective-permute-start | bytes 1179656 | tf_op jit(solution)/shard_map/ppermute | solution.py:30
  3.7 0.0 collective-permute-start.1
  3.7 9.3 %collective-permute-done.2.refs_1_.refs_3_.grad_ref = bf16[128,1536]{1,0:T(8,128)(2,1)S(1)} collective-permute-done((bf16[128,1536]{1,0:T(8,128)(2,1)}, bf16[128,1536]{1,0:T(8,128)(2,1)S(1)}, u32[]{:S(2)}, u32[]{:S(2)}) %collective-permute-start.2) | collective-permute-done | bytes 393248 | tf_op jit(solution)/shard_map/ppermute | solution.py:30
  13.0 0.0 collective-permute-start.3
  13.0 0.0 copy-start.1
  13.0 1.0 %copy-done.1 = bf16[1,1,128,1536]{3,2,1,0:T(8,128)(2,1)S(1)} copy-done((bf16[1,1,128,1536]{3,2,1,0:T(8,128)(2,1)S(1)}, bf16[1,1,128,1536]{3,2,1,0:T(8,128)(2,1)}, u32[]{:S(2)}) %copy-start.1) | copy-done | bytes 393240
  14.0 1.8 %collective-permute-start.4 = (bf16[128,1536]{1,0:T(8,128)(2,1)S(1)}, bf16[128,1536]{1,0:T(8,128)(2,1)S(1)}, u32[]{:S(2)}, u32[]{:S(2)}) collective-permute-start(bf16[128,1536]{1,0:T(8,128)(2,1)S(1)} %choose.1), channel_id=1, source_target_pairs={{0,1},{1,0},{2,3},{3,2},{4,5},{5,4},{6,7},{7,6},{8,9},{9,8},{10,11... | collective-permute-start | bytes 1179656 | tf_op jit(solution)/shard_map/ppermute | solution.py:30
  15.8 1.2 %pack.1 = bf16[2320,128]{1,0:T(8,128)(2,1)S(1)} custom-call(s32[1,128]{1,0:T(1,128)} %bitcast.20, bf16[3,1536,128]{2,1,0:T(8,128)(2,1)} %bitcast.12), custom_call_target="tpu_custom_call" | custom-call | tf_op jit(solution)/shard_map/pack/pallas_call | solution.py:77
  17.0 1.3 %collective-permute-start.7 = (bf16[2320,128]{1,0:T(8,128)(2,1)S(1)}, bf16[2320,128]{1,0:T(8,128)(2,1)S(1)}, u32[]{:S(2)}, u32[]{:S(2)}) collective-permute-start(bf16[2320,128]{1,0:T(8,128)(2,1)S(1)} %pack.1), channel_id=1, source_target_pairs={{8,0},{16,8},{24,16},{9,1},{17,9},{25,17},{10,2},{18,10},{26,18},{... | collective-permute-start | bytes 1781768 | tf_op jit(solution)/shard_map/ppermute | solution.py:40
  18.3 7.0 %forward.1 = (bf16[128,1536]{1,0:T(8,128)(2,1)S(1)}, f32[128,1536]{1,0:T(8,128)S(1)}, bf16[1536,1536]{1,0:T(8,128)(2,1)S(1)}, bf16[1536,1536]{1,0:T(8,128)(2,1)S(1)}, bf16[1536,1536]{1,0:T(8,128)(2,1)S(1)}) custom-call(s32[1,128]{1,0:T(1,128)} %bitcast.21, bf16[3,12,128,128]{3,2,1,0:T(8,128)(2,1)} %bitcast.13, bf16[6144,1536]{1,0:T(8,128)(2,1)} %bitcast.24, ...), custom_call_target="tpu_custom_call" | custom-call | tf_op jit(solution)/shard_map/forward/pallas_call | solution.py:140
  25.3 0.0 collective-permute-done.1.refs_2_.grad_ref
  25.3 0.8 %project.3.carried_ref = f32[128,1536]{1,0:T(8,128)S(1)} custom-call(bf16[1536,1536]{1,0:T(8,128)(2,1)S(1)} %get-tuple-element.12.weight_ref, bf16[128,1536]{1,0:T(8,128)(2,1)S(1)} %collective-permute-done.1.refs_2_.grad_ref, f32[128,1536]{1,0:T(8,128)S(1)} %get-tuple-element.13.carried_ref), custom_call_target="tpu_custom_call" | custom-call | tf_op jit(solution)/shard_map/project/pallas_call | solution.py:271
  26.1 0.0 copy-start
  26.1 0.0 copy-start.3
  26.1 0.8 %project.4.carried_ref = f32[128,1536]{1,0:T(8,128)S(1)} custom-call(bf16[1536,1536]{1,0:T(8,128)(2,1)S(1)} %get-tuple-element.11.weight_ref, bf16[128,1536]{1,0:T(8,128)(2,1)S(1)} %collective-permute-done.2.refs_1_.refs_3_.grad_ref, f32[128,1536]{1,0:T(8,128)S(1)} %project.3.carried_ref), custom_call_target="tpu_custom_call" | custom-call | tf_op jit(solution)/shard_map/project/pallas_call | solution.py:271
  26.9 0.0 copy-start.2
  26.9 0.0 collective-permute-done.3.refs_3_.grad_ref
  27.0 0.8 %project.5 = (bf16[128,768]{1,0:T(8,128)(2,1)S(1)}, bf16[128,768]{1,0:T(8,128)(2,1)S(1)}) custom-call(bf16[1536,1536]{1,0:T(8,128)(2,1)S(1)} %get-tuple-element.10.weight_ref, bf16[128,1536]{1,0:T(8,128)(2,1)S(1)} %collective-permute-done.3.refs_3_.grad_ref, f32[128,1536]{1,0:T(8,128)S(1)} %project.4.carried_ref), custom_call_target="tpu_custom_call" | custom-call | tf_op jit(solution)/shard_map/project/pallas_call | solution.py:271
  27.7 0.0 copy-done
  27.8 0.0 copy-done.3
  27.8 1.9 %late_backward.1 = bf16[3,6,128,128]{3,2,1,0:T(8,128)(2,1)S(1)} custom-call(s32[1,128]{1,0:T(1,128)S(1)} %bitcast.22, bf16[3,12,128,128]{3,2,1,0:T(8,128)(2,1)S(1)} %bitcast.14, bf16[128,768]{1,0:T(8,128)(2,1)S(1)} %get-tuple-element.14.grad_ref), custom_call_target="tpu_custom_call" | custom-call | tf_op jit(solution)/shard_map/late_backward/pallas_call | solution.py:188
  29.6 1.3 %collective-permute-start.6 = (bf16[3,6,128,128]{3,2,1,0:T(8,128)(2,1)S(1)}, bf16[3,6,128,128]{3,2,1,0:T(8,128)(2,1)S(1)}, u32[]{:S(2)}, u32[]{:S(2)}) collective-permute-start(bf16[3,6,128,128]{3,2,1,0:T(8,128)(2,1)S(1)} %late_backward.1), channel_id=1, source_target_pairs={{8,0},{16,8},{24,16},{9,1},{17,9},{25,17},{10,2},{18,10},{26,18},{... | collective-permute-start | bytes 1769480 | tf_op jit(solution)/shard_map/ppermute | solution.py:40
  30.9 0.4 collective-permute-start
  31.3 0.0 collective-permute-done.4.refs_4_
  31.3 0.0 collective-permute-start.5
  31.3 1.3 %collective-permute-start.8 = (bf16[128,768]{1,0:T(8,128)(2,1)S(1)}, bf16[128,768]{1,0:T(8,128)(2,1)S(1)}, u32[]{:S(2)}, u32[]{:S(2)}) collective-permute-start(bf16[128,768]{1,0:T(8,128)(2,1)S(1)} %get-tuple-element.15), channel_id=1, source_target_pairs={{8,0},{16,8},{24,16},{9,1},{17,9},{25,17},{10,2},{18,10},{26,18},{... | collective-permute-start | bytes 589832 | tf_op jit(solution)/shard_map/ppermute | solution.py:40
  32.6 9.6 %collective-permute-done.refs_1_ = bf16[128,1536]{1,0:T(8,128)(2,1)S(1)} collective-permute-done((bf16[128,1536]{1,0:T(8,128)(2,1)S(1)}, bf16[128,1536]{1,0:T(8,128)(2,1)S(1)}, u32[]{:S(2)}, u32[]{:S(2)}) %collective-permute-start) | collective-permute-done | bytes 393248 | tf_op jit(solution)/shard_map/ppermute | solution.py:30
  42.2 0.0 copy-done.2
  42.2 3.2 %weight_gradient.2.refs_5_ = bf16[3072,1536]{1,0:T(8,128)(2,1)} custom-call(bf16[128,1536]{1,0:T(8,128)(2,1)S(1)} %get-tuple-element.9.refs_0_, bf16[128,1536]{1,0:T(8,128)(2,1)S(1)} %collective-permute-done.refs_1_, bf16[128,1536]{1,0:T(8,128)(2,1)S(1)} %bitcast.19, bf16[128,1536]{1,0:T(8,128)(2,1)S(1)} %collective-permute-done.2.refs_1_.refs_3_.grad_ref, ...), custom_call_target="tpu_custom_call" | custom-call | tf_op jit(solution)/shard_map/weight_gradient/pallas_call | solution.py:355
  45.4 0.0 collective-permute-done.7.packed_ref
  45.4 6.4 %collective-permute-done.8.grad_ref = bf16[128,768]{1,0:T(8,128)(2,1)S(1)} collective-permute-done((bf16[128,768]{1,0:T(8,128)(2,1)S(1)}, bf16[128,768]{1,0:T(8,128)(2,1)S(1)}, u32[]{:S(2)}, u32[]{:S(2)}) %collective-permute-start.8) | collective-permute-done | bytes 196640 | tf_op jit(solution)/shard_map/ppermute | solution.py:40
  51.8 2.6 %early_backward.1.whole_ref = bf16[3,12,128,128]{3,2,1,0:T(8,128)(2,1)} custom-call(bf16[2320,128]{1,0:T(8,128)(2,1)S(1)} %collective-permute-done.7.packed_ref, bf16[128,768]{1,0:T(8,128)(2,1)S(1)} %collective-permute-done.8.grad_ref), custom_call_target="tpu_custom_call" | custom-call | tf_op jit(solution)/shard_map/early_backward/pallas_call | solution.py:219
  54.4 0.0 collective-permute-done.5.refs_4_
  54.4 3.2 %weight_gradient.3 = bf16[3072,1536]{1,0:T(8,128)(2,1)} custom-call(bf16[128,1536]{1,0:T(8,128)(2,1)S(1)} %get-tuple-element.9.refs_0_, bf16[128,1536]{1,0:T(8,128)(2,1)S(1)} %collective-permute-done.refs_1_, bf16[128,1536]{1,0:T(8,128)(2,1)S(1)} %collective-permute-done.1.refs_2_.grad_ref, ...), custom_call_target="tpu_custom_call", output_to_operand_aliasing={{}: (5, {})} | custom-call | tf_op jit(solution)/shard_map/weight_gradient/pallas_call | solution.py:355
  57.6 0.0 collective-permute-done.6.late_ref
  57.6 0.8 %fill.1 = bf16[3,12,128,128]{3,2,1,0:T(8,128)(2,1)} custom-call(bf16[3,6,128,128]{3,2,1,0:T(8,128)(2,1)S(1)} %collective-permute-done.6.late_ref, bf16[3,12,128,128]{3,2,1,0:T(8,128)(2,1)} %early_backward.1.whole_ref), custom_call_target="tpu_custom_call", output_to_operand_aliasing={{}: (1, {})} | custom-call | tf_op jit(solution)/shard_map/fill/pallas_call | solution.py:247
  (1 shorter events, 0.0 us)
Async XLA Ops:
  0.6 12.4 %collective-permute-start.2 = (bf16[128,1536]{1,0:T(8,128)(2,1)}, bf16[128,1536]{1,0:T(8,128)(2,1)S(1)}, u32[]{:S(2)}, u32[]{:S(2)}) collective-permute-start(bf16[128,1536]{1,0:T(8,128)(2,1)} %bitcast.15), channel_id=1, source_target_pairs={{0,4},{2,6},{4,0},{6,2},{1,5},{3,7},{5,1},{7,3},{8,12},{10,14},{12... | collective-permute-start | bytes 1179656 | tf_op jit(solution)/shard_map/ppermute | solution.py:30
  3.7 21.6 %collective-permute-start.1 = (bf16[128,1536]{1,0:T(8,128)(2,1)}, bf16[128,1536]{1,0:T(8,128)(2,1)S(1)}, u32[]{:S(2)}, u32[]{:S(2)}) collective-permute-start(bf16[128,1536]{1,0:T(8,128)(2,1)} %bitcast.16), channel_id=1, source_target_pairs={{0,2},{2,0},{4,6},{6,4},{1,3},{3,1},{5,7},{7,5},{8,10},{10,8},{12,... | collective-permute-start | bytes 1179656 | tf_op jit(solution)/shard_map/ppermute | solution.py:35
  13.0 13.9 %collective-permute-start.3 = (bf16[128,1536]{1,0:T(8,128)(2,1)S(1)}, bf16[128,1536]{1,0:T(8,128)(2,1)S(1)}, u32[]{:S(2)}, u32[]{:S(2)}) collective-permute-start(bf16[128,1536]{1,0:T(8,128)(2,1)S(1)} %collective-permute-done.2.refs_1_.refs_3_.grad_ref), channel_id=1, source_target_pairs={{0,2},{2,0},{4,6},{6,4},{1,3},{3,1},{5,7},{7,5},{8,10},{10,8},{12,... | collective-permute-start | bytes 1179656 | tf_op jit(solution)/shard_map/ppermute | solution.py:35
  13.0 1.0 %copy-start.1 = (bf16[1,1,128,1536]{3,2,1,0:T(8,128)(2,1)S(1)}, bf16[1,1,128,1536]{3,2,1,0:T(8,128)(2,1)}, u32[]{:S(2)}) copy-start(bf16[1,1,128,1536]{3,2,1,0:T(8,128)(2,1)} %param.7) | copy-start | bytes 1179652
  14.0 17.3 %collective-permute-start.4 = (bf16[128,1536]{1,0:T(8,128)(2,1)S(1)}, bf16[128,1536]{1,0:T(8,128)(2,1)S(1)}, u32[]{:S(2)}, u32[]{:S(2)}) collective-permute-start(bf16[128,1536]{1,0:T(8,128)(2,1)S(1)} %choose.1), channel_id=1, source_target_pairs={{0,1},{1,0},{2,3},{3,2},{4,5},{5,4},{6,7},{7,6},{8,9},{9,8},{10,11... | collective-permute-start | bytes 1179656 | tf_op jit(solution)/shard_map/ppermute | solution.py:30
  17.0 28.4 %collective-permute-start.7 = (bf16[2320,128]{1,0:T(8,128)(2,1)S(1)}, bf16[2320,128]{1,0:T(8,128)(2,1)S(1)}, u32[]{:S(2)}, u32[]{:S(2)}) collective-permute-start(bf16[2320,128]{1,0:T(8,128)(2,1)S(1)} %pack.1), channel_id=1, source_target_pairs={{8,0},{16,8},{24,16},{9,1},{17,9},{25,17},{10,2},{18,10},{26,18},{... | collective-permute-start | bytes 1781768 | tf_op jit(solution)/shard_map/ppermute | solution.py:40
  26.1 1.6 %copy-start = (bf16[1,1,3,128,12,128]{5,3,4,2,1,0:T(8,128)(2,1)S(1)}, bf16[1,1,3,128,12,128]{5,3,4,2,1,0:T(8,128)(2,1)}, u32[]{:S(2)}) copy-start(bf16[1,1,3,128,12,128]{5,3,4,2,1,0:T(8,128)(2,1)} %param.4) | copy-start | bytes 3538948
  26.1 1.6 %copy-start.3 = (s32[1,1,128]{2,1,0:T(1,128)S(1)}, s32[1,1,128]{2,1,0:T(1,128)}, u32[]{:S(2)}) copy-start(s32[1,1,128]{2,1,0:T(1,128)} %param.5) | copy-start | bytes 1540
  26.9 15.3 %copy-start.2 = (bf16[1,1,128,1536]{3,2,1,0:T(8,128)(2,1)S(1)}, bf16[1,1,128,1536]{3,2,1,0:T(8,128)(2,1)}, u32[]{:S(2)}) copy-start(bf16[1,1,128,1536]{3,2,1,0:T(8,128)(2,1)} %param.7) | copy-start | bytes 1179652
  29.6 28.0 %collective-permute-start.6 = (bf16[3,6,128,128]{3,2,1,0:T(8,128)(2,1)S(1)}, bf16[3,6,128,128]{3,2,1,0:T(8,128)(2,1)S(1)}, u32[]{:S(2)}, u32[]{:S(2)}) collective-permute-start(bf16[3,6,128,128]{3,2,1,0:T(8,128)(2,1)S(1)} %late_backward.1), channel_id=1, source_target_pairs={{8,0},{16,8},{24,16},{9,1},{17,9},{25,17},{10,2},{18,10},{26,18},{... | collective-permute-start | bytes 1769480 | tf_op jit(solution)/shard_map/ppermute | solution.py:40
  30.9 11.3 %collective-permute-start = (bf16[128,1536]{1,0:T(8,128)(2,1)S(1)}, bf16[128,1536]{1,0:T(8,128)(2,1)S(1)}, u32[]{:S(2)}, u32[]{:S(2)}) collective-permute-start(bf16[128,1536]{1,0:T(8,128)(2,1)S(1)} %get-tuple-element.9.refs_0_), channel_id=1, source_target_pairs={{0,1},{1,0},{2,3},{3,2},{4,5},{5,4},{6,7},{7,6},{8,9},{9,8},{10,11... | collective-permute-start | bytes 1179656 | tf_op jit(solution)/shard_map/ppermute | solution.py:30
  31.3 23.1 %collective-permute-start.5 = (bf16[128,1536]{1,0:T(8,128)(2,1)S(1)}, bf16[128,1536]{1,0:T(8,128)(2,1)S(1)}, u32[]{:S(2)}, u32[]{:S(2)}) collective-permute-start(bf16[128,1536]{1,0:T(8,128)(2,1)S(1)} %collective-permute-done.4.refs_4_), channel_id=1, source_target_pairs={{0,2},{2,0},{4,6},{6,4},{1,3},{3,1},{5,7},{7,5},{8,10},{10,8},{12,... | collective-permute-start | bytes 1179656 | tf_op jit(solution)/shard_map/ppermute | solution.py:35
  31.3 20.5 %collective-permute-start.8 = (bf16[128,768]{1,0:T(8,128)(2,1)S(1)}, bf16[128,768]{1,0:T(8,128)(2,1)S(1)}, u32[]{:S(2)}, u32[]{:S(2)}) collective-permute-start(bf16[128,768]{1,0:T(8,128)(2,1)S(1)} %get-tuple-element.15), channel_id=1, source_target_pairs={{8,0},{16,8},{24,16},{9,1},{17,9},{25,17},{10,2},{18,10},{26,18},{... | collective-permute-start | bytes 589832 | tf_op jit(solution)/shard_map/ppermute | solution.py:40

commit v5 on v4

--- a/solution.py
+++ b/solution.py
@@ -53,36 +53,47 @@
     return exponent * (1.0 / jnp.sum(exponent, axis=0, keepdims=True))
 
 
-def pack_kernel(rows, pos_ref, qkv_ref, out_ref, held, sems):
-    gets = [
+def pack_kernel(rows, pos_ref, qkv_ref, own_ref, out_ref, *refs):
+    parts, (held, sems) = refs[:-2], refs[-2:]
+    gets = [pltpu.make_async_copy(pos_ref, held, sems.at[3])]
+    gets += [
         pltpu.make_async_copy(
             qkv_ref.at[i, pl.ds(0, rows)], out_ref.at[pl.ds(i * rows, rows)], sems.at[i]
         )
         for i in range(3)
     ]
-    pos_get = pltpu.make_async_copy(pos_ref, held, sems.at[3])
-    pos_get.start()
+    for number, part in enumerate(parts):
+        size = part.shape[1]
+        gets.append(
+            pltpu.make_async_copy(
+                own_ref.at[:, pl.ds(number * size, size)], part, sems.at[4 + number]
+            )
+        )
     for get in gets:
         get.start()
-    pos_get.wait()
+    gets[0].wait()
     spare = (out_ref.shape[0] - 3 * rows, out_ref.shape[1])
     out_ref[3 * rows :] = jnp.broadcast_to(held[...].astype(F32), spare).astype(BF16)
-    for get in gets:
+    for get in gets[1:]:
         get.wait()
 
 
-def pack(pos, qkv, early):
+def pack(pos, qkv, own, early, pieces):
     _, _, seq, width = qkv.shape
     rows = early * seq
+    part = pltpu.VMEM((seq, own.shape[1] // pieces), BF16)
     return pl.pallas_call(
         functools.partial(pack_kernel, rows),
         name="pack",
-        in_specs=[ANY, ANY],
-        out_specs=VMEM,
-        out_shape=pltpu.VMEM((3 * rows + 16, width), BF16),
-        scratch_shapes=[pltpu.VMEM(pos.shape, pos.dtype), pltpu.SemaphoreType.DMA((4,))],
-        compiler_params=PARAMS,
-    )(in_hbm(pos), in_hbm(qkv.reshape(3, -1, width)))
+        in_specs=[ANY] * 3,
+        out_specs=[VMEM] * (1 + pieces),
+        out_shape=[pltpu.VMEM((3 * rows + 16, width), BF16)] + [part] * pieces,
+        scratch_shapes=[
+            pltpu.VMEM(pos.shape, pos.dtype),
+            pltpu.SemaphoreType.DMA((4 + pieces,)),
+        ],
+        compiler_params=PARAMS,
+    )(in_hbm(pos), in_hbm(qkv.reshape(3, -1, width)), in_hbm(own))
 
 
 def place():
@@ -256,59 +267,87 @@
     )(late, whole)
 
 
-def project_kernel(splits, weight_ref, grad_ref, carried_ref, *outs):
-    total = carried_ref[...] + jnp.dot(
-        grad_ref[...], weight_ref[...], preferred_element_type=F32
-    )
+def project_kernel(terms, splits, *refs):
+    count = 1 + max(number for number, _ in terms)
+    weights, grads = refs[:count], refs[count : count + len(terms)]
+    refs = refs[count + len(terms) :]
+    total = refs[0][...]
+    for (number, start), grad in zip(terms, grads):
+        rows = weights[number][start : start + grad.shape[1]]
+        total = total + jnp.dot(grad[...], rows, preferred_element_type=F32)
     at = 0
-    for out, size in zip(outs, splits):
+    for out, size in zip(refs[1:], splits):
         out[...] = total[:, at : at + size].astype(out.dtype)
         at += size
 
 
-def project(weight, grad, total, splits, dtype):
-    seq = grad.shape[0]
-    return pl.pallas_call(
-        functools.partial(project_kernel, splits),
+def project(items, total, splits, dtype):
+    weights, terms = [], []
+    for weight, start, _ in items:
+        found = [number for number, known in enumerate(weights) if known is weight]
+        if not found:
+            weights.append(weight)
+        terms.append((found[0] if found else len(weights) - 1, start))
+    grads = [grad for _, _, grad in items]
+    seq = grads[0].shape[0]
+    return pl.pallas_call(
+        functools.partial(project_kernel, tuple(terms), splits),
         name="project",
-        in_specs=[VMEM] * 3,
+        in_specs=[VMEM] * (len(weights) + len(grads) + 1),
         out_specs=[VMEM] * len(splits),
         out_shape=[jax.ShapeDtypeStruct((seq, size), dtype) for size in splits],
         compiler_params=PARAMS,
-    )(weight, grad, total)
-
-
-def choose_kernel(chips, per_replica, number, step, replicas, *refs):
+    )(*weights, *grads, total)
+
+
+def counts(options):
+    return tuple(len(pieces) for pieces in options)
+
+
+def grouped(refs, sizes):
+    refs = list(refs)
+    return [[refs.pop(0) for _ in range(size)] for size in sizes]
+
+
+def choose_kernel(sizes, per_replica, number, step, replicas, *refs):
+    chips = len(sizes)
     chip, _ = place()
     target = lax.rem(lax.axis_index("dp") + step, replicas)
     index = lax.rem(chip - (target * per_replica + number) + chips, chips)
     out_ref = refs[-1]
-    for option, ref in enumerate(refs[:-1]):
+    for option, pieces in enumerate(grouped(refs[:-1], sizes)):
 
         @pl.when(index == option)
         def _():
-            out_ref[...] = ref[...]
+            at = 0
+            for piece in pieces:
+                out_ref[:, at : at + piece.shape[1]] = piece[...]
+                at += piece.shape[1]
 
 
 def choose(replicas, number, step, options):
     chips = len(options)
-    return pl.pallas_call(
-        functools.partial(choose_kernel, chips, chips // replicas, number, step, replicas),
+    args = [piece for pieces in options for piece in pieces]
+    return pl.pallas_call(
+        functools.partial(
+            choose_kernel, counts(options), chips // replicas, number, step, replicas
+        ),
         name="choose",
-        in_specs=[VMEM] * chips,
+        in_specs=[VMEM] * len(args),
         out_specs=VMEM,
-        out_shape=jax.ShapeDtypeStruct(options[0].shape, options[0].dtype),
-        compiler_params=PARAMS,
-    )(*options)
-
-
-def weight_kernel(replicas, chips, blocks, *refs):
+        out_shape=jax.ShapeDtypeStruct(options[0][0].shape, options[0][0].dtype),
+        compiler_params=PARAMS,
+    )(*args)
+
+
+def weight_kernel(replicas, sizes, slots, blocks, *refs):
     acts = refs[:replicas]
-    options = refs[replicas : replicas + chips]
+    args = sum(sizes)
+    options = grouped(refs[replicas : replicas + args], sizes)
+    far = refs[replicas + args : replicas + args + slots * (replicas - 1)]
     out_ref, stacked = refs[-2:]
     step = pl.program_id(0)
-    slots = pl.num_programs(0) // blocks
-    far = refs[replicas + chips : replicas + chips + slots * (replicas - 1)]
+    chips = len(sizes)
     seq = acts[0].shape[0]
     size = out_ref.shape[0]
 
@@ -318,34 +357,36 @@
             stacked[number * seq : (number + 1) * seq] = act[...]
 
     chip, _ = place()
-    columns = pl.ds(pl.multiple_of(lax.rem(step, blocks) * size, size), size)
     for slot in range(slots):
-
-        @pl.when(lax.div(step, blocks) == slot)
-        def _():
-            index = lax.rem(chip - (lax.axis_index("dp") * slots + slot) + chips, chips)
-            near = options[0][:, columns]
-            for number in range(1, chips):
-                near = jnp.where(index == number, options[number][:, columns], near)
-            ours = far[slot * (replicas - 1) : (slot + 1) * (replicas - 1)]
-            left = jnp.concatenate([near] + [ref[:, columns] for ref in ours], axis=0)
-            out_ref[...] = dot(left, stacked[...], ((0,), (0,))).astype(BF16)
+        ours = far[slot * (replicas - 1) : (slot + 1) * (replicas - 1)]
+        index = lax.rem(chip - (lax.axis_index("dp") * slots + slot) + chips, chips)
+        for block in range(blocks):
+
+            @pl.when(step == slot * blocks + block)
+            def _():
+                near = None
+                for number, pieces in enumerate(options):
+                    piece, at = divmod(block * size, pieces[0].shape[1])
+                    part = pieces[piece][:, at : at + size]
+                    near = part if near is None else jnp.where(index == number, part, near)
+                columns = slice(block * size, (block + 1) * size)
+                left = jnp.concatenate([near] + [ref[:, columns] for ref in ours], axis=0)
+                out_ref[...] = dot(left, stacked[...], ((0,), (0,))).astype(BF16)
 
 
 def weight_gradient(parity, acts, options, far, begun):
-    replicas, chips, slots = len(acts), len(options), len(far)
+    replicas, slots = len(acts), len(far)
     seq, columns = acts[0].shape
-    features = options[0].shape[1]
-    blocks = max(1, features // 768)
-    while features % blocks or (features // blocks) % 128:
-        blocks -= 1
+    features = far[0][0].shape[1]
+    blocks = max(counts(options))
     size = features // blocks
 
     def target(step):
         core = lax.rem(lax.axis_index("st") + parity, 2)
         return (2 * lax.div(step, blocks) + core) * blocks + lax.rem(step, blocks), 0
 
-    args = [*acts, *options, *[ref for slot in far for ref in slot]]
+    args = [*acts, *[piece for pieces in options for piece in pieces]]
+    args += [ref for slot in far for ref in slot]
     specs = [VMEM] * len(args)
     aliases = {}
     if begun is not None:
@@ -353,7 +394,7 @@
         args.append(begun)
         specs.append(ANY)
     return pl.pallas_call(
-        functools.partial(weight_kernel, replicas, chips, blocks),
+        functools.partial(weight_kernel, replicas, counts(options), slots, blocks),
         name="weight_gradient",
         grid=(slots * blocks,),
         in_specs=specs,
@@ -363,6 +404,10 @@
         input_output_aliases=aliases,
         compiler_params=PARAMS,
     )(*args)
+
+
+def pieces_of(features):
+    return 2 if features % 256 == 0 else 1
 
 
 def local(saved_qkv, positions, w_out, grad_out):
@@ -377,34 +422,41 @@
     chips = shards // 2
     per_replica = chips // replicas
 
-    packed_above = down(pack(pos, qkv, early), "section")
-    same = [grad_out[0, 0]]
+    own = grad_out[0, 0]
+    pieces = pieces_of(own.shape[1])
+    packed, *parts = pack(pos, qkv, own, early, pieces)
+    packed_above = down(packed, "section")
+    same = [[own]]
+    other = []
     for step in range(1, chips):
-        same.append(rotate(same[0], "st", 2 * step))
-    other = []
-    for step in range(chips):
-        other.append(swap(same[step], "st"))
-
-    attended, total, *far_rows = forward(chips, pos, qkv, weight, same[0])
+        same.append([])
+        for piece in range(pieces):
+            same[-1].append(rotate(parts[piece], "st", 2 * step))
+    other.append([swap(own, "st")])
+    for step in range(1, chips):
+        other.append([])
+        for piece in range(pieces):
+            other[-1].append(swap(same[step][piece], "st"))
+
+    attended, total, *far_rows = forward(chips, pos, qkv, weight, own)
     acts = [attended]
     for step in range(1, replicas):
         acts.append(rotate(attended, "dp", step))
 
     whole = (heads * width,)
     halves = (early * width, late * width)
-    (total,) = project(far_rows[0], other[0], total, whole, F32)
+    depth = own.shape[1] // pieces
+    direct, crossed = [], []
     for step in range(1, chips):
-        last = step == chips - 1
-        (total,) = project(far_rows[2 * step - 1], same[step], total, whole, F32)
-        total = project(
-            far_rows[2 * step],
-            other[step],
-            total,
-            halves if last else whole,
-            BF16 if last else F32,
-        )
-        if not last:
-            (total,) = total
+        for piece in range(pieces):
+            start = piece * depth
+            direct.append((far_rows[2 * step - 1], start, same[step][piece]))
+            crossed.append((far_rows[2 * step], start, other[step][piece]))
+    calls = [[(far_rows[0], 0, other[0][0]), direct[0]]]
+    calls += [[direct[i], crossed[i - 1]] for i in range(1, len(direct))]
+    for items in calls:
+        (total,) = project(items, total, whole, F32)
+    total = project([crossed[-1]], total, halves, BF16)
     d_early, d_late = total
     d_above = down(d_early, "section")
     grads_late = late_backward(pos, qkv, d_late)
@@ -412,13 +464,13 @@
 
     near_far, cross_far = [], []
     for number in range(per_replica):
-        direct, crossed = [], []
+        straight, swapped = [], []
         for step in range(1, replicas):
             chosen = choose(replicas, number, step, same)
-            direct.append(rotate(chosen, "dp", step))
-            crossed.append(swap(direct[-1], "st"))
-        near_far.append(direct)
-        cross_far.append(crossed)
+            straight.append(rotate(chosen, "dp", step))
+            swapped.append(swap(straight[-1], "st"))
+        near_far.append(straight)
+        cross_far.append(swapped)
 
     begun = early_backward(packed_above, d_above, heads)
     grad_weight = weight_gradient(0, acts, same, near_far, None)

time: 58.7 us -> 60.2 us (1.026)
  local copies, waits for them, and re-layouts: 1.02 us -> 1.75 us
    unnamed x8, local copies, waits for them, and re-layouts: 1.02 us -> 1.75 us
    ppermute x3 -> x4, starting transfers between devices: 5.21 us -> 4.82 us  [rotate(): lax.ppermute(value, axis, [(i, (i + steps) % count) for i in range(count)])]
    ppermute x3 -> x4, waiting for transfers between devices: 19 us -> 19.3 us  [rotate(): lax.ppermute(value, axis, [(i, (i + steps) % count) for i in range(count)])]
  transfers between devices with their start and end apart: 9 -> 11, of which waited for: 3 -> 4; matrix products, arithmetic and copies ran while one was open for 0% -> 0% of each run, Pallas kernels for 37% -> 32%
where the time goes in v5:
time: 60.2 us; the launch traced here: 59.9 us
  waiting for transfers between devices  25.7 us (43%)
  Pallas kernels  22.4 us (37%)
  starting transfers between devices  9.24 us (15%)
  local copies, waits for them, and re-layouts  1.75 us (3%)
  between operations  0.78 us (1%)
    ppermute x4, waiting for transfers between devices, rotate(): lax.ppermute(value, axis, [(i, (i + steps) % count) for i in range(count)])  19.3 us
    pallas_call x1, Pallas kernels, forward(): pl.pallas_call(functools.partial(forward_kernel, chips, groups), name='fo...  6.99 us
    pallas_call x2, Pallas kernels, weight_gradient(): pl.pallas_call(functools.partial(weight_kernel, replicas, counts(options)...  6.44 us
    ppermute x3, waiting for transfers between devices, down(): return lax.ppermute(value, axis, [(i, i - 1) for i in range(1, count)])  6.39 us
    ppermute x4, starting transfers between devices, rotate(): lax.ppermute(value, axis, [(i, (i + steps) % count) for i in range(count)])  4.82 us
    ppermute x3, starting transfers between devices, down(): return lax.ppermute(value, axis, [(i, i - 1) for i in range(1, count)])  3.85 us
    pallas_call x1, Pallas kernels, early_backward(): pl.pallas_call(early_kernel, name='early_backward', in_specs=[VMEM] * 2,...  2.55 us
    pallas_call x3, Pallas kernels, project(): pl.pallas_call(functools.partial(project_kernel, tuple(terms), splits), n...  2.36 us
  transfers between devices with their start and end apart: 11, of which 4 were waited for; matrix products, arithmetic and copies ran while one was open for 0% of the time, Pallas kernels for 32%

profile of v5, /device:TPU:0, one launch (start us, length us, event | category | flops | bytes accessed | tf_op | source)
XLA Modules:
  0.0 59.9 jit_solution(851517398663301029)
XLA Ops:
  0.6 0.6 collective-permute-start.1
  1.2 1.3 %pack.1 = (bf16[2320,128]{1,0:T(8,128)(2,1)S(1)}, bf16[128,768]{1,0:T(8,128)(2,1)S(1)}, bf16[128,768]{1,0:T(8,128)(2,1)S(1)}) custom-call(s32[1,128]{1,0:T(1,128)} %bitcast.20, bf16[3,1536,128]{2,1,0:T(8,128)(2,1)} %bitcast.12, bf16[128,1536]{1,0:T(8,128)(2,1)} %bitcast.16), custom_call_target="tpu_custom_call" | custom-call | tf_op jit(solution)/shard_map/pack/pallas_call | solution.py:85
  2.5 2.6 %collective-permute-start.2 = (bf16[128,768]{1,0:T(8,128)(2,1)S(1)}, bf16[128,768]{1,0:T(8,128)(2,1)S(1)}, u32[]{:S(2)}, u32[]{:S(2)}) collective-permute-start(bf16[128,768]{1,0:T(8,128)(2,1)S(1)} %get-tuple-element.13), channel_id=1, source_target_pairs={{0,4},{2,6},{4,0},{6,2},{1,5},{3,7},{5,1},{7,3},{8,12},{10,14},{12... | collective-permute-start | bytes 589832 | tf_op jit(solution)/shard_map/ppermute | solution.py:30
  5.1 0.1 collective-permute-start.4
  5.2 5.7 %collective-permute-done.2.refs_1_.refs_3_ = bf16[128,768]{1,0:T(8,128)(2,1)S(1)} collective-permute-done((bf16[128,768]{1,0:T(8,128)(2,1)S(1)}, bf16[128,768]{1,0:T(8,128)(2,1)S(1)}, u32[]{:S(2)}, u32[]{:S(2)}) %collective-permute-start.2) | collective-permute-done | bytes 196640 | tf_op jit(solution)/shard_map/ppermute | solution.py:30
  10.9 0.0 collective-permute-start.3
  10.9 4.0 %collective-permute-done.4.refs_2_.refs_4_ = bf16[128,768]{1,0:T(8,128)(2,1)S(1)} collective-permute-done((bf16[128,768]{1,0:T(8,128)(2,1)S(1)}, bf16[128,768]{1,0:T(8,128)(2,1)S(1)}, u32[]{:S(2)}, u32[]{:S(2)}) %collective-permute-start.4) | collective-permute-done | bytes 196640 | tf_op jit(solution)/shard_map/ppermute | solution.py:30
  14.9 0.0 collective-permute-start.5
  14.9 0.0 copy-start.1
  14.9 1.0 %copy-done.1 = bf16[1,1,128,1536]{3,2,1,0:T(8,128)(2,1)S(1)} copy-done((bf16[1,1,128,1536]{3,2,1,0:T(8,128)(2,1)S(1)}, bf16[1,1,128,1536]{3,2,1,0:T(8,128)(2,1)}, u32[]{:S(2)}) %copy-start.1) | copy-done | bytes 393240
  15.9 1.8 %collective-permute-start.6 = (bf16[128,1536]{1,0:T(8,128)(2,1)S(1)}, bf16[128,1536]{1,0:T(8,128)(2,1)S(1)}, u32[]{:S(2)}, u32[]{:S(2)}) collective-permute-start(bf16[128,1536]{1,0:T(8,128)(2,1)S(1)} %choose.1), channel_id=1, source_target_pairs={{0,1},{1,0},{2,3},{3,2},{4,5},{5,4},{6,7},{7,6},{8,9},{9,8},{10,11... | collective-permute-start | bytes 1179656 | tf_op jit(solution)/shard_map/ppermute | solution.py:30
  17.7 1.3 %collective-permute-start.9 = (bf16[2320,128]{1,0:T(8,128)(2,1)S(1)}, bf16[2320,128]{1,0:T(8,128)(2,1)S(1)}, u32[]{:S(2)}, u32[]{:S(2)}) collective-permute-start(bf16[2320,128]{1,0:T(8,128)(2,1)S(1)} %get-tuple-element.20), channel_id=1, source_target_pairs={{8,0},{16,8},{24,16},{9,1},{17,9},{25,17},{10,2},{18,10},{26,18},{... | collective-permute-start | bytes 1781768 | tf_op jit(solution)/shard_map/ppermute | solution.py:40
  19.0 7.0 %forward.1 = (bf16[128,1536]{1,0:T(8,128)(2,1)S(1)}, f32[128,1536]{1,0:T(8,128)S(1)}, bf16[1536,1536]{1,0:T(8,128)(2,1)S(1)}, bf16[1536,1536]{1,0:T(8,128)(2,1)S(1)}, bf16[1536,1536]{1,0:T(8,128)(2,1)S(1)}) custom-call(s32[1,128]{1,0:T(1,128)} %bitcast.21, bf16[3,12,128,128]{3,2,1,0:T(8,128)(2,1)} %bitcast.13, bf16[6144,1536]{1,0:T(8,128)(2,1)} %bitcast.24, ...), custom_call_target="tpu_custom_call" | custom-call | tf_op jit(solution)/shard_map/forward/pallas_call | solution.py:151
  26.0 0.0 collective-permute-done.1.refs_2_
  26.0 1.1 %project.3.refs_4_ = f32[128,1536]{1,0:T(8,128)S(1)} custom-call(bf16[1536,1536]{1,0:T(8,128)(2,1)S(1)} %get-tuple-element.17.refs_0_, bf16[1536,1536]{1,0:T(8,128)(2,1)S(1)} %get-tuple-element.16.refs_1_.refs_0_, bf16[128,1536]{1,0:T(8,128)(2,1)S(1)} %collective-permute-done.1.refs_2_, bf16[128,768]{1,0:T(8,128)(2,1)S(1)} %collective-permute-done.2.refs_1_.refs_3_, ...), custom_call_target="tpu_custom_call" | custom-call | tf_op jit(solution)/shard_map/project/pallas_call | solution.py:293
  27.1 0.0 collective-permute-done.3.refs_3_
  27.1 0.8 %project.4.refs_2_ = f32[128,1536]{1,0:T(8,128)S(1)} custom-call(bf16[1536,1536]{1,0:T(8,128)(2,1)S(1)} %get-tuple-element.16.refs_1_.refs_0_, bf16[1536,1536]{1,0:T(8,128)(2,1)S(1)} %get-tuple-element.15.refs_1_.refs_0_, bf16[128,768]{1,0:T(8,128)(2,1)S(1)} %collective-permute-done.4.refs_2_.refs_4_, bf16[128,768]{1,0:T(8,128)(2,1)S(1)} %collective-permute-done.3.refs_3_, ...), custom_call_target="tpu_custom_call" | custom-call | tf_op jit(solution)/shard_map/project/pallas_call | solution.py:293
  27.9 0.0 copy-start
  27.9 0.0 copy-start.3
  27.9 0.0 copy-start.2
  27.9 0.0 collective-permute-done.5.refs_4_.refs_1_
  27.9 0.5 project.5
  28.4 0.7 %copy-done = bf16[1,1,3,128,12,128]{5,3,4,2,1,0:T(8,128)(2,1)S(1)} copy-done((bf16[1,1,3,128,12,128]{5,3,4,2,1,0:T(8,128)(2,1)S(1)}, bf16[1,1,3,128,12,128]{5,3,4,2,1,0:T(8,128)(2,1)}, u32[]{:S(2)}) %copy-start) | copy-done | bytes 1179672
  29.2 0.0 copy-done.3
  29.2 1.9 %late_backward.1 = bf16[3,6,128,128]{3,2,1,0:T(8,128)(2,1)S(1)} custom-call(s32[1,128]{1,0:T(1,128)S(1)} %bitcast.22, bf16[3,12,128,128]{3,2,1,0:T(8,128)(2,1)S(1)} %bitcast.14, bf16[128,768]{1,0:T(8,128)(2,1)S(1)} %get-tuple-element.19.grad_ref), custom_call_target="tpu_custom_call" | custom-call | tf_op jit(solution)/shard_map/late_backward/pallas_call | solution.py:199
  31.0 1.3 %collective-permute-start.8 = (bf16[3,6,128,128]{3,2,1,0:T(8,128)(2,1)S(1)}, bf16[3,6,128,128]{3,2,1,0:T(8,128)(2,1)S(1)}, u32[]{:S(2)}, u32[]{:S(2)}) collective-permute-start(bf16[3,6,128,128]{3,2,1,0:T(8,128)(2,1)S(1)} %late_backward.1), channel_id=1, source_target_pairs={{8,0},{16,8},{24,16},{9,1},{17,9},{25,17},{10,2},{18,10},{26,18},{... | collective-permute-start | bytes 1769480 | tf_op jit(solution)/shard_map/ppermute | solution.py:40
  32.3 0.4 collective-permute-start
  32.7 0.0 collective-permute-done.6.refs_5_
  32.7 0.0 collective-permute-start.7
  32.7 1.3 %collective-permute-start.10 = (bf16[128,768]{1,0:T(8,128)(2,1)S(1)}, bf16[128,768]{1,0:T(8,128)(2,1)S(1)}, u32[]{:S(2)}, u32[]{:S(2)}) collective-permute-start(bf16[128,768]{1,0:T(8,128)(2,1)S(1)} %get-tuple-element.21), channel_id=1, source_target_pairs={{8,0},{16,8},{24,16},{9,1},{17,9},{25,17},{10,2},{18,10},{26,18},{... | collective-permute-start | bytes 589832 | tf_op jit(solution)/shard_map/ppermute | solution.py:40
  34.0 9.6 %collective-permute-done.refs_1_ = bf16[128,1536]{1,0:T(8,128)(2,1)S(1)} collective-permute-done((bf16[128,1536]{1,0:T(8,128)(2,1)S(1)}, bf16[128,1536]{1,0:T(8,128)(2,1)S(1)}, u32[]{:S(2)}, u32[]{:S(2)}) %collective-permute-start) | collective-permute-done | bytes 393248 | tf_op jit(solution)/shard_map/ppermute | solution.py:30
  43.6 0.0 copy-done.2
  43.6 3.2 %weight_gradient.2.refs_6_ = bf16[3072,1536]{1,0:T(8,128)(2,1)} custom-call(bf16[128,1536]{1,0:T(8,128)(2,1)S(1)} %get-tuple-element.12.refs_0_, bf16[128,1536]{1,0:T(8,128)(2,1)S(1)} %collective-permute-done.refs_1_, bf16[128,1536]{1,0:T(8,128)(2,1)S(1)} %bitcast.19, bf16[128,768]{1,0:T(8,128)(2,1)S(1)} %collective-permute-done.2.refs_1_.refs_3_, ...), custom_call_target="tpu_custom_call" | custom-call | tf_op jit(solution)/shard_map/weight_gradient/pallas_call | solution.py:396
  46.9 6.4 %collective-permute-done.10.grad_ref = bf16[128,768]{1,0:T(8,128)(2,1)S(1)} collective-permute-done((bf16[128,768]{1,0:T(8,128)(2,1)S(1)}, bf16[128,768]{1,0:T(8,128)(2,1)S(1)}, u32[]{:S(2)}, u32[]{:S(2)}) %collective-permute-start.10) | collective-permute-done | bytes 196640 | tf_op jit(solution)/shard_map/ppermute | solution.py:40
  53.2 0.0 collective-permute-done.9.packed_ref
  53.2 2.6 %early_backward.1.whole_ref = bf16[3,12,128,128]{3,2,1,0:T(8,128)(2,1)} custom-call(bf16[2320,128]{1,0:T(8,128)(2,1)S(1)} %collective-permute-done.9.packed_ref, bf16[128,768]{1,0:T(8,128)(2,1)S(1)} %collective-permute-done.10.grad_ref), custom_call_target="tpu_custom_call" | custom-call | tf_op jit(solution)/shard_map/early_backward/pallas_call | solution.py:230
  55.8 0.0 collective-permute-done.8.late_ref
  55.8 0.8 %fill.1 = bf16[3,12,128,128]{3,2,1,0:T(8,128)(2,1)} custom-call(bf16[3,6,128,128]{3,2,1,0:T(8,128)(2,1)S(1)} %collective-permute-done.8.late_ref, bf16[3,12,128,128]{3,2,1,0:T(8,128)(2,1)} %early_backward.1.whole_ref), custom_call_target="tpu_custom_call", output_to_operand_aliasing={{}: (1, {})} | custom-call | tf_op jit(solution)/shard_map/fill/pallas_call | solution.py:258
  56.6 0.0 collective-permute-done.7.refs_5_
  56.7 3.2 %weight_gradient.3 = bf16[3072,1536]{1,0:T(8,128)(2,1)} custom-call(bf16[128,1536]{1,0:T(8,128)(2,1)S(1)} %get-tuple-element.12.refs_0_, bf16[128,1536]{1,0:T(8,128)(2,1)S(1)} %collective-permute-done.refs_1_, bf16[128,1536]{1,0:T(8,128)(2,1)S(1)} %collective-permute-done.1.refs_2_, ...), custom_call_target="tpu_custom_call", output_to_operand_aliasing={{}: (6, {})} | custom-call | tf_op jit(solution)/shard_map/weight_gradient/pallas_call | solution.py:396
  (1 shorter events, 0.0 us)
Async XLA Ops:
  0.6 25.4 %collective-permute-start.1 = (bf16[128,1536]{1,0:T(8,128)(2,1)}, bf16[128,1536]{1,0:T(8,128)(2,1)S(1)}, u32[]{:S(2)}, u32[]{:S(2)}) collective-permute-start(bf16[128,1536]{1,0:T(8,128)(2,1)} %bitcast.15), channel_id=1, source_target_pairs={{0,2},{2,0},{4,6},{6,4},{1,3},{3,1},{5,7},{7,5},{8,10},{10,8},{12,... | collective-permute-start | bytes 1179656 | tf_op jit(solution)/shard_map/ppermute | solution.py:35
  2.5 8.3 %collective-permute-start.2 = (bf16[128,768]{1,0:T(8,128)(2,1)S(1)}, bf16[128,768]{1,0:T(8,128)(2,1)S(1)}, u32[]{:S(2)}, u32[]{:S(2)}) collective-permute-start(bf16[128,768]{1,0:T(8,128)(2,1)S(1)} %get-tuple-element.13), channel_id=1, source_target_pairs={{0,4},{2,6},{4,0},{6,2},{1,5},{3,7},{5,1},{7,3},{8,12},{10,14},{12... | collective-permute-start | bytes 589832 | tf_op jit(solution)/shard_map/ppermute | solution.py:30
  5.1 9.8 %collective-permute-start.4 = (bf16[128,768]{1,0:T(8,128)(2,1)S(1)}, bf16[128,768]{1,0:T(8,128)(2,1)S(1)}, u32[]{:S(2)}, u32[]{:S(2)}) collective-permute-start(bf16[128,768]{1,0:T(8,128)(2,1)S(1)} %get-tuple-element.14), channel_id=1, source_target_pairs={{0,4},{2,6},{4,0},{6,2},{1,5},{3,7},{5,1},{7,3},{8,12},{10,14},{12... | collective-permute-start | bytes 589832 | tf_op jit(solution)/shard_map/ppermute | solution.py:30
  10.9 16.2 %collective-permute-start.3 = (bf16[128,768]{1,0:T(8,128)(2,1)S(1)}, bf16[128,768]{1,0:T(8,128)(2,1)S(1)}, u32[]{:S(2)}, u32[]{:S(2)}) collective-permute-start(bf16[128,768]{1,0:T(8,128)(2,1)S(1)} %collective-permute-done.2.refs_1_.refs_3_), channel_id=1, source_target_pairs={{0,2},{2,0},{4,6},{6,4},{1,3},{3,1},{5,7},{7,5},{8,10},{10,8},{12,... | collective-permute-start | bytes 589832 | tf_op jit(solution)/shard_map/ppermute | solution.py:35
  14.9 13.0 %collective-permute-start.5 = (bf16[128,768]{1,0:T(8,128)(2,1)S(1)}, bf16[128,768]{1,0:T(8,128)(2,1)S(1)}, u32[]{:S(2)}, u32[]{:S(2)}) collective-permute-start(bf16[128,768]{1,0:T(8,128)(2,1)S(1)} %collective-permute-done.4.refs_2_.refs_4_), channel_id=1, source_target_pairs={{0,2},{2,0},{4,6},{6,4},{1,3},{3,1},{5,7},{7,5},{8,10},{10,8},{12,... | collective-permute-start | bytes 589832 | tf_op jit(solution)/shard_map/ppermute | solution.py:35
  14.9 1.0 %copy-start.1 = (bf16[1,1,128,1536]{3,2,1,0:T(8,128)(2,1)S(1)}, bf16[1,1,128,1536]{3,2,1,0:T(8,128)(2,1)}, u32[]{:S(2)}) copy-start(bf16[1,1,128,1536]{3,2,1,0:T(8,128)(2,1)} %param.7) | copy-start | bytes 1179652
  15.9 16.8 %collective-permute-start.6 = (bf16[128,1536]{1,0:T(8,128)(2,1)S(1)}, bf16[128,1536]{1,0:T(8,128)(2,1)S(1)}, u32[]{:S(2)}, u32[]{:S(2)}) collective-permute-start(bf16[128,1536]{1,0:T(8,128)(2,1)S(1)} %choose.1), channel_id=1, source_target_pairs={{0,1},{1,0},{2,3},{3,2},{4,5},{5,4},{6,7},{7,6},{8,9},{9,8},{10,11... | collective-permute-start | bytes 1179656 | tf_op jit(solution)/shard_map/ppermute | solution.py:30
  17.7 35.5 %collective-permute-start.9 = (bf16[2320,128]{1,0:T(8,128)(2,1)S(1)}, bf16[2320,128]{1,0:T(8,128)(2,1)S(1)}, u32[]{:S(2)}, u32[]{:S(2)}) collective-permute-start(bf16[2320,128]{1,0:T(8,128)(2,1)S(1)} %get-tuple-element.20), channel_id=1, source_target_pairs={{8,0},{16,8},{24,16},{9,1},{17,9},{25,17},{10,2},{18,10},{26,18},{... | collective-permute-start | bytes 1781768 | tf_op jit(solution)/shard_map/ppermute | solution.py:40
  27.9 1.3 %copy-start = (bf16[1,1,3,128,12,128]{5,3,4,2,1,0:T(8,128)(2,1)S(1)}, bf16[1,1,3,128,12,128]{5,3,4,2,1,0:T(8,128)(2,1)}, u32[]{:S(2)}) copy-start(bf16[1,1,3,128,12,128]{5,3,4,2,1,0:T(8,128)(2,1)} %param.4) | copy-start | bytes 3538948
  27.9 1.3 %copy-start.3 = (s32[1,1,128]{2,1,0:T(1,128)S(1)}, s32[1,1,128]{2,1,0:T(1,128)}, u32[]{:S(2)}) copy-start(s32[1,1,128]{2,1,0:T(1,128)} %param.5) | copy-start | bytes 1540
  27.9 15.7 %copy-start.2 = (bf16[1,1,128,1536]{3,2,1,0:T(8,128)(2,1)S(1)}, bf16[1,1,128,1536]{3,2,1,0:T(8,128)(2,1)}, u32[]{:S(2)}) copy-start(bf16[1,1,128,1536]{3,2,1,0:T(8,128)(2,1)} %param.7) | copy-start | bytes 1179652
  31.0 24.8 %collective-permute-start.8 = (bf16[3,6,128,128]{3,2,1,0:T(8,128)(2,1)S(1)}, bf16[3,6,128,128]{3,2,1,0:T(8,128)(2,1)S(1)}, u32[]{:S(2)}, u32[]{:S(2)}) collective-permute-start(bf16[3,6,128,128]{3,2,1,0:T(8,128)(2,1)S(1)} %late_backward.1), channel_id=1, source_target_pairs={{8,0},{16,8},{24,16},{9,1},{17,9},{25,17},{10,2},{18,10},{26,18},{... | collective-permute-start | bytes 1769480 | tf_op jit(solution)/shard_map/ppermute | solution.py:40
  32.3 11.3 %collective-permute-start = (bf16[128,1536]{1,0:T(8,128)(2,1)S(1)}, bf16[128,1536]{1,0:T(8,128)(2,1)S(1)}, u32[]{:S(2)}, u32[]{:S(2)}) collective-permute-start(bf16[128,1536]{1,0:T(8,128)(2,1)S(1)} %get-tuple-element.12.refs_0_), channel_id=1, source_target_pairs={{0,1},{1,0},{2,3},{3,2},{4,5},{5,4},{6,7},{7,6},{8,9},{9,8},{10,11... | collective-permute-start | bytes 1179656 | tf_op jit(solution)/shard_map/ppermute | solution.py:30
  32.7 23.9 %collective-permute-start.7 = (bf16[128,1536]{1,0:T(8,128)(2,1)S(1)}, bf16[128,1536]{1,0:T(8,128)(2,1)S(1)}, u32[]{:S(2)}, u32[]{:S(2)}) collective-permute-start(bf16[128,1536]{1,0:T(8,128)(2,1)S(1)} %collective-permute-done.6.refs_5_), channel_id=1, source_target_pairs={{0,2},{2,0},{4,6},{6,4},{1,3},{3,1},{5,7},{7,5},{8,10},{10,8},{12,... | collective-permute-start | bytes 1179656 | tf_op jit(solution)/shard_map/ppermute | solution.py:35
  32.7 20.5 %collective-permute-start.10 = (bf16[128,768]{1,0:T(8,128)(2,1)S(1)}, bf16[128,768]{1,0:T(8,128)(2,1)S(1)}, u32[]{:S(2)}, u32[]{:S(2)}) collective-permute-start(bf16[128,768]{1,0:T(8,128)(2,1)S(1)} %get-tuple-element.21), channel_id=1, source_target_pairs={{8,0},{16,8},{24,16},{9,1},{17,9},{25,17},{10,2},{18,10},{26,18},{... | collective-permute-start | bytes 589832 | tf_op jit(solution)/shard_map/ppermute | solution.py:40

commit v6 on v5

--- a/solution.py
+++ b/solution.py
@@ -119,7 +119,7 @@
         )
     fetches = [
         pltpu.make_async_copy(
-            rows_of(weight_ref, rows.shape[0], chips, number // 2, number % 2),
+            rows_of(weight_ref, rows.shape[0], chips, max(0, number - 1), number == 1),
             target,
             sems.at[number],
         )
@@ -146,7 +146,7 @@
 def forward(chips, pos, qkv, weight, own):
     _, heads, seq, width = qkv.shape
     depth, columns = own.shape[1], weight.shape[1]
-    count = 2 * chips - 1
+    count = chips
     groups = max(size for size in (1, 2, 3) if heads % size == 0)
     return pl.pallas_call(
         functools.partial(forward_kernel, chips, groups),
@@ -267,6 +267,36 @@
     )(late, whole)
 
 
+def mate_kernel(chips, weight_ref, rows_ref, mate_ref, carried_ref, total_ref, *refs):
+    kept, sems = refs[:-1], refs[-1]
+    depth = mate_ref.shape[1]
+    gets = [
+        pltpu.make_async_copy(rows_of(weight_ref, depth, chips, step, True), ref, sems.at[step])
+        for step, ref in enumerate(kept, 1)
+    ]
+    for get in gets:
+        get.start()
+    total_ref[...] = carried_ref[...] + jnp.dot(
+        mate_ref[...], rows_ref[...], preferred_element_type=F32
+    )
+    for get in gets:
+        get.wait()
+
+
+def project_mate(chips, weight, rows, mate, total):
+    depth, columns = rows.shape
+    return pl.pallas_call(
+        functools.partial(mate_kernel, chips),
+        name="project_mate",
+        in_specs=[ANY, VMEM, VMEM, VMEM],
+        out_specs=[VMEM] * chips,
+        out_shape=[jax.ShapeDtypeStruct(total.shape, F32)]
+        + [pltpu.VMEM((depth, columns), BF16)] * (chips - 1),
+        scratch_shapes=[pltpu.SemaphoreType.DMA((chips,))],
+        compiler_params=PARAMS,
+    )(weight, rows, mate, total)
+
+
 def project_kernel(terms, splits, *refs):
     count = 1 + max(number for number, _ in terms)
     weights, grads = refs[:count], refs[count : count + len(terms)]
@@ -309,42 +339,36 @@
     return [[refs.pop(0) for _ in range(size)] for size in sizes]
 
 
-def choose_kernel(sizes, per_replica, number, step, replicas, *refs):
-    chips = len(sizes)
+def choose_kernel(per_replica, number, step, replicas, *refs):
+    chips = len(refs) - 1
     chip, _ = place()
     target = lax.rem(lax.axis_index("dp") + step, replicas)
     index = lax.rem(chip - (target * per_replica + number) + chips, chips)
-    out_ref = refs[-1]
-    for option, pieces in enumerate(grouped(refs[:-1], sizes)):
+    for option, ref in enumerate(refs[:-1]):
 
         @pl.when(index == option)
         def _():
-            at = 0
-            for piece in pieces:
-                out_ref[:, at : at + piece.shape[1]] = piece[...]
-                at += piece.shape[1]
+            refs[-1][...] = ref[...]
 
 
 def choose(replicas, number, step, options):
     chips = len(options)
-    args = [piece for pieces in options for piece in pieces]
-    return pl.pallas_call(
-        functools.partial(
-            choose_kernel, counts(options), chips // replicas, number, step, replicas
-        ),
+    return pl.pallas_call(
+        functools.partial(choose_kernel, chips // replicas, number, step, replicas),
         name="choose",
-        in_specs=[VMEM] * len(args),
+        in_specs=[VMEM] * chips,
         out_specs=VMEM,
-        out_shape=jax.ShapeDtypeStruct(options[0][0].shape, options[0][0].dtype),
-        compiler_params=PARAMS,
-    )(*args)
-
-
-def weight_kernel(replicas, sizes, slots, blocks, *refs):
+        out_shape=jax.ShapeDtypeStruct(options[0].shape, options[0].dtype),
+        compiler_params=PARAMS,
+    )(*options)
+
+
+def weight_kernel(replicas, sizes, slots, split, blocks, *refs):
     acts = refs[:replicas]
     args = sum(sizes)
     options = grouped(refs[replicas : replicas + args], sizes)
-    far = refs[replicas + args : replicas + args + slots * (replicas - 1)]
+    count = slots * (replicas - 1)
+    far = grouped(refs[replicas + args :], [2 if split else 1] * count)
     out_ref, stacked = refs[-2:]
     step = pl.program_id(0)
     chips = len(sizes)
@@ -358,26 +382,34 @@
 
     chip, _ = place()
     for slot in range(slots):
-        ours = far[slot * (replicas - 1) : (slot + 1) * (replicas - 1)]
         index = lax.rem(chip - (lax.axis_index("dp") * slots + slot) + chips, chips)
         for block in range(blocks):
+
+            def part(pieces):
+                piece, at = divmod(block * size, pieces[0].shape[1])
+                return pieces[piece][:, at : at + size]
 
             @pl.when(step == slot * blocks + block)
             def _():
                 near = None
                 for number, pieces in enumerate(options):
-                    piece, at = divmod(block * size, pieces[0].shape[1])
-                    part = pieces[piece][:, at : at + size]
-                    near = part if near is None else jnp.where(index == number, part, near)
-                columns = slice(block * size, (block + 1) * size)
-                left = jnp.concatenate([near] + [ref[:, columns] for ref in ours], axis=0)
-                out_ref[...] = dot(left, stacked[...], ((0,), (0,))).astype(BF16)
+                    own = part(pieces)
+                    near = own if near is None else jnp.where(index == number, own, near)
+                left = [near]
+                for pieces in far[slot * (replicas - 1) : (slot + 1) * (replicas - 1)]:
+                    if split:
+                        left.append(jnp.where(index == 1, part(pieces), part(pieces[::-1])))
+                    else:
+                        left.append(part(pieces))
+                rows = jnp.concatenate(left, axis=0)
+                out_ref[...] = dot(rows, stacked[...], ((0,), (0,))).astype(BF16)
 
 
 def weight_gradient(parity, acts, options, far, begun):
     replicas, slots = len(acts), len(far)
+    split = len(far[0][0]) == 2
     seq, columns = acts[0].shape
-    features = far[0][0].shape[1]
+    features = sum(piece.shape[1] for piece in far[0][0])
     blocks = max(counts(options))
     size = features // blocks
 
@@ -386,7 +418,7 @@
         return (2 * lax.div(step, blocks) + core) * blocks + lax.rem(step, blocks), 0
 
     args = [*acts, *[piece for pieces in options for piece in pieces]]
-    args += [ref for slot in far for ref in slot]
+    args += [piece for slot in far for pieces in slot for piece in pieces]
     specs = [VMEM] * len(args)
     aliases = {}
     if begun is not None:
@@ -394,7 +426,7 @@
         args.append(begun)
         specs.append(ANY)
     return pl.pallas_call(
-        functools.partial(weight_kernel, replicas, counts(options), slots, blocks),
+        functools.partial(weight_kernel, replicas, counts(options), slots, split, blocks),
         name="weight_gradient",
         grid=(slots * blocks,),
         in_specs=specs,
@@ -415,7 +447,7 @@
     pos = positions[0]
     weight = in_hbm(w_out[0])
     heads, _, width = qkv.shape[1:]
-    early = max(1, heads // 2)
+    early = max(1, heads * 7 // 12)
     late = heads - early
     shards = lax.axis_size("st")
     replicas = lax.axis_size("dp")
@@ -446,29 +478,34 @@
     whole = (heads * width,)
     halves = (early * width, late * width)
     depth = own.shape[1] // pieces
+    total, *crossed_rows = project_mate(chips, weight, far_rows[0], other[0][0], total)
     direct, crossed = [], []
     for step in range(1, chips):
         for piece in range(pieces):
             start = piece * depth
-            direct.append((far_rows[2 * step - 1], start, same[step][piece]))
-            crossed.append((far_rows[2 * step], start, other[step][piece]))
-    calls = [[(far_rows[0], 0, other[0][0]), direct[0]]]
-    calls += [[direct[i], crossed[i - 1]] for i in range(1, len(direct))]
-    for items in calls:
-        (total,) = project(items, total, whole, F32)
+            direct.append((far_rows[step], start, same[step][piece]))
+            crossed.append((crossed_rows[step - 1], start, other[step][piece]))
+    (total,) = project(direct + crossed[:-1], total, whole, F32)
     total = project([crossed[-1]], total, halves, BF16)
     d_early, d_late = total
     d_above = down(d_early, "section")
     grads_late = late_backward(pos, qkv, d_late)
     late_above = down(grads_late, "section")
 
+    split = chips == pieces == 2
     near_far, cross_far = [], []
     for number in range(per_replica):
         straight, swapped = [], []
         for step in range(1, replicas):
-            chosen = choose(replicas, number, step, same)
-            straight.append(rotate(chosen, "dp", step))
-            swapped.append(swap(straight[-1], "st"))
+            options = [parts[1], same[1][0]] if split else [value for (value,) in same]
+            chosen = choose(replicas, number, step, options)
+            got = [rotate(chosen, "dp", step)]
+            mates = [swap(got[0], "st")]
+            if split:
+                got.append(rotate(got[0], "st", 2))
+                mates.append(swap(got[1], "st"))
+            straight.append(got)
+            swapped.append(mates)
         near_far.append(straight)
         cross_far.append(swapped)
 

time: 60.2 us -> 56.9 us (0.945)
  waiting for transfers between devices: 25.7 us -> 20.7 us
  starting transfers between devices: 9.24 us -> 11.1 us
  local copies, waits for them, and re-layouts: 1.75 us -> 0.75 us
  Pallas kernels: 22.4 us -> 23.3 us
    pallas_call x1 -> x2, Pallas kernels: 0.03 us -> 3.03 us  [the longest x1 3.02 us: project_mate(): pl.pallas_call(functools.partial(mate_kernel, chips), name='project_mate'...]
    ppermute x3, waiting for transfers between devices: 6.39 us -> 3.68 us  [down(): return lax.ppermute(value, axis, [(i, i - 1) for i in range(1, count)])]
    ppermute x4 -> x5, waiting for transfers between devices: 19.3 us -> 17 us  [rotate(): lax.ppermute(value, axis, [(i, (i + steps) % count) for i in range(count)])]
    ppermute x4 -> x5, starting transfers between devices: 4.82 us -> 6.57 us  [rotate(): lax.ppermute(value, axis, [(i, (i + steps) % count) for i in range(count)])]
    pallas_call x1, Pallas kernels: 6.99 us -> 5.62 us  [forward(): pl.pallas_call(functools.partial(forward_kernel, chips, groups), name='fo...]
    unnamed x8 -> x6, local copies, waits for them, and re-layouts: 1.75 us -> 0.75 us
    pallas_call x3 -> x2, Pallas kernels: 2.36 us -> 1.58 us  [project(): pl.pallas_call(functools.partial(project_kernel, tuple(terms), splits), n...]
  transfers between devices with their start and end apart: 11 -> 13, of which waited for: 4 -> 5; matrix products, arithmetic and copies ran while one was open for 0% -> 0% of each run, Pallas kernels for 32% -> 40%
where the time goes in v6:
time: 56.9 us; the launch traced here: 56.6 us
  Pallas kernels  23.3 us (41%)
  waiting for transfers between devices  20.7 us (36%)
  starting transfers between devices  11.1 us (20%)
  between operations  0.8 us (1%)
  local copies, waits for them, and re-layouts  0.75 us (1%)
    ppermute x5, waiting for transfers between devices, rotate(): lax.ppermute(value, axis, [(i, (i + steps) % count) for i in range(count)])  17 us
    ppermute x5, starting transfers between devices, rotate(): lax.ppermute(value, axis, [(i, (i + steps) % count) for i in range(count)])  6.57 us
    pallas_call x2, Pallas kernels, weight_gradient(): pl.pallas_call(functools.partial(weight_kernel, replicas, counts(options)...  6.47 us
    pallas_call x1, Pallas kernels, forward(): pl.pallas_call(functools.partial(forward_kernel, chips, groups), name='fo...  5.62 us
    ppermute x3, starting transfers between devices, down(): return lax.ppermute(value, axis, [(i, i - 1) for i in range(1, count)])  3.85 us
    ppermute x3, waiting for transfers between devices, down(): return lax.ppermute(value, axis, [(i, i - 1) for i in range(1, count)])  3.68 us
    pallas_call x1, Pallas kernels, project_mate(): pl.pallas_call(functools.partial(mate_kernel, chips), name='project_mate'...  3.02 us
    pallas_call x1, Pallas kernels, early_backward(): pl.pallas_call(early_kernel, name='early_backward', in_specs=[VMEM] * 2,...  2.82 us
  transfers between devices with their start and end apart: 13, of which 5 were waited for; matrix products, arithmetic and copies ran while one was open for 0% of the time, Pallas kernels for 40%

profile of v6, /device:TPU:0, one launch (start us, length us, event | category | flops | bytes accessed | tf_op | source)
XLA Modules:
  0.0 56.6 jit_solution(3345943465503569290)
XLA Ops:
  0.6 0.6 collective-permute-start.1
  1.2 1.4 %pack.1 = (bf16[2704,128]{1,0:T(8,128)(2,1)S(1)}, bf16[128,768]{1,0:T(8,128)(2,1)S(1)}, bf16[128,768]{1,0:T(8,128)(2,1)S(1)}) custom-call(s32[1,128]{1,0:T(1,128)} %bitcast.19, bf16[3,1536,128]{2,1,0:T(8,128)(2,1)} %bitcast.12, bf16[128,1536]{1,0:T(8,128)(2,1)} %bitcast.16), custom_call_target="tpu_custom_call" | custom-call | tf_op jit(solution)/shard_map/pack/pallas_call | solution.py:85
  2.6 2.6 %collective-permute-start.2 = (bf16[128,768]{1,0:T(8,128)(2,1)S(1)}, bf16[128,768]{1,0:T(8,128)(2,1)S(1)}, u32[]{:S(2)}, u32[]{:S(2)}) collective-permute-start(bf16[128,768]{1,0:T(8,128)(2,1)S(1)} %get-tuple-element.14), channel_id=1, source_target_pairs={{0,4},{2,6},{4,0},{6,2},{1,5},{3,7},{5,1},{7,3},{8,12},{10,14},{12... | collective-permute-start | bytes 589832 | tf_op jit(solution)/shard_map/ppermute | solution.py:30
  5.2 0.1 collective-permute-start.4
  5.3 1.3 %collective-permute-start.11 = (bf16[2704,128]{1,0:T(8,128)(2,1)S(1)}, bf16[2704,128]{1,0:T(8,128)(2,1)S(1)}, u32[]{:S(2)}, u32[]{:S(2)}) collective-permute-start(bf16[2704,128]{1,0:T(8,128)(2,1)S(1)} %get-tuple-element.22), channel_id=1, source_target_pairs={{8,0},{16,8},{24,16},{9,1},{17,9},{25,17},{10,2},{18,10},{26,18},{... | collective-permute-start | bytes 2076680 | tf_op jit(solution)/shard_map/ppermute | solution.py:40
  6.5 4.4 %collective-permute-done.2.refs_1_.refs_3_.refs_2_ = bf16[128,768]{1,0:T(8,128)(2,1)S(1)} collective-permute-done((bf16[128,768]{1,0:T(8,128)(2,1)S(1)}, bf16[128,768]{1,0:T(8,128)(2,1)S(1)}, u32[]{:S(2)}, u32[]{:S(2)}) %collective-permute-start.2) | collective-permute-done | bytes 196640 | tf_op jit(solution)/shard_map/ppermute | solution.py:30
  10.9 0.0 collective-permute-start.3
  10.9 4.0 %collective-permute-done.4.refs_4_.refs_3_ = bf16[128,768]{1,0:T(8,128)(2,1)S(1)} collective-permute-done((bf16[128,768]{1,0:T(8,128)(2,1)S(1)}, bf16[128,768]{1,0:T(8,128)(2,1)S(1)}, u32[]{:S(2)}, u32[]{:S(2)}) %collective-permute-start.4) | collective-permute-done | bytes 196640 | tf_op jit(solution)/shard_map/ppermute | solution.py:30
  14.9 0.0 collective-permute-start.5
  14.9 5.6 %forward.1 = (bf16[128,1536]{1,0:T(8,128)(2,1)S(1)}, f32[128,1536]{1,0:T(8,128)S(1)}, bf16[1536,1536]{1,0:T(8,128)(2,1)S(1)}, bf16[1536,1536]{1,0:T(8,128)(2,1)S(1)}) custom-call(s32[1,128]{1,0:T(1,128)} %bitcast.20, bf16[3,12,128,128]{3,2,1,0:T(8,128)(2,1)} %bitcast.13, bf16[6144,1536]{1,0:T(8,128)(2,1)} %bitcast.22, bf16[128,1536]{1,0:T(8,128)(2,1)} %bitcast.17), custom_call_target="tpu_custom_call" | custom-call | tf_op jit(solution)/shard_map/forward/pallas_call | solution.py:151
  20.6 1.8 %collective-permute-start = (bf16[128,1536]{1,0:T(8,128)(2,1)S(1)}, bf16[128,1536]{1,0:T(8,128)(2,1)S(1)}, u32[]{:S(2)}, u32[]{:S(2)}) collective-permute-start(bf16[128,1536]{1,0:T(8,128)(2,1)S(1)} %get-tuple-element.13.refs_0_), channel_id=1, source_target_pairs={{0,1},{1,0},{2,3},{3,2},{4,5},{5,4},{6,7},{7,6},{8,9},{9,8},{10,11... | collective-permute-start | bytes 1179656 | tf_op jit(solution)/shard_map/ppermute | solution.py:30
  22.4 0.0 collective-permute-done.1.refs_2_.mate_ref
  22.4 0.4 collective-permute-start.6
  22.8 3.0 %project_mate.1 = (f32[128,1536]{1,0:T(8,128)S(1)}, bf16[1536,1536]{1,0:T(8,128)(2,1)S(1)}) custom-call(bf16[6144,1536]{1,0:T(8,128)(2,1)} %bitcast.23, bf16[1536,1536]{1,0:T(8,128)(2,1)S(1)} %get-tuple-element.16.rows_ref, bf16[128,1536]{1,0:T(8,128)(2,1)S(1)} %collective-permute-done.1.refs_2_.mate_ref, f32[128,1536]{1,0:T(8,128)S(1)} %get-tuple-element.17.carried_ref), custom_call_target="tpu_custom_call" | custom-call | tf_op jit(solution)/shard_map/project_mate/pallas_call | solution.py:288
  25.8 0.0 collective-permute-done.3.refs_3_.refs_4_
  25.8 1.1 %project.2.refs_2_ = f32[128,1536]{1,0:T(8,128)S(1)} custom-call(bf16[1536,1536]{1,0:T(8,128)(2,1)S(1)} %get-tuple-element.19.refs_0_, bf16[1536,1536]{1,0:T(8,128)(2,1)S(1)} %get-tuple-element.18.refs_1_.refs_0_, bf16[128,768]{1,0:T(8,128)(2,1)S(1)} %collective-permute-done.2.refs_1_.refs_3_.refs_2_, ...), custom_call_target="tpu_custom_call" | custom-call | tf_op jit(solution)/shard_map/project/pallas_call | solution.py:323
  26.9 0.0 copy-start
  26.9 0.0 copy-start.2
  26.9 0.0 copy-start.1
  26.9 0.0 collective-permute-done.5.refs_4_.refs_1_
  26.9 0.5 project.3
  27.4 0.7 %copy-done = bf16[1,1,3,128,12,128]{5,3,4,2,1,0:T(8,128)(2,1)S(1)} copy-done((bf16[1,1,3,128,12,128]{5,3,4,2,1,0:T(8,128)(2,1)S(1)}, bf16[1,1,3,128,12,128]{5,3,4,2,1,0:T(8,128)(2,1)}, u32[]{:S(2)}) %copy-start) | copy-done | bytes 1179672
  28.2 0.0 copy-done.2
  28.2 1.6 %late_backward.1 = bf16[3,5,128,128]{3,2,1,0:T(8,128)(2,1)S(1)} custom-call(s32[1,128]{1,0:T(1,128)S(1)} %bitcast.21, bf16[3,12,128,128]{3,2,1,0:T(8,128)(2,1)S(1)} %bitcast.14, bf16[128,640]{1,0:T(8,128)(2,1)S(1)} %get-tuple-element.21.grad_ref), custom_call_target="tpu_custom_call" | custom-call | tf_op jit(solution)/shard_map/late_backward/pallas_call | solution.py:199
  29.8 1.3 %collective-permute-start.10 = (bf16[3,5,128,128]{3,2,1,0:T(8,128)(2,1)S(1)}, bf16[3,5,128,128]{3,2,1,0:T(8,128)(2,1)S(1)}, u32[]{:S(2)}, u32[]{:S(2)}) collective-permute-start(bf16[3,5,128,128]{3,2,1,0:T(8,128)(2,1)S(1)} %late_backward.1), channel_id=1, source_target_pairs={{8,0},{16,8},{24,16},{9,1},{17,9},{25,17},{10,2},{18,10},{26,18},{... | collective-permute-start | bytes 1474568 | tf_op jit(solution)/shard_map/ppermute | solution.py:40
  31.1 5.3 %collective-permute-done.6.refs_5_ = bf16[128,768]{1,0:T(8,128)(2,1)S(1)} collective-permute-done((bf16[128,768]{1,0:T(8,128)(2,1)S(1)}, bf16[128,768]{1,0:T(8,128)(2,1)S(1)}, u32[]{:S(2)}, u32[]{:S(2)}) %collective-permute-start.6) | collective-permute-done | bytes 196640 | tf_op jit(solution)/shard_map/ppermute | solution.py:30
  36.4 1.7 %collective-permute-start.8 = (bf16[128,768]{1,0:T(8,128)(2,1)S(1)}, bf16[128,768]{1,0:T(8,128)(2,1)S(1)}, u32[]{:S(2)}, u32[]{:S(2)}) collective-permute-start(bf16[128,768]{1,0:T(8,128)(2,1)S(1)} %collective-permute-done.6.refs_5_), channel_id=1, source_target_pairs={{0,4},{2,6},{4,0},{6,2},{1,5},{3,7},{5,1},{7,3},{8,12},{10,14},{12... | collective-permute-start | bytes 589832 | tf_op jit(solution)/shard_map/ppermute | solution.py:30
  38.1 1.3 %collective-permute-start.12 = (bf16[128,896]{1,0:T(8,128)(2,1)S(1)}, bf16[128,896]{1,0:T(8,128)(2,1)S(1)}, u32[]{:S(2)}, u32[]{:S(2)}) collective-permute-start(bf16[128,896]{1,0:T(8,128)(2,1)S(1)} %get-tuple-element.23), channel_id=1, source_target_pairs={{8,0},{16,8},{24,16},{9,1},{17,9},{25,17},{10,2},{18,10},{26,18},{... | collective-permute-start | bytes 688136 | tf_op jit(solution)/shard_map/ppermute | solution.py:40
  39.4 0.0 collective-permute-done.refs_1_
  39.4 0.1 collective-permute-start.7
  39.5 3.3 %collective-permute-done.8.refs_6_ = bf16[128,768]{1,0:T(8,128)(2,1)S(1)} collective-permute-done((bf16[128,768]{1,0:T(8,128)(2,1)S(1)}, bf16[128,768]{1,0:T(8,128)(2,1)S(1)}, u32[]{:S(2)}, u32[]{:S(2)}) %collective-permute-start.8) | collective-permute-done | bytes 196640 | tf_op jit(solution)/shard_map/ppermute | solution.py:30
  42.8 0.0 collective-permute-start.9
  42.8 0.0 copy-done.1
  42.8 3.2 %weight_gradient.2.refs_7_ = bf16[3072,1536]{1,0:T(8,128)(2,1)} custom-call(bf16[128,1536]{1,0:T(8,128)(2,1)S(1)} %get-tuple-element.13.refs_0_, bf16[128,1536]{1,0:T(8,128)(2,1)S(1)} %collective-permute-done.refs_1_, bf16[128,1536]{1,0:T(8,128)(2,1)S(1)} %bitcast.18, bf16[128,768]{1,0:T(8,128)(2,1)S(1)} %collective-permute-done.2.refs_1_.refs_3_.refs_2_, ...), custom_call_target="tpu_custom_call" | custom-call | tf_op jit(solution)/shard_map/weight_gradient/pallas_call | solution.py:428
  46.0 3.7 %collective-permute-done.12.grad_ref = bf16[128,896]{1,0:T(8,128)(2,1)S(1)} collective-permute-done((bf16[128,896]{1,0:T(8,128)(2,1)S(1)}, bf16[128,896]{1,0:T(8,128)(2,1)S(1)}, u32[]{:S(2)}, u32[]{:S(2)}) %collective-permute-start.12) | collective-permute-done | bytes 229408 | tf_op jit(solution)/shard_map/ppermute | solution.py:40
  49.7 0.0 collective-permute-done.11.packed_ref
  49.7 2.8 %early_backward.1.whole_ref = bf16[3,12,128,128]{3,2,1,0:T(8,128)(2,1)} custom-call(bf16[2704,128]{1,0:T(8,128)(2,1)S(1)} %collective-permute-done.11.packed_ref, bf16[128,896]{1,0:T(8,128)(2,1)S(1)} %collective-permute-done.12.grad_ref), custom_call_target="tpu_custom_call" | custom-call | tf_op jit(solution)/shard_map/early_backward/pallas_call | solution.py:230
  52.6 0.0 collective-permute-done.7.refs_5_
  52.6 0.0 collective-permute-done.9.refs_6_
  52.6 3.3 %weight_gradient.3 = bf16[3072,1536]{1,0:T(8,128)(2,1)} custom-call(bf16[128,1536]{1,0:T(8,128)(2,1)S(1)} %get-tuple-element.13.refs_0_, bf16[128,1536]{1,0:T(8,128)(2,1)S(1)} %collective-permute-done.refs_1_, bf16[128,1536]{1,0:T(8,128)(2,1)S(1)} %collective-permute-done.1.refs_2_.mate_ref, ...), custom_call_target="tpu_custom_call", output_to_operand_aliasing={{}: (7, {})} | custom-call | tf_op jit(solution)/shard_map/weight_gradient/pallas_call | solution.py:428
  55.8 0.0 collective-permute-done.10.late_ref
  55.8 0.8 %fill.1 = bf16[3,12,128,128]{3,2,1,0:T(8,128)(2,1)} custom-call(bf16[3,5,128,128]{3,2,1,0:T(8,128)(2,1)S(1)} %collective-permute-done.10.late_ref, bf16[3,12,128,128]{3,2,1,0:T(8,128)(2,1)} %early_backward.1.whole_ref), custom_call_target="tpu_custom_call", output_to_operand_aliasing={{}: (1, {})} | custom-call | tf_op jit(solution)/shard_map/fill/pallas_call | solution.py:258
  (1 shorter events, 0.0 us)
Async XLA Ops:
  0.6 21.7 %collective-permute-start.1 = (bf16[128,1536]{1,0:T(8,128)(2,1)}, bf16[128,1536]{1,0:T(8,128)(2,1)S(1)}, u32[]{:S(2)}, u32[]{:S(2)}) collective-permute-start(bf16[128,1536]{1,0:T(8,128)(2,1)} %bitcast.15), channel_id=1, source_target_pairs={{0,2},{2,0},{4,6},{6,4},{1,3},{3,1},{5,7},{7,5},{8,10},{10,8},{12,... | collective-permute-start | bytes 1179656 | tf_op jit(solution)/shard_map/ppermute | solution.py:35
  2.6 8.3 %collective-permute-start.2 = (bf16[128,768]{1,0:T(8,128)(2,1)S(1)}, bf16[128,768]{1,0:T(8,128)(2,1)S(1)}, u32[]{:S(2)}, u32[]{:S(2)}) collective-permute-start(bf16[128,768]{1,0:T(8,128)(2,1)S(1)} %get-tuple-element.14), channel_id=1, source_target_pairs={{0,4},{2,6},{4,0},{6,2},{1,5},{3,7},{5,1},{7,3},{8,12},{10,14},{12... | collective-permute-start | bytes 589832 | tf_op jit(solution)/shard_map/ppermute | solution.py:30
  5.2 9.8 %collective-permute-start.4 = (bf16[128,768]{1,0:T(8,128)(2,1)S(1)}, bf16[128,768]{1,0:T(8,128)(2,1)S(1)}, u32[]{:S(2)}, u32[]{:S(2)}) collective-permute-start(bf16[128,768]{1,0:T(8,128)(2,1)S(1)} %get-tuple-element.15.refs_0_), channel_id=1, source_target_pairs={{0,4},{2,6},{4,0},{6,2},{1,5},{3,7},{5,1},{7,3},{8,12},{10,14},{12... | collective-permute-start | bytes 589832 | tf_op jit(solution)/shard_map/ppermute | solution.py:30
  5.3 44.5 %collective-permute-start.11 = (bf16[2704,128]{1,0:T(8,128)(2,1)S(1)}, bf16[2704,128]{1,0:T(8,128)(2,1)S(1)}, u32[]{:S(2)}, u32[]{:S(2)}) collective-permute-start(bf16[2704,128]{1,0:T(8,128)(2,1)S(1)} %get-tuple-element.22), channel_id=1, source_target_pairs={{8,0},{16,8},{24,16},{9,1},{17,9},{25,17},{10,2},{18,10},{26,18},{... | collective-permute-start | bytes 2076680 | tf_op jit(solution)/shard_map/ppermute | solution.py:40
  10.9 14.9 %collective-permute-start.3 = (bf16[128,768]{1,0:T(8,128)(2,1)S(1)}, bf16[128,768]{1,0:T(8,128)(2,1)S(1)}, u32[]{:S(2)}, u32[]{:S(2)}) collective-permute-start(bf16[128,768]{1,0:T(8,128)(2,1)S(1)} %collective-permute-done.2.refs_1_.refs_3_.refs_2_), channel_id=1, source_target_pairs={{0,2},{2,0},{4,6},{6,4},{1,3},{3,1},{5,7},{7,5},{8,10},{10,8},{12,... | collective-permute-start | bytes 589832 | tf_op jit(solution)/shard_map/ppermute | solution.py:35
  14.9 12.0 %collective-permute-start.5 = (bf16[128,768]{1,0:T(8,128)(2,1)S(1)}, bf16[128,768]{1,0:T(8,128)(2,1)S(1)}, u32[]{:S(2)}, u32[]{:S(2)}) collective-permute-start(bf16[128,768]{1,0:T(8,128)(2,1)S(1)} %collective-permute-done.4.refs_4_.refs_3_), channel_id=1, source_target_pairs={{0,2},{2,0},{4,6},{6,4},{1,3},{3,1},{5,7},{7,5},{8,10},{10,8},{12,... | collective-permute-start | bytes 589832 | tf_op jit(solution)/shard_map/ppermute | solution.py:35
  20.6 18.8 %collective-permute-start = (bf16[128,1536]{1,0:T(8,128)(2,1)S(1)}, bf16[128,1536]{1,0:T(8,128)(2,1)S(1)}, u32[]{:S(2)}, u32[]{:S(2)}) collective-permute-start(bf16[128,1536]{1,0:T(8,128)(2,1)S(1)} %get-tuple-element.13.refs_0_), channel_id=1, source_target_pairs={{0,1},{1,0},{2,3},{3,2},{4,5},{5,4},{6,7},{7,6},{8,9},{9,8},{10,11... | collective-permute-start | bytes 1179656 | tf_op jit(solution)/shard_map/ppermute | solution.py:30
  22.4 14.0 %collective-permute-start.6 = (bf16[128,768]{1,0:T(8,128)(2,1)S(1)}, bf16[128,768]{1,0:T(8,128)(2,1)S(1)}, u32[]{:S(2)}, u32[]{:S(2)}) collective-permute-start(bf16[128,768]{1,0:T(8,128)(2,1)S(1)} %choose.1), channel_id=1, source_target_pairs={{0,1},{1,0},{2,3},{3,2},{4,5},{5,4},{6,7},{7,6},{8,9},{9,8},{10,11... | collective-permute-start | bytes 589832 | tf_op jit(solution)/shard_map/ppermute | solution.py:30
  26.9 1.3 %copy-start = (bf16[1,1,3,128,12,128]{5,3,4,2,1,0:T(8,128)(2,1)S(1)}, bf16[1,1,3,128,12,128]{5,3,4,2,1,0:T(8,128)(2,1)}, u32[]{:S(2)}) copy-start(bf16[1,1,3,128,12,128]{5,3,4,2,1,0:T(8,128)(2,1)} %param.4) | copy-start | bytes 3538948
  26.9 1.3 %copy-start.2 = (s32[1,1,128]{2,1,0:T(1,128)S(1)}, s32[1,1,128]{2,1,0:T(1,128)}, u32[]{:S(2)}) copy-start(s32[1,1,128]{2,1,0:T(1,128)} %param.5) | copy-start | bytes 1540
  26.9 15.9 %copy-start.1 = (bf16[1,1,128,1536]{3,2,1,0:T(8,128)(2,1)S(1)}, bf16[1,1,128,1536]{3,2,1,0:T(8,128)(2,1)}, u32[]{:S(2)}) copy-start(bf16[1,1,128,1536]{3,2,1,0:T(8,128)(2,1)} %param.7) | copy-start | bytes 1179652
  29.8 26.1 %collective-permute-start.10 = (bf16[3,5,128,128]{3,2,1,0:T(8,128)(2,1)S(1)}, bf16[3,5,128,128]{3,2,1,0:T(8,128)(2,1)S(1)}, u32[]{:S(2)}, u32[]{:S(2)}) collective-permute-start(bf16[3,5,128,128]{3,2,1,0:T(8,128)(2,1)S(1)} %late_backward.1), channel_id=1, source_target_pairs={{8,0},{16,8},{24,16},{9,1},{17,9},{25,17},{10,2},{18,10},{26,18},{... | collective-permute-start | bytes 1474568 | tf_op jit(solution)/shard_map/ppermute | solution.py:40
  36.4 6.5 %collective-permute-start.8 = (bf16[128,768]{1,0:T(8,128)(2,1)S(1)}, bf16[128,768]{1,0:T(8,128)(2,1)S(1)}, u32[]{:S(2)}, u32[]{:S(2)}) collective-permute-start(bf16[128,768]{1,0:T(8,128)(2,1)S(1)} %collective-permute-done.6.refs_5_), channel_id=1, source_target_pairs={{0,4},{2,6},{4,0},{6,2},{1,5},{3,7},{5,1},{7,3},{8,12},{10,14},{12... | collective-permute-start | bytes 589832 | tf_op jit(solution)/shard_map/ppermute | solution.py:30
  38.1 11.6 %collective-permute-start.12 = (bf16[128,896]{1,0:T(8,128)(2,1)S(1)}, bf16[128,896]{1,0:T(8,128)(2,1)S(1)}, u32[]{:S(2)}, u32[]{:S(2)}) collective-permute-start(bf16[128,896]{1,0:T(8,128)(2,1)S(1)} %get-tuple-element.23), channel_id=1, source_target_pairs={{8,0},{16,8},{24,16},{9,1},{17,9},{25,17},{10,2},{18,10},{26,18},{... | collective-permute-start | bytes 688136 | tf_op jit(solution)/shard_map/ppermute | solution.py:40
  39.4 13.1 %collective-permute-start.7 = (bf16[128,768]{1,0:T(8,128)(2,1)S(1)}, bf16[128,768]{1,0:T(8,128)(2,1)S(1)}, u32[]{:S(2)}, u32[]{:S(2)}) collective-permute-start(bf16[128,768]{1,0:T(8,128)(2,1)S(1)} %collective-permute-done.6.refs_5_), channel_id=1, source_target_pairs={{0,2},{2,0},{4,6},{6,4},{1,3},{3,1},{5,7},{7,5},{8,10},{10,8},{12,... | collective-permute-start | bytes 589832 | tf_op jit(solution)/shard_map/ppermute | solution.py:35
  42.8 9.7 %collective-permute-start.9 = (bf16[128,768]{1,0:T(8,128)(2,1)S(1)}, bf16[128,768]{1,0:T(8,128)(2,1)S(1)}, u32[]{:S(2)}, u32[]{:S(2)}) collective-permute-start(bf16[128,768]{1,0:T(8,128)(2,1)S(1)} %collective-permute-done.8.refs_6_), channel_id=1, source_target_pairs={{0,2},{2,0},{4,6},{6,4},{1,3},{3,1},{5,7},{7,5},{8,10},{10,8},{12,... | collective-permute-start | bytes 589832 | tf_op jit(solution)/shard_map/ppermute | solution.py:35

commit v7 on v6

--- a/solution.py
+++ b/solution.py
@@ -119,7 +119,7 @@
         )
     fetches = [
         pltpu.make_async_copy(
-            rows_of(weight_ref, rows.shape[0], chips, max(0, number - 1), number == 1),
+            rows_of(weight_ref, rows.shape[0], chips, number // 2, number % 2),
             target,
             sems.at[number],
         )
@@ -146,7 +146,7 @@
 def forward(chips, pos, qkv, weight, own):
     _, heads, seq, width = qkv.shape
     depth, columns = own.shape[1], weight.shape[1]
-    count = chips
+    count = 2 * chips - 1
     groups = max(size for size in (1, 2, 3) if heads % size == 0)
     return pl.pallas_call(
         functools.partial(forward_kernel, chips, groups),
@@ -267,36 +267,6 @@
     )(late, whole)
 
 
-def mate_kernel(chips, weight_ref, rows_ref, mate_ref, carried_ref, total_ref, *refs):
-    kept, sems = refs[:-1], refs[-1]
-    depth = mate_ref.shape[1]
-    gets = [
-        pltpu.make_async_copy(rows_of(weight_ref, depth, chips, step, True), ref, sems.at[step])
-        for step, ref in enumerate(kept, 1)
-    ]
-    for get in gets:
-        get.start()
-    total_ref[...] = carried_ref[...] + jnp.dot(
-        mate_ref[...], rows_ref[...], preferred_element_type=F32
-    )
-    for get in gets:
-        get.wait()
-
-
-def project_mate(chips, weight, rows, mate, total):
-    depth, columns = rows.shape
-    return pl.pallas_call(
-        functools.partial(mate_kernel, chips),
-        name="project_mate",
-        in_specs=[ANY, VMEM, VMEM, VMEM],
-        out_specs=[VMEM] * chips,
-        out_shape=[jax.ShapeDtypeStruct(total.shape, F32)]
-        + [pltpu.VMEM((depth, columns), BF16)] * (chips - 1),
-        scratch_shapes=[pltpu.SemaphoreType.DMA((chips,))],
-        compiler_params=PARAMS,
-    )(weight, rows, mate, total)
-
-
 def project_kernel(terms, splits, *refs):
     count = 1 + max(number for number, _ in terms)
     weights, grads = refs[:count], refs[count : count + len(terms)]
@@ -478,14 +448,14 @@
     whole = (heads * width,)
     halves = (early * width, late * width)
     depth = own.shape[1] // pieces
-    total, *crossed_rows = project_mate(chips, weight, far_rows[0], other[0][0], total)
     direct, crossed = [], []
     for step in range(1, chips):
         for piece in range(pieces):
             start = piece * depth
-            direct.append((far_rows[step], start, same[step][piece]))
-            crossed.append((crossed_rows[step - 1], start, other[step][piece]))
-    (total,) = project(direct + crossed[:-1], total, whole, F32)
+            direct.append((far_rows[2 * step - 1], start, same[step][piece]))
+            crossed.append((far_rows[2 * step], start, other[step][piece]))
+    mate = (far_rows[0], 0, other[0][0])
+    (total,) = project([mate] + direct + crossed[:-1], total, whole, F32)
     total = project([crossed[-1]], total, halves, BF16)
     d_early, d_late = total
     d_above = down(d_early, "section")

time: 56.9 us -> 55.8 us (0.981)
  Pallas kernels: 23.3 us -> 22.2 us
    pallas_call x1 -> x0, Pallas kernels: 3.02 us -> none  [project_mate(): pl.pallas_call(functools.partial(mate_kernel, chips), name='project_mate'...]
    ppermute x5, waiting for transfers between devices: 17 us -> 19.5 us  [rotate(): lax.ppermute(value, axis, [(i, (i + steps) % count) for i in range(count)])]
    ppermute x3, waiting for transfers between devices: 3.68 us -> 1.26 us  [down(): return lax.ppermute(value, axis, [(i, i - 1) for i in range(1, count)])]
    pallas_call x1, Pallas kernels: 5.62 us -> 6.98 us  [forward(): pl.pallas_call(functools.partial(forward_kernel, chips, groups), name='fo...]
    pallas_call x2, Pallas kernels: 1.58 us -> 2.17 us  [project(): pl.pallas_call(functools.partial(project_kernel, tuple(terms), splits), n...]
  transfers between devices with their start and end apart: 13 -> 13, of which waited for: 5 -> 5; matrix products, arithmetic and copies ran while one was open for 0% -> 0% of each run, Pallas kernels for 40% -> 39%
where the time goes in v7:
time: 55.8 us; the launch traced here: 55.6 us
  Pallas kernels  22.2 us (40%)
  waiting for transfers between devices  20.7 us (37%)
  starting transfers between devices  11.1 us (20%)
  between operations  0.78 us (1%)
  local copies, waits for them, and re-layouts  0.76 us (1%)
    ppermute x5, waiting for transfers between devices, rotate(): lax.ppermute(value, axis, [(i, (i + steps) % count) for i in range(count)])  19.5 us
    pallas_call x1, Pallas kernels, forward(): pl.pallas_call(functools.partial(forward_kernel, chips, groups), name='fo...  6.98 us
    ppermute x5, starting transfers between devices, rotate(): lax.ppermute(value, axis, [(i, (i + steps) % count) for i in range(count)])  6.57 us
    pallas_call x2, Pallas kernels, weight_gradient(): pl.pallas_call(functools.partial(weight_kernel, replicas, counts(options)...  6.44 us
    ppermute x3, starting transfers between devices, down(): return lax.ppermute(value, axis, [(i, i - 1) for i in range(1, count)])  3.85 us
    pallas_call x1, Pallas kernels, early_backward(): pl.pallas_call(early_kernel, name='early_backward', in_specs=[VMEM] * 2,...  2.82 us
    pallas_call x2, Pallas kernels, project(): pl.pallas_call(functools.partial(project_kernel, tuple(terms), splits), n...  2.17 us
    pallas_call x1, Pallas kernels, late_backward(): pl.pallas_call(late_kernel, name='late_backward', in_specs=[VMEM] * 3, ou...  1.6 us
  transfers between devices with their start and end apart: 13, of which 5 were waited for; matrix products, arithmetic and copies ran while one was open for 0% of the time, Pallas kernels for 39%

profile of v7, /device:TPU:0, one launch (start us, length us, event | category | flops | bytes accessed | tf_op | source)
XLA Modules:
  0.0 55.6 jit_solution(15706813480142333290)
XLA Ops:
  0.6 0.6 %collective-permute-start.1 = (bf16[128,1536]{1,0:T(8,128)(2,1)}, bf16[128,1536]{1,0:T(8,128)(2,1)S(1)}, u32[]{:S(2)}, u32[]{:S(2)}) collective-permute-start(bf16[128,1536]{1,0:T(8,128)(2,1)} %bitcast.15), channel_id=1, source_target_pairs={{0,2},{2,0},{4,6},{6,4},{1,3},{3,1},{5,7},{7,5},{8,10},{10,8},{12,... | collective-permute-start | bytes 1179656 | tf_op jit(solution)/shard_map/ppermute | solution.py:35
  1.2 1.4 %pack.1 = (bf16[2704,128]{1,0:T(8,128)(2,1)S(1)}, bf16[128,768]{1,0:T(8,128)(2,1)S(1)}, bf16[128,768]{1,0:T(8,128)(2,1)S(1)}) custom-call(s32[1,128]{1,0:T(1,128)} %bitcast.19, bf16[3,1536,128]{2,1,0:T(8,128)(2,1)} %bitcast.12, bf16[128,1536]{1,0:T(8,128)(2,1)} %bitcast.16), custom_call_target="tpu_custom_call" | custom-call | tf_op jit(solution)/shard_map/pack/pallas_call | solution.py:85
  2.6 2.6 %collective-permute-start.2 = (bf16[128,768]{1,0:T(8,128)(2,1)S(1)}, bf16[128,768]{1,0:T(8,128)(2,1)S(1)}, u32[]{:S(2)}, u32[]{:S(2)}) collective-permute-start(bf16[128,768]{1,0:T(8,128)(2,1)S(1)} %get-tuple-element.13), channel_id=1, source_target_pairs={{0,4},{2,6},{4,0},{6,2},{1,5},{3,7},{5,1},{7,3},{8,12},{10,14},{12... | collective-permute-start | bytes 589832 | tf_op jit(solution)/shard_map/ppermute | solution.py:30
  5.2 0.1 collective-permute-start.4
  5.3 1.3 %collective-permute-start.11 = (bf16[2704,128]{1,0:T(8,128)(2,1)S(1)}, bf16[2704,128]{1,0:T(8,128)(2,1)S(1)}, u32[]{:S(2)}, u32[]{:S(2)}) collective-permute-start(bf16[2704,128]{1,0:T(8,128)(2,1)S(1)} %get-tuple-element.20), channel_id=1, source_target_pairs={{8,0},{16,8},{24,16},{9,1},{17,9},{25,17},{10,2},{18,10},{26,18},{... | collective-permute-start | bytes 2076680 | tf_op jit(solution)/shard_map/ppermute | solution.py:40
  6.5 4.4 %collective-permute-done.2.refs_1_.refs_3_.refs_4_ = bf16[128,768]{1,0:T(8,128)(2,1)S(1)} collective-permute-done((bf16[128,768]{1,0:T(8,128)(2,1)S(1)}, bf16[128,768]{1,0:T(8,128)(2,1)S(1)}, u32[]{:S(2)}, u32[]{:S(2)}) %collective-permute-start.2) | collective-permute-done | bytes 196640 | tf_op jit(solution)/shard_map/ppermute | solution.py:30
  10.9 0.0 collective-permute-start.3
  10.9 4.0 %collective-permute-done.4.refs_4_.refs_5_ = bf16[128,768]{1,0:T(8,128)(2,1)S(1)} collective-permute-done((bf16[128,768]{1,0:T(8,128)(2,1)S(1)}, bf16[128,768]{1,0:T(8,128)(2,1)S(1)}, u32[]{:S(2)}, u32[]{:S(2)}) %collective-permute-start.4) | collective-permute-done | bytes 196640 | tf_op jit(solution)/shard_map/ppermute | solution.py:30
  14.9 0.0 collective-permute-start.5
  14.9 7.0 %forward.1 = (bf16[128,1536]{1,0:T(8,128)(2,1)S(1)}, f32[128,1536]{1,0:T(8,128)S(1)}, bf16[1536,1536]{1,0:T(8,128)(2,1)S(1)}, bf16[1536,1536]{1,0:T(8,128)(2,1)S(1)}, bf16[1536,1536]{1,0:T(8,128)(2,1)S(1)}) custom-call(s32[1,128]{1,0:T(1,128)} %bitcast.20, bf16[3,12,128,128]{3,2,1,0:T(8,128)(2,1)} %bitcast.13, bf16[6144,1536]{1,0:T(8,128)(2,1)} %bitcast.23, ...), custom_call_target="tpu_custom_call" | custom-call | tf_op jit(solution)/shard_map/forward/pallas_call | solution.py:151
  21.9 1.8 %collective-permute-start = (bf16[128,1536]{1,0:T(8,128)(2,1)S(1)}, bf16[128,1536]{1,0:T(8,128)(2,1)S(1)}, u32[]{:S(2)}, u32[]{:S(2)}) collective-permute-start(bf16[128,1536]{1,0:T(8,128)(2,1)S(1)} %get-tuple-element.12.refs_0_), channel_id=1, source_target_pairs={{0,1},{1,0},{2,3},{3,2},{4,5},{5,4},{6,7},{7,6},{8,9},{9,8},{10,11... | collective-permute-start | bytes 1179656 | tf_op jit(solution)/shard_map/ppermute | solution.py:30
  23.7 0.0 collective-permute-done.1.refs_2_.refs_3_
  23.7 0.4 collective-permute-start.6
  24.1 0.0 collective-permute-done.3.refs_3_.refs_6_
  24.1 1.7 %project.2.refs_2_ = f32[128,1536]{1,0:T(8,128)S(1)} custom-call(bf16[1536,1536]{1,0:T(8,128)(2,1)S(1)} %get-tuple-element.16.refs_0_, bf16[1536,1536]{1,0:T(8,128)(2,1)S(1)} %get-tuple-element.17.refs_1_, bf16[1536,1536]{1,0:T(8,128)(2,1)S(1)} %get-tuple-element.15.refs_2_.refs_0_, bf16[128,1536]{1,0:T(8,128)(2,1)S(1)} %collective-permute-done.1.refs_2_.refs_3_, ...), custom_call_target="tpu_custom_call" | custom-call | tf_op jit(solution)/shard_map/project/pallas_call | solution.py:293
  25.8 0.0 copy-start
  25.8 0.0 copy-start.2
  25.8 0.0 copy-start.1
  25.9 0.0 collective-permute-done.5.refs_4_.refs_1_
  25.9 0.5 project.3
  26.4 0.7 %copy-done = bf16[1,1,3,128,12,128]{5,3,4,2,1,0:T(8,128)(2,1)S(1)} copy-done((bf16[1,1,3,128,12,128]{5,3,4,2,1,0:T(8,128)(2,1)S(1)}, bf16[1,1,3,128,12,128]{5,3,4,2,1,0:T(8,128)(2,1)}, u32[]{:S(2)}) %copy-start) | copy-done | bytes 1179672
  27.1 0.0 copy-done.2
  27.1 1.6 %late_backward.1 = bf16[3,5,128,128]{3,2,1,0:T(8,128)(2,1)S(1)} custom-call(s32[1,128]{1,0:T(1,128)S(1)} %bitcast.21, bf16[3,12,128,128]{3,2,1,0:T(8,128)(2,1)S(1)} %bitcast.14, bf16[128,640]{1,0:T(8,128)(2,1)S(1)} %get-tuple-element.19.grad_ref), custom_call_target="tpu_custom_call" | custom-call | tf_op jit(solution)/shard_map/late_backward/pallas_call | solution.py:199
  28.7 1.3 %collective-permute-start.10 = (bf16[3,5,128,128]{3,2,1,0:T(8,128)(2,1)S(1)}, bf16[3,5,128,128]{3,2,1,0:T(8,128)(2,1)S(1)}, u32[]{:S(2)}, u32[]{:S(2)}) collective-permute-start(bf16[3,5,128,128]{3,2,1,0:T(8,128)(2,1)S(1)} %late_backward.1), channel_id=1, source_target_pairs={{8,0},{16,8},{24,16},{9,1},{17,9},{25,17},{10,2},{18,10},{26,18},{... | collective-permute-start | bytes 1474568 | tf_op jit(solution)/shard_map/ppermute | solution.py:40
  30.0 7.7 %collective-permute-done.6.refs_5_ = bf16[128,768]{1,0:T(8,128)(2,1)S(1)} collective-permute-done((bf16[128,768]{1,0:T(8,128)(2,1)S(1)}, bf16[128,768]{1,0:T(8,128)(2,1)S(1)}, u32[]{:S(2)}, u32[]{:S(2)}) %collective-permute-start.6) | collective-permute-done | bytes 196640 | tf_op jit(solution)/shard_map/ppermute | solution.py:30
  37.7 1.7 %collective-permute-start.8 = (bf16[128,768]{1,0:T(8,128)(2,1)S(1)}, bf16[128,768]{1,0:T(8,128)(2,1)S(1)}, u32[]{:S(2)}, u32[]{:S(2)}) collective-permute-start(bf16[128,768]{1,0:T(8,128)(2,1)S(1)} %collective-permute-done.6.refs_5_), channel_id=1, source_target_pairs={{0,4},{2,6},{4,0},{6,2},{1,5},{3,7},{5,1},{7,3},{8,12},{10,14},{12... | collective-permute-start | bytes 589832 | tf_op jit(solution)/shard_map/ppermute | solution.py:30
  39.5 1.3 %collective-permute-start.12 = (bf16[128,896]{1,0:T(8,128)(2,1)S(1)}, bf16[128,896]{1,0:T(8,128)(2,1)S(1)}, u32[]{:S(2)}, u32[]{:S(2)}) collective-permute-start(bf16[128,896]{1,0:T(8,128)(2,1)S(1)} %get-tuple-element.21), channel_id=1, source_target_pairs={{8,0},{16,8},{24,16},{9,1},{17,9},{25,17},{10,2},{18,10},{26,18},{... | collective-permute-start | bytes 688136 | tf_op jit(solution)/shard_map/ppermute | solution.py:40
  40.8 0.0 collective-permute-done.refs_1_
  40.8 0.1 collective-permute-start.7
  40.9 3.3 %collective-permute-done.8.refs_6_ = bf16[128,768]{1,0:T(8,128)(2,1)S(1)} collective-permute-done((bf16[128,768]{1,0:T(8,128)(2,1)S(1)}, bf16[128,768]{1,0:T(8,128)(2,1)S(1)}, u32[]{:S(2)}, u32[]{:S(2)}) %collective-permute-start.8) | collective-permute-done | bytes 196640 | tf_op jit(solution)/shard_map/ppermute | solution.py:30
  44.2 0.0 collective-permute-start.9
  44.2 0.0 copy-done.1
  44.2 3.2 %weight_gradient.2.refs_7_ = bf16[3072,1536]{1,0:T(8,128)(2,1)} custom-call(bf16[128,1536]{1,0:T(8,128)(2,1)S(1)} %get-tuple-element.12.refs_0_, bf16[128,1536]{1,0:T(8,128)(2,1)S(1)} %collective-permute-done.refs_1_, bf16[128,1536]{1,0:T(8,128)(2,1)S(1)} %bitcast.18, bf16[128,768]{1,0:T(8,128)(2,1)S(1)} %collective-permute-done.2.refs_1_.refs_3_.refs_4_, ...), custom_call_target="tpu_custom_call" | custom-call | tf_op jit(solution)/shard_map/weight_gradient/pallas_call | solution.py:398
  47.4 1.3 %collective-permute-done.12.grad_ref = bf16[128,896]{1,0:T(8,128)(2,1)S(1)} collective-permute-done((bf16[128,896]{1,0:T(8,128)(2,1)S(1)}, bf16[128,896]{1,0:T(8,128)(2,1)S(1)}, u32[]{:S(2)}, u32[]{:S(2)}) %collective-permute-start.12) | collective-permute-done | bytes 229408 | tf_op jit(solution)/shard_map/ppermute | solution.py:40
  48.7 0.0 collective-permute-done.11.packed_ref
  48.7 2.8 %early_backward.1.whole_ref = bf16[3,12,128,128]{3,2,1,0:T(8,128)(2,1)} custom-call(bf16[2704,128]{1,0:T(8,128)(2,1)S(1)} %collective-permute-done.11.packed_ref, bf16[128,896]{1,0:T(8,128)(2,1)S(1)} %collective-permute-done.12.grad_ref), custom_call_target="tpu_custom_call" | custom-call | tf_op jit(solution)/shard_map/early_backward/pallas_call | solution.py:230
  51.5 0.0 collective-permute-done.7.refs_5_
  51.5 0.0 collective-permute-done.9.refs_6_
  51.5 3.2 %weight_gradient.3 = bf16[3072,1536]{1,0:T(8,128)(2,1)} custom-call(bf16[128,1536]{1,0:T(8,128)(2,1)S(1)} %get-tuple-element.12.refs_0_, bf16[128,1536]{1,0:T(8,128)(2,1)S(1)} %collective-permute-done.refs_1_, bf16[128,1536]{1,0:T(8,128)(2,1)S(1)} %collective-permute-done.1.refs_2_.refs_3_, ...), custom_call_target="tpu_custom_call", output_to_operand_aliasing={{}: (7, {})} | custom-call | tf_op jit(solution)/shard_map/weight_gradient/pallas_call | solution.py:398
  54.8 0.0 collective-permute-done.10.late_ref
  54.8 0.8 %fill.1 = bf16[3,12,128,128]{3,2,1,0:T(8,128)(2,1)} custom-call(bf16[3,5,128,128]{3,2,1,0:T(8,128)(2,1)S(1)} %collective-permute-done.10.late_ref, bf16[3,12,128,128]{3,2,1,0:T(8,128)(2,1)} %early_backward.1.whole_ref), custom_call_target="tpu_custom_call", output_to_operand_aliasing={{}: (1, {})} | custom-call | tf_op jit(solution)/shard_map/fill/pallas_call | solution.py:258
  (1 shorter events, 0.0 us)
Async XLA Ops:
  0.6 23.1 %collective-permute-start.1 = (bf16[128,1536]{1,0:T(8,128)(2,1)}, bf16[128,1536]{1,0:T(8,128)(2,1)S(1)}, u32[]{:S(2)}, u32[]{:S(2)}) collective-permute-start(bf16[128,1536]{1,0:T(8,128)(2,1)} %bitcast.15), channel_id=1, source_target_pairs={{0,2},{2,0},{4,6},{6,4},{1,3},{3,1},{5,7},{7,5},{8,10},{10,8},{12,... | collective-permute-start | bytes 1179656 | tf_op jit(solution)/shard_map/ppermute | solution.py:35
  2.6 8.3 %collective-permute-start.2 = (bf16[128,768]{1,0:T(8,128)(2,1)S(1)}, bf16[128,768]{1,0:T(8,128)(2,1)S(1)}, u32[]{:S(2)}, u32[]{:S(2)}) collective-permute-start(bf16[128,768]{1,0:T(8,128)(2,1)S(1)} %get-tuple-element.13), channel_id=1, source_target_pairs={{0,4},{2,6},{4,0},{6,2},{1,5},{3,7},{5,1},{7,3},{8,12},{10,14},{12... | collective-permute-start | bytes 589832 | tf_op jit(solution)/shard_map/ppermute | solution.py:30
  5.2 9.8 %collective-permute-start.4 = (bf16[128,768]{1,0:T(8,128)(2,1)S(1)}, bf16[128,768]{1,0:T(8,128)(2,1)S(1)}, u32[]{:S(2)}, u32[]{:S(2)}) collective-permute-start(bf16[128,768]{1,0:T(8,128)(2,1)S(1)} %get-tuple-element.14.refs_0_), channel_id=1, source_target_pairs={{0,4},{2,6},{4,0},{6,2},{1,5},{3,7},{5,1},{7,3},{8,12},{10,14},{12... | collective-permute-start | bytes 589832 | tf_op jit(solution)/shard_map/ppermute | solution.py:30
  5.3 43.4 %collective-permute-start.11 = (bf16[2704,128]{1,0:T(8,128)(2,1)S(1)}, bf16[2704,128]{1,0:T(8,128)(2,1)S(1)}, u32[]{:S(2)}, u32[]{:S(2)}) collective-permute-start(bf16[2704,128]{1,0:T(8,128)(2,1)S(1)} %get-tuple-element.20), channel_id=1, source_target_pairs={{8,0},{16,8},{24,16},{9,1},{17,9},{25,17},{10,2},{18,10},{26,18},{... | collective-permute-start | bytes 2076680 | tf_op jit(solution)/shard_map/ppermute | solution.py:40
  10.9 13.2 %collective-permute-start.3 = (bf16[128,768]{1,0:T(8,128)(2,1)S(1)}, bf16[128,768]{1,0:T(8,128)(2,1)S(1)}, u32[]{:S(2)}, u32[]{:S(2)}) collective-permute-start(bf16[128,768]{1,0:T(8,128)(2,1)S(1)} %collective-permute-done.2.refs_1_.refs_3_.refs_4_), channel_id=1, source_target_pairs={{0,2},{2,0},{4,6},{6,4},{1,3},{3,1},{5,7},{7,5},{8,10},{10,8},{12,... | collective-permute-start | bytes 589832 | tf_op jit(solution)/shard_map/ppermute | solution.py:35
  14.9 10.9 %collective-permute-start.5 = (bf16[128,768]{1,0:T(8,128)(2,1)S(1)}, bf16[128,768]{1,0:T(8,128)(2,1)S(1)}, u32[]{:S(2)}, u32[]{:S(2)}) collective-permute-start(bf16[128,768]{1,0:T(8,128)(2,1)S(1)} %collective-permute-done.4.refs_4_.refs_5_), channel_id=1, source_target_pairs={{0,2},{2,0},{4,6},{6,4},{1,3},{3,1},{5,7},{7,5},{8,10},{10,8},{12,... | collective-permute-start | bytes 589832 | tf_op jit(solution)/shard_map/ppermute | solution.py:35
  21.9 18.8 %collective-permute-start = (bf16[128,1536]{1,0:T(8,128)(2,1)S(1)}, bf16[128,1536]{1,0:T(8,128)(2,1)S(1)}, u32[]{:S(2)}, u32[]{:S(2)}) collective-permute-start(bf16[128,1536]{1,0:T(8,128)(2,1)S(1)} %get-tuple-element.12.refs_0_), channel_id=1, source_target_pairs={{0,1},{1,0},{2,3},{3,2},{4,5},{5,4},{6,7},{7,6},{8,9},{9,8},{10,11... | collective-permute-start | bytes 1179656 | tf_op jit(solution)/shard_map/ppermute | solution.py:30
  23.7 14.0 %collective-permute-start.6 = (bf16[128,768]{1,0:T(8,128)(2,1)S(1)}, bf16[128,768]{1,0:T(8,128)(2,1)S(1)}, u32[]{:S(2)}, u32[]{:S(2)}) collective-permute-start(bf16[128,768]{1,0:T(8,128)(2,1)S(1)} %choose.1), channel_id=1, source_target_pairs={{0,1},{1,0},{2,3},{3,2},{4,5},{5,4},{6,7},{7,6},{8,9},{9,8},{10,11... | collective-permute-start | bytes 589832 | tf_op jit(solution)/shard_map/ppermute | solution.py:30
  25.8 1.3 %copy-start = (bf16[1,1,3,128,12,128]{5,3,4,2,1,0:T(8,128)(2,1)S(1)}, bf16[1,1,3,128,12,128]{5,3,4,2,1,0:T(8,128)(2,1)}, u32[]{:S(2)}) copy-start(bf16[1,1,3,128,12,128]{5,3,4,2,1,0:T(8,128)(2,1)} %param.4) | copy-start | bytes 3538948
  25.8 1.3 %copy-start.2 = (s32[1,1,128]{2,1,0:T(1,128)S(1)}, s32[1,1,128]{2,1,0:T(1,128)}, u32[]{:S(2)}) copy-start(s32[1,1,128]{2,1,0:T(1,128)} %param.5) | copy-start | bytes 1540
  25.8 18.4 %copy-start.1 = (bf16[1,1,128,1536]{3,2,1,0:T(8,128)(2,1)S(1)}, bf16[1,1,128,1536]{3,2,1,0:T(8,128)(2,1)}, u32[]{:S(2)}) copy-start(bf16[1,1,128,1536]{3,2,1,0:T(8,128)(2,1)} %param.7) | copy-start | bytes 1179652
  28.7 26.0 %collective-permute-start.10 = (bf16[3,5,128,128]{3,2,1,0:T(8,128)(2,1)S(1)}, bf16[3,5,128,128]{3,2,1,0:T(8,128)(2,1)S(1)}, u32[]{:S(2)}, u32[]{:S(2)}) collective-permute-start(bf16[3,5,128,128]{3,2,1,0:T(8,128)(2,1)S(1)} %late_backward.1), channel_id=1, source_target_pairs={{8,0},{16,8},{24,16},{9,1},{17,9},{25,17},{10,2},{18,10},{26,18},{... | collective-permute-start | bytes 1474568 | tf_op jit(solution)/shard_map/ppermute | solution.py:40
  37.7 6.5 %collective-permute-start.8 = (bf16[128,768]{1,0:T(8,128)(2,1)S(1)}, bf16[128,768]{1,0:T(8,128)(2,1)S(1)}, u32[]{:S(2)}, u32[]{:S(2)}) collective-permute-start(bf16[128,768]{1,0:T(8,128)(2,1)S(1)} %collective-permute-done.6.refs_5_), channel_id=1, source_target_pairs={{0,4},{2,6},{4,0},{6,2},{1,5},{3,7},{5,1},{7,3},{8,12},{10,14},{12... | collective-permute-start | bytes 589832 | tf_op jit(solution)/shard_map/ppermute | solution.py:30
  39.5 9.2 %collective-permute-start.12 = (bf16[128,896]{1,0:T(8,128)(2,1)S(1)}, bf16[128,896]{1,0:T(8,128)(2,1)S(1)}, u32[]{:S(2)}, u32[]{:S(2)}) collective-permute-start(bf16[128,896]{1,0:T(8,128)(2,1)S(1)} %get-tuple-element.21), channel_id=1, source_target_pairs={{8,0},{16,8},{24,16},{9,1},{17,9},{25,17},{10,2},{18,10},{26,18},{... | collective-permute-start | bytes 688136 | tf_op jit(solution)/shard_map/ppermute | solution.py:40
  40.8 10.7 %collective-permute-start.7 = (bf16[128,768]{1,0:T(8,128)(2,1)S(1)}, bf16[128,768]{1,0:T(8,128)(2,1)S(1)}, u32[]{:S(2)}, u32[]{:S(2)}) collective-permute-start(bf16[128,768]{1,0:T(8,128)(2,1)S(1)} %collective-permute-done.6.refs_5_), channel_id=1, source_target_pairs={{0,2},{2,0},{4,6},{6,4},{1,3},{3,1},{5,7},{7,5},{8,10},{10,8},{12,... | collective-permute-start | bytes 589832 | tf_op jit(solution)/shard_map/ppermute | solution.py:35
  44.2 7.3 %collective-permute-start.9 = (bf16[128,768]{1,0:T(8,128)(2,1)S(1)}, bf16[128,768]{1,0:T(8,128)(2,1)S(1)}, u32[]{:S(2)}, u32[]{:S(2)}) collective-permute-start(bf16[128,768]{1,0:T(8,128)(2,1)S(1)} %collective-permute-done.8.refs_6_), channel_id=1, source_target_pairs={{0,2},{2,0},{4,6},{6,4},{1,3},{3,1},{5,7},{7,5},{8,10},{10,8},{12,... | collective-permute-start | bytes 589832 | tf_op jit(solution)/shard_map/ppermute | solution.py:35

commit v8 on v7

--- a/solution.py
+++ b/solution.py
@@ -119,7 +119,7 @@
         )
     fetches = [
         pltpu.make_async_copy(
-            rows_of(weight_ref, rows.shape[0], chips, number // 2, number % 2),
+            rows_of(weight_ref, rows.shape[0], chips, max(0, number - 1), number == 1),
             target,
             sems.at[number],
         )
@@ -146,7 +146,7 @@
 def forward(chips, pos, qkv, weight, own):
     _, heads, seq, width = qkv.shape
     depth, columns = own.shape[1], weight.shape[1]
-    count = 2 * chips - 1
+    count = chips
     groups = max(size for size in (1, 2, 3) if heads % size == 0)
     return pl.pallas_call(
         functools.partial(forward_kernel, chips, groups),
@@ -267,37 +267,76 @@
     )(late, whole)
 
 
-def project_kernel(terms, splits, *refs):
-    count = 1 + max(number for number, _ in terms)
-    weights, grads = refs[:count], refs[count : count + len(terms)]
-    refs = refs[count + len(terms) :]
-    total = refs[0][...]
-    for (number, start), grad in zip(terms, grads):
-        rows = weights[number][start : start + grad.shape[1]]
-        total = total + jnp.dot(grad[...], rows, preferred_element_type=F32)
+def middle_kernel(chips, pieces, weight_ref, *refs):
+    steps = chips - 1
+    count = 1 + steps * pieces
+    rows, refs = refs[: 1 + steps], refs[1 + steps :]
+    direct, crossed = refs[:count], refs[count : 2 * count - 2]
+    carried_ref, total_ref = refs[2 * count - 2 : 2 * count]
+    kept, sems = refs[2 * count : -1], refs[-1]
+    depth = kept[0].shape[0]
+    size = depth // pieces
+    gets = []
+    for step in range(1, chips):
+        source = rows_of(weight_ref, depth, chips, step, True)
+        for piece in range(pieces):
+            part = pl.ds(piece * size, size)
+            gets.append(
+                pltpu.make_async_copy(
+                    source.at[part], kept[step - 1].at[part], sems.at[len(gets)]
+                )
+            )
+    for get in gets:
+        get.start()
+    total = carried_ref[...]
+    total = total + jnp.dot(direct[0][...], rows[0][...], preferred_element_type=F32)
+    for number, grad in enumerate(direct[1:]):
+        step, piece = divmod(number, pieces)
+        part = rows[1 + step][piece * size : (piece + 1) * size]
+        total = total + jnp.dot(grad[...], part, preferred_element_type=F32)
+    for number, grad in enumerate(crossed):
+        step, piece = divmod(number, pieces)
+        gets[number].wait()
+        part = kept[step][piece * size : (piece + 1) * size]
+        total = total + jnp.dot(grad[...], part, preferred_element_type=F32)
+    total_ref[...] = total
+    for get in gets[len(crossed) :]:
+        get.wait()
+
+
+def project_middle(chips, pieces, weight, rows, direct, crossed, total):
+    depth, columns = rows[0].shape
+    return pl.pallas_call(
+        functools.partial(middle_kernel, chips, pieces),
+        name="project_middle",
+        in_specs=[ANY] + [VMEM] * (len(rows) + len(direct) + len(crossed) + 1),
+        out_specs=[VMEM] * chips,
+        out_shape=[jax.ShapeDtypeStruct(total.shape, F32)]
+        + [pltpu.VMEM((depth, columns), BF16)] * (chips - 1),
+        scratch_shapes=[pltpu.SemaphoreType.DMA(((chips - 1) * pieces,))],
+        compiler_params=PARAMS,
+    )(weight, *rows, *direct, *crossed, total)
+
+
+def project_kernel(first, splits, rows_ref, grad_ref, carried_ref, *outs):
+    rows = rows_ref[first : first + grad_ref.shape[1]]
+    total = carried_ref[...] + jnp.dot(grad_ref[...], rows, preferred_element_type=F32)
     at = 0
-    for out, size in zip(refs[1:], splits):
-        out[...] = total[:, at : at + size].astype(out.dtype)
+    for out, size in zip(outs, splits):
+        out[...] = total[:, at : at + size].astype(BF16)
         at += size
 
 
-def project(items, total, splits, dtype):
-    weights, terms = [], []
-    for weight, start, _ in items:
-        found = [number for number, known in enumerate(weights) if known is weight]
-        if not found:
-            weights.append(weight)
-        terms.append((found[0] if found else len(weights) - 1, start))
-    grads = [grad for _, _, grad in items]
-    seq = grads[0].shape[0]
-    return pl.pallas_call(
-        functools.partial(project_kernel, tuple(terms), splits),
-        name="project",
-        in_specs=[VMEM] * (len(weights) + len(grads) + 1),
+def project_last(rows, first, grad, total, splits):
+    seq = grad.shape[0]
+    return pl.pallas_call(
+        functools.partial(project_kernel, first, splits),
+        name="project_last",
+        in_specs=[VMEM] * 3,
         out_specs=[VMEM] * len(splits),
-        out_shape=[jax.ShapeDtypeStruct((seq, size), dtype) for size in splits],
-        compiler_params=PARAMS,
-    )(*weights, *grads, total)
+        out_shape=[jax.ShapeDtypeStruct((seq, size), BF16) for size in splits],
+        compiler_params=PARAMS,
+    )(rows, grad, total)
 
 
 def counts(options):
@@ -445,18 +484,14 @@
     for step in range(1, replicas):
         acts.append(rotate(attended, "dp", step))
 
-    whole = (heads * width,)
     halves = (early * width, late * width)
     depth = own.shape[1] // pieces
-    direct, crossed = [], []
-    for step in range(1, chips):
-        for piece in range(pieces):
-            start = piece * depth
-            direct.append((far_rows[2 * step - 1], start, same[step][piece]))
-            crossed.append((far_rows[2 * step], start, other[step][piece]))
-    mate = (far_rows[0], 0, other[0][0])
-    (total,) = project([mate] + direct + crossed[:-1], total, whole, F32)
-    total = project([crossed[-1]], total, halves, BF16)
+    direct = [other[0][0]] + [value for values in same[1:] for value in values]
+    crossed = [value for values in other[1:] for value in values]
+    total, *crossed_rows = project_middle(
+        chips, pieces, weight, far_rows, direct, crossed[:-1], total
+    )
+    total = project_last(crossed_rows[-1], (pieces - 1) * depth, crossed[-1], total, halves)
     d_early, d_late = total
     d_above = down(d_early, "section")
     grads_late = late_backward(pos, qkv, d_late)

time: 55.8 us -> 56.1 us (level)
    ppermute x5, waiting for transfers between devices: 19.5 us -> 17.8 us  [rotate(): lax.ppermute(value, axis, [(i, (i + steps) % count) for i in range(count)])]
    pallas_call x2, Pallas kernels: 2.17 us -> 3.82 us  [the longest x1 3.34 us: project_middle(): pl.pallas_call(functools.partial(middle_kernel, chips, pieces), name='pro...]
    ppermute x3, waiting for transfers between devices: 1.26 us -> 2.91 us  [down(): return lax.ppermute(value, axis, [(i, i - 1) for i in range(1, count)])]
    pallas_call x1, Pallas kernels: 6.98 us -> 5.62 us  [forward(): pl.pallas_call(functools.partial(forward_kernel, chips, groups), name='fo...]
where the time goes in v8:
time: 56.1 us; the launch traced here: 55.9 us
  Pallas kernels  22.5 us (40%)
  waiting for transfers between devices  20.7 us (37%)
  starting transfers between devices  11.1 us (20%)
  between operations  0.79 us (1%)
  local copies, waits for them, and re-layouts  0.76 us (1%)
    ppermute x5, waiting for transfers between devices, rotate(): lax.ppermute(value, axis, [(i, (i + steps) % count) for i in range(count)])  17.8 us
    ppermute x5, starting transfers between devices, rotate(): lax.ppermute(value, axis, [(i, (i + steps) % count) for i in range(count)])  6.57 us
    pallas_call x2, Pallas kernels, weight_gradient(): pl.pallas_call(functools.partial(weight_kernel, replicas, counts(options)...  6.46 us
    pallas_call x1, Pallas kernels, forward(): pl.pallas_call(functools.partial(forward_kernel, chips, groups), name='fo...  5.62 us
    ppermute x3, starting transfers between devices, down(): return lax.ppermute(value, axis, [(i, i - 1) for i in range(1, count)])  3.85 us
    pallas_call x1, Pallas kernels, project_middle(): pl.pallas_call(functools.partial(middle_kernel, chips, pieces), name='pro...  3.34 us
    ppermute x3, waiting for transfers between devices, down(): return lax.ppermute(value, axis, [(i, i - 1) for i in range(1, count)])  2.91 us
    pallas_call x1, Pallas kernels, early_backward(): pl.pallas_call(early_kernel, name='early_backward', in_specs=[VMEM] * 2,...  2.82 us
  transfers between devices with their start and end apart: 13, of which 5 were waited for; matrix products, arithmetic and copies ran while one was open for 0% of the time, Pallas kernels for 39%

profile of v8, /device:TPU:0, one launch (start us, length us, event | category | flops | bytes accessed | tf_op | source)
XLA Modules:
  0.0 55.9 jit_solution(17738751993263722796)
XLA Ops:
  0.6 0.6 collective-permute-start.1
  1.2 1.4 %pack.1 = (bf16[2704,128]{1,0:T(8,128)(2,1)S(1)}, bf16[128,768]{1,0:T(8,128)(2,1)S(1)}, bf16[128,768]{1,0:T(8,128)(2,1)S(1)}) custom-call(s32[1,128]{1,0:T(1,128)} %bitcast.19, bf16[3,1536,128]{2,1,0:T(8,128)(2,1)} %bitcast.12, bf16[128,1536]{1,0:T(8,128)(2,1)} %bitcast.16), custom_call_target="tpu_custom_call" | custom-call | tf_op jit(solution)/shard_map/pack/pallas_call | solution.py:85
  2.6 2.6 %collective-permute-start.2 = (bf16[128,768]{1,0:T(8,128)(2,1)S(1)}, bf16[128,768]{1,0:T(8,128)(2,1)S(1)}, u32[]{:S(2)}, u32[]{:S(2)}) collective-permute-start(bf16[128,768]{1,0:T(8,128)(2,1)S(1)} %get-tuple-element.14), channel_id=1, source_target_pairs={{0,4},{2,6},{4,0},{6,2},{1,5},{3,7},{5,1},{7,3},{8,12},{10,14},{12... | collective-permute-start | bytes 589832 | tf_op jit(solution)/shard_map/ppermute | solution.py:30
  5.2 0.1 collective-permute-start.4
  5.3 1.3 %collective-permute-start.11 = (bf16[2704,128]{1,0:T(8,128)(2,1)S(1)}, bf16[2704,128]{1,0:T(8,128)(2,1)S(1)}, u32[]{:S(2)}, u32[]{:S(2)}) collective-permute-start(bf16[2704,128]{1,0:T(8,128)(2,1)S(1)} %get-tuple-element.22), channel_id=1, source_target_pairs={{8,0},{16,8},{24,16},{9,1},{17,9},{25,17},{10,2},{18,10},{26,18},{... | collective-permute-start | bytes 2076680 | tf_op jit(solution)/shard_map/ppermute | solution.py:40
  6.5 4.4 %collective-permute-done.2.refs_1_.refs_3_ = bf16[128,768]{1,0:T(8,128)(2,1)S(1)} collective-permute-done((bf16[128,768]{1,0:T(8,128)(2,1)S(1)}, bf16[128,768]{1,0:T(8,128)(2,1)S(1)}, u32[]{:S(2)}, u32[]{:S(2)}) %collective-permute-start.2) | collective-permute-done | bytes 196640 | tf_op jit(solution)/shard_map/ppermute | solution.py:30
  10.9 0.0 collective-permute-start.3
  10.9 4.0 %collective-permute-done.4.refs_4_ = bf16[128,768]{1,0:T(8,128)(2,1)S(1)} collective-permute-done((bf16[128,768]{1,0:T(8,128)(2,1)S(1)}, bf16[128,768]{1,0:T(8,128)(2,1)S(1)}, u32[]{:S(2)}, u32[]{:S(2)}) %collective-permute-start.4) | collective-permute-done | bytes 196640 | tf_op jit(solution)/shard_map/ppermute | solution.py:30
  14.9 0.0 collective-permute-start.5
  14.9 5.6 %forward.1 = (bf16[128,1536]{1,0:T(8,128)(2,1)S(1)}, f32[128,1536]{1,0:T(8,128)S(1)}, bf16[1536,1536]{1,0:T(8,128)(2,1)S(1)}, bf16[1536,1536]{1,0:T(8,128)(2,1)S(1)}) custom-call(s32[1,128]{1,0:T(1,128)} %bitcast.20, bf16[3,12,128,128]{3,2,1,0:T(8,128)(2,1)} %bitcast.13, bf16[6144,1536]{1,0:T(8,128)(2,1)} %bitcast.22, bf16[128,1536]{1,0:T(8,128)(2,1)} %bitcast.17), custom_call_target="tpu_custom_call" | custom-call | tf_op jit(solution)/shard_map/forward/pallas_call | solution.py:151
  20.6 1.8 %collective-permute-start = (bf16[128,1536]{1,0:T(8,128)(2,1)S(1)}, bf16[128,1536]{1,0:T(8,128)(2,1)S(1)}, u32[]{:S(2)}, u32[]{:S(2)}) collective-permute-start(bf16[128,1536]{1,0:T(8,128)(2,1)S(1)} %get-tuple-element.13.refs_0_), channel_id=1, source_target_pairs={{0,1},{1,0},{2,3},{3,2},{4,5},{5,4},{6,7},{7,6},{8,9},{9,8},{10,11... | collective-permute-start | bytes 1179656 | tf_op jit(solution)/shard_map/ppermute | solution.py:30
  22.4 0.0 collective-permute-done.1.refs_2_
  22.4 0.4 collective-permute-start.6
  22.8 0.0 collective-permute-done.3.refs_3_.refs_5_
  22.8 3.3 %project_middle.1 = (f32[128,1536]{1,0:T(8,128)S(1)}, bf16[1536,1536]{1,0:T(8,128)(2,1)S(1)}) custom-call(bf16[6144,1536]{1,0:T(8,128)(2,1)} %bitcast.23, bf16[1536,1536]{1,0:T(8,128)(2,1)S(1)} %get-tuple-element.16.refs_0_, bf16[1536,1536]{1,0:T(8,128)(2,1)S(1)} %get-tuple-element.17.refs_1_, bf16[128,1536]{1,0:T(8,128)(2,1)S(1)} %collective-permute-done.1.refs_2_, ...), custom_call_target="tpu_custom_call" | custom-call | tf_op jit(solution)/shard_map/project_middle/pallas_call | solution.py:309
  26.1 0.0 copy-start
  26.1 0.0 copy-start.2
  26.1 0.0 copy-start.1
  26.2 0.0 collective-permute-done.5.refs_4_.grad_ref
  26.2 0.5 project_last.1
  26.7 0.7 %copy-done = bf16[1,1,3,128,12,128]{5,3,4,2,1,0:T(8,128)(2,1)S(1)} copy-done((bf16[1,1,3,128,12,128]{5,3,4,2,1,0:T(8,128)(2,1)S(1)}, bf16[1,1,3,128,12,128]{5,3,4,2,1,0:T(8,128)(2,1)}, u32[]{:S(2)}) %copy-start) | copy-done | bytes 1179672
  27.4 0.0 copy-done.2
  27.4 1.6 %late_backward.1 = bf16[3,5,128,128]{3,2,1,0:T(8,128)(2,1)S(1)} custom-call(s32[1,128]{1,0:T(1,128)S(1)} %bitcast.21, bf16[3,12,128,128]{3,2,1,0:T(8,128)(2,1)S(1)} %bitcast.14, bf16[128,640]{1,0:T(8,128)(2,1)S(1)} %get-tuple-element.21.grad_ref), custom_call_target="tpu_custom_call" | custom-call | tf_op jit(solution)/shard_map/late_backward/pallas_call | solution.py:199
  29.0 1.3 %collective-permute-start.10 = (bf16[3,5,128,128]{3,2,1,0:T(8,128)(2,1)S(1)}, bf16[3,5,128,128]{3,2,1,0:T(8,128)(2,1)S(1)}, u32[]{:S(2)}, u32[]{:S(2)}) collective-permute-start(bf16[3,5,128,128]{3,2,1,0:T(8,128)(2,1)S(1)} %late_backward.1), channel_id=1, source_target_pairs={{8,0},{16,8},{24,16},{9,1},{17,9},{25,17},{10,2},{18,10},{26,18},{... | collective-permute-start | bytes 1474568 | tf_op jit(solution)/shard_map/ppermute | solution.py:40
  30.3 6.1 %collective-permute-done.6.refs_5_ = bf16[128,768]{1,0:T(8,128)(2,1)S(1)} collective-permute-done((bf16[128,768]{1,0:T(8,128)(2,1)S(1)}, bf16[128,768]{1,0:T(8,128)(2,1)S(1)}, u32[]{:S(2)}, u32[]{:S(2)}) %collective-permute-start.6) | collective-permute-done | bytes 196640 | tf_op jit(solution)/shard_map/ppermute | solution.py:30
  36.4 1.7 %collective-permute-start.8 = (bf16[128,768]{1,0:T(8,128)(2,1)S(1)}, bf16[128,768]{1,0:T(8,128)(2,1)S(1)}, u32[]{:S(2)}, u32[]{:S(2)}) collective-permute-start(bf16[128,768]{1,0:T(8,128)(2,1)S(1)} %collective-permute-done.6.refs_5_), channel_id=1, source_target_pairs={{0,4},{2,6},{4,0},{6,2},{1,5},{3,7},{5,1},{7,3},{8,12},{10,14},{12... | collective-permute-start | bytes 589832 | tf_op jit(solution)/shard_map/ppermute | solution.py:30
  38.1 1.3 %collective-permute-start.12 = (bf16[128,896]{1,0:T(8,128)(2,1)S(1)}, bf16[128,896]{1,0:T(8,128)(2,1)S(1)}, u32[]{:S(2)}, u32[]{:S(2)}) collective-permute-start(bf16[128,896]{1,0:T(8,128)(2,1)S(1)} %get-tuple-element.23), channel_id=1, source_target_pairs={{8,0},{16,8},{24,16},{9,1},{17,9},{25,17},{10,2},{18,10},{26,18},{... | collective-permute-start | bytes 688136 | tf_op jit(solution)/shard_map/ppermute | solution.py:40
  39.4 0.0 collective-permute-done.refs_1_
  39.4 0.1 collective-permute-start.7
  39.5 3.3 %collective-permute-done.8.refs_6_ = bf16[128,768]{1,0:T(8,128)(2,1)S(1)} collective-permute-done((bf16[128,768]{1,0:T(8,128)(2,1)S(1)}, bf16[128,768]{1,0:T(8,128)(2,1)S(1)}, u32[]{:S(2)}, u32[]{:S(2)}) %collective-permute-start.8) | collective-permute-done | bytes 196640 | tf_op jit(solution)/shard_map/ppermute | solution.py:30
  42.8 0.0 collective-permute-start.9
  42.8 0.0 copy-done.1
  42.8 3.2 %weight_gradient.2.refs_7_ = bf16[3072,1536]{1,0:T(8,128)(2,1)} custom-call(bf16[128,1536]{1,0:T(8,128)(2,1)S(1)} %get-tuple-element.13.refs_0_, bf16[128,1536]{1,0:T(8,128)(2,1)S(1)} %collective-permute-done.refs_1_, bf16[128,1536]{1,0:T(8,128)(2,1)S(1)} %bitcast.18, bf16[128,768]{1,0:T(8,128)(2,1)S(1)} %collective-permute-done.2.refs_1_.refs_3_, ...), custom_call_target="tpu_custom_call" | custom-call | tf_op jit(solution)/shard_map/weight_gradient/pallas_call | solution.py:437
  46.0 2.9 %collective-permute-done.12.grad_ref = bf16[128,896]{1,0:T(8,128)(2,1)S(1)} collective-permute-done((bf16[128,896]{1,0:T(8,128)(2,1)S(1)}, bf16[128,896]{1,0:T(8,128)(2,1)S(1)}, u32[]{:S(2)}, u32[]{:S(2)}) %collective-permute-start.12) | collective-permute-done | bytes 229408 | tf_op jit(solution)/shard_map/ppermute | solution.py:40
  49.0 0.0 collective-permute-done.11.packed_ref
  49.0 2.8 %early_backward.1.whole_ref = bf16[3,12,128,128]{3,2,1,0:T(8,128)(2,1)} custom-call(bf16[2704,128]{1,0:T(8,128)(2,1)S(1)} %collective-permute-done.11.packed_ref, bf16[128,896]{1,0:T(8,128)(2,1)S(1)} %collective-permute-done.12.grad_ref), custom_call_target="tpu_custom_call" | custom-call | tf_op jit(solution)/shard_map/early_backward/pallas_call | solution.py:230
  51.8 0.0 collective-permute-done.7.refs_5_
  51.8 0.0 collective-permute-done.9.refs_6_
  51.8 3.3 %weight_gradient.3 = bf16[3072,1536]{1,0:T(8,128)(2,1)} custom-call(bf16[128,1536]{1,0:T(8,128)(2,1)S(1)} %get-tuple-element.13.refs_0_, bf16[128,1536]{1,0:T(8,128)(2,1)S(1)} %collective-permute-done.refs_1_, bf16[128,1536]{1,0:T(8,128)(2,1)S(1)} %collective-permute-done.1.refs_2_, ...), custom_call_target="tpu_custom_call", output_to_operand_aliasing={{}: (7, {})} | custom-call | tf_op jit(solution)/shard_map/weight_gradient/pallas_call | solution.py:437
  55.1 0.0 collective-permute-done.10.late_ref
  55.1 0.8 %fill.1 = bf16[3,12,128,128]{3,2,1,0:T(8,128)(2,1)} custom-call(bf16[3,5,128,128]{3,2,1,0:T(8,128)(2,1)S(1)} %collective-permute-done.10.late_ref, bf16[3,12,128,128]{3,2,1,0:T(8,128)(2,1)} %early_backward.1.whole_ref), custom_call_target="tpu_custom_call", output_to_operand_aliasing={{}: (1, {})} | custom-call | tf_op jit(solution)/shard_map/fill/pallas_call | solution.py:258
  (1 shorter events, 0.0 us)
Async XLA Ops:
  0.6 21.7 %collective-permute-start.1 = (bf16[128,1536]{1,0:T(8,128)(2,1)}, bf16[128,1536]{1,0:T(8,128)(2,1)S(1)}, u32[]{:S(2)}, u32[]{:S(2)}) collective-permute-start(bf16[128,1536]{1,0:T(8,128)(2,1)} %bitcast.15), channel_id=1, source_target_pairs={{0,2},{2,0},{4,6},{6,4},{1,3},{3,1},{5,7},{7,5},{8,10},{10,8},{12,... | collective-permute-start | bytes 1179656 | tf_op jit(solution)/shard_map/ppermute | solution.py:35
  2.6 8.3 %collective-permute-start.2 = (bf16[128,768]{1,0:T(8,128)(2,1)S(1)}, bf16[128,768]{1,0:T(8,128)(2,1)S(1)}, u32[]{:S(2)}, u32[]{:S(2)}) collective-permute-start(bf16[128,768]{1,0:T(8,128)(2,1)S(1)} %get-tuple-element.14), channel_id=1, source_target_pairs={{0,4},{2,6},{4,0},{6,2},{1,5},{3,7},{5,1},{7,3},{8,12},{10,14},{12... | collective-permute-start | bytes 589832 | tf_op jit(solution)/shard_map/ppermute | solution.py:30
  5.2 9.8 %collective-permute-start.4 = (bf16[128,768]{1,0:T(8,128)(2,1)S(1)}, bf16[128,768]{1,0:T(8,128)(2,1)S(1)}, u32[]{:S(2)}, u32[]{:S(2)}) collective-permute-start(bf16[128,768]{1,0:T(8,128)(2,1)S(1)} %get-tuple-element.15.refs_0_), channel_id=1, source_target_pairs={{0,4},{2,6},{4,0},{6,2},{1,5},{3,7},{5,1},{7,3},{8,12},{10,14},{12... | collective-permute-start | bytes 589832 | tf_op jit(solution)/shard_map/ppermute | solution.py:30
  5.3 43.7 %collective-permute-start.11 = (bf16[2704,128]{1,0:T(8,128)(2,1)S(1)}, bf16[2704,128]{1,0:T(8,128)(2,1)S(1)}, u32[]{:S(2)}, u32[]{:S(2)}) collective-permute-start(bf16[2704,128]{1,0:T(8,128)(2,1)S(1)} %get-tuple-element.22), channel_id=1, source_target_pairs={{8,0},{16,8},{24,16},{9,1},{17,9},{25,17},{10,2},{18,10},{26,18},{... | collective-permute-start | bytes 2076680 | tf_op jit(solution)/shard_map/ppermute | solution.py:40
  10.9 11.8 %collective-permute-start.3 = (bf16[128,768]{1,0:T(8,128)(2,1)S(1)}, bf16[128,768]{1,0:T(8,128)(2,1)S(1)}, u32[]{:S(2)}, u32[]{:S(2)}) collective-permute-start(bf16[128,768]{1,0:T(8,128)(2,1)S(1)} %collective-permute-done.2.refs_1_.refs_3_), channel_id=1, source_target_pairs={{0,2},{2,0},{4,6},{6,4},{1,3},{3,1},{5,7},{7,5},{8,10},{10,8},{12,... | collective-permute-start | bytes 589832 | tf_op jit(solution)/shard_map/ppermute | solution.py:35
  14.9 11.2 %collective-permute-start.5 = (bf16[128,768]{1,0:T(8,128)(2,1)S(1)}, bf16[128,768]{1,0:T(8,128)(2,1)S(1)}, u32[]{:S(2)}, u32[]{:S(2)}) collective-permute-start(bf16[128,768]{1,0:T(8,128)(2,1)S(1)} %collective-permute-done.4.refs_4_), channel_id=1, source_target_pairs={{0,2},{2,0},{4,6},{6,4},{1,3},{3,1},{5,7},{7,5},{8,10},{10,8},{12,... | collective-permute-start | bytes 589832 | tf_op jit(solution)/shard_map/ppermute | solution.py:35
  20.6 18.8 %collective-permute-start = (bf16[128,1536]{1,0:T(8,128)(2,1)S(1)}, bf16[128,1536]{1,0:T(8,128)(2,1)S(1)}, u32[]{:S(2)}, u32[]{:S(2)}) collective-permute-start(bf16[128,1536]{1,0:T(8,128)(2,1)S(1)} %get-tuple-element.13.refs_0_), channel_id=1, source_target_pairs={{0,1},{1,0},{2,3},{3,2},{4,5},{5,4},{6,7},{7,6},{8,9},{9,8},{10,11... | collective-permute-start | bytes 1179656 | tf_op jit(solution)/shard_map/ppermute | solution.py:30
  22.4 14.0 %collective-permute-start.6 = (bf16[128,768]{1,0:T(8,128)(2,1)S(1)}, bf16[128,768]{1,0:T(8,128)(2,1)S(1)}, u32[]{:S(2)}, u32[]{:S(2)}) collective-permute-start(bf16[128,768]{1,0:T(8,128)(2,1)S(1)} %choose.1), channel_id=1, source_target_pairs={{0,1},{1,0},{2,3},{3,2},{4,5},{5,4},{6,7},{7,6},{8,9},{9,8},{10,11... | collective-permute-start | bytes 589832 | tf_op jit(solution)/shard_map/ppermute | solution.py:30
  26.1 1.3 %copy-start = (bf16[1,1,3,128,12,128]{5,3,4,2,1,0:T(8,128)(2,1)S(1)}, bf16[1,1,3,128,12,128]{5,3,4,2,1,0:T(8,128)(2,1)}, u32[]{:S(2)}) copy-start(bf16[1,1,3,128,12,128]{5,3,4,2,1,0:T(8,128)(2,1)} %param.4) | copy-start | bytes 3538948
  26.1 1.3 %copy-start.2 = (s32[1,1,128]{2,1,0:T(1,128)S(1)}, s32[1,1,128]{2,1,0:T(1,128)}, u32[]{:S(2)}) copy-start(s32[1,1,128]{2,1,0:T(1,128)} %param.5) | copy-start | bytes 1540
  26.1 16.7 %copy-start.1 = (bf16[1,1,128,1536]{3,2,1,0:T(8,128)(2,1)S(1)}, bf16[1,1,128,1536]{3,2,1,0:T(8,128)(2,1)}, u32[]{:S(2)}) copy-start(bf16[1,1,128,1536]{3,2,1,0:T(8,128)(2,1)} %param.7) | copy-start | bytes 1179652
  29.0 26.1 %collective-permute-start.10 = (bf16[3,5,128,128]{3,2,1,0:T(8,128)(2,1)S(1)}, bf16[3,5,128,128]{3,2,1,0:T(8,128)(2,1)S(1)}, u32[]{:S(2)}, u32[]{:S(2)}) collective-permute-start(bf16[3,5,128,128]{3,2,1,0:T(8,128)(2,1)S(1)} %late_backward.1), channel_id=1, source_target_pairs={{8,0},{16,8},{24,16},{9,1},{17,9},{25,17},{10,2},{18,10},{26,18},{... | collective-permute-start | bytes 1474568 | tf_op jit(solution)/shard_map/ppermute | solution.py:40
  36.4 6.5 %collective-permute-start.8 = (bf16[128,768]{1,0:T(8,128)(2,1)S(1)}, bf16[128,768]{1,0:T(8,128)(2,1)S(1)}, u32[]{:S(2)}, u32[]{:S(2)}) collective-permute-start(bf16[128,768]{1,0:T(8,128)(2,1)S(1)} %collective-permute-done.6.refs_5_), channel_id=1, source_target_pairs={{0,4},{2,6},{4,0},{6,2},{1,5},{3,7},{5,1},{7,3},{8,12},{10,14},{12... | collective-permute-start | bytes 589832 | tf_op jit(solution)/shard_map/ppermute | solution.py:30
  38.1 10.8 %collective-permute-start.12 = (bf16[128,896]{1,0:T(8,128)(2,1)S(1)}, bf16[128,896]{1,0:T(8,128)(2,1)S(1)}, u32[]{:S(2)}, u32[]{:S(2)}) collective-permute-start(bf16[128,896]{1,0:T(8,128)(2,1)S(1)} %get-tuple-element.23), channel_id=1, source_target_pairs={{8,0},{16,8},{24,16},{9,1},{17,9},{25,17},{10,2},{18,10},{26,18},{... | collective-permute-start | bytes 688136 | tf_op jit(solution)/shard_map/ppermute | solution.py:40
  39.4 12.4 %collective-permute-start.7 = (bf16[128,768]{1,0:T(8,128)(2,1)S(1)}, bf16[128,768]{1,0:T(8,128)(2,1)S(1)}, u32[]{:S(2)}, u32[]{:S(2)}) collective-permute-start(bf16[128,768]{1,0:T(8,128)(2,1)S(1)} %collective-permute-done.6.refs_5_), channel_id=1, source_target_pairs={{0,2},{2,0},{4,6},{6,4},{1,3},{3,1},{5,7},{7,5},{8,10},{10,8},{12,... | collective-permute-start | bytes 589832 | tf_op jit(solution)/shard_map/ppermute | solution.py:35
  42.8 9.0 %collective-permute-start.9 = (bf16[128,768]{1,0:T(8,128)(2,1)S(1)}, bf16[128,768]{1,0:T(8,128)(2,1)S(1)}, u32[]{:S(2)}, u32[]{:S(2)}) collective-permute-start(bf16[128,768]{1,0:T(8,128)(2,1)S(1)} %collective-permute-done.8.refs_6_), channel_id=1, source_target_pairs={{0,2},{2,0},{4,6},{6,4},{1,3},{3,1},{5,7},{7,5},{8,10},{10,8},{12,... | collective-permute-start | bytes 589832 | tf_op jit(solution)/shard_map/ppermute | solution.py:35

commit v9 on v7

--- a/solution.py
+++ b/solution.py
@@ -333,15 +333,14 @@
     )(*options)
 
 
-def weight_kernel(replicas, sizes, slots, split, blocks, *refs):
-    acts = refs[:replicas]
-    args = sum(sizes)
-    options = grouped(refs[replicas : replicas + args], sizes)
-    count = slots * (replicas - 1)
-    far = grouped(refs[replicas + args :], [2 if split else 1] * count)
+def weight_kernel(replicas, sizes, far_sizes, slots, blocks, *refs):
+    refs = list(refs)
+    acts = [refs.pop(0) for _ in range(replicas)]
+    options = grouped(refs, sizes)
+    far = grouped(refs[sum(sizes) :], far_sizes)
     out_ref, stacked = refs[-2:]
     step = pl.program_id(0)
-    chips = len(sizes)
+    chips = len(sizes) // 2
     seq = acts[0].shape[0]
     size = out_ref.shape[0]
 
@@ -351,7 +350,8 @@
             stacked[number * seq : (number + 1) * seq] = act[...]
 
     chip, _ = place()
-    for slot in range(slots):
+    for turn in range(2 * slots):
+        parity, slot = divmod(turn, slots)
         index = lax.rem(chip - (lax.axis_index("dp") * slots + slot) + chips, chips)
         for block in range(blocks):
 
@@ -359,15 +359,15 @@
                 piece, at = divmod(block * size, pieces[0].shape[1])
                 return pieces[piece][:, at : at + size]
 
-            @pl.when(step == slot * blocks + block)
+            @pl.when(step == turn * blocks + block)
             def _():
                 near = None
-                for number, pieces in enumerate(options):
+                for number, pieces in enumerate(options[parity * chips : (parity + 1) * chips]):
                     own = part(pieces)
                     near = own if near is None else jnp.where(index == number, own, near)
                 left = [near]
-                for pieces in far[slot * (replicas - 1) : (slot + 1) * (replicas - 1)]:
-                    if split:
+                for pieces in far[turn * (replicas - 1) : (turn + 1) * (replicas - 1)]:
+                    if len(pieces) == 2:
                         left.append(jnp.where(index == 1, part(pieces), part(pieces[::-1])))
                     else:
                         left.append(part(pieces))
@@ -375,35 +375,29 @@
                 out_ref[...] = dot(rows, stacked[...], ((0,), (0,))).astype(BF16)
 
 
-def weight_gradient(parity, acts, options, far, begun):
-    replicas, slots = len(acts), len(far)
-    split = len(far[0][0]) == 2
+def weight_gradient(acts, options, far):
+    replicas, slots = len(acts), len(far) // 2
+    far = [pieces for slot in far for pieces in slot]
     seq, columns = acts[0].shape
-    features = sum(piece.shape[1] for piece in far[0][0])
+    features = sum(piece.shape[1] for piece in far[0])
     blocks = max(counts(options))
     size = features // blocks
 
     def target(step):
-        core = lax.rem(lax.axis_index("st") + parity, 2)
-        return (2 * lax.div(step, blocks) + core) * blocks + lax.rem(step, blocks), 0
+        turn = lax.div(step, blocks)
+        core = lax.rem(lax.axis_index("st") + lax.div(turn, slots), 2)
+        return (2 * lax.rem(turn, slots) + core) * blocks + lax.rem(step, blocks), 0
 
     args = [*acts, *[piece for pieces in options for piece in pieces]]
-    args += [piece for slot in far for pieces in slot for piece in pieces]
-    specs = [VMEM] * len(args)
-    aliases = {}
-    if begun is not None:
-        aliases = {len(args): 0}
-        args.append(begun)
-        specs.append(ANY)
-    return pl.pallas_call(
-        functools.partial(weight_kernel, replicas, counts(options), slots, split, blocks),
+    args += [piece for pieces in far for piece in pieces]
+    return pl.pallas_call(
+        functools.partial(weight_kernel, replicas, counts(options), counts(far), slots, blocks),
         name="weight_gradient",
-        grid=(slots * blocks,),
-        in_specs=specs,
+        grid=(2 * slots * blocks,),
+        in_specs=[VMEM] * len(args),
         out_specs=pl.BlockSpec((size, columns), target),
         scratch_shapes=[pltpu.VMEM((replicas * seq, columns), BF16)],
         out_shape=jax.ShapeDtypeStruct((2 * slots * features, columns), BF16),
-        input_output_aliases=aliases,
         compiler_params=PARAMS,
     )(*args)
 
@@ -417,7 +411,7 @@
     pos = positions[0]
     weight = in_hbm(w_out[0])
     heads, _, width = qkv.shape[1:]
-    early = max(1, heads * 7 // 12)
+    early = max(1, heads * 8 // 12)
     late = heads - early
     shards = lax.axis_size("st")
     replicas = lax.axis_size("dp")
@@ -480,8 +474,7 @@
         cross_far.append(swapped)
 
     begun = early_backward(packed_above, d_above, heads)
-    grad_weight = weight_gradient(0, acts, same, near_far, None)
-    grad_weight = weight_gradient(1, acts, other, cross_far, grad_weight)
+    grad_weight = weight_gradient(acts, same + other, near_far + cross_far)
     upstream = fill(late_above, begun)
     return (grad_weight[None], upstream.transpose(0, 2, 1, 3)[None, None])
 

time: 55.8 us -> 49.1 us (0.88)
  waiting for transfers between devices: 20.7 us -> 14 us
  starting transfers between devices: 11.1 us -> 12.3 us
  Pallas kernels: 22.2 us -> 21.1 us
    ppermute x5, waiting for transfers between devices: 19.5 us -> 5.6 us  [rotate(): lax.ppermute(value, axis, [(i, (i + steps) % count) for i in range(count)])]
    ppermute x3, waiting for transfers between devices: 1.26 us -> 7.2 us  [down(): return lax.ppermute(value, axis, [(i, i - 1) for i in range(1, count)])]
    ppermute x5, waiting for transfers between devices: 0.01 us -> 1.22 us  [swap(): return lax.ppermute(value, axis, [(i, i ^ 1) for i in range(count)])]
    ppermute x5, starting transfers between devices: 6.57 us -> 7.59 us  [rotate(): lax.ppermute(value, axis, [(i, (i + steps) % count) for i in range(count)])]
    pallas_call x2 -> x1, Pallas kernels: 6.44 us -> 5.45 us  [weight_gradient(): pl.pallas_call(functools.partial(weight_kernel, replicas, counts(options)...]
where the time goes in v9:
time: 49.1 us; the launch traced here: 48.9 us
  Pallas kernels  21.1 us (43%)
  waiting for transfers between devices  14 us (29%)
  starting transfers between devices  12.3 us (25%)
  between operations  0.77 us (2%)
  local copies, waits for them, and re-layouts  0.76 us (2%)
    ppermute x5, starting transfers between devices, rotate(): lax.ppermute(value, axis, [(i, (i + steps) % count) for i in range(count)])  7.59 us
    ppermute x3, waiting for transfers between devices, down(): return lax.ppermute(value, axis, [(i, i - 1) for i in range(1, count)])  7.2 us
    pallas_call x1, Pallas kernels, forward(): pl.pallas_call(functools.partial(forward_kernel, chips, groups), name='fo...  6.98 us
    ppermute x5, waiting for transfers between devices, rotate(): lax.ppermute(value, axis, [(i, (i + steps) % count) for i in range(count)])  5.6 us
    pallas_call x1, Pallas kernels, weight_gradient(): pl.pallas_call(functools.partial(weight_kernel, replicas, counts(options)...  5.45 us
    ppermute x3, starting transfers between devices, down(): return lax.ppermute(value, axis, [(i, i - 1) for i in range(1, count)])  3.86 us
    pallas_call x1, Pallas kernels, early_backward(): pl.pallas_call(early_kernel, name='early_backward', in_specs=[VMEM] * 2,...  3.09 us
    pallas_call x2, Pallas kernels, project(): pl.pallas_call(functools.partial(project_kernel, tuple(terms), splits), n...  2.17 us
  transfers between devices with their start and end apart: 13, of which 5 were waited for; matrix products, arithmetic and copies ran while one was open for 0% of the time, Pallas kernels for 39%

profile of v9, /device:TPU:0, one launch (start us, length us, event | category | flops | bytes accessed | tf_op | source)
XLA Modules:
  0.0 48.9 jit_solution(17789585886848368808)
XLA Ops:
  0.6 1.3 %pack.1 = (bf16[3088,128]{1,0:T(8,128)(2,1)S(1)}, bf16[128,768]{1,0:T(8,128)(2,1)S(1)}, bf16[128,768]{1,0:T(8,128)(2,1)S(1)}) custom-call(s32[1,128]{1,0:T(1,128)} %bitcast.19, bf16[3,1536,128]{2,1,0:T(8,128)(2,1)} %bitcast.12, bf16[128,1536]{1,0:T(8,128)(2,1)} %bitcast.15), custom_call_target="tpu_custom_call" | custom-call | tf_op jit(solution)/shard_map/pack/pallas_call | solution.py:85
  1.9 3.1 %collective-permute-start.1 = (bf16[128,768]{1,0:T(8,128)(2,1)S(1)}, bf16[128,768]{1,0:T(8,128)(2,1)S(1)}, u32[]{:S(2)}, u32[]{:S(2)}) collective-permute-start(bf16[128,768]{1,0:T(8,128)(2,1)S(1)} %get-tuple-element.13), channel_id=1, source_target_pairs={{0,4},{2,6},{4,0},{6,2},{1,5},{3,7},{5,1},{7,3},{8,12},{10,14},{12... | collective-permute-start | bytes 589832 | tf_op jit(solution)/shard_map/ppermute | solution.py:30
  5.0 1.3 %collective-permute-start.11 = (bf16[3088,128]{1,0:T(8,128)(2,1)S(1)}, bf16[3088,128]{1,0:T(8,128)(2,1)S(1)}, u32[]{:S(2)}, u32[]{:S(2)}) collective-permute-start(bf16[3088,128]{1,0:T(8,128)(2,1)S(1)} %get-tuple-element.20), channel_id=1, source_target_pairs={{8,0},{16,8},{24,16},{9,1},{17,9},{25,17},{10,2},{18,10},{26,18},{... | collective-permute-start | bytes 2371592 | tf_op jit(solution)/shard_map/ppermute | solution.py:40
  6.3 0.1 collective-permute-start.3
  6.4 0.1 collective-permute-start.2
  6.5 3.9 %collective-permute-done.1.refs_1_.refs_3_.refs_4_ = bf16[128,768]{1,0:T(8,128)(2,1)S(1)} collective-permute-done((bf16[128,768]{1,0:T(8,128)(2,1)S(1)}, bf16[128,768]{1,0:T(8,128)(2,1)S(1)}, u32[]{:S(2)}, u32[]{:S(2)}) %collective-permute-start.1) | collective-permute-done | bytes 196640 | tf_op jit(solution)/shard_map/ppermute | solution.py:30
  10.3 0.0 collective-permute-start.4
  10.4 2.0 %collective-permute-start.6 = (bf16[128,768]{1,0:T(8,128)(2,1)S(1)}, bf16[128,768]{1,0:T(8,128)(2,1)S(1)}, u32[]{:S(2)}, u32[]{:S(2)}) collective-permute-start(bf16[128,768]{1,0:T(8,128)(2,1)S(1)} %choose.1), channel_id=1, source_target_pairs={{0,1},{1,0},{2,3},{3,2},{4,5},{5,4},{6,7},{7,6},{8,9},{9,8},{10,11... | collective-permute-start | bytes 589832 | tf_op jit(solution)/shard_map/ppermute | solution.py:30
  12.4 7.0 %forward.1 = (bf16[128,1536]{1,0:T(8,128)(2,1)S(1)}, f32[128,1536]{1,0:T(8,128)S(1)}, bf16[1536,1536]{1,0:T(8,128)(2,1)S(1)}, bf16[1536,1536]{1,0:T(8,128)(2,1)S(1)}, bf16[1536,1536]{1,0:T(8,128)(2,1)S(1)}) custom-call(s32[1,128]{1,0:T(1,128)} %bitcast.20, bf16[3,12,128,128]{3,2,1,0:T(8,128)(2,1)} %bitcast.13, bf16[6144,1536]{1,0:T(8,128)(2,1)} %bitcast.22, ...), custom_call_target="tpu_custom_call" | custom-call | tf_op jit(solution)/shard_map/forward/pallas_call | solution.py:151
  19.4 0.0 collective-permute-done.2.refs_4_.refs_5_
  19.4 0.1 collective-permute-start
  19.5 0.0 collective-permute-done.4.refs_6_
  19.5 0.2 collective-permute-start.5
  19.7 0.0 collective-permute-done.6.refs_8_
  19.7 2.3 %collective-permute-start.7 = (bf16[128,768]{1,0:T(8,128)(2,1)S(1)}, bf16[128,768]{1,0:T(8,128)(2,1)S(1)}, u32[]{:S(2)}, u32[]{:S(2)}) collective-permute-start(bf16[128,768]{1,0:T(8,128)(2,1)S(1)} %collective-permute-done.6.refs_8_), channel_id=1, source_target_pairs={{0,4},{2,6},{4,0},{6,2},{1,5},{3,7},{5,1},{7,3},{8,12},{10,14},{12... | collective-permute-start | bytes 589832 | tf_op jit(solution)/shard_map/ppermute | solution.py:30
  22.0 0.0 collective-permute-done.3.refs_5_.refs_3_
  22.0 1.7 %project.2.refs_2_ = f32[128,1536]{1,0:T(8,128)S(1)} custom-call(bf16[1536,1536]{1,0:T(8,128)(2,1)S(1)} %get-tuple-element.16.refs_0_, bf16[1536,1536]{1,0:T(8,128)(2,1)S(1)} %get-tuple-element.17.refs_1_, bf16[1536,1536]{1,0:T(8,128)(2,1)S(1)} %get-tuple-element.15.refs_2_.refs_0_, bf16[128,1536]{1,0:T(8,128)(2,1)S(1)} %collective-permute-done.3.refs_5_.refs_3_, ...), custom_call_target="tpu_custom_call" | custom-call | tf_op jit(solution)/shard_map/project/pallas_call | solution.py:293
  23.7 0.0 copy-start
  23.7 0.0 copy-start.2
  23.8 0.0 copy-start.1
  23.8 0.0 collective-permute-done.5.refs_7_.refs_1_
  23.8 0.5 project.3
  24.3 0.7 %copy-done = bf16[1,1,3,128,12,128]{5,3,4,2,1,0:T(8,128)(2,1)S(1)} copy-done((bf16[1,1,3,128,12,128]{5,3,4,2,1,0:T(8,128)(2,1)S(1)}, bf16[1,1,3,128,12,128]{5,3,4,2,1,0:T(8,128)(2,1)}, u32[]{:S(2)}) %copy-start) | copy-done | bytes 1179672
  25.0 0.0 copy-done.2
  25.0 1.3 %late_backward.1 = bf16[3,4,128,128]{3,2,1,0:T(8,128)(2,1)S(1)} custom-call(s32[1,128]{1,0:T(1,128)S(1)} %bitcast.21, bf16[3,12,128,128]{3,2,1,0:T(8,128)(2,1)S(1)} %bitcast.14, bf16[128,512]{1,0:T(8,128)(2,1)S(1)} %get-tuple-element.19.grad_ref), custom_call_target="tpu_custom_call" | custom-call | tf_op jit(solution)/shard_map/late_backward/pallas_call | solution.py:199
  26.4 1.3 %collective-permute-start.10 = (bf16[3,4,128,128]{3,2,1,0:T(8,128)(2,1)S(1)}, bf16[3,4,128,128]{3,2,1,0:T(8,128)(2,1)S(1)}, u32[]{:S(2)}, u32[]{:S(2)}) collective-permute-start(bf16[3,4,128,128]{3,2,1,0:T(8,128)(2,1)S(1)} %late_backward.1), channel_id=1, source_target_pairs={{8,0},{16,8},{24,16},{9,1},{17,9},{25,17},{10,2},{18,10},{26,18},{... | collective-permute-start | bytes 1179656 | tf_op jit(solution)/shard_map/ppermute | solution.py:40
  27.7 1.3 %collective-permute-start.12 = (bf16[128,1024]{1,0:T(8,128)(2,1)S(1)}, bf16[128,1024]{1,0:T(8,128)(2,1)S(1)}, u32[]{:S(2)}, u32[]{:S(2)}) collective-permute-start(bf16[128,1024]{1,0:T(8,128)(2,1)S(1)} %get-tuple-element.21), channel_id=1, source_target_pairs={{8,0},{16,8},{24,16},{9,1},{17,9},{25,17},{10,2},{18,10},{26,18},{... | collective-permute-start | bytes 786440 | tf_op jit(solution)/shard_map/ppermute | solution.py:40
  29.0 1.7 %collective-permute-done.refs_1_ = bf16[128,1536]{1,0:T(8,128)(2,1)S(1)} collective-permute-done((bf16[128,1536]{1,0:T(8,128)(2,1)S(1)}, bf16[128,1536]{1,0:T(8,128)(2,1)S(1)}, u32[]{:S(2)}, u32[]{:S(2)}) %collective-permute-start) | collective-permute-done | bytes 393248 | tf_op jit(solution)/shard_map/ppermute | solution.py:30
  30.7 0.0 collective-permute-start.8
  30.7 0.0 collective-permute-done.7.refs_9_
  30.7 0.5 %collective-permute-start.9 = (bf16[128,768]{1,0:T(8,128)(2,1)S(1)}, bf16[128,768]{1,0:T(8,128)(2,1)S(1)}, u32[]{:S(2)}, u32[]{:S(2)}) collective-permute-start(bf16[128,768]{1,0:T(8,128)(2,1)S(1)} %collective-permute-done.7.refs_9_), channel_id=1, source_target_pairs={{0,2},{2,0},{4,6},{6,4},{1,3},{3,1},{5,7},{7,5},{8,10},{10,8},{12,... | collective-permute-start | bytes 589832 | tf_op jit(solution)/shard_map/ppermute | solution.py:35
  31.2 0.9 %collective-permute-done.8.refs_10_ = bf16[128,768]{1,0:T(8,128)(2,1)S(1)} collective-permute-done((bf16[128,768]{1,0:T(8,128)(2,1)S(1)}, bf16[128,768]{1,0:T(8,128)(2,1)S(1)}, u32[]{:S(2)}, u32[]{:S(2)}) %collective-permute-start.8) | collective-permute-done | bytes 196640 | tf_op jit(solution)/shard_map/ppermute | solution.py:35
  32.1 0.3 collective-permute-done.9.refs_11_
  32.4 0.0 copy-done.1
  32.4 5.4 %weight_gradient.1 = bf16[3072,1536]{1,0:T(8,128)(2,1)} custom-call(bf16[128,1536]{1,0:T(8,128)(2,1)S(1)} %get-tuple-element.12.refs_0_, bf16[128,1536]{1,0:T(8,128)(2,1)S(1)} %collective-permute-done.refs_1_, bf16[128,1536]{1,0:T(8,128)(2,1)S(1)} %bitcast.18, bf16[128,768]{1,0:T(8,128)(2,1)S(1)} %collective-permute-done.1.refs_1_.refs_3_.refs_4_, ...), custom_call_target="tpu_custom_call" | custom-call | tf_op jit(solution)/shard_map/weight_gradient/pallas_call | solution.py:393
  37.8 7.2 %collective-permute-done.12.grad_ref = bf16[128,1024]{1,0:T(8,128)(2,1)S(1)} collective-permute-done((bf16[128,1024]{1,0:T(8,128)(2,1)S(1)}, bf16[128,1024]{1,0:T(8,128)(2,1)S(1)}, u32[]{:S(2)}, u32[]{:S(2)}) %collective-permute-start.12) | collective-permute-done | bytes 262176 | tf_op jit(solution)/shard_map/ppermute | solution.py:40
  45.0 0.0 collective-permute-done.11.packed_ref
  45.0 3.1 %early_backward.1.whole_ref = bf16[3,12,128,128]{3,2,1,0:T(8,128)(2,1)} custom-call(bf16[3088,128]{1,0:T(8,128)(2,1)S(1)} %collective-permute-done.11.packed_ref, bf16[128,1024]{1,0:T(8,128)(2,1)S(1)} %collective-permute-done.12.grad_ref), custom_call_target="tpu_custom_call" | custom-call | tf_op jit(solution)/shard_map/early_backward/pallas_call | solution.py:230
  48.1 0.0 collective-permute-done.10.late_ref
  48.2 0.8 %fill.1 = bf16[3,12,128,128]{3,2,1,0:T(8,128)(2,1)} custom-call(bf16[3,4,128,128]{3,2,1,0:T(8,128)(2,1)S(1)} %collective-permute-done.10.late_ref, bf16[3,12,128,128]{3,2,1,0:T(8,128)(2,1)} %early_backward.1.whole_ref), custom_call_target="tpu_custom_call", output_to_operand_aliasing={{}: (1, {})} | custom-call | tf_op jit(solution)/shard_map/fill/pallas_call | solution.py:258
  (1 shorter events, 0.0 us)
Async XLA Ops:
  1.9 8.4 %collective-permute-start.1 = (bf16[128,768]{1,0:T(8,128)(2,1)S(1)}, bf16[128,768]{1,0:T(8,128)(2,1)S(1)}, u32[]{:S(2)}, u32[]{:S(2)}) collective-permute-start(bf16[128,768]{1,0:T(8,128)(2,1)S(1)} %get-tuple-element.13), channel_id=1, source_target_pairs={{0,4},{2,6},{4,0},{6,2},{1,5},{3,7},{5,1},{7,3},{8,12},{10,14},{12... | collective-permute-start | bytes 589832 | tf_op jit(solution)/shard_map/ppermute | solution.py:30
  5.0 40.1 %collective-permute-start.11 = (bf16[3088,128]{1,0:T(8,128)(2,1)S(1)}, bf16[3088,128]{1,0:T(8,128)(2,1)S(1)}, u32[]{:S(2)}, u32[]{:S(2)}) collective-permute-start(bf16[3088,128]{1,0:T(8,128)(2,1)S(1)} %get-tuple-element.20), channel_id=1, source_target_pairs={{8,0},{16,8},{24,16},{9,1},{17,9},{25,17},{10,2},{18,10},{26,18},{... | collective-permute-start | bytes 2371592 | tf_op jit(solution)/shard_map/ppermute | solution.py:40
  6.3 15.7 %collective-permute-start.3 = (bf16[128,1536]{1,0:T(8,128)(2,1)}, bf16[128,1536]{1,0:T(8,128)(2,1)S(1)}, u32[]{:S(2)}, u32[]{:S(2)}) collective-permute-start(bf16[128,1536]{1,0:T(8,128)(2,1)} %bitcast.16), channel_id=1, source_target_pairs={{0,2},{2,0},{4,6},{6,4},{1,3},{3,1},{5,7},{7,5},{8,10},{10,8},{12,... | collective-permute-start | bytes 1179656 | tf_op jit(solution)/shard_map/ppermute | solution.py:35
  6.4 13.0 %collective-permute-start.2 = (bf16[128,768]{1,0:T(8,128)(2,1)S(1)}, bf16[128,768]{1,0:T(8,128)(2,1)S(1)}, u32[]{:S(2)}, u32[]{:S(2)}) collective-permute-start(bf16[128,768]{1,0:T(8,128)(2,1)S(1)} %get-tuple-element.14.refs_0_), channel_id=1, source_target_pairs={{0,4},{2,6},{4,0},{6,2},{1,5},{3,7},{5,1},{7,3},{8,12},{10,14},{12... | collective-permute-start | bytes 589832 | tf_op jit(solution)/shard_map/ppermute | solution.py:30
  10.3 9.2 %collective-permute-start.4 = (bf16[128,768]{1,0:T(8,128)(2,1)S(1)}, bf16[128,768]{1,0:T(8,128)(2,1)S(1)}, u32[]{:S(2)}, u32[]{:S(2)}) collective-permute-start(bf16[128,768]{1,0:T(8,128)(2,1)S(1)} %collective-permute-done.1.refs_1_.refs_3_.refs_4_), channel_id=1, source_target_pairs={{0,2},{2,0},{4,6},{6,4},{1,3},{3,1},{5,7},{7,5},{8,10},{10,8},{12,... | collective-permute-start | bytes 589832 | tf_op jit(solution)/shard_map/ppermute | solution.py:35
  10.4 9.4 %collective-permute-start.6 = (bf16[128,768]{1,0:T(8,128)(2,1)S(1)}, bf16[128,768]{1,0:T(8,128)(2,1)S(1)}, u32[]{:S(2)}, u32[]{:S(2)}) collective-permute-start(bf16[128,768]{1,0:T(8,128)(2,1)S(1)} %choose.1), channel_id=1, source_target_pairs={{0,1},{1,0},{2,3},{3,2},{4,5},{5,4},{6,7},{7,6},{8,9},{9,8},{10,11... | collective-permute-start | bytes 589832 | tf_op jit(solution)/shard_map/ppermute | solution.py:30
  19.4 11.3 %collective-permute-start = (bf16[128,1536]{1,0:T(8,128)(2,1)S(1)}, bf16[128,1536]{1,0:T(8,128)(2,1)S(1)}, u32[]{:S(2)}, u32[]{:S(2)}) collective-permute-start(bf16[128,1536]{1,0:T(8,128)(2,1)S(1)} %get-tuple-element.12.refs_0_), channel_id=1, source_target_pairs={{0,1},{1,0},{2,3},{3,2},{4,5},{5,4},{6,7},{7,6},{8,9},{9,8},{10,11... | collective-permute-start | bytes 1179656 | tf_op jit(solution)/shard_map/ppermute | solution.py:30
  19.5 4.3 %collective-permute-start.5 = (bf16[128,768]{1,0:T(8,128)(2,1)S(1)}, bf16[128,768]{1,0:T(8,128)(2,1)S(1)}, u32[]{:S(2)}, u32[]{:S(2)}) collective-permute-start(bf16[128,768]{1,0:T(8,128)(2,1)S(1)} %collective-permute-done.2.refs_4_.refs_5_), channel_id=1, source_target_pairs={{0,2},{2,0},{4,6},{6,4},{1,3},{3,1},{5,7},{7,5},{8,10},{10,8},{12,... | collective-permute-start | bytes 589832 | tf_op jit(solution)/shard_map/ppermute | solution.py:35
  19.7 10.9 %collective-permute-start.7 = (bf16[128,768]{1,0:T(8,128)(2,1)S(1)}, bf16[128,768]{1,0:T(8,128)(2,1)S(1)}, u32[]{:S(2)}, u32[]{:S(2)}) collective-permute-start(bf16[128,768]{1,0:T(8,128)(2,1)S(1)} %collective-permute-done.6.refs_8_), channel_id=1, source_target_pairs={{0,4},{2,6},{4,0},{6,2},{1,5},{3,7},{5,1},{7,3},{8,12},{10,14},{12... | collective-permute-start | bytes 589832 | tf_op jit(solution)/shard_map/ppermute | solution.py:30
  23.7 1.3 %copy-start = (bf16[1,1,3,128,12,128]{5,3,4,2,1,0:T(8,128)(2,1)S(1)}, bf16[1,1,3,128,12,128]{5,3,4,2,1,0:T(8,128)(2,1)}, u32[]{:S(2)}) copy-start(bf16[1,1,3,128,12,128]{5,3,4,2,1,0:T(8,128)(2,1)} %param.4) | copy-start | bytes 3538948
  23.7 1.3 %copy-start.2 = (s32[1,1,128]{2,1,0:T(1,128)S(1)}, s32[1,1,128]{2,1,0:T(1,128)}, u32[]{:S(2)}) copy-start(s32[1,1,128]{2,1,0:T(1,128)} %param.5) | copy-start | bytes 1540
  23.8 8.6 %copy-start.1 = (bf16[1,1,128,1536]{3,2,1,0:T(8,128)(2,1)S(1)}, bf16[1,1,128,1536]{3,2,1,0:T(8,128)(2,1)}, u32[]{:S(2)}) copy-start(bf16[1,1,128,1536]{3,2,1,0:T(8,128)(2,1)} %param.7) | copy-start | bytes 1179652
  26.4 21.8 %collective-permute-start.10 = (bf16[3,4,128,128]{3,2,1,0:T(8,128)(2,1)S(1)}, bf16[3,4,128,128]{3,2,1,0:T(8,128)(2,1)S(1)}, u32[]{:S(2)}, u32[]{:S(2)}) collective-permute-start(bf16[3,4,128,128]{3,2,1,0:T(8,128)(2,1)S(1)} %late_backward.1), channel_id=1, source_target_pairs={{8,0},{16,8},{24,16},{9,1},{17,9},{25,17},{10,2},{18,10},{26,18},{... | collective-permute-start | bytes 1179656 | tf_op jit(solution)/shard_map/ppermute | solution.py:40
  27.7 17.4 %collective-permute-start.12 = (bf16[128,1024]{1,0:T(8,128)(2,1)S(1)}, bf16[128,1024]{1,0:T(8,128)(2,1)S(1)}, u32[]{:S(2)}, u32[]{:S(2)}) collective-permute-start(bf16[128,1024]{1,0:T(8,128)(2,1)S(1)} %get-tuple-element.21), channel_id=1, source_target_pairs={{8,0},{16,8},{24,16},{9,1},{17,9},{25,17},{10,2},{18,10},{26,18},{... | collective-permute-start | bytes 786440 | tf_op jit(solution)/shard_map/ppermute | solution.py:40
  30.7 1.4 %collective-permute-start.8 = (bf16[128,768]{1,0:T(8,128)(2,1)S(1)}, bf16[128,768]{1,0:T(8,128)(2,1)S(1)}, u32[]{:S(2)}, u32[]{:S(2)}) collective-permute-start(bf16[128,768]{1,0:T(8,128)(2,1)S(1)} %collective-permute-done.6.refs_8_), channel_id=1, source_target_pairs={{0,2},{2,0},{4,6},{6,4},{1,3},{3,1},{5,7},{7,5},{8,10},{10,8},{12,... | collective-permute-start | bytes 589832 | tf_op jit(solution)/shard_map/ppermute | solution.py:35
  30.7 1.7 %collective-permute-start.9 = (bf16[128,768]{1,0:T(8,128)(2,1)S(1)}, bf16[128,768]{1,0:T(8,128)(2,1)S(1)}, u32[]{:S(2)}, u32[]{:S(2)}) collective-permute-start(bf16[128,768]{1,0:T(8,128)(2,1)S(1)} %collective-permute-done.7.refs_9_), channel_id=1, source_target_pairs={{0,2},{2,0},{4,6},{6,4},{1,3},{3,1},{5,7},{7,5},{8,10},{10,8},{12,... | collective-permute-start | bytes 589832 | tf_op jit(solution)/shard_map/ppermute | solution.py:35

commit v10 on v9

--- a/solution.py
+++ b/solution.py
@@ -206,41 +206,6 @@
     )(pos, qkv, grad)
 
 
-def early_kernel(packed_ref, grad_ref, out_ref, buffer, sems):
-    heads, seq, width = buffer.shape[1:]
-    visible = visibility(packed_ref[3 * heads * seq :][:1])
-    copies = []
-    for head in range(heads):
-        query, key, value = (
-            packed_ref[(i * heads + head) * seq : (i * heads + head + 1) * seq] for i in range(3)
-        )
-        grad = grad_ref[:, head * width : (head + 1) * width]
-        for i, result in enumerate(head_gradients(visible, query, key, value, grad)):
-            buffer[i, head] = result
-        copy = pltpu.make_async_copy(buffer.at[:, head], out_ref.at[:, head], sems.at[head])
-        copy.start()
-        copies.append(copy)
-    for copy in copies:
-        copy.wait()
-
-
-def early_backward(packed, grad, total):
-    seq, width = grad.shape[0], packed.shape[1]
-    heads = grad.shape[1] // width
-    return pl.pallas_call(
-        early_kernel,
-        name="early_backward",
-        in_specs=[VMEM] * 2,
-        out_specs=ANY,
-        out_shape=jax.ShapeDtypeStruct((3, total, seq, width), BF16),
-        scratch_shapes=[
-            pltpu.VMEM((3, heads, seq, width), BF16),
-            pltpu.SemaphoreType.DMA((heads,)),
-        ],
-        compiler_params=PARAMS,
-    )(packed, grad)
-
-
 def fill_kernel(late_ref, whole_ref, out_ref, sems):
     late = late_ref.shape[1]
     first = out_ref.shape[1] - late
@@ -333,73 +298,97 @@
     )(*options)
 
 
-def weight_kernel(replicas, sizes, far_sizes, slots, blocks, *refs):
+def finish_kernel(replicas, sizes, far_sizes, slots, blocks, packed_ref, grad_ref, *refs):
     refs = list(refs)
     acts = [refs.pop(0) for _ in range(replicas)]
     options = grouped(refs, sizes)
     far = grouped(refs[sum(sizes) :], far_sizes)
-    out_ref, stacked = refs[-2:]
-    step = pl.program_id(0)
+    out_ref, weight_ref, held, stacked, ready, head_sems, sems = refs[-7:]
+    heads, seq, width = held.shape[1:]
+    copies = []
+    visible = visibility(packed_ref[3 * heads * seq :][:1])
+    for head in range(heads):
+        query, key, value = (
+            packed_ref[(i * heads + head) * seq : (i * heads + head + 1) * seq] for i in range(3)
+        )
+        grad = grad_ref[:, head * width : (head + 1) * width]
+        for i, result in enumerate(head_gradients(visible, query, key, value, grad)):
+            held[i, head] = result
+        copies.append(
+            pltpu.make_async_copy(held.at[:, head], out_ref.at[:, head], head_sems.at[head])
+        )
+        copies[-1].start()
+
+    for number, act in enumerate(acts):
+        stacked[number * seq : (number + 1) * seq] = act[...]
+    chip, core = place()
     chips = len(sizes) // 2
-    seq = acts[0].shape[0]
-    size = out_ref.shape[0]
-
-    @pl.when(step == 0)
-    def _():
-        for number, act in enumerate(acts):
-            stacked[number * seq : (number + 1) * seq] = act[...]
-
-    chip, _ = place()
-    for turn in range(2 * slots):
+    size = ready.shape[1]
+    spans = [(turn, block * size, size) for turn in range(2 * slots) for block in range(blocks)]
+    if size % 256 == 0:
+        turn, first, _ = spans.pop()
+        spans += [(turn, first, size // 2), (turn, first + size // 2, size // 2)]
+    puts = []
+    for number, (turn, first, count) in enumerate(spans):
         parity, slot = divmod(turn, slots)
         index = lax.rem(chip - (lax.axis_index("dp") * slots + slot) + chips, chips)
-        for block in range(blocks):
-
-            def part(pieces):
-                piece, at = divmod(block * size, pieces[0].shape[1])
-                return pieces[piece][:, at : at + size]
-
-            @pl.when(step == turn * blocks + block)
-            def _():
-                near = None
-                for number, pieces in enumerate(options[parity * chips : (parity + 1) * chips]):
-                    own = part(pieces)
-                    near = own if near is None else jnp.where(index == number, own, near)
-                left = [near]
-                for pieces in far[turn * (replicas - 1) : (turn + 1) * (replicas - 1)]:
-                    if len(pieces) == 2:
-                        left.append(jnp.where(index == 1, part(pieces), part(pieces[::-1])))
-                    else:
-                        left.append(part(pieces))
-                rows = jnp.concatenate(left, axis=0)
-                out_ref[...] = dot(rows, stacked[...], ((0,), (0,))).astype(BF16)
-
-
-def weight_gradient(acts, options, far):
+
+        def part(pieces):
+            piece, at = divmod(first, pieces[0].shape[1])
+            return pieces[piece][:, at : at + count]
+
+        near = None
+        for option, pieces in enumerate(options[parity * chips : (parity + 1) * chips]):
+            own = part(pieces)
+            near = own if near is None else jnp.where(index == option, own, near)
+        left = [near]
+        for pieces in far[turn * (replicas - 1) : (turn + 1) * (replicas - 1)]:
+            if len(pieces) == 2:
+                left.append(jnp.where(index == 1, part(pieces), part(pieces[::-1])))
+            else:
+                left.append(part(pieces))
+        block = dot(jnp.concatenate(left, axis=0), stacked[...], ((0,), (0,))).astype(BF16)
+        if number >= 2:
+            puts[number - 2].wait()
+        place_in = ready.at[number % 2, pl.ds(0, count)]
+        place_in[...] = block
+        row = (2 * slot + lax.rem(core + parity, 2)) * (size * blocks) + first
+        target = weight_ref.at[pl.ds(pl.multiple_of(row, 128), count)]
+        puts.append(pltpu.make_async_copy(place_in, target, sems.at[number % 2]))
+        puts[-1].start()
+    for copy in copies + puts[-2:]:
+        copy.wait()
+
+
+def finish(packed, grad, total, acts, options, far):
+    seq, width = grad.shape[0], packed.shape[1]
+    heads = grad.shape[1] // width
     replicas, slots = len(acts), len(far) // 2
     far = [pieces for slot in far for pieces in slot]
-    seq, columns = acts[0].shape
+    columns = acts[0].shape[1]
     features = sum(piece.shape[1] for piece in far[0])
     blocks = max(counts(options))
     size = features // blocks
-
-    def target(step):
-        turn = lax.div(step, blocks)
-        core = lax.rem(lax.axis_index("st") + lax.div(turn, slots), 2)
-        return (2 * lax.rem(turn, slots) + core) * blocks + lax.rem(step, blocks), 0
-
     args = [*acts, *[piece for pieces in options for piece in pieces]]
     args += [piece for pieces in far for piece in pieces]
     return pl.pallas_call(
-        functools.partial(weight_kernel, replicas, counts(options), counts(far), slots, blocks),
-        name="weight_gradient",
-        grid=(2 * slots * blocks,),
-        in_specs=[VMEM] * len(args),
-        out_specs=pl.BlockSpec((size, columns), target),
-        scratch_shapes=[pltpu.VMEM((replicas * seq, columns), BF16)],
-        out_shape=jax.ShapeDtypeStruct((2 * slots * features, columns), BF16),
-        compiler_params=PARAMS,
-    )(*args)
+        functools.partial(finish_kernel, replicas, counts(options), counts(far), slots, blocks),
+        name="finish",
+        in_specs=[VMEM] * (2 + len(args)),
+        out_specs=[ANY, ANY],
+        out_shape=[
+            jax.ShapeDtypeStruct((3, total, seq, width), BF16),
+            jax.ShapeDtypeStruct((2 * slots * features, columns), BF16),
+        ],
+        scratch_shapes=[
+            pltpu.VMEM((3, heads, seq, width), BF16),
+            pltpu.VMEM((replicas * seq, columns), BF16),
+            pltpu.VMEM((2, size, columns), BF16),
+            pltpu.SemaphoreType.DMA((heads,)),
+            pltpu.SemaphoreType.DMA((2,)),
+        ],
+        compiler_params=PARAMS,
+    )(packed, grad, *args)
 
 
 def pieces_of(features):
@@ -473,8 +462,9 @@
         near_far.append(straight)
         cross_far.append(swapped)
 
-    begun = early_backward(packed_above, d_above, heads)
-    grad_weight = weight_gradient(acts, same + other, near_far + cross_far)
+    begun, grad_weight = finish(
+        packed_above, d_above, heads, acts, same + other, near_far + cross_far
+    )
     upstream = fill(late_above, begun)
     return (grad_weight[None], upstream.transpose(0, 2, 1, 3)[None, None])
 

time: 49.1 us -> 53.8 us (1.096)
  waiting for transfers between devices: 14 us -> 19.5 us
  Pallas kernels: 21.1 us -> 20.3 us
    ppermute x3, waiting for transfers between devices: 7.2 us -> 12.9 us  [down(): return lax.ppermute(value, axis, [(i, i - 1) for i in range(1, count)])]
    pallas_call x2 -> x1, Pallas kernels: 8.54 us -> 7.75 us  [finish(): pl.pallas_call(functools.partial(finish_kernel, replicas, counts(options)...]
  transfers between devices with their start and end apart: 13 -> 13, of which waited for: 5 -> 4; matrix products, arithmetic and copies ran while one was open for 0% -> 0% of each run, Pallas kernels for 39% -> 34%
where the time goes in v10:
time: 53.8 us; the launch traced here: 53.6 us
  Pallas kernels  20.3 us (38%)
  waiting for transfers between devices  19.5 us (36%)
  starting transfers between devices  12.3 us (23%)
  between operations  0.77 us (1%)
  local copies, waits for them, and re-layouts  0.76 us (1%)
    ppermute x3, waiting for transfers between devices, down(): return lax.ppermute(value, axis, [(i, i - 1) for i in range(1, count)])  12.9 us
    pallas_call x1, Pallas kernels, finish(): pl.pallas_call(functools.partial(finish_kernel, replicas, counts(options)...  7.75 us
    ppermute x5, starting transfers between devices, rotate(): lax.ppermute(value, axis, [(i, (i + steps) % count) for i in range(count)])  7.59 us
    pallas_call x1, Pallas kernels, forward(): pl.pallas_call(functools.partial(forward_kernel, chips, groups), name='fo...  6.98 us
    ppermute x5, waiting for transfers between devices, rotate(): lax.ppermute(value, axis, [(i, (i + steps) % count) for i in range(count)])  5.6 us
    ppermute x3, starting transfers between devices, down(): return lax.ppermute(value, axis, [(i, i - 1) for i in range(1, count)])  3.86 us
    pallas_call x2, Pallas kernels, project(): pl.pallas_call(functools.partial(project_kernel, tuple(terms), splits), n...  2.17 us
    pallas_call x1, Pallas kernels, late_backward(): pl.pallas_call(late_kernel, name='late_backward', in_specs=[VMEM] * 3, ou...  1.34 us
  transfers between devices with their start and end apart: 13, of which 4 were waited for; matrix products, arithmetic and copies ran while one was open for 0% of the time, Pallas kernels for 34%

profile of v10, /device:TPU:0, one launch (start us, length us, event | category | flops | bytes accessed | tf_op | source)
XLA Modules:
  0.0 53.6 jit_solution(6676516404949760253)
XLA Ops:
  0.6 1.3 %pack.1 = (bf16[3088,128]{1,0:T(8,128)(2,1)S(1)}, bf16[128,768]{1,0:T(8,128)(2,1)S(1)}, bf16[128,768]{1,0:T(8,128)(2,1)S(1)}) custom-call(s32[1,128]{1,0:T(1,128)} %bitcast.19, bf16[3,1536,128]{2,1,0:T(8,128)(2,1)} %bitcast.12, bf16[128,1536]{1,0:T(8,128)(2,1)} %bitcast.15), custom_call_target="tpu_custom_call" | custom-call | tf_op jit(solution)/shard_map/pack/pallas_call | solution.py:85
  1.9 3.1 %collective-permute-start.4 = (bf16[128,768]{1,0:T(8,128)(2,1)S(1)}, bf16[128,768]{1,0:T(8,128)(2,1)S(1)}, u32[]{:S(2)}, u32[]{:S(2)}) collective-permute-start(bf16[128,768]{1,0:T(8,128)(2,1)S(1)} %get-tuple-element.19), channel_id=1, source_target_pairs={{0,4},{2,6},{4,0},{6,2},{1,5},{3,7},{5,1},{7,3},{8,12},{10,14},{12... | collective-permute-start | bytes 589832 | tf_op jit(solution)/shard_map/ppermute | solution.py:30
  5.0 1.3 %collective-permute-start = (bf16[3088,128]{1,0:T(8,128)(2,1)S(1)}, bf16[3088,128]{1,0:T(8,128)(2,1)S(1)}, u32[]{:S(2)}, u32[]{:S(2)}) collective-permute-start(bf16[3088,128]{1,0:T(8,128)(2,1)S(1)} %get-tuple-element.14), channel_id=1, source_target_pairs={{8,0},{16,8},{24,16},{9,1},{17,9},{25,17},{10,2},{18,10},{26,18},{... | collective-permute-start | bytes 2371592 | tf_op jit(solution)/shard_map/ppermute | solution.py:40
  6.3 0.1 collective-permute-start.3
  6.4 0.1 collective-permute-start.1
  6.5 3.9 %collective-permute-done.4.refs_4_.refs_1_.refs_3_ = bf16[128,768]{1,0:T(8,128)(2,1)S(1)} collective-permute-done((bf16[128,768]{1,0:T(8,128)(2,1)S(1)}, bf16[128,768]{1,0:T(8,128)(2,1)S(1)}, u32[]{:S(2)}, u32[]{:S(2)}) %collective-permute-start.4) | collective-permute-done | bytes 196640 | tf_op jit(solution)/shard_map/ppermute | solution.py:30
  10.3 0.0 collective-permute-start.5
  10.4 2.0 %collective-permute-start.8 = (bf16[128,768]{1,0:T(8,128)(2,1)S(1)}, bf16[128,768]{1,0:T(8,128)(2,1)S(1)}, u32[]{:S(2)}, u32[]{:S(2)}) collective-permute-start(bf16[128,768]{1,0:T(8,128)(2,1)S(1)} %choose.1), channel_id=1, source_target_pairs={{0,1},{1,0},{2,3},{3,2},{4,5},{5,4},{6,7},{7,6},{8,9},{9,8},{10,11... | collective-permute-start | bytes 589832 | tf_op jit(solution)/shard_map/ppermute | solution.py:30
  12.4 7.0 %forward.1 = (bf16[128,1536]{1,0:T(8,128)(2,1)S(1)}, f32[128,1536]{1,0:T(8,128)S(1)}, bf16[1536,1536]{1,0:T(8,128)(2,1)S(1)}, bf16[1536,1536]{1,0:T(8,128)(2,1)S(1)}, bf16[1536,1536]{1,0:T(8,128)(2,1)S(1)}) custom-call(s32[1,128]{1,0:T(1,128)} %bitcast.20, bf16[3,12,128,128]{3,2,1,0:T(8,128)(2,1)} %bitcast.13, bf16[6144,1536]{1,0:T(8,128)(2,1)} %bitcast.22, ...), custom_call_target="tpu_custom_call" | custom-call | tf_op jit(solution)/shard_map/forward/pallas_call | solution.py:151
  19.4 0.0 collective-permute-done.1.refs_5_.refs_4_
  19.4 0.1 collective-permute-start.7
  19.5 0.0 collective-permute-done.5.refs_6_
  19.5 0.2 collective-permute-start.2
  19.7 0.0 collective-permute-done.8.refs_8_
  19.7 2.3 %collective-permute-start.9 = (bf16[128,768]{1,0:T(8,128)(2,1)S(1)}, bf16[128,768]{1,0:T(8,128)(2,1)S(1)}, u32[]{:S(2)}, u32[]{:S(2)}) collective-permute-start(bf16[128,768]{1,0:T(8,128)(2,1)S(1)} %collective-permute-done.8.refs_8_), channel_id=1, source_target_pairs={{0,4},{2,6},{4,0},{6,2},{1,5},{3,7},{5,1},{7,3},{8,12},{10,14},{12... | collective-permute-start | bytes 589832 | tf_op jit(solution)/shard_map/ppermute | solution.py:30
  22.0 0.0 collective-permute-done.3.refs_3_.refs_5_
  22.0 1.7 %project.2.refs_2_ = f32[128,1536]{1,0:T(8,128)S(1)} custom-call(bf16[1536,1536]{1,0:T(8,128)(2,1)S(1)} %get-tuple-element.17.refs_0_, bf16[1536,1536]{1,0:T(8,128)(2,1)S(1)} %get-tuple-element.18.refs_1_, bf16[1536,1536]{1,0:T(8,128)(2,1)S(1)} %get-tuple-element.15.refs_2_.refs_0_, bf16[128,1536]{1,0:T(8,128)(2,1)S(1)} %collective-permute-done.3.refs_3_.refs_5_, ...), custom_call_target="tpu_custom_call" | custom-call | tf_op jit(solution)/shard_map/project/pallas_call | solution.py:258
  23.7 0.0 copy-start
  23.7 0.0 copy-start.2
  23.8 0.0 copy-start.1
  23.8 0.0 collective-permute-done.2.refs_1_.refs_7_
  23.8 0.5 project.3
  24.3 0.7 %copy-done = bf16[1,1,3,128,12,128]{5,3,4,2,1,0:T(8,128)(2,1)S(1)} copy-done((bf16[1,1,3,128,12,128]{5,3,4,2,1,0:T(8,128)(2,1)S(1)}, bf16[1,1,3,128,12,128]{5,3,4,2,1,0:T(8,128)(2,1)}, u32[]{:S(2)}) %copy-start) | copy-done | bytes 1179672
  25.0 0.0 copy-done.2
  25.0 1.3 %late_backward.1 = bf16[3,4,128,128]{3,2,1,0:T(8,128)(2,1)S(1)} custom-call(s32[1,128]{1,0:T(1,128)S(1)} %bitcast.21, bf16[3,12,128,128]{3,2,1,0:T(8,128)(2,1)S(1)} %bitcast.14, bf16[128,512]{1,0:T(8,128)(2,1)S(1)} %get-tuple-element.24.grad_ref), custom_call_target="tpu_custom_call" | custom-call | tf_op jit(solution)/shard_map/late_backward/pallas_call | solution.py:199
  26.4 1.3 %collective-permute-start.12 = (bf16[3,4,128,128]{3,2,1,0:T(8,128)(2,1)S(1)}, bf16[3,4,128,128]{3,2,1,0:T(8,128)(2,1)S(1)}, u32[]{:S(2)}, u32[]{:S(2)}) collective-permute-start(bf16[3,4,128,128]{3,2,1,0:T(8,128)(2,1)S(1)} %late_backward.1), channel_id=1, source_target_pairs={{8,0},{16,8},{24,16},{9,1},{17,9},{25,17},{10,2},{18,10},{26,18},{... | collective-permute-start | bytes 1179656 | tf_op jit(solution)/shard_map/ppermute | solution.py:40
  27.7 1.3 %collective-permute-start.6 = (bf16[128,1024]{1,0:T(8,128)(2,1)S(1)}, bf16[128,1024]{1,0:T(8,128)(2,1)S(1)}, u32[]{:S(2)}, u32[]{:S(2)}) collective-permute-start(bf16[128,1024]{1,0:T(8,128)(2,1)S(1)} %get-tuple-element.21), channel_id=1, source_target_pairs={{8,0},{16,8},{24,16},{9,1},{17,9},{25,17},{10,2},{18,10},{26,18},{... | collective-permute-start | bytes 786440 | tf_op jit(solution)/shard_map/ppermute | solution.py:40
  29.0 1.7 %collective-permute-done.7.refs_1_ = bf16[128,1536]{1,0:T(8,128)(2,1)S(1)} collective-permute-done((bf16[128,1536]{1,0:T(8,128)(2,1)S(1)}, bf16[128,1536]{1,0:T(8,128)(2,1)S(1)}, u32[]{:S(2)}, u32[]{:S(2)}) %collective-permute-start.7) | collective-permute-done | bytes 393248 | tf_op jit(solution)/shard_map/ppermute | solution.py:30
  30.7 0.0 collective-permute-start.10
  30.7 0.0 collective-permute-done.9.refs_9_
  30.7 0.5 collective-permute-start.11
  31.2 0.9 %collective-permute-done.10.refs_10_ = bf16[128,768]{1,0:T(8,128)(2,1)S(1)} collective-permute-done((bf16[128,768]{1,0:T(8,128)(2,1)S(1)}, bf16[128,768]{1,0:T(8,128)(2,1)S(1)}, u32[]{:S(2)}, u32[]{:S(2)}) %collective-permute-start.10) | collective-permute-done | bytes 196640 | tf_op jit(solution)/shard_map/ppermute | solution.py:35
  32.1 12.9 %collective-permute-done.6.grad_ref = bf16[128,1024]{1,0:T(8,128)(2,1)S(1)} collective-permute-done((bf16[128,1024]{1,0:T(8,128)(2,1)S(1)}, bf16[128,1024]{1,0:T(8,128)(2,1)S(1)}, u32[]{:S(2)}, u32[]{:S(2)}) %collective-permute-start.6) | collective-permute-done | bytes 262176 | tf_op jit(solution)/shard_map/ppermute | solution.py:40
  45.0 0.0 collective-permute-done.11.refs_11_
  45.0 0.0 collective-permute-done.packed_ref
  45.1 0.0 copy-done.1
  45.1 7.7 %finish.1 = (bf16[3,12,128,128]{3,2,1,0:T(8,128)(2,1)}, bf16[3072,1536]{1,0:T(8,128)(2,1)}) custom-call(bf16[3088,128]{1,0:T(8,128)(2,1)S(1)} %collective-permute-done.packed_ref, bf16[128,1024]{1,0:T(8,128)(2,1)S(1)} %collective-permute-done.6.grad_ref, bf16[128,1536]{1,0:T(8,128)(2,1)S(1)} %get-tuple-element.22.refs_0_, ...), custom_call_target="tpu_custom_call" | custom-call | tf_op jit(solution)/shard_map/finish/pallas_call | solution.py:374
  52.8 0.0 collective-permute-done.12.late_ref
  52.8 0.8 %fill.1 = bf16[3,12,128,128]{3,2,1,0:T(8,128)(2,1)} custom-call(bf16[3,4,128,128]{3,2,1,0:T(8,128)(2,1)S(1)} %collective-permute-done.12.late_ref, bf16[3,12,128,128]{3,2,1,0:T(8,128)(2,1)} %get-tuple-element.25.whole_ref), custom_call_target="tpu_custom_call", output_to_operand_aliasing={{}: (1, {})} | custom-call | tf_op jit(solution)/shard_map/fill/pallas_call | solution.py:223
  (1 shorter events, 0.0 us)
Async XLA Ops:
  1.9 8.4 %collective-permute-start.4 = (bf16[128,768]{1,0:T(8,128)(2,1)S(1)}, bf16[128,768]{1,0:T(8,128)(2,1)S(1)}, u32[]{:S(2)}, u32[]{:S(2)}) collective-permute-start(bf16[128,768]{1,0:T(8,128)(2,1)S(1)} %get-tuple-element.19), channel_id=1, source_target_pairs={{0,4},{2,6},{4,0},{6,2},{1,5},{3,7},{5,1},{7,3},{8,12},{10,14},{12... | collective-permute-start | bytes 589832 | tf_op jit(solution)/shard_map/ppermute | solution.py:30
  5.0 40.1 %collective-permute-start = (bf16[3088,128]{1,0:T(8,128)(2,1)S(1)}, bf16[3088,128]{1,0:T(8,128)(2,1)S(1)}, u32[]{:S(2)}, u32[]{:S(2)}) collective-permute-start(bf16[3088,128]{1,0:T(8,128)(2,1)S(1)} %get-tuple-element.14), channel_id=1, source_target_pairs={{8,0},{16,8},{24,16},{9,1},{17,9},{25,17},{10,2},{18,10},{26,18},{... | collective-permute-start | bytes 2371592 | tf_op jit(solution)/shard_map/ppermute | solution.py:40
  6.3 15.7 %collective-permute-start.3 = (bf16[128,1536]{1,0:T(8,128)(2,1)}, bf16[128,1536]{1,0:T(8,128)(2,1)S(1)}, u32[]{:S(2)}, u32[]{:S(2)}) collective-permute-start(bf16[128,1536]{1,0:T(8,128)(2,1)} %bitcast.16), channel_id=1, source_target_pairs={{0,2},{2,0},{4,6},{6,4},{1,3},{3,1},{5,7},{7,5},{8,10},{10,8},{12,... | collective-permute-start | bytes 1179656 | tf_op jit(solution)/shard_map/ppermute | solution.py:35
  6.4 13.0 %collective-permute-start.1 = (bf16[128,768]{1,0:T(8,128)(2,1)S(1)}, bf16[128,768]{1,0:T(8,128)(2,1)S(1)}, u32[]{:S(2)}, u32[]{:S(2)}) collective-permute-start(bf16[128,768]{1,0:T(8,128)(2,1)S(1)} %get-tuple-element.16.refs_0_), channel_id=1, source_target_pairs={{0,4},{2,6},{4,0},{6,2},{1,5},{3,7},{5,1},{7,3},{8,12},{10,14},{12... | collective-permute-start | bytes 589832 | tf_op jit(solution)/shard_map/ppermute | solution.py:30
  10.3 9.2 %collective-permute-start.5 = (bf16[128,768]{1,0:T(8,128)(2,1)S(1)}, bf16[128,768]{1,0:T(8,128)(2,1)S(1)}, u32[]{:S(2)}, u32[]{:S(2)}) collective-permute-start(bf16[128,768]{1,0:T(8,128)(2,1)S(1)} %collective-permute-done.4.refs_4_.refs_1_.refs_3_), channel_id=1, source_target_pairs={{0,2},{2,0},{4,6},{6,4},{1,3},{3,1},{5,7},{7,5},{8,10},{10,8},{12,... | collective-permute-start | bytes 589832 | tf_op jit(solution)/shard_map/ppermute | solution.py:35
  10.4 9.4 %collective-permute-start.8 = (bf16[128,768]{1,0:T(8,128)(2,1)S(1)}, bf16[128,768]{1,0:T(8,128)(2,1)S(1)}, u32[]{:S(2)}, u32[]{:S(2)}) collective-permute-start(bf16[128,768]{1,0:T(8,128)(2,1)S(1)} %choose.1), channel_id=1, source_target_pairs={{0,1},{1,0},{2,3},{3,2},{4,5},{5,4},{6,7},{7,6},{8,9},{9,8},{10,11... | collective-permute-start | bytes 589832 | tf_op jit(solution)/shard_map/ppermute | solution.py:30
  19.4 11.3 %collective-permute-start.7 = (bf16[128,1536]{1,0:T(8,128)(2,1)S(1)}, bf16[128,1536]{1,0:T(8,128)(2,1)S(1)}, u32[]{:S(2)}, u32[]{:S(2)}) collective-permute-start(bf16[128,1536]{1,0:T(8,128)(2,1)S(1)} %get-tuple-element.22.refs_0_), channel_id=1, source_target_pairs={{0,1},{1,0},{2,3},{3,2},{4,5},{5,4},{6,7},{7,6},{8,9},{9,8},{10,11... | collective-permute-start | bytes 1179656 | tf_op jit(solution)/shard_map/ppermute | solution.py:30
  19.5 4.3 %collective-permute-start.2 = (bf16[128,768]{1,0:T(8,128)(2,1)S(1)}, bf16[128,768]{1,0:T(8,128)(2,1)S(1)}, u32[]{:S(2)}, u32[]{:S(2)}) collective-permute-start(bf16[128,768]{1,0:T(8,128)(2,1)S(1)} %collective-permute-done.1.refs_5_.refs_4_), channel_id=1, source_target_pairs={{0,2},{2,0},{4,6},{6,4},{1,3},{3,1},{5,7},{7,5},{8,10},{10,8},{12,... | collective-permute-start | bytes 589832 | tf_op jit(solution)/shard_map/ppermute | solution.py:35
  19.7 10.9 %collective-permute-start.9 = (bf16[128,768]{1,0:T(8,128)(2,1)S(1)}, bf16[128,768]{1,0:T(8,128)(2,1)S(1)}, u32[]{:S(2)}, u32[]{:S(2)}) collective-permute-start(bf16[128,768]{1,0:T(8,128)(2,1)S(1)} %collective-permute-done.8.refs_8_), channel_id=1, source_target_pairs={{0,4},{2,6},{4,0},{6,2},{1,5},{3,7},{5,1},{7,3},{8,12},{10,14},{12... | collective-permute-start | bytes 589832 | tf_op jit(solution)/shard_map/ppermute | solution.py:30
  23.7 1.3 %copy-start = (bf16[1,1,3,128,12,128]{5,3,4,2,1,0:T(8,128)(2,1)S(1)}, bf16[1,1,3,128,12,128]{5,3,4,2,1,0:T(8,128)(2,1)}, u32[]{:S(2)}) copy-start(bf16[1,1,3,128,12,128]{5,3,4,2,1,0:T(8,128)(2,1)} %param.4) | copy-start | bytes 3538948
  23.7 1.3 %copy-start.2 = (s32[1,1,128]{2,1,0:T(1,128)S(1)}, s32[1,1,128]{2,1,0:T(1,128)}, u32[]{:S(2)}) copy-start(s32[1,1,128]{2,1,0:T(1,128)} %param.5) | copy-start | bytes 1540
  23.8 21.3 %copy-start.1 = (bf16[1,1,128,1536]{3,2,1,0:T(8,128)(2,1)S(1)}, bf16[1,1,128,1536]{3,2,1,0:T(8,128)(2,1)}, u32[]{:S(2)}) copy-start(bf16[1,1,128,1536]{3,2,1,0:T(8,128)(2,1)} %param.7) | copy-start | bytes 1179652
  26.4 26.5 %collective-permute-start.12 = (bf16[3,4,128,128]{3,2,1,0:T(8,128)(2,1)S(1)}, bf16[3,4,128,128]{3,2,1,0:T(8,128)(2,1)S(1)}, u32[]{:S(2)}, u32[]{:S(2)}) collective-permute-start(bf16[3,4,128,128]{3,2,1,0:T(8,128)(2,1)S(1)} %late_backward.1), channel_id=1, source_target_pairs={{8,0},{16,8},{24,16},{9,1},{17,9},{25,17},{10,2},{18,10},{26,18},{... | collective-permute-start | bytes 1179656 | tf_op jit(solution)/shard_map/ppermute | solution.py:40
  27.7 17.4 %collective-permute-start.6 = (bf16[128,1024]{1,0:T(8,128)(2,1)S(1)}, bf16[128,1024]{1,0:T(8,128)(2,1)S(1)}, u32[]{:S(2)}, u32[]{:S(2)}) collective-permute-start(bf16[128,1024]{1,0:T(8,128)(2,1)S(1)} %get-tuple-element.21), channel_id=1, source_target_pairs={{8,0},{16,8},{24,16},{9,1},{17,9},{25,17},{10,2},{18,10},{26,18},{... | collective-permute-start | bytes 786440 | tf_op jit(solution)/shard_map/ppermute | solution.py:40
  30.7 1.4 %collective-permute-start.10 = (bf16[128,768]{1,0:T(8,128)(2,1)S(1)}, bf16[128,768]{1,0:T(8,128)(2,1)S(1)}, u32[]{:S(2)}, u32[]{:S(2)}) collective-permute-start(bf16[128,768]{1,0:T(8,128)(2,1)S(1)} %collective-permute-done.8.refs_8_), channel_id=1, source_target_pairs={{0,2},{2,0},{4,6},{6,4},{1,3},{3,1},{5,7},{7,5},{8,10},{10,8},{12,... | collective-permute-start | bytes 589832 | tf_op jit(solution)/shard_map/ppermute | solution.py:35
  30.7 14.4 %collective-permute-start.11 = (bf16[128,768]{1,0:T(8,128)(2,1)S(1)}, bf16[128,768]{1,0:T(8,128)(2,1)S(1)}, u32[]{:S(2)}, u32[]{:S(2)}) collective-permute-start(bf16[128,768]{1,0:T(8,128)(2,1)S(1)} %collective-permute-done.9.refs_9_), channel_id=1, source_target_pairs={{0,2},{2,0},{4,6},{6,4},{1,3},{3,1},{5,7},{7,5},{8,10},{10,8},{12,... | collective-permute-start | bytes 589832 | tf_op jit(solution)/shard_map/ppermute | solution.py:35

commit v11 on v10

--- a/solution.py
+++ b/solution.py
@@ -298,12 +298,54 @@
     )(*options)
 
 
-def finish_kernel(replicas, sizes, far_sizes, slots, blocks, packed_ref, grad_ref, *refs):
+def write_rows(parity, replicas, sizes, far_sizes, slots, blocks, refs, out_ref, scratch):
     refs = list(refs)
     acts = [refs.pop(0) for _ in range(replicas)]
     options = grouped(refs, sizes)
     far = grouped(refs[sum(sizes) :], far_sizes)
-    out_ref, weight_ref, held, stacked, ready, head_sems, sems = refs[-7:]
+    stacked, ready, sems = scratch
+    seq = acts[0].shape[0]
+    for number, act in enumerate(acts):
+        stacked[number * seq : (number + 1) * seq] = act[...]
+    chip, core = place()
+    chips = len(sizes)
+    size = ready.shape[1]
+    spans = [(slot, block * size, size) for slot in range(slots) for block in range(blocks)]
+    if parity and size % 256 == 0:
+        slot, first, _ = spans.pop()
+        spans += [(slot, first, size // 2), (slot, first + size // 2, size // 2)]
+    puts = []
+    for number, (slot, first, count) in enumerate(spans):
+        index = lax.rem(chip - (lax.axis_index("dp") * slots + slot) + chips, chips)
+
+        def part(pieces):
+            piece, at = divmod(first, pieces[0].shape[1])
+            return pieces[piece][:, at : at + count]
+
+        near = None
+        for option, pieces in enumerate(options):
+            own = part(pieces)
+            near = own if near is None else jnp.where(index == option, own, near)
+        left = [near]
+        for pieces in far[slot * (replicas - 1) : (slot + 1) * (replicas - 1)]:
+            if len(pieces) == 2:
+                left.append(jnp.where(index == 1, part(pieces), part(pieces[::-1])))
+            else:
+                left.append(part(pieces))
+        block = dot(jnp.concatenate(left, axis=0), stacked[...], ((0,), (0,))).astype(BF16)
+        if number >= 2:
+            puts[number - 2].wait()
+        place_in = ready.at[number % 2, pl.ds(0, count)]
+        place_in[...] = block
+        row = (2 * slot + lax.rem(core + parity, 2)) * (size * blocks) + first
+        target = out_ref.at[pl.ds(pl.multiple_of(row, 128), count)]
+        puts.append(pltpu.make_async_copy(place_in, target, sems.at[number % 2]))
+        puts[-1].start()
+    return puts[-2:]
+
+
+def finish_kernel(setting, packed_ref, grad_ref, *refs):
+    args, (out_ref, weight_ref, held, head_sems), scratch = refs[:-7], refs[-7:-3], refs[-3:]
     heads, seq, width = held.shape[1:]
     copies = []
     visible = visibility(packed_ref[3 * heads * seq :][:1])
@@ -318,77 +360,65 @@
             pltpu.make_async_copy(held.at[:, head], out_ref.at[:, head], head_sems.at[head])
         )
         copies[-1].start()
-
-    for number, act in enumerate(acts):
-        stacked[number * seq : (number + 1) * seq] = act[...]
-    chip, core = place()
-    chips = len(sizes) // 2
-    size = ready.shape[1]
-    spans = [(turn, block * size, size) for turn in range(2 * slots) for block in range(blocks)]
-    if size % 256 == 0:
-        turn, first, _ = spans.pop()
-        spans += [(turn, first, size // 2), (turn, first + size // 2, size // 2)]
-    puts = []
-    for number, (turn, first, count) in enumerate(spans):
-        parity, slot = divmod(turn, slots)
-        index = lax.rem(chip - (lax.axis_index("dp") * slots + slot) + chips, chips)
-
-        def part(pieces):
-            piece, at = divmod(first, pieces[0].shape[1])
-            return pieces[piece][:, at : at + count]
-
-        near = None
-        for option, pieces in enumerate(options[parity * chips : (parity + 1) * chips]):
-            own = part(pieces)
-            near = own if near is None else jnp.where(index == option, own, near)
-        left = [near]
-        for pieces in far[turn * (replicas - 1) : (turn + 1) * (replicas - 1)]:
-            if len(pieces) == 2:
-                left.append(jnp.where(index == 1, part(pieces), part(pieces[::-1])))
-            else:
-                left.append(part(pieces))
-        block = dot(jnp.concatenate(left, axis=0), stacked[...], ((0,), (0,))).astype(BF16)
-        if number >= 2:
-            puts[number - 2].wait()
-        place_in = ready.at[number % 2, pl.ds(0, count)]
-        place_in[...] = block
-        row = (2 * slot + lax.rem(core + parity, 2)) * (size * blocks) + first
-        target = weight_ref.at[pl.ds(pl.multiple_of(row, 128), count)]
-        puts.append(pltpu.make_async_copy(place_in, target, sems.at[number % 2]))
-        puts[-1].start()
-    for copy in copies + puts[-2:]:
+    copies += write_rows(0, *setting, args, weight_ref, scratch)
+    for copy in copies:
         copy.wait()
+
+
+def complete_kernel(setting, *refs):
+    args, weight_ref, scratch = refs[:-5], refs[-4], refs[-3:]
+    for copy in write_rows(1, *setting, args, weight_ref, scratch):
+        copy.wait()
+
+
+def weight_call(acts, options, far):
+    replicas, slots = len(acts), len(far)
+    far = [pieces for slot in far for pieces in slot]
+    seq, columns = acts[0].shape
+    features = sum(piece.shape[1] for piece in far[0])
+    blocks = max(counts(options))
+    args = [*acts, *[piece for pieces in options for piece in pieces]]
+    args += [piece for pieces in far for piece in pieces]
+    scratch = [
+        pltpu.VMEM((replicas * seq, columns), BF16),
+        pltpu.VMEM((2, features // blocks, columns), BF16),
+        pltpu.SemaphoreType.DMA((2,)),
+    ]
+    setting = (replicas, counts(options), counts(far), slots, blocks)
+    return setting, args, scratch, jax.ShapeDtypeStruct((2 * slots * features, columns), BF16)
 
 
 def finish(packed, grad, total, acts, options, far):
     seq, width = grad.shape[0], packed.shape[1]
     heads = grad.shape[1] // width
-    replicas, slots = len(acts), len(far) // 2
-    far = [pieces for slot in far for pieces in slot]
-    columns = acts[0].shape[1]
-    features = sum(piece.shape[1] for piece in far[0])
-    blocks = max(counts(options))
-    size = features // blocks
-    args = [*acts, *[piece for pieces in options for piece in pieces]]
-    args += [piece for pieces in far for piece in pieces]
-    return pl.pallas_call(
-        functools.partial(finish_kernel, replicas, counts(options), counts(far), slots, blocks),
+    setting, args, scratch, shape = weight_call(acts, options, far)
+    return pl.pallas_call(
+        functools.partial(finish_kernel, setting),
         name="finish",
         in_specs=[VMEM] * (2 + len(args)),
         out_specs=[ANY, ANY],
-        out_shape=[
-            jax.ShapeDtypeStruct((3, total, seq, width), BF16),
-            jax.ShapeDtypeStruct((2 * slots * features, columns), BF16),
-        ],
+        out_shape=[jax.ShapeDtypeStruct((3, total, seq, width), BF16), shape],
         scratch_shapes=[
             pltpu.VMEM((3, heads, seq, width), BF16),
-            pltpu.VMEM((replicas * seq, columns), BF16),
-            pltpu.VMEM((2, size, columns), BF16),
             pltpu.SemaphoreType.DMA((heads,)),
-            pltpu.SemaphoreType.DMA((2,)),
+            *scratch,
         ],
         compiler_params=PARAMS,
     )(packed, grad, *args)
+
+
+def complete(acts, options, far, begun):
+    setting, args, scratch, shape = weight_call(acts, options, far)
+    return pl.pallas_call(
+        functools.partial(complete_kernel, setting),
+        name="complete",
+        in_specs=[VMEM] * len(args) + [ANY],
+        out_specs=ANY,
+        out_shape=shape,
+        scratch_shapes=scratch,
+        input_output_aliases={len(args): 0},
+        compiler_params=PARAMS,
+    )(*args, begun)
 
 
 def pieces_of(features):
@@ -462,9 +492,8 @@
         near_far.append(straight)
         cross_far.append(swapped)
 
-    begun, grad_weight = finish(
-        packed_above, d_above, heads, acts, same + other, near_far + cross_far
-    )
+    begun, grad_weight = finish(packed_above, d_above, heads, acts, same, near_far)
+    grad_weight = complete(acts, other, cross_far, grad_weight)
     upstream = fill(late_above, begun)
     return (grad_weight[None], upstream.transpose(0, 2, 1, 3)[None, None])
 

time: 53.8 us -> 57.8 us (1.074)
  waiting for transfers between devices: 19.5 us -> 23.7 us
  starting transfers between devices: 12.3 us -> 11.1 us
  Pallas kernels: 20.3 us -> 21.3 us
    ppermute x5, waiting for transfers between devices: 5.6 us -> 19 us  [rotate(): lax.ppermute(value, axis, [(i, (i + steps) % count) for i in range(count)])]
    ppermute x3, waiting for transfers between devices: 12.9 us -> 4.75 us  [down(): return lax.ppermute(value, axis, [(i, i - 1) for i in range(1, count)])]
    pallas_call x1 -> x2, Pallas kernels: 7.75 us -> 8.68 us  [the longest x1 5.3 us: finish(): pl.pallas_call(functools.partial(finish_kernel, setting), name='finish',...]
    ppermute x5, waiting for transfers between devices: 0.94 us -> 0.01 us  [swap(): return lax.ppermute(value, axis, [(i, i ^ 1) for i in range(count)])]
    ppermute x5, starting transfers between devices: 0.81 us -> 0.15 us  [swap(): return lax.ppermute(value, axis, [(i, i ^ 1) for i in range(count)])]
  transfers between devices with their start and end apart: 13 -> 13, of which waited for: 4 -> 5; matrix products, arithmetic and copies ran while one was open for 0% -> 0% of each run, Pallas kernels for 34% -> 29%
where the time goes in v11:
time: 57.8 us; the launch traced here: 57.6 us
  waiting for transfers between devices  23.7 us (41%)
  Pallas kernels  21.3 us (37%)
  starting transfers between devices  11.1 us (19%)
  between operations  0.8 us (1%)
  local copies, waits for them, and re-layouts  0.76 us (1%)
    ppermute x5, waiting for transfers between devices, rotate(): lax.ppermute(value, axis, [(i, (i + steps) % count) for i in range(count)])  19 us
    ppermute x5, starting transfers between devices, rotate(): lax.ppermute(value, axis, [(i, (i + steps) % count) for i in range(count)])  7.05 us
    pallas_call x1, Pallas kernels, forward(): pl.pallas_call(functools.partial(forward_kernel, chips, groups), name='fo...  6.98 us
    pallas_call x1, Pallas kernels, finish(): pl.pallas_call(functools.partial(finish_kernel, setting), name='finish',...  5.3 us
    ppermute x3, waiting for transfers between devices, down(): return lax.ppermute(value, axis, [(i, i - 1) for i in range(1, count)])  4.75 us
    ppermute x3, starting transfers between devices, down(): return lax.ppermute(value, axis, [(i, i - 1) for i in range(1, count)])  3.85 us
    pallas_call x1, Pallas kernels, complete(): pl.pallas_call(functools.partial(complete_kernel, setting), name='complet...  3.38 us
    pallas_call x2, Pallas kernels, project(): pl.pallas_call(functools.partial(project_kernel, tuple(terms), splits), n...  2.18 us
  transfers between devices with their start and end apart: 13, of which 5 were waited for; matrix products, arithmetic and copies ran while one was open for 0% of the time, Pallas kernels for 29%

profile of v11, /device:TPU:0, one launch (start us, length us, event | category | flops | bytes accessed | tf_op | source)
XLA Modules:
  0.0 57.6 jit_solution(9971656653246501096)
XLA Ops:
  0.6 1.3 %pack.1 = (bf16[3088,128]{1,0:T(8,128)(2,1)S(1)}, bf16[128,768]{1,0:T(8,128)(2,1)S(1)}, bf16[128,768]{1,0:T(8,128)(2,1)S(1)}) custom-call(s32[1,128]{1,0:T(1,128)} %bitcast.19, bf16[3,1536,128]{2,1,0:T(8,128)(2,1)} %bitcast.12, bf16[128,1536]{1,0:T(8,128)(2,1)} %bitcast.15), custom_call_target="tpu_custom_call" | custom-call | tf_op jit(solution)/shard_map/pack/pallas_call | solution.py:85
  1.9 3.1 %collective-permute-start.2 = (bf16[128,768]{1,0:T(8,128)(2,1)S(1)}, bf16[128,768]{1,0:T(8,128)(2,1)S(1)}, u32[]{:S(2)}, u32[]{:S(2)}) collective-permute-start(bf16[128,768]{1,0:T(8,128)(2,1)S(1)} %get-tuple-element.15), channel_id=1, source_target_pairs={{0,4},{2,6},{4,0},{6,2},{1,5},{3,7},{5,1},{7,3},{8,12},{10,14},{12... | collective-permute-start | bytes 589832 | tf_op jit(solution)/shard_map/ppermute | solution.py:30
  5.0 1.3 %collective-permute-start.10 = (bf16[3088,128]{1,0:T(8,128)(2,1)S(1)}, bf16[3088,128]{1,0:T(8,128)(2,1)S(1)}, u32[]{:S(2)}, u32[]{:S(2)}) collective-permute-start(bf16[3088,128]{1,0:T(8,128)(2,1)S(1)} %get-tuple-element.17), channel_id=1, source_target_pairs={{8,0},{16,8},{24,16},{9,1},{17,9},{25,17},{10,2},{18,10},{26,18},{... | collective-permute-start | bytes 2371592 | tf_op jit(solution)/shard_map/ppermute | solution.py:40
  6.3 0.1 collective-permute-start.1
  6.4 0.1 collective-permute-start.4
  6.5 3.9 %collective-permute-done.2.refs_1_.refs_4_.refs_3_ = bf16[128,768]{1,0:T(8,128)(2,1)S(1)} collective-permute-done((bf16[128,768]{1,0:T(8,128)(2,1)S(1)}, bf16[128,768]{1,0:T(8,128)(2,1)S(1)}, u32[]{:S(2)}, u32[]{:S(2)}) %collective-permute-start.2) | collective-permute-done | bytes 196640 | tf_op jit(solution)/shard_map/ppermute | solution.py:30
  10.3 0.0 collective-permute-start.3
  10.3 3.8 %collective-permute-done.4.refs_5_.refs_4_ = bf16[128,768]{1,0:T(8,128)(2,1)S(1)} collective-permute-done((bf16[128,768]{1,0:T(8,128)(2,1)S(1)}, bf16[128,768]{1,0:T(8,128)(2,1)S(1)}, u32[]{:S(2)}, u32[]{:S(2)}) %collective-permute-start.4) | collective-permute-done | bytes 196640 | tf_op jit(solution)/shard_map/ppermute | solution.py:30
  14.1 0.0 collective-permute-start.5
  14.1 7.0 %forward.1 = (bf16[128,1536]{1,0:T(8,128)(2,1)S(1)}, f32[128,1536]{1,0:T(8,128)S(1)}, bf16[1536,1536]{1,0:T(8,128)(2,1)S(1)}, bf16[1536,1536]{1,0:T(8,128)(2,1)S(1)}, bf16[1536,1536]{1,0:T(8,128)(2,1)S(1)}) custom-call(s32[1,128]{1,0:T(1,128)} %bitcast.20, bf16[3,12,128,128]{3,2,1,0:T(8,128)(2,1)} %bitcast.13, bf16[6144,1536]{1,0:T(8,128)(2,1)} %bitcast.22, ...), custom_call_target="tpu_custom_call" | custom-call | tf_op jit(solution)/shard_map/forward/pallas_call | solution.py:151
  21.1 1.8 %collective-permute-start = (bf16[128,1536]{1,0:T(8,128)(2,1)S(1)}, bf16[128,1536]{1,0:T(8,128)(2,1)S(1)}, u32[]{:S(2)}, u32[]{:S(2)}) collective-permute-start(bf16[128,1536]{1,0:T(8,128)(2,1)S(1)} %get-tuple-element.14.refs_0_), channel_id=1, source_target_pairs={{0,1},{1,0},{2,3},{3,2},{4,5},{5,4},{6,7},{7,6},{8,9},{9,8},{10,11... | collective-permute-start | bytes 1179656 | tf_op jit(solution)/shard_map/ppermute | solution.py:30
  22.9 0.0 collective-permute-done.3.refs_6_.refs_3_
  22.9 0.4 collective-permute-start.6
  23.3 0.0 collective-permute-done.1.refs_3_.refs_2_
  23.3 1.7 %project.2.refs_2_ = f32[128,1536]{1,0:T(8,128)S(1)} custom-call(bf16[1536,1536]{1,0:T(8,128)(2,1)S(1)} %get-tuple-element.19.refs_0_, bf16[1536,1536]{1,0:T(8,128)(2,1)S(1)} %get-tuple-element.20.refs_1_, bf16[1536,1536]{1,0:T(8,128)(2,1)S(1)} %get-tuple-element.18.refs_2_.refs_0_, bf16[128,1536]{1,0:T(8,128)(2,1)S(1)} %collective-permute-done.1.refs_3_.refs_2_, ...), custom_call_target="tpu_custom_call" | custom-call | tf_op jit(solution)/shard_map/project/pallas_call | solution.py:258
  25.0 0.0 copy-start
  25.0 0.0 copy-start.2
  25.0 0.0 copy-start.1
  25.0 0.0 collective-permute-done.5.refs_1_.refs_4_
  25.1 0.5 project.3
  25.5 0.7 %copy-done = bf16[1,1,3,128,12,128]{5,3,4,2,1,0:T(8,128)(2,1)S(1)} copy-done((bf16[1,1,3,128,12,128]{5,3,4,2,1,0:T(8,128)(2,1)S(1)}, bf16[1,1,3,128,12,128]{5,3,4,2,1,0:T(8,128)(2,1)}, u32[]{:S(2)}) %copy-start) | copy-done | bytes 1179672
  26.3 0.0 copy-done.2
  26.3 1.3 %late_backward.1 = bf16[3,4,128,128]{3,2,1,0:T(8,128)(2,1)S(1)} custom-call(s32[1,128]{1,0:T(1,128)S(1)} %bitcast.21, bf16[3,12,128,128]{3,2,1,0:T(8,128)(2,1)S(1)} %bitcast.14, bf16[128,512]{1,0:T(8,128)(2,1)S(1)} %get-tuple-element.24.grad_ref), custom_call_target="tpu_custom_call" | custom-call | tf_op jit(solution)/shard_map/late_backward/pallas_call | solution.py:199
  27.6 1.3 %collective-permute-start.12 = (bf16[3,4,128,128]{3,2,1,0:T(8,128)(2,1)S(1)}, bf16[3,4,128,128]{3,2,1,0:T(8,128)(2,1)S(1)}, u32[]{:S(2)}, u32[]{:S(2)}) collective-permute-start(bf16[3,4,128,128]{3,2,1,0:T(8,128)(2,1)S(1)} %late_backward.1), channel_id=1, source_target_pairs={{8,0},{16,8},{24,16},{9,1},{17,9},{25,17},{10,2},{18,10},{26,18},{... | collective-permute-start | bytes 1179656 | tf_op jit(solution)/shard_map/ppermute | solution.py:40
  28.9 8.0 %collective-permute-done.6.refs_5_ = bf16[128,768]{1,0:T(8,128)(2,1)S(1)} collective-permute-done((bf16[128,768]{1,0:T(8,128)(2,1)S(1)}, bf16[128,768]{1,0:T(8,128)(2,1)S(1)}, u32[]{:S(2)}, u32[]{:S(2)}) %collective-permute-start.6) | collective-permute-done | bytes 196640 | tf_op jit(solution)/shard_map/ppermute | solution.py:30
  36.9 1.7 %collective-permute-start.8 = (bf16[128,768]{1,0:T(8,128)(2,1)S(1)}, bf16[128,768]{1,0:T(8,128)(2,1)S(1)}, u32[]{:S(2)}, u32[]{:S(2)}) collective-permute-start(bf16[128,768]{1,0:T(8,128)(2,1)S(1)} %collective-permute-done.6.refs_5_), channel_id=1, source_target_pairs={{0,4},{2,6},{4,0},{6,2},{1,5},{3,7},{5,1},{7,3},{8,12},{10,14},{12... | collective-permute-start | bytes 589832 | tf_op jit(solution)/shard_map/ppermute | solution.py:30
  38.6 1.3 %collective-permute-start.11 = (bf16[128,1024]{1,0:T(8,128)(2,1)S(1)}, bf16[128,1024]{1,0:T(8,128)(2,1)S(1)}, u32[]{:S(2)}, u32[]{:S(2)}) collective-permute-start(bf16[128,1024]{1,0:T(8,128)(2,1)S(1)} %get-tuple-element.22), channel_id=1, source_target_pairs={{8,0},{16,8},{24,16},{9,1},{17,9},{25,17},{10,2},{18,10},{26,18},{... | collective-permute-start | bytes 786440 | tf_op jit(solution)/shard_map/ppermute | solution.py:40
  39.9 0.0 collective-permute-done.refs_1_
  39.9 0.1 collective-permute-start.7
  40.0 3.3 %collective-permute-done.8.refs_6_ = bf16[128,768]{1,0:T(8,128)(2,1)S(1)} collective-permute-done((bf16[128,768]{1,0:T(8,128)(2,1)S(1)}, bf16[128,768]{1,0:T(8,128)(2,1)S(1)}, u32[]{:S(2)}, u32[]{:S(2)}) %collective-permute-start.8) | collective-permute-done | bytes 196640 | tf_op jit(solution)/shard_map/ppermute | solution.py:30
  43.4 0.0 collective-permute-start.9
  43.4 4.7 %collective-permute-done.11.grad_ref = bf16[128,1024]{1,0:T(8,128)(2,1)S(1)} collective-permute-done((bf16[128,1024]{1,0:T(8,128)(2,1)S(1)}, bf16[128,1024]{1,0:T(8,128)(2,1)S(1)}, u32[]{:S(2)}, u32[]{:S(2)}) %collective-permute-start.11) | collective-permute-done | bytes 262176 | tf_op jit(solution)/shard_map/ppermute | solution.py:40
  48.1 0.0 collective-permute-done.10.packed_ref
  48.1 0.0 copy-done.1
  48.1 5.3 %finish.1 = (bf16[3,12,128,128]{3,2,1,0:T(8,128)(2,1)}, bf16[3072,1536]{1,0:T(8,128)(2,1)}) custom-call(bf16[3088,128]{1,0:T(8,128)(2,1)S(1)} %collective-permute-done.10.packed_ref, bf16[128,1024]{1,0:T(8,128)(2,1)S(1)} %collective-permute-done.11.grad_ref, bf16[128,1536]{1,0:T(8,128)(2,1)S(1)} %get-tuple-element.14.refs_0_, ...), custom_call_target="tpu_custom_call" | custom-call | tf_op jit(solution)/shard_map/finish/pallas_call | solution.py:395
  53.4 0.0 collective-permute-done.12.late_ref
  53.4 0.8 %fill.1 = bf16[3,12,128,128]{3,2,1,0:T(8,128)(2,1)} custom-call(bf16[3,4,128,128]{3,2,1,0:T(8,128)(2,1)S(1)} %collective-permute-done.12.late_ref, bf16[3,12,128,128]{3,2,1,0:T(8,128)(2,1)} %get-tuple-element.25.whole_ref), custom_call_target="tpu_custom_call", output_to_operand_aliasing={{}: (1, {})} | custom-call | tf_op jit(solution)/shard_map/fill/pallas_call | solution.py:223
  54.2 0.0 collective-permute-done.7.refs_5_
  54.2 0.0 collective-permute-done.9.refs_6_
  54.2 3.4 %complete.1 = bf16[3072,1536]{1,0:T(8,128)(2,1)} custom-call(bf16[128,1536]{1,0:T(8,128)(2,1)S(1)} %get-tuple-element.14.refs_0_, bf16[128,1536]{1,0:T(8,128)(2,1)S(1)} %collective-permute-done.refs_1_, bf16[128,1536]{1,0:T(8,128)(2,1)S(1)} %collective-permute-done.1.refs_3_.refs_2_, ...), custom_call_target="tpu_custom_call", output_to_operand_aliasing={{}: (7, {})} | custom-call | tf_op jit(solution)/shard_map/complete/pallas_call | solution.py:412
  (1 shorter events, 0.0 us)
Async XLA Ops:
  1.9 8.4 %collective-permute-start.2 = (bf16[128,768]{1,0:T(8,128)(2,1)S(1)}, bf16[128,768]{1,0:T(8,128)(2,1)S(1)}, u32[]{:S(2)}, u32[]{:S(2)}) collective-permute-start(bf16[128,768]{1,0:T(8,128)(2,1)S(1)} %get-tuple-element.15), channel_id=1, source_target_pairs={{0,4},{2,6},{4,0},{6,2},{1,5},{3,7},{5,1},{7,3},{8,12},{10,14},{12... | collective-permute-start | bytes 589832 | tf_op jit(solution)/shard_map/ppermute | solution.py:30
  5.0 43.1 %collective-permute-start.10 = (bf16[3088,128]{1,0:T(8,128)(2,1)S(1)}, bf16[3088,128]{1,0:T(8,128)(2,1)S(1)}, u32[]{:S(2)}, u32[]{:S(2)}) collective-permute-start(bf16[3088,128]{1,0:T(8,128)(2,1)S(1)} %get-tuple-element.17), channel_id=1, source_target_pairs={{8,0},{16,8},{24,16},{9,1},{17,9},{25,17},{10,2},{18,10},{26,18},{... | collective-permute-start | bytes 2371592 | tf_op jit(solution)/shard_map/ppermute | solution.py:40
  6.3 17.0 %collective-permute-start.1 = (bf16[128,1536]{1,0:T(8,128)(2,1)}, bf16[128,1536]{1,0:T(8,128)(2,1)S(1)}, u32[]{:S(2)}, u32[]{:S(2)}) collective-permute-start(bf16[128,1536]{1,0:T(8,128)(2,1)} %bitcast.16), channel_id=1, source_target_pairs={{0,2},{2,0},{4,6},{6,4},{1,3},{3,1},{5,7},{7,5},{8,10},{10,8},{12,... | collective-permute-start | bytes 1179656 | tf_op jit(solution)/shard_map/ppermute | solution.py:35
  6.4 7.7 %collective-permute-start.4 = (bf16[128,768]{1,0:T(8,128)(2,1)S(1)}, bf16[128,768]{1,0:T(8,128)(2,1)S(1)}, u32[]{:S(2)}, u32[]{:S(2)}) collective-permute-start(bf16[128,768]{1,0:T(8,128)(2,1)S(1)} %get-tuple-element.16.refs_0_), channel_id=1, source_target_pairs={{0,4},{2,6},{4,0},{6,2},{1,5},{3,7},{5,1},{7,3},{8,12},{10,14},{12... | collective-permute-start | bytes 589832 | tf_op jit(solution)/shard_map/ppermute | solution.py:30
  10.3 12.6 %collective-permute-start.3 = (bf16[128,768]{1,0:T(8,128)(2,1)S(1)}, bf16[128,768]{1,0:T(8,128)(2,1)S(1)}, u32[]{:S(2)}, u32[]{:S(2)}) collective-permute-start(bf16[128,768]{1,0:T(8,128)(2,1)S(1)} %collective-permute-done.2.refs_1_.refs_4_.refs_3_), channel_id=1, source_target_pairs={{0,2},{2,0},{4,6},{6,4},{1,3},{3,1},{5,7},{7,5},{8,10},{10,8},{12,... | collective-permute-start | bytes 589832 | tf_op jit(solution)/shard_map/ppermute | solution.py:35
  14.1 10.9 %collective-permute-start.5 = (bf16[128,768]{1,0:T(8,128)(2,1)S(1)}, bf16[128,768]{1,0:T(8,128)(2,1)S(1)}, u32[]{:S(2)}, u32[]{:S(2)}) collective-permute-start(bf16[128,768]{1,0:T(8,128)(2,1)S(1)} %collective-permute-done.4.refs_5_.refs_4_), channel_id=1, source_target_pairs={{0,2},{2,0},{4,6},{6,4},{1,3},{3,1},{5,7},{7,5},{8,10},{10,8},{12,... | collective-permute-start | bytes 589832 | tf_op jit(solution)/shard_map/ppermute | solution.py:35
  21.1 18.8 %collective-permute-start = (bf16[128,1536]{1,0:T(8,128)(2,1)S(1)}, bf16[128,1536]{1,0:T(8,128)(2,1)S(1)}, u32[]{:S(2)}, u32[]{:S(2)}) collective-permute-start(bf16[128,1536]{1,0:T(8,128)(2,1)S(1)} %get-tuple-element.14.refs_0_), channel_id=1, source_target_pairs={{0,1},{1,0},{2,3},{3,2},{4,5},{5,4},{6,7},{7,6},{8,9},{9,8},{10,11... | collective-permute-start | bytes 1179656 | tf_op jit(solution)/shard_map/ppermute | solution.py:30
  22.9 14.0 %collective-permute-start.6 = (bf16[128,768]{1,0:T(8,128)(2,1)S(1)}, bf16[128,768]{1,0:T(8,128)(2,1)S(1)}, u32[]{:S(2)}, u32[]{:S(2)}) collective-permute-start(bf16[128,768]{1,0:T(8,128)(2,1)S(1)} %choose.1), channel_id=1, source_target_pairs={{0,1},{1,0},{2,3},{3,2},{4,5},{5,4},{6,7},{7,6},{8,9},{9,8},{10,11... | collective-permute-start | bytes 589832 | tf_op jit(solution)/shard_map/ppermute | solution.py:30
  25.0 1.3 %copy-start = (bf16[1,1,3,128,12,128]{5,3,4,2,1,0:T(8,128)(2,1)S(1)}, bf16[1,1,3,128,12,128]{5,3,4,2,1,0:T(8,128)(2,1)}, u32[]{:S(2)}) copy-start(bf16[1,1,3,128,12,128]{5,3,4,2,1,0:T(8,128)(2,1)} %param.4) | copy-start | bytes 3538948
  25.0 1.3 %copy-start.2 = (s32[1,1,128]{2,1,0:T(1,128)S(1)}, s32[1,1,128]{2,1,0:T(1,128)}, u32[]{:S(2)}) copy-start(s32[1,1,128]{2,1,0:T(1,128)} %param.5) | copy-start | bytes 1540
  25.0 23.1 %copy-start.1 = (bf16[1,1,128,1536]{3,2,1,0:T(8,128)(2,1)S(1)}, bf16[1,1,128,1536]{3,2,1,0:T(8,128)(2,1)}, u32[]{:S(2)}) copy-start(bf16[1,1,128,1536]{3,2,1,0:T(8,128)(2,1)} %param.7) | copy-start | bytes 1179652
  27.6 25.8 %collective-permute-start.12 = (bf16[3,4,128,128]{3,2,1,0:T(8,128)(2,1)S(1)}, bf16[3,4,128,128]{3,2,1,0:T(8,128)(2,1)S(1)}, u32[]{:S(2)}, u32[]{:S(2)}) collective-permute-start(bf16[3,4,128,128]{3,2,1,0:T(8,128)(2,1)S(1)} %late_backward.1), channel_id=1, source_target_pairs={{8,0},{16,8},{24,16},{9,1},{17,9},{25,17},{10,2},{18,10},{26,18},{... | collective-permute-start | bytes 1179656 | tf_op jit(solution)/shard_map/ppermute | solution.py:40
  36.9 6.5 %collective-permute-start.8 = (bf16[128,768]{1,0:T(8,128)(2,1)S(1)}, bf16[128,768]{1,0:T(8,128)(2,1)S(1)}, u32[]{:S(2)}, u32[]{:S(2)}) collective-permute-start(bf16[128,768]{1,0:T(8,128)(2,1)S(1)} %collective-permute-done.6.refs_5_), channel_id=1, source_target_pairs={{0,4},{2,6},{4,0},{6,2},{1,5},{3,7},{5,1},{7,3},{8,12},{10,14},{12... | collective-permute-start | bytes 589832 | tf_op jit(solution)/shard_map/ppermute | solution.py:30
  38.6 9.5 %collective-permute-start.11 = (bf16[128,1024]{1,0:T(8,128)(2,1)S(1)}, bf16[128,1024]{1,0:T(8,128)(2,1)S(1)}, u32[]{:S(2)}, u32[]{:S(2)}) collective-permute-start(bf16[128,1024]{1,0:T(8,128)(2,1)S(1)} %get-tuple-element.22), channel_id=1, source_target_pairs={{8,0},{16,8},{24,16},{9,1},{17,9},{25,17},{10,2},{18,10},{26,18},{... | collective-permute-start | bytes 786440 | tf_op jit(solution)/shard_map/ppermute | solution.py:40
  39.9 14.3 %collective-permute-start.7 = (bf16[128,768]{1,0:T(8,128)(2,1)S(1)}, bf16[128,768]{1,0:T(8,128)(2,1)S(1)}, u32[]{:S(2)}, u32[]{:S(2)}) collective-permute-start(bf16[128,768]{1,0:T(8,128)(2,1)S(1)} %collective-permute-done.6.refs_5_), channel_id=1, source_target_pairs={{0,2},{2,0},{4,6},{6,4},{1,3},{3,1},{5,7},{7,5},{8,10},{10,8},{12,... | collective-permute-start | bytes 589832 | tf_op jit(solution)/shard_map/ppermute | solution.py:35
  43.4 10.9 %collective-permute-start.9 = (bf16[128,768]{1,0:T(8,128)(2,1)S(1)}, bf16[128,768]{1,0:T(8,128)(2,1)S(1)}, u32[]{:S(2)}, u32[]{:S(2)}) collective-permute-start(bf16[128,768]{1,0:T(8,128)(2,1)S(1)} %collective-permute-done.8.refs_6_), channel_id=1, source_target_pairs={{0,2},{2,0},{4,6},{6,4},{1,3},{3,1},{5,7},{7,5},{8,10},{10,8},{12,... | collective-permute-start | bytes 589832 | tf_op jit(solution)/shard_map/ppermute | solution.py:35

commit v12 on v10

--- a/solution.py
+++ b/solution.py
@@ -107,16 +107,11 @@
     return weight_ref.at[pl.ds(pl.multiple_of(owner * depth, depth), depth)]
 
 
-def forward_kernel(chips, groups, pos_ref, qkv_ref, weight_ref, own_ref, out_ref, total_ref, *refs):
-    kept, (held, shard, buffer, rows, head_sems, sems) = refs[:-6], refs[-6:]
-    heads, _, width = buffer.shape[1:]
-    size = heads // groups
-    gets = [pltpu.make_async_copy(pos_ref, held, head_sems.at[groups])]
-    for group in range(groups):
-        part = pl.ds(group * size, size)
-        gets.append(
-            pltpu.make_async_copy(qkv_ref.at[:, part], buffer.at[:, part], head_sems.at[group])
-        )
+def forward_kernel(chips, early, pieces, qkv_ref, weight_ref, packed_ref, *refs):
+    parts, refs = refs[:pieces], refs[pieces:]
+    out_ref, total_ref = refs[:2]
+    kept, (buffer, rows, late_sem, sems) = refs[2:-4], refs[-4:]
+    late, seq, width = buffer.shape[1:]
     fetches = [
         pltpu.make_async_copy(
             rows_of(weight_ref, rows.shape[0], chips, number // 2, number % 2),
@@ -125,33 +120,45 @@
         )
         for number, target in enumerate((rows, *kept))
     ]
-    gets.append(pltpu.make_async_copy(own_ref, shard, head_sems.at[groups + 1]))
-    for get in gets + fetches:
-        get.start()
-    gets[0].wait()
-    visible = visibility(held[...])
-    for head in range(heads):
-        if head % size == 0:
-            gets[1 + head // size].wait()
-        probs = softmax(visible, buffer[0, head], buffer[1, head])
-        attended = dot(probs.astype(BF16), buffer[2, head], ((0,), (0,)))
+    get = pltpu.make_async_copy(qkv_ref.at[:, pl.ds(early, late)], buffer, late_sem.at[0])
+    get.start()
+    for fetch in fetches:
+        fetch.start()
+    visible = visibility(packed_ref[3 * early * seq :][:1])
+    for head in range(early + late):
+        if head < early:
+            query, key, value = (
+                packed_ref[(i * early + head) * seq : (i * early + head + 1) * seq]
+                for i in range(3)
+            )
+        else:
+            if head == early:
+                get.wait()
+            query, key, value = (buffer[i, head - early] for i in range(3))
+        probs = softmax(visible, query, key)
+        attended = dot(probs.astype(BF16), value, ((0,), (0,)))
         out_ref[:, head * width : (head + 1) * width] = attended.astype(BF16)
-    gets[-1].wait()
     fetches[0].wait()
-    total_ref[...] = jnp.dot(shard[...], rows[...], preferred_element_type=F32)
+    size = rows.shape[0] // pieces
+    total = None
+    for number, part in enumerate(parts):
+        product = jnp.dot(
+            part[...], rows[number * size : (number + 1) * size], preferred_element_type=F32
+        )
+        total = product if total is None else total + product
+    total_ref[...] = total
     for fetch in fetches[1:]:
         fetch.wait()
 
 
-def forward(chips, pos, qkv, weight, own):
+def forward(chips, early, qkv, weight, packed, parts):
     _, heads, seq, width = qkv.shape
-    depth, columns = own.shape[1], weight.shape[1]
+    depth, columns = len(parts) * parts[0].shape[1], weight.shape[1]
     count = 2 * chips - 1
-    groups = max(size for size in (1, 2, 3) if heads % size == 0)
-    return pl.pallas_call(
-        functools.partial(forward_kernel, chips, groups),
+    return pl.pallas_call(
+        functools.partial(forward_kernel, chips, early, len(parts)),
         name="forward",
-        in_specs=[ANY] * 4,
+        in_specs=[ANY, ANY] + [VMEM] * (1 + len(parts)),
         out_specs=[VMEM] * (2 + count),
         out_shape=[
             jax.ShapeDtypeStruct((seq, heads * width), BF16),
@@ -159,15 +166,13 @@
         ]
         + [pltpu.VMEM((depth, columns), BF16)] * count,
         scratch_shapes=[
-            pltpu.VMEM(pos.shape, pos.dtype),
-            pltpu.VMEM(own.shape, BF16),
-            pltpu.VMEM(qkv.shape, BF16),
+            pltpu.VMEM((3, heads - early, seq, width), BF16),
             pltpu.VMEM((depth, columns), BF16),
-            pltpu.SemaphoreType.DMA((groups + 2,)),
+            pltpu.SemaphoreType.DMA((1,)),
             pltpu.SemaphoreType.DMA((count + 1,)),
         ],
         compiler_params=PARAMS,
-    )(in_hbm(pos), in_hbm(qkv), weight, in_hbm(own))
+    )(in_hbm(qkv), weight, packed, *parts)
 
 
 def head_gradients(visible, query, key, value, grad):
@@ -423,7 +428,7 @@
         for piece in range(pieces):
             other[-1].append(swap(same[step][piece], "st"))
 
-    attended, total, *far_rows = forward(chips, pos, qkv, weight, own)
+    attended, total, *far_rows = forward(chips, early, qkv, weight, packed, parts)
     acts = [attended]
     for step in range(1, replicas):
         acts.append(rotate(attended, "dp", step))

time: 53.8 us -> 55.6 us (1.033)
  Pallas kernels: 20.3 us -> 22.1 us
    pallas_call x1, Pallas kernels: 6.98 us -> 8.68 us  [forward(): pl.pallas_call(functools.partial(forward_kernel, chips, early, len(parts)...]
  transfers between devices with their start and end apart: 13 -> 13, of which waited for: 4 -> 4; matrix products, arithmetic and copies ran while one was open for 0% -> 0% of each run, Pallas kernels for 34% -> 36%
where the time goes in v12:
time: 55.6 us; the launch traced here: 55.3 us
  Pallas kernels  22.1 us (40%)
  waiting for transfers between devices  19.5 us (35%)
  starting transfers between devices  12.3 us (22%)
  between operations  0.77 us (1%)
  local copies, waits for them, and re-layouts  0.75 us (1%)
    ppermute x3, waiting for transfers between devices, down(): return lax.ppermute(value, axis, [(i, i - 1) for i in range(1, count)])  13 us
    pallas_call x1, Pallas kernels, forward(): pl.pallas_call(functools.partial(forward_kernel, chips, early, len(parts)...  8.68 us
    pallas_call x1, Pallas kernels, finish(): pl.pallas_call(functools.partial(finish_kernel, replicas, counts(options)...  7.75 us
    ppermute x5, starting transfers between devices, rotate(): lax.ppermute(value, axis, [(i, (i + steps) % count) for i in range(count)])  7.59 us
    ppermute x5, waiting for transfers between devices, rotate(): lax.ppermute(value, axis, [(i, (i + steps) % count) for i in range(count)])  5.58 us
    ppermute x3, starting transfers between devices, down(): return lax.ppermute(value, axis, [(i, i - 1) for i in range(1, count)])  3.86 us
    pallas_call x2, Pallas kernels, project(): pl.pallas_call(functools.partial(project_kernel, tuple(terms), splits), n...  2.2 us
    pallas_call x1, Pallas kernels, late_backward(): pl.pallas_call(late_kernel, name='late_backward', in_specs=[VMEM] * 3, ou...  1.34 us
  transfers between devices with their start and end apart: 13, of which 4 were waited for; matrix products, arithmetic and copies ran while one was open for 0% of the time, Pallas kernels for 36%

profile of v12, /device:TPU:0, one launch (start us, length us, event | category | flops | bytes accessed | tf_op | source)
XLA Modules:
  0.0 55.3 jit_solution(14583190175677230294)
XLA Ops:
  0.6 1.3 %pack.1 = (bf16[3088,128]{1,0:T(8,128)(2,1)S(1)}, bf16[128,768]{1,0:T(8,128)(2,1)S(1)}, bf16[128,768]{1,0:T(8,128)(2,1)S(1)}) custom-call(s32[1,128]{1,0:T(1,128)} %bitcast.18, bf16[3,1536,128]{2,1,0:T(8,128)(2,1)} %bitcast.12, bf16[128,1536]{1,0:T(8,128)(2,1)} %bitcast.15), custom_call_target="tpu_custom_call" | custom-call | tf_op jit(solution)/shard_map/pack/pallas_call | solution.py:85
  1.9 3.1 %collective-permute-start.4 = (bf16[128,768]{1,0:T(8,128)(2,1)S(1)}, bf16[128,768]{1,0:T(8,128)(2,1)S(1)}, u32[]{:S(2)}, u32[]{:S(2)}) collective-permute-start(bf16[128,768]{1,0:T(8,128)(2,1)S(1)} %get-tuple-element.15.refs_0_), channel_id=1, source_target_pairs={{0,4},{2,6},{4,0},{6,2},{1,5},{3,7},{5,1},{7,3},{8,12},{10,14},{12... | collective-permute-start | bytes 589832 | tf_op jit(solution)/shard_map/ppermute | solution.py:30
  5.0 1.3 %collective-permute-start = (bf16[3088,128]{1,0:T(8,128)(2,1)S(1)}, bf16[3088,128]{1,0:T(8,128)(2,1)S(1)}, u32[]{:S(2)}, u32[]{:S(2)}) collective-permute-start(bf16[3088,128]{1,0:T(8,128)(2,1)S(1)} %get-tuple-element.14.packed_ref), channel_id=1, source_target_pairs={{8,0},{16,8},{24,16},{9,1},{17,9},{25,17},{10,2},{18,10},{26,18},{... | collective-permute-start | bytes 2371592 | tf_op jit(solution)/shard_map/ppermute | solution.py:40
  6.3 0.1 collective-permute-start.3
  6.4 0.1 collective-permute-start.1
  6.5 3.9 %collective-permute-done.4.refs_4_.refs_1_.refs_3_ = bf16[128,768]{1,0:T(8,128)(2,1)S(1)} collective-permute-done((bf16[128,768]{1,0:T(8,128)(2,1)S(1)}, bf16[128,768]{1,0:T(8,128)(2,1)S(1)}, u32[]{:S(2)}, u32[]{:S(2)}) %collective-permute-start.4) | collective-permute-done | bytes 196640 | tf_op jit(solution)/shard_map/ppermute | solution.py:30
  10.3 0.0 collective-permute-start.5
  10.4 2.0 %collective-permute-start.8 = (bf16[128,768]{1,0:T(8,128)(2,1)S(1)}, bf16[128,768]{1,0:T(8,128)(2,1)S(1)}, u32[]{:S(2)}, u32[]{:S(2)}) collective-permute-start(bf16[128,768]{1,0:T(8,128)(2,1)S(1)} %choose.1), channel_id=1, source_target_pairs={{0,1},{1,0},{2,3},{3,2},{4,5},{5,4},{6,7},{7,6},{8,9},{9,8},{10,11... | collective-permute-start | bytes 589832 | tf_op jit(solution)/shard_map/ppermute | solution.py:30
  12.4 8.7 %forward.1 = (bf16[128,1536]{1,0:T(8,128)(2,1)S(1)}, f32[128,1536]{1,0:T(8,128)S(1)}, bf16[1536,1536]{1,0:T(8,128)(2,1)S(1)}, bf16[1536,1536]{1,0:T(8,128)(2,1)S(1)}, bf16[1536,1536]{1,0:T(8,128)(2,1)S(1)}) custom-call(bf16[3,12,128,128]{3,2,1,0:T(8,128)(2,1)} %bitcast.13, bf16[6144,1536]{1,0:T(8,128)(2,1)} %bitcast.20, ...), custom_call_target="tpu_custom_call" | custom-call | tf_op jit(solution)/shard_map/forward/pallas_call | solution.py:158
  21.1 0.0 collective-permute-done.1.refs_5_.refs_4_
  21.1 0.1 collective-permute-start.7
  21.2 0.0 collective-permute-done.5.refs_6_
  21.2 0.2 collective-permute-start.2
  21.4 0.0 collective-permute-done.8.refs_8_
  21.4 2.3 %collective-permute-start.9 = (bf16[128,768]{1,0:T(8,128)(2,1)S(1)}, bf16[128,768]{1,0:T(8,128)(2,1)S(1)}, u32[]{:S(2)}, u32[]{:S(2)}) collective-permute-start(bf16[128,768]{1,0:T(8,128)(2,1)S(1)} %collective-permute-done.8.refs_8_), channel_id=1, source_target_pairs={{0,4},{2,6},{4,0},{6,2},{1,5},{3,7},{5,1},{7,3},{8,12},{10,14},{12... | collective-permute-start | bytes 589832 | tf_op jit(solution)/shard_map/ppermute | solution.py:30
  23.7 0.0 collective-permute-done.3.refs_3_.refs_5_
  23.7 1.7 %project.2.refs_2_ = f32[128,1536]{1,0:T(8,128)S(1)} custom-call(bf16[1536,1536]{1,0:T(8,128)(2,1)S(1)} %get-tuple-element.18.refs_0_, bf16[1536,1536]{1,0:T(8,128)(2,1)S(1)} %get-tuple-element.19.refs_1_, bf16[1536,1536]{1,0:T(8,128)(2,1)S(1)} %get-tuple-element.17.refs_2_.refs_0_, bf16[128,1536]{1,0:T(8,128)(2,1)S(1)} %collective-permute-done.3.refs_3_.refs_5_, ...), custom_call_target="tpu_custom_call" | custom-call | tf_op jit(solution)/shard_map/project/pallas_call | solution.py:263
  25.5 0.0 copy-start
  25.5 0.0 copy-start.2
  25.5 0.0 copy-start.1
  25.5 0.0 collective-permute-done.2.refs_1_.refs_7_
  25.5 0.5 project.3
  26.0 0.7 %copy-done = bf16[1,1,3,128,12,128]{5,3,4,2,1,0:T(8,128)(2,1)S(1)} copy-done((bf16[1,1,3,128,12,128]{5,3,4,2,1,0:T(8,128)(2,1)S(1)}, bf16[1,1,3,128,12,128]{5,3,4,2,1,0:T(8,128)(2,1)}, u32[]{:S(2)}) %copy-start) | copy-done | bytes 1179672
  26.7 0.0 copy-done.2
  26.7 1.3 %late_backward.1 = bf16[3,4,128,128]{3,2,1,0:T(8,128)(2,1)S(1)} custom-call(s32[1,128]{1,0:T(1,128)S(1)} %bitcast.19, bf16[3,12,128,128]{3,2,1,0:T(8,128)(2,1)S(1)} %bitcast.14, bf16[128,512]{1,0:T(8,128)(2,1)S(1)} %get-tuple-element.24.grad_ref), custom_call_target="tpu_custom_call" | custom-call | tf_op jit(solution)/shard_map/late_backward/pallas_call | solution.py:204
  28.1 1.3 %collective-permute-start.12 = (bf16[3,4,128,128]{3,2,1,0:T(8,128)(2,1)S(1)}, bf16[3,4,128,128]{3,2,1,0:T(8,128)(2,1)S(1)}, u32[]{:S(2)}, u32[]{:S(2)}) collective-permute-start(bf16[3,4,128,128]{3,2,1,0:T(8,128)(2,1)S(1)} %late_backward.1), channel_id=1, source_target_pairs={{8,0},{16,8},{24,16},{9,1},{17,9},{25,17},{10,2},{18,10},{26,18},{... | collective-permute-start | bytes 1179656 | tf_op jit(solution)/shard_map/ppermute | solution.py:40
  29.4 1.3 %collective-permute-start.6 = (bf16[128,1024]{1,0:T(8,128)(2,1)S(1)}, bf16[128,1024]{1,0:T(8,128)(2,1)S(1)}, u32[]{:S(2)}, u32[]{:S(2)}) collective-permute-start(bf16[128,1024]{1,0:T(8,128)(2,1)S(1)} %get-tuple-element.21), channel_id=1, source_target_pairs={{8,0},{16,8},{24,16},{9,1},{17,9},{25,17},{10,2},{18,10},{26,18},{... | collective-permute-start | bytes 786440 | tf_op jit(solution)/shard_map/ppermute | solution.py:40
  30.7 1.7 %collective-permute-done.7.refs_1_ = bf16[128,1536]{1,0:T(8,128)(2,1)S(1)} collective-permute-done((bf16[128,1536]{1,0:T(8,128)(2,1)S(1)}, bf16[128,1536]{1,0:T(8,128)(2,1)S(1)}, u32[]{:S(2)}, u32[]{:S(2)}) %collective-permute-start.7) | collective-permute-done | bytes 393248 | tf_op jit(solution)/shard_map/ppermute | solution.py:30
  32.4 0.0 collective-permute-start.10
  32.4 0.0 collective-permute-done.9.refs_9_
  32.4 0.5 collective-permute-start.11
  32.9 0.9 %collective-permute-done.10.refs_10_ = bf16[128,768]{1,0:T(8,128)(2,1)S(1)} collective-permute-done((bf16[128,768]{1,0:T(8,128)(2,1)S(1)}, bf16[128,768]{1,0:T(8,128)(2,1)S(1)}, u32[]{:S(2)}, u32[]{:S(2)}) %collective-permute-start.10) | collective-permute-done | bytes 196640 | tf_op jit(solution)/shard_map/ppermute | solution.py:35
  33.8 13.0 %collective-permute-done.6.grad_ref = bf16[128,1024]{1,0:T(8,128)(2,1)S(1)} collective-permute-done((bf16[128,1024]{1,0:T(8,128)(2,1)S(1)}, bf16[128,1024]{1,0:T(8,128)(2,1)S(1)}, u32[]{:S(2)}, u32[]{:S(2)}) %collective-permute-start.6) | collective-permute-done | bytes 262176 | tf_op jit(solution)/shard_map/ppermute | solution.py:40
  46.8 0.0 collective-permute-done.11.refs_11_
  46.8 0.0 collective-permute-done.packed_ref
  46.8 0.0 copy-done.1
  46.8 7.8 %finish.1 = (bf16[3,12,128,128]{3,2,1,0:T(8,128)(2,1)}, bf16[3072,1536]{1,0:T(8,128)(2,1)}) custom-call(bf16[3088,128]{1,0:T(8,128)(2,1)S(1)} %collective-permute-done.packed_ref, bf16[128,1024]{1,0:T(8,128)(2,1)S(1)} %collective-permute-done.6.grad_ref, bf16[128,1536]{1,0:T(8,128)(2,1)S(1)} %get-tuple-element.22.refs_0_, ...), custom_call_target="tpu_custom_call" | custom-call | tf_op jit(solution)/shard_map/finish/pallas_call | solution.py:379
  54.6 0.0 collective-permute-done.12.late_ref
  54.6 0.8 %fill.1 = bf16[3,12,128,128]{3,2,1,0:T(8,128)(2,1)} custom-call(bf16[3,4,128,128]{3,2,1,0:T(8,128)(2,1)S(1)} %collective-permute-done.12.late_ref, bf16[3,12,128,128]{3,2,1,0:T(8,128)(2,1)} %get-tuple-element.25.whole_ref), custom_call_target="tpu_custom_call", output_to_operand_aliasing={{}: (1, {})} | custom-call | tf_op jit(solution)/shard_map/fill/pallas_call | solution.py:228
  (1 shorter events, 0.0 us)
Async XLA Ops:
  1.9 8.4 %collective-permute-start.4 = (bf16[128,768]{1,0:T(8,128)(2,1)S(1)}, bf16[128,768]{1,0:T(8,128)(2,1)S(1)}, u32[]{:S(2)}, u32[]{:S(2)}) collective-permute-start(bf16[128,768]{1,0:T(8,128)(2,1)S(1)} %get-tuple-element.15.refs_0_), channel_id=1, source_target_pairs={{0,4},{2,6},{4,0},{6,2},{1,5},{3,7},{5,1},{7,3},{8,12},{10,14},{12... | collective-permute-start | bytes 589832 | tf_op jit(solution)/shard_map/ppermute | solution.py:30
  5.0 41.8 %collective-permute-start = (bf16[3088,128]{1,0:T(8,128)(2,1)S(1)}, bf16[3088,128]{1,0:T(8,128)(2,1)S(1)}, u32[]{:S(2)}, u32[]{:S(2)}) collective-permute-start(bf16[3088,128]{1,0:T(8,128)(2,1)S(1)} %get-tuple-element.14.packed_ref), channel_id=1, source_target_pairs={{8,0},{16,8},{24,16},{9,1},{17,9},{25,17},{10,2},{18,10},{26,18},{... | collective-permute-start | bytes 2371592 | tf_op jit(solution)/shard_map/ppermute | solution.py:40
  6.3 17.4 %collective-permute-start.3 = (bf16[128,1536]{1,0:T(8,128)(2,1)}, bf16[128,1536]{1,0:T(8,128)(2,1)S(1)}, u32[]{:S(2)}, u32[]{:S(2)}) collective-permute-start(bf16[128,1536]{1,0:T(8,128)(2,1)} %bitcast.16), channel_id=1, source_target_pairs={{0,2},{2,0},{4,6},{6,4},{1,3},{3,1},{5,7},{7,5},{8,10},{10,8},{12,... | collective-permute-start | bytes 1179656 | tf_op jit(solution)/shard_map/ppermute | solution.py:35
  6.4 14.7 %collective-permute-start.1 = (bf16[128,768]{1,0:T(8,128)(2,1)S(1)}, bf16[128,768]{1,0:T(8,128)(2,1)S(1)}, u32[]{:S(2)}, u32[]{:S(2)}) collective-permute-start(bf16[128,768]{1,0:T(8,128)(2,1)S(1)} %get-tuple-element.16.refs_1_.refs_0_), channel_id=1, source_target_pairs={{0,4},{2,6},{4,0},{6,2},{1,5},{3,7},{5,1},{7,3},{8,12},{10,14},{12... | collective-permute-start | bytes 589832 | tf_op jit(solution)/shard_map/ppermute | solution.py:30
  10.3 10.9 %collective-permute-start.5 = (bf16[128,768]{1,0:T(8,128)(2,1)S(1)}, bf16[128,768]{1,0:T(8,128)(2,1)S(1)}, u32[]{:S(2)}, u32[]{:S(2)}) collective-permute-start(bf16[128,768]{1,0:T(8,128)(2,1)S(1)} %collective-permute-done.4.refs_4_.refs_1_.refs_3_), channel_id=1, source_target_pairs={{0,2},{2,0},{4,6},{6,4},{1,3},{3,1},{5,7},{7,5},{8,10},{10,8},{12,... | collective-permute-start | bytes 589832 | tf_op jit(solution)/shard_map/ppermute | solution.py:35
  10.4 11.1 %collective-permute-start.8 = (bf16[128,768]{1,0:T(8,128)(2,1)S(1)}, bf16[128,768]{1,0:T(8,128)(2,1)S(1)}, u32[]{:S(2)}, u32[]{:S(2)}) collective-permute-start(bf16[128,768]{1,0:T(8,128)(2,1)S(1)} %choose.1), channel_id=1, source_target_pairs={{0,1},{1,0},{2,3},{3,2},{4,5},{5,4},{6,7},{7,6},{8,9},{9,8},{10,11... | collective-permute-start | bytes 589832 | tf_op jit(solution)/shard_map/ppermute | solution.py:30
  21.1 11.3 %collective-permute-start.7 = (bf16[128,1536]{1,0:T(8,128)(2,1)S(1)}, bf16[128,1536]{1,0:T(8,128)(2,1)S(1)}, u32[]{:S(2)}, u32[]{:S(2)}) collective-permute-start(bf16[128,1536]{1,0:T(8,128)(2,1)S(1)} %get-tuple-element.22.refs_0_), channel_id=1, source_target_pairs={{0,1},{1,0},{2,3},{3,2},{4,5},{5,4},{6,7},{7,6},{8,9},{9,8},{10,11... | collective-permute-start | bytes 1179656 | tf_op jit(solution)/shard_map/ppermute | solution.py:30
  21.2 4.3 %collective-permute-start.2 = (bf16[128,768]{1,0:T(8,128)(2,1)S(1)}, bf16[128,768]{1,0:T(8,128)(2,1)S(1)}, u32[]{:S(2)}, u32[]{:S(2)}) collective-permute-start(bf16[128,768]{1,0:T(8,128)(2,1)S(1)} %collective-permute-done.1.refs_5_.refs_4_), channel_id=1, source_target_pairs={{0,2},{2,0},{4,6},{6,4},{1,3},{3,1},{5,7},{7,5},{8,10},{10,8},{12,... | collective-permute-start | bytes 589832 | tf_op jit(solution)/shard_map/ppermute | solution.py:35
  21.4 10.9 %collective-permute-start.9 = (bf16[128,768]{1,0:T(8,128)(2,1)S(1)}, bf16[128,768]{1,0:T(8,128)(2,1)S(1)}, u32[]{:S(2)}, u32[]{:S(2)}) collective-permute-start(bf16[128,768]{1,0:T(8,128)(2,1)S(1)} %collective-permute-done.8.refs_8_), channel_id=1, source_target_pairs={{0,4},{2,6},{4,0},{6,2},{1,5},{3,7},{5,1},{7,3},{8,12},{10,14},{12... | collective-permute-start | bytes 589832 | tf_op jit(solution)/shard_map/ppermute | solution.py:30
  25.5 1.3 %copy-start = (bf16[1,1,3,128,12,128]{5,3,4,2,1,0:T(8,128)(2,1)S(1)}, bf16[1,1,3,128,12,128]{5,3,4,2,1,0:T(8,128)(2,1)}, u32[]{:S(2)}) copy-start(bf16[1,1,3,128,12,128]{5,3,4,2,1,0:T(8,128)(2,1)} %param.4) | copy-start | bytes 3538948
  25.5 1.3 %copy-start.2 = (s32[1,1,128]{2,1,0:T(1,128)S(1)}, s32[1,1,128]{2,1,0:T(1,128)}, u32[]{:S(2)}) copy-start(s32[1,1,128]{2,1,0:T(1,128)} %param.5) | copy-start | bytes 1540
  25.5 21.3 %copy-start.1 = (bf16[1,1,128,1536]{3,2,1,0:T(8,128)(2,1)S(1)}, bf16[1,1,128,1536]{3,2,1,0:T(8,128)(2,1)}, u32[]{:S(2)}) copy-start(bf16[1,1,128,1536]{3,2,1,0:T(8,128)(2,1)} %param.7) | copy-start | bytes 1179652
  28.1 26.5 %collective-permute-start.12 = (bf16[3,4,128,128]{3,2,1,0:T(8,128)(2,1)S(1)}, bf16[3,4,128,128]{3,2,1,0:T(8,128)(2,1)S(1)}, u32[]{:S(2)}, u32[]{:S(2)}) collective-permute-start(bf16[3,4,128,128]{3,2,1,0:T(8,128)(2,1)S(1)} %late_backward.1), channel_id=1, source_target_pairs={{8,0},{16,8},{24,16},{9,1},{17,9},{25,17},{10,2},{18,10},{26,18},{... | collective-permute-start | bytes 1179656 | tf_op jit(solution)/shard_map/ppermute | solution.py:40
  29.4 17.4 %collective-permute-start.6 = (bf16[128,1024]{1,0:T(8,128)(2,1)S(1)}, bf16[128,1024]{1,0:T(8,128)(2,1)S(1)}, u32[]{:S(2)}, u32[]{:S(2)}) collective-permute-start(bf16[128,1024]{1,0:T(8,128)(2,1)S(1)} %get-tuple-element.21), channel_id=1, source_target_pairs={{8,0},{16,8},{24,16},{9,1},{17,9},{25,17},{10,2},{18,10},{26,18},{... | collective-permute-start | bytes 786440 | tf_op jit(solution)/shard_map/ppermute | solution.py:40
  32.4 1.4 %collective-permute-start.10 = (bf16[128,768]{1,0:T(8,128)(2,1)S(1)}, bf16[128,768]{1,0:T(8,128)(2,1)S(1)}, u32[]{:S(2)}, u32[]{:S(2)}) collective-permute-start(bf16[128,768]{1,0:T(8,128)(2,1)S(1)} %collective-permute-done.8.refs_8_), channel_id=1, source_target_pairs={{0,2},{2,0},{4,6},{6,4},{1,3},{3,1},{5,7},{7,5},{8,10},{10,8},{12,... | collective-permute-start | bytes 589832 | tf_op jit(solution)/shard_map/ppermute | solution.py:35
  32.4 14.4 %collective-permute-start.11 = (bf16[128,768]{1,0:T(8,128)(2,1)S(1)}, bf16[128,768]{1,0:T(8,128)(2,1)S(1)}, u32[]{:S(2)}, u32[]{:S(2)}) collective-permute-start(bf16[128,768]{1,0:T(8,128)(2,1)S(1)} %collective-permute-done.9.refs_9_), channel_id=1, source_target_pairs={{0,2},{2,0},{4,6},{6,4},{1,3},{3,1},{5,7},{7,5},{8,10},{10,8},{12,... | collective-permute-start | bytes 589832 | tf_op jit(solution)/shard_map/ppermute | solution.py:35

commit v13 on v12

--- a/solution.py
+++ b/solution.py
@@ -125,19 +125,25 @@
     for fetch in fetches:
         fetch.start()
     visible = visibility(packed_ref[3 * early * seq :][:1])
-    for head in range(early + late):
-        if head < early:
-            query, key, value = (
-                packed_ref[(i * early + head) * seq : (i * early + head + 1) * seq]
-                for i in range(3)
-            )
-        else:
-            if head == early:
-                get.wait()
-            query, key, value = (buffer[i, head - early] for i in range(3))
-        probs = softmax(visible, query, key)
-        attended = dot(probs.astype(BF16), value, ((0,), (0,)))
-        out_ref[:, head * width : (head + 1) * width] = attended.astype(BF16)
+    chip, _ = place()
+
+    def attend(heads):
+        for head in heads:
+            if head < early:
+                query, key, value = (
+                    packed_ref[(i * early + head) * seq : (i * early + head + 1) * seq]
+                    for i in range(3)
+                )
+            else:
+                query, key, value = (buffer[i, head - early] for i in range(3))
+            probs = softmax(visible, query, key)
+            attended = dot(probs.astype(BF16), value, ((0,), (0,)))
+            out_ref[:, head * width : (head + 1) * width] = attended.astype(BF16)
+
+    for first in range(0, early, 4):
+        pl.when(chip >= 0)(functools.partial(attend, range(first, min(first + 4, early))))
+    get.wait()
+    attend(range(early, early + late))
     fetches[0].wait()
     size = rows.shape[0] // pieces
     total = None
@@ -310,23 +316,29 @@
     far = grouped(refs[sum(sizes) :], far_sizes)
     out_ref, weight_ref, held, stacked, ready, head_sems, sems = refs[-7:]
     heads, seq, width = held.shape[1:]
-    copies = []
     visible = visibility(packed_ref[3 * heads * seq :][:1])
-    for head in range(heads):
-        query, key, value = (
-            packed_ref[(i * heads + head) * seq : (i * heads + head + 1) * seq] for i in range(3)
-        )
-        grad = grad_ref[:, head * width : (head + 1) * width]
-        for i, result in enumerate(head_gradients(visible, query, key, value, grad)):
-            held[i, head] = result
-        copies.append(
-            pltpu.make_async_copy(held.at[:, head], out_ref.at[:, head], head_sems.at[head])
-        )
-        copies[-1].start()
+    copies = [
+        pltpu.make_async_copy(held.at[:, head], out_ref.at[:, head], head_sems.at[head])
+        for head in range(heads)
+    ]
+    chip, core = place()
+
+    def differentiate(group):
+        for head in group:
+            query, key, value = (
+                packed_ref[(i * heads + head) * seq : (i * heads + head + 1) * seq]
+                for i in range(3)
+            )
+            grad = grad_ref[:, head * width : (head + 1) * width]
+            for i, result in enumerate(head_gradients(visible, query, key, value, grad)):
+                held[i, head] = result
+            copies[head].start()
+
+    for first in range(0, heads, 4):
+        pl.when(chip >= 0)(functools.partial(differentiate, range(first, min(first + 4, heads))))
 
     for number, act in enumerate(acts):
         stacked[number * seq : (number + 1) * seq] = act[...]
-    chip, core = place()
     chips = len(sizes) // 2
     size = ready.shape[1]
     spans = [(turn, block * size, size) for turn in range(2 * slots) for block in range(blocks)]

time: 55.6 us -> 53.7 us (0.966)
  Pallas kernels: 22.1 us -> 20.2 us
    pallas_call x1, Pallas kernels: 8.68 us -> 6.63 us  [forward(): pl.pallas_call(functools.partial(forward_kernel, chips, early, len(parts)...]
  transfers between devices with their start and end apart: 13 -> 13, of which waited for: 4 -> 4; matrix products, arithmetic and copies ran while one was open for 0% -> 0% of each run, Pallas kernels for 36% -> 34%
where the time goes in v13:
time: 53.7 us; the launch traced here: 53.5 us
  Pallas kernels  20.2 us (38%)
  waiting for transfers between devices  19.5 us (36%)
  starting transfers between devices  12.3 us (23%)
  between operations  0.77 us (1%)
  local copies, waits for them, and re-layouts  0.76 us (1%)
    ppermute x3, waiting for transfers between devices, down(): return lax.ppermute(value, axis, [(i, i - 1) for i in range(1, count)])  13 us
    pallas_call x1, Pallas kernels, finish(): pl.pallas_call(functools.partial(finish_kernel, replicas, counts(options)...  7.93 us
    ppermute x5, starting transfers between devices, rotate(): lax.ppermute(value, axis, [(i, (i + steps) % count) for i in range(count)])  7.59 us
    pallas_call x1, Pallas kernels, forward(): pl.pallas_call(functools.partial(forward_kernel, chips, early, len(parts)...  6.63 us
    ppermute x5, waiting for transfers between devices, rotate(): lax.ppermute(value, axis, [(i, (i + steps) % count) for i in range(count)])  5.57 us
    ppermute x3, starting transfers between devices, down(): return lax.ppermute(value, axis, [(i, i - 1) for i in range(1, count)])  3.86 us
    pallas_call x2, Pallas kernels, project(): pl.pallas_call(functools.partial(project_kernel, tuple(terms), splits), n...  2.2 us
    pallas_call x1, Pallas kernels, late_backward(): pl.pallas_call(late_kernel, name='late_backward', in_specs=[VMEM] * 3, ou...  1.35 us
  transfers between devices with their start and end apart: 13, of which 4 were waited for; matrix products, arithmetic and copies ran while one was open for 0% of the time, Pallas kernels for 34%

profile of v13, /device:TPU:0, one launch (start us, length us, event | category | flops | bytes accessed | tf_op | source)
XLA Modules:
  0.0 53.5 jit_solution(5174005815227672839)
XLA Ops:
  0.6 1.3 %pack.1 = (bf16[3088,128]{1,0:T(8,128)(2,1)S(1)}, bf16[128,768]{1,0:T(8,128)(2,1)S(1)}, bf16[128,768]{1,0:T(8,128)(2,1)S(1)}) custom-call(s32[1,128]{1,0:T(1,128)} %bitcast.18, bf16[3,1536,128]{2,1,0:T(8,128)(2,1)} %bitcast.12, bf16[128,1536]{1,0:T(8,128)(2,1)} %bitcast.15), custom_call_target="tpu_custom_call" | custom-call | tf_op jit(solution)/shard_map/pack/pallas_call | solution.py:85
  1.9 3.1 %collective-permute-start.4 = (bf16[128,768]{1,0:T(8,128)(2,1)S(1)}, bf16[128,768]{1,0:T(8,128)(2,1)S(1)}, u32[]{:S(2)}, u32[]{:S(2)}) collective-permute-start(bf16[128,768]{1,0:T(8,128)(2,1)S(1)} %get-tuple-element.15.refs_0_), channel_id=1, source_target_pairs={{0,4},{2,6},{4,0},{6,2},{1,5},{3,7},{5,1},{7,3},{8,12},{10,14},{12... | collective-permute-start | bytes 589832 | tf_op jit(solution)/shard_map/ppermute | solution.py:30
  5.0 1.3 %collective-permute-start = (bf16[3088,128]{1,0:T(8,128)(2,1)S(1)}, bf16[3088,128]{1,0:T(8,128)(2,1)S(1)}, u32[]{:S(2)}, u32[]{:S(2)}) collective-permute-start(bf16[3088,128]{1,0:T(8,128)(2,1)S(1)} %get-tuple-element.14.packed_ref), channel_id=1, source_target_pairs={{8,0},{16,8},{24,16},{9,1},{17,9},{25,17},{10,2},{18,10},{26,18},{... | collective-permute-start | bytes 2371592 | tf_op jit(solution)/shard_map/ppermute | solution.py:40
  6.3 0.1 collective-permute-start.3
  6.4 0.1 collective-permute-start.1
  6.5 3.9 %collective-permute-done.4.refs_4_.refs_1_.refs_3_ = bf16[128,768]{1,0:T(8,128)(2,1)S(1)} collective-permute-done((bf16[128,768]{1,0:T(8,128)(2,1)S(1)}, bf16[128,768]{1,0:T(8,128)(2,1)S(1)}, u32[]{:S(2)}, u32[]{:S(2)}) %collective-permute-start.4) | collective-permute-done | bytes 196640 | tf_op jit(solution)/shard_map/ppermute | solution.py:30
  10.3 0.0 collective-permute-start.5
  10.4 2.0 %collective-permute-start.8 = (bf16[128,768]{1,0:T(8,128)(2,1)S(1)}, bf16[128,768]{1,0:T(8,128)(2,1)S(1)}, u32[]{:S(2)}, u32[]{:S(2)}) collective-permute-start(bf16[128,768]{1,0:T(8,128)(2,1)S(1)} %choose.1), channel_id=1, source_target_pairs={{0,1},{1,0},{2,3},{3,2},{4,5},{5,4},{6,7},{7,6},{8,9},{9,8},{10,11... | collective-permute-start | bytes 589832 | tf_op jit(solution)/shard_map/ppermute | solution.py:30
  12.4 6.6 %forward.1 = (bf16[128,1536]{1,0:T(8,128)(2,1)S(1)}, f32[128,1536]{1,0:T(8,128)S(1)}, bf16[1536,1536]{1,0:T(8,128)(2,1)S(1)}, bf16[1536,1536]{1,0:T(8,128)(2,1)S(1)}, bf16[1536,1536]{1,0:T(8,128)(2,1)S(1)}) custom-call(bf16[3,12,128,128]{3,2,1,0:T(8,128)(2,1)} %bitcast.13, bf16[6144,1536]{1,0:T(8,128)(2,1)} %bitcast.20, ...), custom_call_target="tpu_custom_call" | custom-call | tf_op jit(solution)/shard_map/forward/pallas_call | solution.py:164
  19.0 0.0 collective-permute-done.1.refs_5_.refs_4_
  19.0 0.1 collective-permute-start.7
  19.2 0.0 collective-permute-done.5.refs_6_
  19.2 0.2 collective-permute-start.2
  19.4 0.0 collective-permute-done.8.refs_8_
  19.4 2.3 %collective-permute-start.9 = (bf16[128,768]{1,0:T(8,128)(2,1)S(1)}, bf16[128,768]{1,0:T(8,128)(2,1)S(1)}, u32[]{:S(2)}, u32[]{:S(2)}) collective-permute-start(bf16[128,768]{1,0:T(8,128)(2,1)S(1)} %collective-permute-done.8.refs_8_), channel_id=1, source_target_pairs={{0,4},{2,6},{4,0},{6,2},{1,5},{3,7},{5,1},{7,3},{8,12},{10,14},{12... | collective-permute-start | bytes 589832 | tf_op jit(solution)/shard_map/ppermute | solution.py:30
  21.7 0.0 collective-permute-done.3.refs_3_.refs_5_
  21.7 1.7 %project.2.refs_2_ = f32[128,1536]{1,0:T(8,128)S(1)} custom-call(bf16[1536,1536]{1,0:T(8,128)(2,1)S(1)} %get-tuple-element.18.refs_0_, bf16[1536,1536]{1,0:T(8,128)(2,1)S(1)} %get-tuple-element.19.refs_1_, bf16[1536,1536]{1,0:T(8,128)(2,1)S(1)} %get-tuple-element.17.refs_2_.refs_0_, bf16[128,1536]{1,0:T(8,128)(2,1)S(1)} %collective-permute-done.3.refs_3_.refs_5_, ...), custom_call_target="tpu_custom_call" | custom-call | tf_op jit(solution)/shard_map/project/pallas_call | solution.py:269
  23.4 0.0 copy-start
  23.4 0.0 copy-start.2
  23.4 0.0 copy-start.1
  23.4 0.0 collective-permute-done.2.refs_1_.refs_7_
  23.5 0.5 project.3
  23.9 0.7 %copy-done = bf16[1,1,3,128,12,128]{5,3,4,2,1,0:T(8,128)(2,1)S(1)} copy-done((bf16[1,1,3,128,12,128]{5,3,4,2,1,0:T(8,128)(2,1)S(1)}, bf16[1,1,3,128,12,128]{5,3,4,2,1,0:T(8,128)(2,1)}, u32[]{:S(2)}) %copy-start) | copy-done | bytes 1179672
  24.7 0.0 copy-done.2
  24.7 1.3 %late_backward.1 = bf16[3,4,128,128]{3,2,1,0:T(8,128)(2,1)S(1)} custom-call(s32[1,128]{1,0:T(1,128)S(1)} %bitcast.19, bf16[3,12,128,128]{3,2,1,0:T(8,128)(2,1)S(1)} %bitcast.14, bf16[128,512]{1,0:T(8,128)(2,1)S(1)} %get-tuple-element.24.grad_ref), custom_call_target="tpu_custom_call" | custom-call | tf_op jit(solution)/shard_map/late_backward/pallas_call | solution.py:210
  26.0 1.3 %collective-permute-start.12 = (bf16[3,4,128,128]{3,2,1,0:T(8,128)(2,1)S(1)}, bf16[3,4,128,128]{3,2,1,0:T(8,128)(2,1)S(1)}, u32[]{:S(2)}, u32[]{:S(2)}) collective-permute-start(bf16[3,4,128,128]{3,2,1,0:T(8,128)(2,1)S(1)} %late_backward.1), channel_id=1, source_target_pairs={{8,0},{16,8},{24,16},{9,1},{17,9},{25,17},{10,2},{18,10},{26,18},{... | collective-permute-start | bytes 1179656 | tf_op jit(solution)/shard_map/ppermute | solution.py:40
  27.3 1.3 %collective-permute-start.6 = (bf16[128,1024]{1,0:T(8,128)(2,1)S(1)}, bf16[128,1024]{1,0:T(8,128)(2,1)S(1)}, u32[]{:S(2)}, u32[]{:S(2)}) collective-permute-start(bf16[128,1024]{1,0:T(8,128)(2,1)S(1)} %get-tuple-element.21), channel_id=1, source_target_pairs={{8,0},{16,8},{24,16},{9,1},{17,9},{25,17},{10,2},{18,10},{26,18},{... | collective-permute-start | bytes 786440 | tf_op jit(solution)/shard_map/ppermute | solution.py:40
  28.6 1.7 %collective-permute-done.7.refs_1_ = bf16[128,1536]{1,0:T(8,128)(2,1)S(1)} collective-permute-done((bf16[128,1536]{1,0:T(8,128)(2,1)S(1)}, bf16[128,1536]{1,0:T(8,128)(2,1)S(1)}, u32[]{:S(2)}, u32[]{:S(2)}) %collective-permute-start.7) | collective-permute-done | bytes 393248 | tf_op jit(solution)/shard_map/ppermute | solution.py:30
  30.3 0.0 collective-permute-start.10
  30.3 0.0 collective-permute-done.9.refs_9_
  30.3 0.5 collective-permute-start.11
  30.8 0.9 %collective-permute-done.10.refs_10_ = bf16[128,768]{1,0:T(8,128)(2,1)S(1)} collective-permute-done((bf16[128,768]{1,0:T(8,128)(2,1)S(1)}, bf16[128,768]{1,0:T(8,128)(2,1)S(1)}, u32[]{:S(2)}, u32[]{:S(2)}) %collective-permute-start.10) | collective-permute-done | bytes 196640 | tf_op jit(solution)/shard_map/ppermute | solution.py:35
  31.8 13.0 %collective-permute-done.6.grad_ref = bf16[128,1024]{1,0:T(8,128)(2,1)S(1)} collective-permute-done((bf16[128,1024]{1,0:T(8,128)(2,1)S(1)}, bf16[128,1024]{1,0:T(8,128)(2,1)S(1)}, u32[]{:S(2)}, u32[]{:S(2)}) %collective-permute-start.6) | collective-permute-done | bytes 262176 | tf_op jit(solution)/shard_map/ppermute | solution.py:40
  44.7 0.0 collective-permute-done.11.refs_11_
  44.7 0.0 collective-permute-done.packed_ref
  44.7 0.0 copy-done.1
  44.7 7.9 %finish.1 = (bf16[3,12,128,128]{3,2,1,0:T(8,128)(2,1)}, bf16[3072,1536]{1,0:T(8,128)(2,1)}) custom-call(bf16[3088,128]{1,0:T(8,128)(2,1)S(1)} %collective-permute-done.packed_ref, bf16[128,1024]{1,0:T(8,128)(2,1)S(1)} %collective-permute-done.6.grad_ref, bf16[128,1536]{1,0:T(8,128)(2,1)S(1)} %get-tuple-element.22.refs_0_, ...), custom_call_target="tpu_custom_call" | custom-call | tf_op jit(solution)/shard_map/finish/pallas_call | solution.py:391
  52.7 0.0 collective-permute-done.12.late_ref
  52.7 0.8 %fill.1 = bf16[3,12,128,128]{3,2,1,0:T(8,128)(2,1)} custom-call(bf16[3,4,128,128]{3,2,1,0:T(8,128)(2,1)S(1)} %collective-permute-done.12.late_ref, bf16[3,12,128,128]{3,2,1,0:T(8,128)(2,1)} %get-tuple-element.25.whole_ref), custom_call_target="tpu_custom_call", output_to_operand_aliasing={{}: (1, {})} | custom-call | tf_op jit(solution)/shard_map/fill/pallas_call | solution.py:234
  (1 shorter events, 0.0 us)
Async XLA Ops:
  1.9 8.4 %collective-permute-start.4 = (bf16[128,768]{1,0:T(8,128)(2,1)S(1)}, bf16[128,768]{1,0:T(8,128)(2,1)S(1)}, u32[]{:S(2)}, u32[]{:S(2)}) collective-permute-start(bf16[128,768]{1,0:T(8,128)(2,1)S(1)} %get-tuple-element.15.refs_0_), channel_id=1, source_target_pairs={{0,4},{2,6},{4,0},{6,2},{1,5},{3,7},{5,1},{7,3},{8,12},{10,14},{12... | collective-permute-start | bytes 589832 | tf_op jit(solution)/shard_map/ppermute | solution.py:30
  5.0 39.7 %collective-permute-start = (bf16[3088,128]{1,0:T(8,128)(2,1)S(1)}, bf16[3088,128]{1,0:T(8,128)(2,1)S(1)}, u32[]{:S(2)}, u32[]{:S(2)}) collective-permute-start(bf16[3088,128]{1,0:T(8,128)(2,1)S(1)} %get-tuple-element.14.packed_ref), channel_id=1, source_target_pairs={{8,0},{16,8},{24,16},{9,1},{17,9},{25,17},{10,2},{18,10},{26,18},{... | collective-permute-start | bytes 2371592 | tf_op jit(solution)/shard_map/ppermute | solution.py:40
  6.3 15.4 %collective-permute-start.3 = (bf16[128,1536]{1,0:T(8,128)(2,1)}, bf16[128,1536]{1,0:T(8,128)(2,1)S(1)}, u32[]{:S(2)}, u32[]{:S(2)}) collective-permute-start(bf16[128,1536]{1,0:T(8,128)(2,1)} %bitcast.16), channel_id=1, source_target_pairs={{0,2},{2,0},{4,6},{6,4},{1,3},{3,1},{5,7},{7,5},{8,10},{10,8},{12,... | collective-permute-start | bytes 1179656 | tf_op jit(solution)/shard_map/ppermute | solution.py:35
  6.4 12.6 %collective-permute-start.1 = (bf16[128,768]{1,0:T(8,128)(2,1)S(1)}, bf16[128,768]{1,0:T(8,128)(2,1)S(1)}, u32[]{:S(2)}, u32[]{:S(2)}) collective-permute-start(bf16[128,768]{1,0:T(8,128)(2,1)S(1)} %get-tuple-element.16.refs_1_.refs_0_), channel_id=1, source_target_pairs={{0,4},{2,6},{4,0},{6,2},{1,5},{3,7},{5,1},{7,3},{8,12},{10,14},{12... | collective-permute-start | bytes 589832 | tf_op jit(solution)/shard_map/ppermute | solution.py:30
  10.3 8.8 %collective-permute-start.5 = (bf16[128,768]{1,0:T(8,128)(2,1)S(1)}, bf16[128,768]{1,0:T(8,128)(2,1)S(1)}, u32[]{:S(2)}, u32[]{:S(2)}) collective-permute-start(bf16[128,768]{1,0:T(8,128)(2,1)S(1)} %collective-permute-done.4.refs_4_.refs_1_.refs_3_), channel_id=1, source_target_pairs={{0,2},{2,0},{4,6},{6,4},{1,3},{3,1},{5,7},{7,5},{8,10},{10,8},{12,... | collective-permute-start | bytes 589832 | tf_op jit(solution)/shard_map/ppermute | solution.py:35
  10.4 9.0 %collective-permute-start.8 = (bf16[128,768]{1,0:T(8,128)(2,1)S(1)}, bf16[128,768]{1,0:T(8,128)(2,1)S(1)}, u32[]{:S(2)}, u32[]{:S(2)}) collective-permute-start(bf16[128,768]{1,0:T(8,128)(2,1)S(1)} %choose.1), channel_id=1, source_target_pairs={{0,1},{1,0},{2,3},{3,2},{4,5},{5,4},{6,7},{7,6},{8,9},{9,8},{10,11... | collective-permute-start | bytes 589832 | tf_op jit(solution)/shard_map/ppermute | solution.py:30
  19.0 11.3 %collective-permute-start.7 = (bf16[128,1536]{1,0:T(8,128)(2,1)S(1)}, bf16[128,1536]{1,0:T(8,128)(2,1)S(1)}, u32[]{:S(2)}, u32[]{:S(2)}) collective-permute-start(bf16[128,1536]{1,0:T(8,128)(2,1)S(1)} %get-tuple-element.22.refs_0_), channel_id=1, source_target_pairs={{0,1},{1,0},{2,3},{3,2},{4,5},{5,4},{6,7},{7,6},{8,9},{9,8},{10,11... | collective-permute-start | bytes 1179656 | tf_op jit(solution)/shard_map/ppermute | solution.py:30
  19.2 4.3 %collective-permute-start.2 = (bf16[128,768]{1,0:T(8,128)(2,1)S(1)}, bf16[128,768]{1,0:T(8,128)(2,1)S(1)}, u32[]{:S(2)}, u32[]{:S(2)}) collective-permute-start(bf16[128,768]{1,0:T(8,128)(2,1)S(1)} %collective-permute-done.1.refs_5_.refs_4_), channel_id=1, source_target_pairs={{0,2},{2,0},{4,6},{6,4},{1,3},{3,1},{5,7},{7,5},{8,10},{10,8},{12,... | collective-permute-start | bytes 589832 | tf_op jit(solution)/shard_map/ppermute | solution.py:35
  19.4 10.9 %collective-permute-start.9 = (bf16[128,768]{1,0:T(8,128)(2,1)S(1)}, bf16[128,768]{1,0:T(8,128)(2,1)S(1)}, u32[]{:S(2)}, u32[]{:S(2)}) collective-permute-start(bf16[128,768]{1,0:T(8,128)(2,1)S(1)} %collective-permute-done.8.refs_8_), channel_id=1, source_target_pairs={{0,4},{2,6},{4,0},{6,2},{1,5},{3,7},{5,1},{7,3},{8,12},{10,14},{12... | collective-permute-start | bytes 589832 | tf_op jit(solution)/shard_map/ppermute | solution.py:30
  23.4 1.3 %copy-start = (bf16[1,1,3,128,12,128]{5,3,4,2,1,0:T(8,128)(2,1)S(1)}, bf16[1,1,3,128,12,128]{5,3,4,2,1,0:T(8,128)(2,1)}, u32[]{:S(2)}) copy-start(bf16[1,1,3,128,12,128]{5,3,4,2,1,0:T(8,128)(2,1)} %param.4) | copy-start | bytes 3538948
  23.4 1.3 %copy-start.2 = (s32[1,1,128]{2,1,0:T(1,128)S(1)}, s32[1,1,128]{2,1,0:T(1,128)}, u32[]{:S(2)}) copy-start(s32[1,1,128]{2,1,0:T(1,128)} %param.5) | copy-start | bytes 1540
  23.4 21.3 %copy-start.1 = (bf16[1,1,128,1536]{3,2,1,0:T(8,128)(2,1)S(1)}, bf16[1,1,128,1536]{3,2,1,0:T(8,128)(2,1)}, u32[]{:S(2)}) copy-start(bf16[1,1,128,1536]{3,2,1,0:T(8,128)(2,1)} %param.7) | copy-start | bytes 1179652
  26.0 26.6 %collective-permute-start.12 = (bf16[3,4,128,128]{3,2,1,0:T(8,128)(2,1)S(1)}, bf16[3,4,128,128]{3,2,1,0:T(8,128)(2,1)S(1)}, u32[]{:S(2)}, u32[]{:S(2)}) collective-permute-start(bf16[3,4,128,128]{3,2,1,0:T(8,128)(2,1)S(1)} %late_backward.1), channel_id=1, source_target_pairs={{8,0},{16,8},{24,16},{9,1},{17,9},{25,17},{10,2},{18,10},{26,18},{... | collective-permute-start | bytes 1179656 | tf_op jit(solution)/shard_map/ppermute | solution.py:40
  27.3 17.4 %collective-permute-start.6 = (bf16[128,1024]{1,0:T(8,128)(2,1)S(1)}, bf16[128,1024]{1,0:T(8,128)(2,1)S(1)}, u32[]{:S(2)}, u32[]{:S(2)}) collective-permute-start(bf16[128,1024]{1,0:T(8,128)(2,1)S(1)} %get-tuple-element.21), channel_id=1, source_target_pairs={{8,0},{16,8},{24,16},{9,1},{17,9},{25,17},{10,2},{18,10},{26,18},{... | collective-permute-start | bytes 786440 | tf_op jit(solution)/shard_map/ppermute | solution.py:40
  30.3 1.4 %collective-permute-start.10 = (bf16[128,768]{1,0:T(8,128)(2,1)S(1)}, bf16[128,768]{1,0:T(8,128)(2,1)S(1)}, u32[]{:S(2)}, u32[]{:S(2)}) collective-permute-start(bf16[128,768]{1,0:T(8,128)(2,1)S(1)} %collective-permute-done.8.refs_8_), channel_id=1, source_target_pairs={{0,2},{2,0},{4,6},{6,4},{1,3},{3,1},{5,7},{7,5},{8,10},{10,8},{12,... | collective-permute-start | bytes 589832 | tf_op jit(solution)/shard_map/ppermute | solution.py:35
  30.3 14.4 %collective-permute-start.11 = (bf16[128,768]{1,0:T(8,128)(2,1)S(1)}, bf16[128,768]{1,0:T(8,128)(2,1)S(1)}, u32[]{:S(2)}, u32[]{:S(2)}) collective-permute-start(bf16[128,768]{1,0:T(8,128)(2,1)S(1)} %collective-permute-done.9.refs_9_), channel_id=1, source_target_pairs={{0,2},{2,0},{4,6},{6,4},{1,3},{3,1},{5,7},{7,5},{8,10},{10,8},{12,... | collective-permute-start | bytes 589832 | tf_op jit(solution)/shard_map/ppermute | solution.py:35

commit v14 on v13

--- a/solution.py
+++ b/solution.py
@@ -316,35 +316,26 @@
     far = grouped(refs[sum(sizes) :], far_sizes)
     out_ref, weight_ref, held, stacked, ready, head_sems, sems = refs[-7:]
     heads, seq, width = held.shape[1:]
+    copies = []
     visible = visibility(packed_ref[3 * heads * seq :][:1])
-    copies = [
-        pltpu.make_async_copy(held.at[:, head], out_ref.at[:, head], head_sems.at[head])
-        for head in range(heads)
-    ]
-    chip, core = place()
-
-    def differentiate(group):
-        for head in group:
-            query, key, value = (
-                packed_ref[(i * heads + head) * seq : (i * heads + head + 1) * seq]
-                for i in range(3)
-            )
-            grad = grad_ref[:, head * width : (head + 1) * width]
-            for i, result in enumerate(head_gradients(visible, query, key, value, grad)):
-                held[i, head] = result
-            copies[head].start()
-
-    for first in range(0, heads, 4):
-        pl.when(chip >= 0)(functools.partial(differentiate, range(first, min(first + 4, heads))))
+    for head in range(heads):
+        query, key, value = (
+            packed_ref[(i * heads + head) * seq : (i * heads + head + 1) * seq] for i in range(3)
+        )
+        grad = grad_ref[:, head * width : (head + 1) * width]
+        for i, result in enumerate(head_gradients(visible, query, key, value, grad)):
+            held[i, head] = result
+        copies.append(
+            pltpu.make_async_copy(held.at[:, head], out_ref.at[:, head], head_sems.at[head])
+        )
+        copies[-1].start()
 
     for number, act in enumerate(acts):
         stacked[number * seq : (number + 1) * seq] = act[...]
+    chip, core = place()
     chips = len(sizes) // 2
     size = ready.shape[1]
     spans = [(turn, block * size, size) for turn in range(2 * slots) for block in range(blocks)]
-    if size % 256 == 0:
-        turn, first, _ = spans.pop()
-        spans += [(turn, first, size // 2), (turn, first + size // 2, size // 2)]
     puts = []
     for number, (turn, first, count) in enumerate(spans):
         parity, slot = divmod(turn, slots)

time: 53.7 us -> 53.5 us (level)
  no operation moved by 1% of the time
where the time goes in v14:
time: 53.5 us; the launch traced here: 53.3 us
  Pallas kernels  20 us (37%)
  waiting for transfers between devices  19.5 us (36%)
  starting transfers between devices  12.3 us (23%)
  between operations  0.77 us (1%)
  local copies, waits for them, and re-layouts  0.76 us (1%)
    ppermute x3, waiting for transfers between devices, down(): return lax.ppermute(value, axis, [(i, i - 1) for i in range(1, count)])  13 us
    pallas_call x1, Pallas kernels, finish(): pl.pallas_call(functools.partial(finish_kernel, replicas, counts(options)...  7.72 us
    ppermute x5, starting transfers between devices, rotate(): lax.ppermute(value, axis, [(i, (i + steps) % count) for i in range(count)])  7.59 us
    pallas_call x1, Pallas kernels, forward(): pl.pallas_call(functools.partial(forward_kernel, chips, early, len(parts)...  6.63 us
    ppermute x5, waiting for transfers between devices, rotate(): lax.ppermute(value, axis, [(i, (i + steps) % count) for i in range(count)])  5.57 us
    ppermute x3, starting transfers between devices, down(): return lax.ppermute(value, axis, [(i, i - 1) for i in range(1, count)])  3.86 us
    pallas_call x2, Pallas kernels, project(): pl.pallas_call(functools.partial(project_kernel, tuple(terms), splits), n...  2.2 us
    pallas_call x1, Pallas kernels, late_backward(): pl.pallas_call(late_kernel, name='late_backward', in_specs=[VMEM] * 3, ou...  1.35 us
  transfers between devices with their start and end apart: 13, of which 4 were waited for; matrix products, arithmetic and copies ran while one was open for 0% of the time, Pallas kernels for 34%

profile of v14, /device:TPU:0, one launch (start us, length us, event | category | flops | bytes accessed | tf_op | source)
XLA Modules:
  0.0 53.3 jit_solution(1958193416309730810)
XLA Ops:
  0.6 1.3 %pack.1 = (bf16[3088,128]{1,0:T(8,128)(2,1)S(1)}, bf16[128,768]{1,0:T(8,128)(2,1)S(1)}, bf16[128,768]{1,0:T(8,128)(2,1)S(1)}) custom-call(s32[1,128]{1,0:T(1,128)} %bitcast.18, bf16[3,1536,128]{2,1,0:T(8,128)(2,1)} %bitcast.12, bf16[128,1536]{1,0:T(8,128)(2,1)} %bitcast.15), custom_call_target="tpu_custom_call" | custom-call | tf_op jit(solution)/shard_map/pack/pallas_call | solution.py:85
  1.9 3.1 %collective-permute-start.4 = (bf16[128,768]{1,0:T(8,128)(2,1)S(1)}, bf16[128,768]{1,0:T(8,128)(2,1)S(1)}, u32[]{:S(2)}, u32[]{:S(2)}) collective-permute-start(bf16[128,768]{1,0:T(8,128)(2,1)S(1)} %get-tuple-element.15.refs_0_), channel_id=1, source_target_pairs={{0,4},{2,6},{4,0},{6,2},{1,5},{3,7},{5,1},{7,3},{8,12},{10,14},{12... | collective-permute-start | bytes 589832 | tf_op jit(solution)/shard_map/ppermute | solution.py:30
  5.0 1.3 %collective-permute-start = (bf16[3088,128]{1,0:T(8,128)(2,1)S(1)}, bf16[3088,128]{1,0:T(8,128)(2,1)S(1)}, u32[]{:S(2)}, u32[]{:S(2)}) collective-permute-start(bf16[3088,128]{1,0:T(8,128)(2,1)S(1)} %get-tuple-element.14.packed_ref), channel_id=1, source_target_pairs={{8,0},{16,8},{24,16},{9,1},{17,9},{25,17},{10,2},{18,10},{26,18},{... | collective-permute-start | bytes 2371592 | tf_op jit(solution)/shard_map/ppermute | solution.py:40
  6.3 0.1 collective-permute-start.3
  6.4 0.1 collective-permute-start.1
  6.5 3.9 %collective-permute-done.4.refs_4_.refs_1_.refs_3_ = bf16[128,768]{1,0:T(8,128)(2,1)S(1)} collective-permute-done((bf16[128,768]{1,0:T(8,128)(2,1)S(1)}, bf16[128,768]{1,0:T(8,128)(2,1)S(1)}, u32[]{:S(2)}, u32[]{:S(2)}) %collective-permute-start.4) | collective-permute-done | bytes 196640 | tf_op jit(solution)/shard_map/ppermute | solution.py:30
  10.3 0.0 collective-permute-start.5
  10.4 2.0 %collective-permute-start.8 = (bf16[128,768]{1,0:T(8,128)(2,1)S(1)}, bf16[128,768]{1,0:T(8,128)(2,1)S(1)}, u32[]{:S(2)}, u32[]{:S(2)}) collective-permute-start(bf16[128,768]{1,0:T(8,128)(2,1)S(1)} %choose.1), channel_id=1, source_target_pairs={{0,1},{1,0},{2,3},{3,2},{4,5},{5,4},{6,7},{7,6},{8,9},{9,8},{10,11... | collective-permute-start | bytes 589832 | tf_op jit(solution)/shard_map/ppermute | solution.py:30
  12.4 6.6 %forward.1 = (bf16[128,1536]{1,0:T(8,128)(2,1)S(1)}, f32[128,1536]{1,0:T(8,128)S(1)}, bf16[1536,1536]{1,0:T(8,128)(2,1)S(1)}, bf16[1536,1536]{1,0:T(8,128)(2,1)S(1)}, bf16[1536,1536]{1,0:T(8,128)(2,1)S(1)}) custom-call(bf16[3,12,128,128]{3,2,1,0:T(8,128)(2,1)} %bitcast.13, bf16[6144,1536]{1,0:T(8,128)(2,1)} %bitcast.20, ...), custom_call_target="tpu_custom_call" | custom-call | tf_op jit(solution)/shard_map/forward/pallas_call | solution.py:164
  19.0 0.0 collective-permute-done.1.refs_5_.refs_4_
  19.0 0.1 collective-permute-start.7
  19.2 0.0 collective-permute-done.5.refs_6_
  19.2 0.2 collective-permute-start.2
  19.4 0.0 collective-permute-done.8.refs_8_
  19.4 2.3 %collective-permute-start.9 = (bf16[128,768]{1,0:T(8,128)(2,1)S(1)}, bf16[128,768]{1,0:T(8,128)(2,1)S(1)}, u32[]{:S(2)}, u32[]{:S(2)}) collective-permute-start(bf16[128,768]{1,0:T(8,128)(2,1)S(1)} %collective-permute-done.8.refs_8_), channel_id=1, source_target_pairs={{0,4},{2,6},{4,0},{6,2},{1,5},{3,7},{5,1},{7,3},{8,12},{10,14},{12... | collective-permute-start | bytes 589832 | tf_op jit(solution)/shard_map/ppermute | solution.py:30
  21.7 0.0 collective-permute-done.3.refs_3_.refs_5_
  21.7 1.7 %project.2.refs_2_ = f32[128,1536]{1,0:T(8,128)S(1)} custom-call(bf16[1536,1536]{1,0:T(8,128)(2,1)S(1)} %get-tuple-element.18.refs_0_, bf16[1536,1536]{1,0:T(8,128)(2,1)S(1)} %get-tuple-element.19.refs_1_, bf16[1536,1536]{1,0:T(8,128)(2,1)S(1)} %get-tuple-element.17.refs_2_.refs_0_, bf16[128,1536]{1,0:T(8,128)(2,1)S(1)} %collective-permute-done.3.refs_3_.refs_5_, ...), custom_call_target="tpu_custom_call" | custom-call | tf_op jit(solution)/shard_map/project/pallas_call | solution.py:269
  23.4 0.0 copy-start
  23.4 0.0 copy-start.2
  23.4 0.0 copy-start.1
  23.4 0.0 collective-permute-done.2.refs_1_.refs_7_
  23.5 0.5 project.3
  23.9 0.7 %copy-done = bf16[1,1,3,128,12,128]{5,3,4,2,1,0:T(8,128)(2,1)S(1)} copy-done((bf16[1,1,3,128,12,128]{5,3,4,2,1,0:T(8,128)(2,1)S(1)}, bf16[1,1,3,128,12,128]{5,3,4,2,1,0:T(8,128)(2,1)}, u32[]{:S(2)}) %copy-start) | copy-done | bytes 1179672
  24.7 0.0 copy-done.2
  24.7 1.3 %late_backward.1 = bf16[3,4,128,128]{3,2,1,0:T(8,128)(2,1)S(1)} custom-call(s32[1,128]{1,0:T(1,128)S(1)} %bitcast.19, bf16[3,12,128,128]{3,2,1,0:T(8,128)(2,1)S(1)} %bitcast.14, bf16[128,512]{1,0:T(8,128)(2,1)S(1)} %get-tuple-element.24.grad_ref), custom_call_target="tpu_custom_call" | custom-call | tf_op jit(solution)/shard_map/late_backward/pallas_call | solution.py:210
  26.0 1.3 %collective-permute-start.12 = (bf16[3,4,128,128]{3,2,1,0:T(8,128)(2,1)S(1)}, bf16[3,4,128,128]{3,2,1,0:T(8,128)(2,1)S(1)}, u32[]{:S(2)}, u32[]{:S(2)}) collective-permute-start(bf16[3,4,128,128]{3,2,1,0:T(8,128)(2,1)S(1)} %late_backward.1), channel_id=1, source_target_pairs={{8,0},{16,8},{24,16},{9,1},{17,9},{25,17},{10,2},{18,10},{26,18},{... | collective-permute-start | bytes 1179656 | tf_op jit(solution)/shard_map/ppermute | solution.py:40
  27.3 1.3 %collective-permute-start.6 = (bf16[128,1024]{1,0:T(8,128)(2,1)S(1)}, bf16[128,1024]{1,0:T(8,128)(2,1)S(1)}, u32[]{:S(2)}, u32[]{:S(2)}) collective-permute-start(bf16[128,1024]{1,0:T(8,128)(2,1)S(1)} %get-tuple-element.21), channel_id=1, source_target_pairs={{8,0},{16,8},{24,16},{9,1},{17,9},{25,17},{10,2},{18,10},{26,18},{... | collective-permute-start | bytes 786440 | tf_op jit(solution)/shard_map/ppermute | solution.py:40
  28.6 1.7 %collective-permute-done.7.refs_1_ = bf16[128,1536]{1,0:T(8,128)(2,1)S(1)} collective-permute-done((bf16[128,1536]{1,0:T(8,128)(2,1)S(1)}, bf16[128,1536]{1,0:T(8,128)(2,1)S(1)}, u32[]{:S(2)}, u32[]{:S(2)}) %collective-permute-start.7) | collective-permute-done | bytes 393248 | tf_op jit(solution)/shard_map/ppermute | solution.py:30
  30.3 0.0 collective-permute-start.10
  30.3 0.0 collective-permute-done.9.refs_9_
  30.3 0.5 collective-permute-start.11
  30.8 0.9 %collective-permute-done.10.refs_10_ = bf16[128,768]{1,0:T(8,128)(2,1)S(1)} collective-permute-done((bf16[128,768]{1,0:T(8,128)(2,1)S(1)}, bf16[128,768]{1,0:T(8,128)(2,1)S(1)}, u32[]{:S(2)}, u32[]{:S(2)}) %collective-permute-start.10) | collective-permute-done | bytes 196640 | tf_op jit(solution)/shard_map/ppermute | solution.py:35
  31.8 13.0 %collective-permute-done.6.grad_ref = bf16[128,1024]{1,0:T(8,128)(2,1)S(1)} collective-permute-done((bf16[128,1024]{1,0:T(8,128)(2,1)S(1)}, bf16[128,1024]{1,0:T(8,128)(2,1)S(1)}, u32[]{:S(2)}, u32[]{:S(2)}) %collective-permute-start.6) | collective-permute-done | bytes 262176 | tf_op jit(solution)/shard_map/ppermute | solution.py:40
  44.7 0.0 collective-permute-done.11.refs_11_
  44.7 0.0 collective-permute-done.packed_ref
  44.7 0.0 copy-done.1
  44.7 7.7 %finish.1 = (bf16[3,12,128,128]{3,2,1,0:T(8,128)(2,1)}, bf16[3072,1536]{1,0:T(8,128)(2,1)}) custom-call(bf16[3088,128]{1,0:T(8,128)(2,1)S(1)} %collective-permute-done.packed_ref, bf16[128,1024]{1,0:T(8,128)(2,1)S(1)} %collective-permute-done.6.grad_ref, bf16[128,1536]{1,0:T(8,128)(2,1)S(1)} %get-tuple-element.22.refs_0_, ...), custom_call_target="tpu_custom_call" | custom-call | tf_op jit(solution)/shard_map/finish/pallas_call | solution.py:382
  52.5 0.0 collective-permute-done.12.late_ref
  52.5 0.8 %fill.1 = bf16[3,12,128,128]{3,2,1,0:T(8,128)(2,1)} custom-call(bf16[3,4,128,128]{3,2,1,0:T(8,128)(2,1)S(1)} %collective-permute-done.12.late_ref, bf16[3,12,128,128]{3,2,1,0:T(8,128)(2,1)} %get-tuple-element.25.whole_ref), custom_call_target="tpu_custom_call", output_to_operand_aliasing={{}: (1, {})} | custom-call | tf_op jit(solution)/shard_map/fill/pallas_call | solution.py:234
  (1 shorter events, 0.0 us)
Async XLA Ops:
  1.9 8.4 %collective-permute-start.4 = (bf16[128,768]{1,0:T(8,128)(2,1)S(1)}, bf16[128,768]{1,0:T(8,128)(2,1)S(1)}, u32[]{:S(2)}, u32[]{:S(2)}) collective-permute-start(bf16[128,768]{1,0:T(8,128)(2,1)S(1)} %get-tuple-element.15.refs_0_), channel_id=1, source_target_pairs={{0,4},{2,6},{4,0},{6,2},{1,5},{3,7},{5,1},{7,3},{8,12},{10,14},{12... | collective-permute-start | bytes 589832 | tf_op jit(solution)/shard_map/ppermute | solution.py:30
  5.0 39.7 %collective-permute-start = (bf16[3088,128]{1,0:T(8,128)(2,1)S(1)}, bf16[3088,128]{1,0:T(8,128)(2,1)S(1)}, u32[]{:S(2)}, u32[]{:S(2)}) collective-permute-start(bf16[3088,128]{1,0:T(8,128)(2,1)S(1)} %get-tuple-element.14.packed_ref), channel_id=1, source_target_pairs={{8,0},{16,8},{24,16},{9,1},{17,9},{25,17},{10,2},{18,10},{26,18},{... | collective-permute-start | bytes 2371592 | tf_op jit(solution)/shard_map/ppermute | solution.py:40
  6.3 15.4 %collective-permute-start.3 = (bf16[128,1536]{1,0:T(8,128)(2,1)}, bf16[128,1536]{1,0:T(8,128)(2,1)S(1)}, u32[]{:S(2)}, u32[]{:S(2)}) collective-permute-start(bf16[128,1536]{1,0:T(8,128)(2,1)} %bitcast.16), channel_id=1, source_target_pairs={{0,2},{2,0},{4,6},{6,4},{1,3},{3,1},{5,7},{7,5},{8,10},{10,8},{12,... | collective-permute-start | bytes 1179656 | tf_op jit(solution)/shard_map/ppermute | solution.py:35
  6.4 12.6 %collective-permute-start.1 = (bf16[128,768]{1,0:T(8,128)(2,1)S(1)}, bf16[128,768]{1,0:T(8,128)(2,1)S(1)}, u32[]{:S(2)}, u32[]{:S(2)}) collective-permute-start(bf16[128,768]{1,0:T(8,128)(2,1)S(1)} %get-tuple-element.16.refs_1_.refs_0_), channel_id=1, source_target_pairs={{0,4},{2,6},{4,0},{6,2},{1,5},{3,7},{5,1},{7,3},{8,12},{10,14},{12... | collective-permute-start | bytes 589832 | tf_op jit(solution)/shard_map/ppermute | solution.py:30
  10.3 8.8 %collective-permute-start.5 = (bf16[128,768]{1,0:T(8,128)(2,1)S(1)}, bf16[128,768]{1,0:T(8,128)(2,1)S(1)}, u32[]{:S(2)}, u32[]{:S(2)}) collective-permute-start(bf16[128,768]{1,0:T(8,128)(2,1)S(1)} %collective-permute-done.4.refs_4_.refs_1_.refs_3_), channel_id=1, source_target_pairs={{0,2},{2,0},{4,6},{6,4},{1,3},{3,1},{5,7},{7,5},{8,10},{10,8},{12,... | collective-permute-start | bytes 589832 | tf_op jit(solution)/shard_map/ppermute | solution.py:35
  10.4 9.0 %collective-permute-start.8 = (bf16[128,768]{1,0:T(8,128)(2,1)S(1)}, bf16[128,768]{1,0:T(8,128)(2,1)S(1)}, u32[]{:S(2)}, u32[]{:S(2)}) collective-permute-start(bf16[128,768]{1,0:T(8,128)(2,1)S(1)} %choose.1), channel_id=1, source_target_pairs={{0,1},{1,0},{2,3},{3,2},{4,5},{5,4},{6,7},{7,6},{8,9},{9,8},{10,11... | collective-permute-start | bytes 589832 | tf_op jit(solution)/shard_map/ppermute | solution.py:30
  19.0 11.3 %collective-permute-start.7 = (bf16[128,1536]{1,0:T(8,128)(2,1)S(1)}, bf16[128,1536]{1,0:T(8,128)(2,1)S(1)}, u32[]{:S(2)}, u32[]{:S(2)}) collective-permute-start(bf16[128,1536]{1,0:T(8,128)(2,1)S(1)} %get-tuple-element.22.refs_0_), channel_id=1, source_target_pairs={{0,1},{1,0},{2,3},{3,2},{4,5},{5,4},{6,7},{7,6},{8,9},{9,8},{10,11... | collective-permute-start | bytes 1179656 | tf_op jit(solution)/shard_map/ppermute | solution.py:30
  19.2 4.3 %collective-permute-start.2 = (bf16[128,768]{1,0:T(8,128)(2,1)S(1)}, bf16[128,768]{1,0:T(8,128)(2,1)S(1)}, u32[]{:S(2)}, u32[]{:S(2)}) collective-permute-start(bf16[128,768]{1,0:T(8,128)(2,1)S(1)} %collective-permute-done.1.refs_5_.refs_4_), channel_id=1, source_target_pairs={{0,2},{2,0},{4,6},{6,4},{1,3},{3,1},{5,7},{7,5},{8,10},{10,8},{12,... | collective-permute-start | bytes 589832 | tf_op jit(solution)/shard_map/ppermute | solution.py:35
  19.4 10.9 %collective-permute-start.9 = (bf16[128,768]{1,0:T(8,128)(2,1)S(1)}, bf16[128,768]{1,0:T(8,128)(2,1)S(1)}, u32[]{:S(2)}, u32[]{:S(2)}) collective-permute-start(bf16[128,768]{1,0:T(8,128)(2,1)S(1)} %collective-permute-done.8.refs_8_), channel_id=1, source_target_pairs={{0,4},{2,6},{4,0},{6,2},{1,5},{3,7},{5,1},{7,3},{8,12},{10,14},{12... | collective-permute-start | bytes 589832 | tf_op jit(solution)/shard_map/ppermute | solution.py:30
  23.4 1.3 %copy-start = (bf16[1,1,3,128,12,128]{5,3,4,2,1,0:T(8,128)(2,1)S(1)}, bf16[1,1,3,128,12,128]{5,3,4,2,1,0:T(8,128)(2,1)}, u32[]{:S(2)}) copy-start(bf16[1,1,3,128,12,128]{5,3,4,2,1,0:T(8,128)(2,1)} %param.4) | copy-start | bytes 3538948
  23.4 1.3 %copy-start.2 = (s32[1,1,128]{2,1,0:T(1,128)S(1)}, s32[1,1,128]{2,1,0:T(1,128)}, u32[]{:S(2)}) copy-start(s32[1,1,128]{2,1,0:T(1,128)} %param.5) | copy-start | bytes 1540
  23.4 21.3 %copy-start.1 = (bf16[1,1,128,1536]{3,2,1,0:T(8,128)(2,1)S(1)}, bf16[1,1,128,1536]{3,2,1,0:T(8,128)(2,1)}, u32[]{:S(2)}) copy-start(bf16[1,1,128,1536]{3,2,1,0:T(8,128)(2,1)} %param.7) | copy-start | bytes 1179652
  26.0 26.4 %collective-permute-start.12 = (bf16[3,4,128,128]{3,2,1,0:T(8,128)(2,1)S(1)}, bf16[3,4,128,128]{3,2,1,0:T(8,128)(2,1)S(1)}, u32[]{:S(2)}, u32[]{:S(2)}) collective-permute-start(bf16[3,4,128,128]{3,2,1,0:T(8,128)(2,1)S(1)} %late_backward.1), channel_id=1, source_target_pairs={{8,0},{16,8},{24,16},{9,1},{17,9},{25,17},{10,2},{18,10},{26,18},{... | collective-permute-start | bytes 1179656 | tf_op jit(solution)/shard_map/ppermute | solution.py:40
  27.3 17.4 %collective-permute-start.6 = (bf16[128,1024]{1,0:T(8,128)(2,1)S(1)}, bf16[128,1024]{1,0:T(8,128)(2,1)S(1)}, u32[]{:S(2)}, u32[]{:S(2)}) collective-permute-start(bf16[128,1024]{1,0:T(8,128)(2,1)S(1)} %get-tuple-element.21), channel_id=1, source_target_pairs={{8,0},{16,8},{24,16},{9,1},{17,9},{25,17},{10,2},{18,10},{26,18},{... | collective-permute-start | bytes 786440 | tf_op jit(solution)/shard_map/ppermute | solution.py:40
  30.3 1.4 %collective-permute-start.10 = (bf16[128,768]{1,0:T(8,128)(2,1)S(1)}, bf16[128,768]{1,0:T(8,128)(2,1)S(1)}, u32[]{:S(2)}, u32[]{:S(2)}) collective-permute-start(bf16[128,768]{1,0:T(8,128)(2,1)S(1)} %collective-permute-done.8.refs_8_), channel_id=1, source_target_pairs={{0,2},{2,0},{4,6},{6,4},{1,3},{3,1},{5,7},{7,5},{8,10},{10,8},{12,... | collective-permute-start | bytes 589832 | tf_op jit(solution)/shard_map/ppermute | solution.py:35
  30.3 14.4 %collective-permute-start.11 = (bf16[128,768]{1,0:T(8,128)(2,1)S(1)}, bf16[128,768]{1,0:T(8,128)(2,1)S(1)}, u32[]{:S(2)}, u32[]{:S(2)}) collective-permute-start(bf16[128,768]{1,0:T(8,128)(2,1)S(1)} %collective-permute-done.9.refs_9_), channel_id=1, source_target_pairs={{0,2},{2,0},{4,6},{6,4},{1,3},{3,1},{5,7},{7,5},{8,10},{10,8},{12,... | collective-permute-start | bytes 589832 | tf_op jit(solution)/shard_map/ppermute | solution.py:35
